TPU v7x, 32 devices: a whole 2x2x4 slice. The times are simulated.
32 devices in a mesh: items: 16 (over z, y, core), seq: 2 (over x).
Axes of the slice: x: 2, y: 2, z: 4, core: 2. Of those that a mesh axis runs over, the one named last changes fastest.
Arguments:
- tokens: bfloat16 [16, 1280, 1024], P('items', 'seq'), may hold values from -6 to 6
- cotangent: bfloat16 [16, 1280, 1024], P('items', 'seq'), may hold values from -6 to 6
- prompt_len: int32 [16], P('items'), may hold values from 150 to 600
- section_ids: int32 [16], P('items'), may hold values from 0 to 7
- section_table: bfloat16 [8, 1024], replicated, may hold values from -6 to 6
- w_query: bfloat16 [1024, 1024], P('items'), may hold values from -0.1875 to 0.1875
- w_key: bfloat16 [1024, 1024], P('items'), may hold values from -0.1875 to 0.1875
- w_value: bfloat16 [1024, 1024], P('items'), may hold values from -0.1875 to 0.1875
- w_out: bfloat16 [1024, 1024], P('items'), may hold values from -4 to 4
- w_up: bfloat16 [1024, 4096], P('items'), may hold values from -0.1875 to 0.1875
- w_down: bfloat16 [4096, 1024], P('items'), may hold values from -0.09375 to 0.09375
- w_ada_one: bfloat16 [1024, 2048], P('items'), may hold values from -0.09375 to 0.09375
- w_ada_two: bfloat16 [1024, 2048], P('items'), may hold values from -0.09375 to 0.09375
Outputs:
- layer_out: bfloat16 [16, 1280, 1024], P('items', 'seq')
- input_grad: float32 [16, 1280, 1024], P('items', 'seq')
- grad_query: float32 [1024, 1024], P(('items', 'seq'))
- grad_key: float32 [1024, 1024], P(('items', 'seq'))
- grad_value: float32 [1024, 1024], P(('items', 'seq'))
- grad_out: float32 [1024, 1024], P(('items', 'seq'))
- grad_up: float32 [1024, 4096], P(('items', 'seq'))
- grad_down: float32 [4096, 1024], P(('items', 'seq'))
- grad_ada_one: float32 [1024, 2048], P(('items', 'seq'))
- grad_ada_two: float32 [1024, 2048], P(('items', 'seq'))
- grad_table: float32 [8, 1024], P(None, ('items', 'seq'))
Inputs may be any that keep to these rules, and one draw needn't show every extreme that they name: `prompt_len`: prompt frames at and past an item's length are padding. `section_ids`: the number of items per section is uneven across sections.
All inputs are finite; a program needn't handle non-finite values.
Results may differ from a plain program's by a relative error of at most 0.019.
Values may be sent and summed in bfloat16 or wider, within the bound.
No kernel may reach another device: no remote copies, remote signals or barrier semaphores. Data moves between devices by JAX's collectives and lax.ppermute only.
A program may use at most 384 MiB of HBM per device.

v0:
```python
from functools import partial
import math

import jax
import jax.numpy as jnp
from jax import lax
from jax.sharding import PartitionSpec as P

HEADS = 16
HEAD_DIM = 64
PROMPT = 640


EPSILON = 1e-05
MASKED = -1e30


def exact(left, right):
    return jnp.dot(left, right, precision=lax.Precision.HIGHEST)


def dot_rows(left, right):
    return lax.dot_general(
        left, right, (((0,), (0,)), ((), ())), preferred_element_type=jnp.float32
    )


def dot_last(left, right):
    return lax.dot_general(
        left, right, (((1,), (1,)), ((), ())), preferred_element_type=jnp.float32
    )


def ada_norm(values, ada):
    width = values.shape[-1]
    centred = values - jnp.mean(values, axis=-1, keepdims=True)
    spread = jnp.mean(centred * centred, axis=-1, keepdims=True)
    normed = centred * lax.rsqrt(spread + EPSILON)
    return (1.0 + ada[:, None, :width]) * normed + ada[:, None, width:]


def split_heads(block):
    return block.reshape(block.shape[0], HEADS, HEAD_DIM)


def frames_major(grad, dim, items_count, seq_count):
    shape = grad.shape
    piece = shape[dim] // (items_count * seq_count)
    parted = grad.reshape(shape[:dim] + (items_count, seq_count, piece) + shape[dim + 1 :])
    return jnp.swapaxes(parted, dim, dim + 1).reshape(shape)


def shards(
    tokens,
    cotangent,
    prompt_len,
    section_ids,
    section_table,
    w_query,
    w_key,
    w_value,
    w_out,
    w_up,
    w_down,
    w_ada_one,
    w_ada_two,
):
    full_query, full_key, full_value, full_out, full_up, full_down, full_ada_one, full_ada_two = (
        lax.all_gather(w_query, "items", axis=0, tiled=True),
        lax.all_gather(w_key, "items", axis=0, tiled=True),
        lax.all_gather(w_value, "items", axis=0, tiled=True),
        lax.all_gather(w_out, "items", axis=0, tiled=True),
        lax.all_gather(w_up, "items", axis=0, tiled=True),
        lax.all_gather(w_down, "items", axis=0, tiled=True),
        lax.all_gather(w_ada_one, "items", axis=0, tiled=True),
        lax.all_gather(w_ada_two, "items", axis=0, tiled=True),
    )
    batch, rows, width = tokens.shape
    items_count = lax.axis_size("items")
    seq_count = lax.axis_size("seq")
    frames_all = rows * seq_count
    scale = 1.0 / math.sqrt(HEAD_DIM)
    position = lax.axis_index("seq") * rows + jnp.arange(rows)
    key_place = jnp.arange(frames_all)
    inputs = tokens.astype(jnp.float32)
    choose = (section_ids[:, None] == jnp.arange(section_table.shape[0])[None, :]).astype(
        jnp.float32
    )
    cond = exact(choose, section_table.astype(jnp.float32))
    ada_one_w = full_ada_one.astype(jnp.float32)
    ada_two_w = full_ada_two.astype(jnp.float32)
    ada_one = exact(cond, ada_one_w)
    ada_two = exact(cond, ada_two_w)
    normed_one, back_one = jax.vjp(ada_norm, inputs, ada_one)
    low_one = normed_one.astype(jnp.bfloat16).reshape(-1, width)
    query = (
        jnp.dot(low_one, full_query, preferred_element_type=jnp.float32)
        .astype(jnp.bfloat16)
        .reshape(batch, rows, width)
    )
    keys_here = (
        jnp.dot(low_one, full_key, preferred_element_type=jnp.float32)
        .astype(jnp.bfloat16)
        .reshape(batch, rows, width)
    )
    values_here = (
        jnp.dot(low_one, full_value, preferred_element_type=jnp.float32)
        .astype(jnp.bfloat16)
        .reshape(batch, rows, width)
    )
    keys_all, values_all = (
        lax.all_gather(keys_here, "seq", axis=1, tiled=True),
        lax.all_gather(values_here, "seq", axis=1, tiled=True),
    )

    def masked_scores(query_item, keys_item, length, query_place, key_spot):
        raw = (
            jnp.einsum(
                "qhd,khd->hqk",
                split_heads(query_item),
                split_heads(keys_item),
                preferred_element_type=jnp.float32,
            )
            * scale
        )
        allowed = (key_spot[None, :] < length) | (key_spot[None, :] >= PROMPT) & (
            query_place[:, None] >= PROMPT
        )
        return jnp.where(allowed[None], raw, MASKED)

    def attend(packed):
        query_item, keys_item, values_item, length = packed
        scores = masked_scores(query_item, keys_item, length, position, key_place)
        peak = jnp.max(scores, axis=-1, keepdims=True)
        expo = jnp.exp(scores - peak)
        total = jnp.sum(expo, axis=-1, keepdims=True)
        probs = (expo / total).astype(jnp.bfloat16)
        mixed_item = jnp.einsum(
            "hqk,khd->qhd", probs, split_heads(values_item), preferred_element_type=jnp.float32
        )
        return (
            mixed_item.astype(jnp.bfloat16).reshape(rows, width),
            (peak + jnp.log(total))[..., 0],
        )

    mixed, log_total = lax.map(attend, (query, keys_all, values_all, prompt_len))
    mixed_flat = mixed.reshape(-1, width)
    attended = inputs + jnp.dot(mixed_flat, full_out, preferred_element_type=jnp.float32).reshape(
        batch, rows, width
    )
    normed_two, back_two = jax.vjp(ada_norm, attended, ada_two)
    low_two = normed_two.astype(jnp.bfloat16).reshape(-1, width)
    upward = jnp.dot(low_two, full_up, preferred_element_type=jnp.float32)
    active, gelu_back = jax.vjp(partial(jax.nn.gelu, approximate=False), upward)
    active_low = active.astype(jnp.bfloat16)
    layer_out = (
        attended
        + jnp.dot(active_low, full_down, preferred_element_type=jnp.float32).reshape(
            batch, rows, width
        )
    ).astype(jnp.bfloat16)
    grad_top = cotangent.astype(jnp.float32)
    grad_low = cotangent.reshape(-1, width)
    grad_down = dot_rows(active_low, grad_low)
    (grad_upward,) = gelu_back(dot_last(grad_low, full_down))
    upward_low = grad_upward.astype(jnp.bfloat16)
    grad_up = dot_rows(low_two, upward_low)
    grad_normed_two = dot_last(upward_low, full_up).reshape(batch, rows, width)
    back_mid, grad_ada_two_rows = back_two(grad_normed_two)
    grad_attended = grad_top + back_mid
    grad_ada_two = exact(cond.T, grad_ada_two_rows)
    attended_low = grad_attended.astype(jnp.bfloat16).reshape(-1, width)
    grad_out = dot_rows(mixed_flat, attended_low)
    grad_mixed = dot_last(attended_low, full_out).astype(jnp.bfloat16).reshape(batch, rows, width)

    def score_grads(
        query_item, keys_item, values_item, length, log_item, grad_item, query_place, key_spot
    ):
        scores = masked_scores(query_item, keys_item, length, query_place, key_spot)
        probs = jnp.exp(scores - log_item[..., None])
        grad_heads = split_heads(grad_item)
        grad_probs = jnp.einsum(
            "qhd,khd->hqk", grad_heads, split_heads(values_item), preferred_element_type=jnp.float32
        )
        inner = jnp.sum(probs * grad_probs, axis=-1, keepdims=True)
        grad_scores = (probs * (grad_probs - inner)).astype(jnp.bfloat16)
        return (probs, grad_heads, grad_scores, inner[..., 0])

    def attend_back(packed):
        query_item, keys_item, values_item, length, log_item, grad_item = packed
        probs, grad_heads, grad_scores, inner = score_grads(
            query_item, keys_item, values_item, length, log_item, grad_item, position, key_place
        )
        grad_query_item = (
            jnp.einsum(
                "hqk,khd->qhd",
                grad_scores,
                split_heads(keys_item),
                preferred_element_type=jnp.float32,
            )
            * scale
        )
        grad_keys_item = (
            jnp.einsum(
                "hqk,qhd->khd",
                grad_scores,
                split_heads(query_item),
                preferred_element_type=jnp.float32,
            )
            * scale
        )
        grad_values_item = jnp.einsum(
            "hqk,qhd->khd",
            probs.astype(jnp.bfloat16),
            grad_heads,
            preferred_element_type=jnp.float32,
        )
        return (
            grad_query_item.reshape(rows, width),
            grad_keys_item.reshape(frames_all, width),
            grad_values_item.reshape(frames_all, width),
        )

    grad_query_rows, grad_keys_all, grad_values_all = lax.map(
        attend_back, (query, keys_all, values_all, prompt_len, log_total, grad_mixed)
    )
    grad_keys_here, grad_values_here = (
        lax.psum_scatter(
            grad_keys_all.astype(jnp.bfloat16), "seq", scatter_dimension=1, tiled=True
        ).astype(jnp.float32),
        lax.psum_scatter(
            grad_values_all.astype(jnp.bfloat16), "seq", scatter_dimension=1, tiled=True
        ).astype(jnp.float32),
    )
    query_low = grad_query_rows.astype(jnp.bfloat16).reshape(-1, width)
    keys_low = grad_keys_here.astype(jnp.bfloat16).reshape(-1, width)
    values_low = grad_values_here.astype(jnp.bfloat16).reshape(-1, width)
    grad_query = dot_rows(low_one, query_low)
    grad_key = dot_rows(low_one, keys_low)
    grad_value = dot_rows(low_one, values_low)
    grad_normed_one = (
        dot_last(query_low, full_query)
        + dot_last(keys_low, full_key)
        + dot_last(values_low, full_value)
    )
    back_in, grad_ada_one_rows = back_one(grad_normed_one.reshape(batch, rows, width))
    input_grad = grad_attended + back_in
    grad_ada_one = exact(cond.T, grad_ada_one_rows)
    grad_cond = exact(grad_ada_one_rows, ada_one_w.T) + exact(grad_ada_two_rows, ada_two_w.T)
    grad_table = exact(choose.T, grad_cond)
    table_t = frames_major(grad_table, 1, items_count, seq_count)
    part_query = frames_major(grad_query, 0, items_count, seq_count)
    part_key = frames_major(grad_key, 0, items_count, seq_count)
    part_value = frames_major(grad_value, 0, items_count, seq_count)
    part_out = frames_major(grad_out, 0, items_count, seq_count)
    part_ada_one = frames_major(grad_ada_one, 0, items_count, seq_count)
    part_up = frames_major(grad_up, 0, items_count, seq_count)
    part_down = frames_major(grad_down, 0, items_count, seq_count)
    part_ada_two = frames_major(grad_ada_two, 0, items_count, seq_count)
    (
        seq_query,
        seq_key,
        seq_value,
        seq_out,
        seq_up,
        seq_down,
        seq_ada_one,
        seq_ada_two,
        seq_table,
    ) = (
        lax.psum_scatter(
            part_query.astype(jnp.bfloat16), "seq", scatter_dimension=0, tiled=True
        ).astype(jnp.float32),
        lax.psum_scatter(
            part_key.astype(jnp.bfloat16), "seq", scatter_dimension=0, tiled=True
        ).astype(jnp.float32),
        lax.psum_scatter(
            part_value.astype(jnp.bfloat16), "seq", scatter_dimension=0, tiled=True
        ).astype(jnp.float32),
        lax.psum_scatter(
            part_out.astype(jnp.bfloat16), "seq", scatter_dimension=0, tiled=True
        ).astype(jnp.float32),
        lax.psum_scatter(
            part_up.astype(jnp.bfloat16), "seq", scatter_dimension=0, tiled=True
        ).astype(jnp.float32),
        lax.psum_scatter(
            part_down.astype(jnp.bfloat16), "seq", scatter_dimension=0, tiled=True
        ).astype(jnp.float32),
        lax.psum_scatter(
            part_ada_one.astype(jnp.bfloat16), "seq", scatter_dimension=0, tiled=True
        ).astype(jnp.float32),
        lax.psum_scatter(
            part_ada_two.astype(jnp.bfloat16), "seq", scatter_dimension=0, tiled=True
        ).astype(jnp.float32),
        lax.psum_scatter(
            table_t.astype(jnp.bfloat16), "seq", scatter_dimension=1, tiled=True
        ).astype(jnp.float32),
    )
    (
        grad_query,
        grad_key,
        grad_value,
        grad_out,
        grad_up,
        grad_down,
        grad_ada_one,
        grad_ada_two,
        grad_table,
    ) = (
        lax.psum_scatter(
            seq_query.astype(jnp.bfloat16), "items", scatter_dimension=0, tiled=True
        ).astype(jnp.float32),
        lax.psum_scatter(
            seq_key.astype(jnp.bfloat16), "items", scatter_dimension=0, tiled=True
        ).astype(jnp.float32),
        lax.psum_scatter(
            seq_value.astype(jnp.bfloat16), "items", scatter_dimension=0, tiled=True
        ).astype(jnp.float32),
        lax.psum_scatter(
            seq_out.astype(jnp.bfloat16), "items", scatter_dimension=0, tiled=True
        ).astype(jnp.float32),
        lax.psum_scatter(
            seq_up.astype(jnp.bfloat16), "items", scatter_dimension=0, tiled=True
        ).astype(jnp.float32),
        lax.psum_scatter(
            seq_down.astype(jnp.bfloat16), "items", scatter_dimension=0, tiled=True
        ).astype(jnp.float32),
        lax.psum_scatter(
            seq_ada_one.astype(jnp.bfloat16), "items", scatter_dimension=0, tiled=True
        ).astype(jnp.float32),
        lax.psum_scatter(
            seq_ada_two.astype(jnp.bfloat16), "items", scatter_dimension=0, tiled=True
        ).astype(jnp.float32),
        lax.psum_scatter(
            seq_table.astype(jnp.bfloat16), "items", scatter_dimension=1, tiled=True
        ).astype(jnp.float32),
    )
    return (
        layer_out,
        input_grad,
        grad_query,
        grad_key,
        grad_value,
        grad_out,
        grad_up,
        grad_down,
        grad_ada_one,
        grad_ada_two,
        grad_table,
    )


def solution(mesh):
    return jax.shard_map(
        shards,
        mesh=mesh,
        in_specs=(
            P("items", "seq", None),
            P("items", "seq", None),
            P("items"),
            P("items"),
            P(),
            P("items", None),
            P("items", None),
            P("items", None),
            P("items", None),
            P("items", None),
            P("items", None),
            P("items", None),
            P("items", None),
        ),
        out_specs=(
            P("items", "seq", None),
            P("items", "seq", None),
            P(("items", "seq"), None),
            P(("items", "seq"), None),
            P(("items", "seq"), None),
            P(("items", "seq"), None),
            P(("items", "seq"), None),
            P(("items", "seq"), None),
            P(("items", "seq"), None),
            P(("items", "seq"), None),
            P(None, ("items", "seq")),
        ),
        check_vma=False,
    )
```

profile of v0, /device:TPU:0, one launch (start us, length us, event | category | flops | bytes accessed | tf_op | source)
XLA Modules:
  0.0 1794.9 jit_solution(3981334618277993144)
XLA Ops:
  14.1 49.4 %all-gather.13.cloned.1.call-done = bf16[1024,2048]{1,0:T(8,128)(2,1)} async-done(((bf16[64,2048]{1,0:T(8,128)(2,1)}), bf16[1024,2048]{1,0:T(8,128)(2,1)}) %all-gather.13.cloned.1.call-update) | async-done | bytes 4194320 | tf_op jit(solution)/shard_map/all_gather | solution.py:75
  67.4 38.1 %all-gather.19.cloned.1.call-done = bf16[1024,1024]{1,0:T(8,128)(2,1)} async-done(((bf16[64,1024]{1,0:T(8,128)(2,1)}), bf16[1024,1024]{1,0:T(8,128)(2,1)}) %all-gather.19.cloned.1.call-update) | async-done | bytes 2097168 | tf_op jit(solution)/shard_map/all_gather | solution.py:70
  109.9 38.1 %all-gather.15.cloned.1.call-done = bf16[1024,1024]{1,0:T(8,128)(2,1)} async-done(((bf16[64,1024]{1,0:T(8,128)(2,1)}), bf16[1024,1024]{1,0:T(8,128)(2,1)}) %all-gather.15.cloned.1.call-update) | async-done | bytes 2097168 | tf_op jit(solution)/shard_map/all_gather | solution.py:71
  156.1 43.2 %all-gather.23.cloned.1.call-done = bf16[1024,2048]{1,0:T(8,128)(2,1)} async-done(((bf16[64,2048]{1,0:T(8,128)(2,1)}), bf16[1024,2048]{1,0:T(8,128)(2,1)}) %all-gather.23.cloned.1.call-update) | async-done | bytes 4194320 | tf_op jit(solution)/shard_map/all_gather | solution.py:76
  203.3 38.0 %all-gather.17.cloned.1.call-done = bf16[1024,1024]{1,0:T(8,128)(2,1)} async-done(((bf16[64,1024]{1,0:T(8,128)(2,1)}), bf16[1024,1024]{1,0:T(8,128)(2,1)}) %all-gather.17.cloned.1.call-update) | async-done | bytes 2097168 | tf_op jit(solution)/shard_map/all_gather | solution.py:69
  245.9 35.2 %all-gather.31.cloned.1.call-done = bf16[1280,1024]{1,0:T(8,128)(2,1)} async-done(((bf16[640,1024]{1,0:T(8,128)(2,1)}), bf16[1280,1024]{1,0:T(8,128)(2,1)}) %all-gather.31.cloned.1.call-update) | async-done | bytes 2621456 | tf_op jit(solution)/shard_map/all_gather | solution.py:112
  284.1 23.1 %fusion.93 = (f32[16,640]{1,0:T(8,128)S(1)}, f32[16,640,1280]{2,1,0:T(8,128)}) fusion(bf16[640,16,64]{0,2,1:T(8,128)(2,1)} %bitcast.284, bf16[1280,16,64]{0,2,1:T(8,128)(2,1)S(1)} %bitcast.278, pred[640,1280]{1,0:T(8,128)(4,1)S(1)} %and_or_fusion), kind=kOutput, calls=%fused_computation.153 | convolution fusion | flops 1717032960 | bytes 57221120 | tf_op jit(solution)/shard_map/while/body/eval_jaxpr/qhd,khd->hqk/dot_general | solution.py:118
  307.2 16.8 fusion
  328.4 20.2 %fusion.50 = bf16[16,64,640]{2,1,0:T(8,128)(2,1)S(1)} fusion(bf16[1280,16,64]{0,2,1:T(8,128)(2,1)} %bitcast.289, f32[16,640,1280]{2,1,0:T(8,128)} %get-tuple-element.90, f32[16,640]{1,0:T(8,128)S(1)} %fusion, f32[16,640]{1,0:T(8,128)S(1)} %get-tuple-element.89), kind=kOutput, calls=%fused_computation.97 | convolution fusion | flops 1717698560 | bytes 56442880 | tf_op jit(solution)/shard_map/while/body/eval_jaxpr/hqk,khd->qhd/dot_general | solution.py:138
  348.6 17.3 all-gather.21.cloned.1.call-done
  371.1 70.7 %all-gather.25.cloned.1.call-done = bf16[1024,4096]{1,0:T(8,128)(2,1)} async-done(((bf16[64,4096]{1,0:T(8,128)(2,1)}), bf16[1024,4096]{1,0:T(8,128)(2,1)}) %all-gather.25.cloned.1.call-update) | async-done | bytes 8388624 | tf_op jit(solution)/shard_map/all_gather | solution.py:73
  441.8 32.3 %fusion.6 = (f32[640,4096]{1,0:T(8,128)}, f32[640,4096]{1,0:T(8,128)}) fusion(bf16[1024,4096]{1,0:T(8,128)(2,1)} %all-gather.25.cloned.1.call-done, f32[1024]{0:T(1024)S(1)} %bitcast.330, f32[640]{0:T(1024)S(1)} %fusion.78, f32[1,640,1024]{2,1,0:T(8,128)} %copy-done.6, f32[640]{0:T(1024)S(1)} %broadcast_multiply_fusion, f32[1024]{0:T(1024)S(1)} %bitcast.310), kind=kOutput, calls=%fused_computation.13 | convolution fusion | flops 5534515200 | bytes 31994880 | tf_op jit(solution)/shard_map/dot_general | solution.py:153
  474.2 42.8 %all-gather.27.cloned.1.call-done = bf16[4096,1024]{1,0:T(8,128)(2,1)} async-done(((bf16[256,1024]{1,0:T(8,128)(2,1)}), bf16[4096,1024]{1,0:T(8,128)(2,1)}) %all-gather.27.cloned.1.call-update) | async-done | bytes 8388624 | tf_op jit(solution)/shard_map/all_gather | solution.py:74
  517.0 16.8 add_convert_fusion
  533.8 10.0 fusion.95
  551.9 38.6 %multiply_reduce_fusion = (f32[16,640]{1,0:T(8,128)S(1)}, f32[16,640,1280]{2,1,0:T(8,128)}) fusion(f32[16,640,1280]{2,1,0:T(8,128)} %get-tuple-element.90, f32[16,640]{1,0:T(8,128)S(1)} %log_add_fusion, bf16[640,16,64]{0,2,1:T(8,128)(2,1)S(1)} %bitcast.287, bf16[1280,16,64]{0,2,1:T(8,128)(2,1)} %bitcast.290), kind=kOutput, calls=%fused_computation.1 | convolution fusion | flops 1717032960 | bytes 108871680 | tf_op jit(solution)/shard_map/while/body/eval_jaxpr/qhd,khd->hqk/dot_general | solution.py:182
  590.6 42.5 %multiply_convert_fusion = bf16[16,640,1280]{2,1,0:T(8,128)(2,1)} fusion(f32[16,640,1280]{2,1,0:T(8,128)} %get-tuple-element.96, f32[16,640,1280]{2,1,0:T(8,128)} %get-tuple-element.90, f32[16,640]{1,0:T(8,128)S(1)} %get-tuple-element.95, f32[16,640]{1,0:T(8,128)S(1)} %log_add_fusion), kind=kLoop, calls=%fused_computation | loop fusion | flops 52428800 | bytes 131153920 | tf_op jit(solution)/shard_map/while/body/eval_jaxpr/convert_element_type | solution.py:186
  633.0 14.6 multiply_convert_fusion.5
  652.2 21.5 %fusion.36 = bf16[16,64,1280]{2,1,0:T(8,128)(2,1)} fusion(bf16[640,16,64]{0,2,1:T(8,128)(2,1)S(1)} %bitcast.288, f32[16,640,1280]{2,1,0:T(8,128)} %get-tuple-element.90, f32[16,640]{1,0:T(8,128)S(1)} %log_add_fusion), kind=kOutput, calls=%fused_computation.67 | convolution fusion | flops 1705246720 | bytes 56401920 | tf_op jit(solution)/shard_map/while/body/eval_jaxpr/hqk,qhd->khd/dot_general | solution.py:212
  678.3 5.7 fusion.69
  684.0 14.8 multiply_convert_fusion.6
  698.8 5.2 fusion.96
  708.4 19.5 %reduce-scatter.25.cloned.1.call-done = bf16[1,640,1024]{2,1,0:T(8,128)(2,1)} async-done(((bf16[1,1280,1024]{2,1,0:T(8,128)(2,1)}), bf16[1,640,1024]{2,1,0:T(8,128)(2,1)}) %reduce-scatter.25.cloned.1.call-update) | async-done | bytes 1310736 | tf_op jit(solution)/shard_map/reduce_scatter | solution.py:231
  728.0 5.9 fusion.45
  737.0 5.5 fusion.71
  766.5 6.4 multiply_convert_fusion.2
  775.0 11.5 convert_bitcast_fusion.1
  786.5 7.8 copy.71
  794.4 24.5 %fusion.9 = bf16[4096,640]{0,1:T(8,128)(2,1)} fusion(f32[640,4096]{1,0:T(8,128)} %get-tuple-element.94), kind=kLoop, calls=%fused_computation.16 | loop fusion | flops 170393600 | bytes 15728640 | tf_op jit(solution)/shard_map/convert_element_type | solution.py:155
  818.9 7.9 copy.83
  826.8 11.5 convert_bitcast_fusion
  838.3 8.2 copy.73
  849.5 5.9 reduce-scatter.27.cloned.1.call-done
  855.5 34.0 %reduce-scatter.31.cloned.1.call-done = bf16[512,1024]{1,0:T(8,128)(2,1)} async-done(((bf16[1024,1024]{1,0:T(8,128)(2,1)}), bf16[512,1024]{1,0:T(8,128)(2,1)}) %reduce-scatter.31.cloned.1.call-update) | async-done | bytes 1048592 | tf_op jit(solution)/shard_map/reduce_scatter | solution.py:274
  889.5 56.4 %reduce-scatter.55.cloned.1.call-done = bf16[512,2048]{1,0:T(8,128)(2,1)} async-done(((bf16[1024,2048]{1,0:T(8,128)(2,1)}), bf16[512,2048]{1,0:T(8,128)(2,1)}) %reduce-scatter.55.cloned.1.call-update) | async-done | bytes 2097168 | tf_op jit(solution)/shard_map/reduce_scatter | solution.py:292
  946.0 56.7 %reduce-scatter.51.cloned.1.call-done = bf16[512,2048]{1,0:T(8,128)(2,1)} async-done(((bf16[1024,2048]{1,0:T(8,128)(2,1)}), bf16[512,2048]{1,0:T(8,128)(2,1)}) %reduce-scatter.51.cloned.1.call-update) | async-done | bytes 2097168 | tf_op jit(solution)/shard_map/reduce_scatter | solution.py:289
  1002.8 101.3 %reduce-scatter.43.cloned.1.call-done = bf16[512,4096]{1,0:T(8,128)(2,1)} async-done(((bf16[1024,4096]{1,0:T(8,128)(2,1)}), bf16[512,4096]{1,0:T(8,128)(2,1)}) %reduce-scatter.43.cloned.1.call-update) | async-done | bytes 4194320 | tf_op jit(solution)/shard_map/reduce_scatter | solution.py:283
  1104.5 101.3 %reduce-scatter.47.cloned.1.call-done = bf16[2048,1024]{1,0:T(8,128)(2,1)} async-done(((bf16[4096,1024]{1,0:T(8,128)(2,1)}), bf16[2048,1024]{1,0:T(8,128)(2,1)}) %reduce-scatter.47.cloned.1.call-update) | async-done | bytes 4194320 | tf_op jit(solution)/shard_map/reduce_scatter | solution.py:286
  1205.8 13.2 fusion.48
  1219.0 46.0 %reduce-scatter.61.cloned.1.call-done = bf16[32,8]{1,0:T(8,128)(2,1)} async-done(((bf16[512,8]{1,0:T(8,128)(2,1)}), bf16[32,8]{1,0:T(8,128)(2,1)}) %reduce-scatter.61.cloned.1.call-update) | async-done | bytes 528
  1266.3 58.8 %reduce-scatter.41.cloned.1.call-done = bf16[32,1024]{1,0:T(8,128)(2,1)} async-done(((bf16[512,1024]{1,0:T(8,128)(2,1)}), bf16[32,1024]{1,0:T(8,128)(2,1)}) %reduce-scatter.41.cloned.1.call-update) | async-done | bytes 65552 | tf_op jit(solution)/shard_map/reduce_scatter | solution.py:319
  1326.6 58.9 %reduce-scatter.37.cloned.1.call-done = bf16[32,1024]{1,0:T(8,128)(2,1)} async-done(((bf16[512,1024]{1,0:T(8,128)(2,1)}), bf16[32,1024]{1,0:T(8,128)(2,1)}) %reduce-scatter.37.cloned.1.call-update) | async-done | bytes 65552 | tf_op jit(solution)/shard_map/reduce_scatter | solution.py:316
  1387.0 58.6 %reduce-scatter.29.cloned.1.call-done = bf16[32,1024]{1,0:T(8,128)(2,1)} async-done(((bf16[512,1024]{1,0:T(8,128)(2,1)}), bf16[32,1024]{1,0:T(8,128)(2,1)}) %reduce-scatter.29.cloned.1.call-update) | async-done | bytes 65552 | tf_op jit(solution)/shard_map/reduce_scatter | solution.py:310
  1447.0 58.8 %reduce-scatter.33.cloned.1.call-done = bf16[32,1024]{1,0:T(8,128)(2,1)} async-done(((bf16[512,1024]{1,0:T(8,128)(2,1)}), bf16[32,1024]{1,0:T(8,128)(2,1)}) %reduce-scatter.33.cloned.1.call-update) | async-done | bytes 65552 | tf_op jit(solution)/shard_map/reduce_scatter | solution.py:313
  1507.4 62.7 %reduce-scatter.57.cloned.1.call-done = bf16[32,2048]{1,0:T(8,128)(2,1)} async-done(((bf16[512,2048]{1,0:T(8,128)(2,1)}), bf16[32,2048]{1,0:T(8,128)(2,1)}) %reduce-scatter.57.cloned.1.call-update) | async-done | bytes 131088 | tf_op jit(solution)/shard_map/reduce_scatter | solution.py:331
  1571.7 63.2 %reduce-scatter.53.cloned.1.call-done = bf16[32,2048]{1,0:T(8,128)(2,1)} async-done(((bf16[512,2048]{1,0:T(8,128)(2,1)}), bf16[32,2048]{1,0:T(8,128)(2,1)}) %reduce-scatter.53.cloned.1.call-update) | async-done | bytes 131088 | tf_op jit(solution)/shard_map/reduce_scatter | solution.py:328
  1636.5 73.7 %reduce-scatter.45.cloned.1.call-done = bf16[32,4096]{1,0:T(8,128)(2,1)} async-done(((bf16[512,4096]{1,0:T(8,128)(2,1)}), bf16[32,4096]{1,0:T(8,128)(2,1)}) %reduce-scatter.45.cloned.1.call-update) | async-done | bytes 262160 | tf_op jit(solution)/shard_map/reduce_scatter | solution.py:322
  1712.0 73.8 %reduce-scatter.49.cloned.1.call-done = bf16[128,1024]{1,0:T(8,128)(2,1)} async-done(((bf16[2048,1024]{1,0:T(8,128)(2,1)}), bf16[128,1024]{1,0:T(8,128)(2,1)}) %reduce-scatter.49.cloned.1.call-update) | async-done | bytes 262160 | tf_op jit(solution)/shard_map/reduce_scatter | solution.py:325
  (200 shorter events, 111.2 us)
Async XLA Ops:
  7.2 6.8 copy-start
  7.2 56.3 %all-gather.13.cloned.1.call-start = ((), (), s32[]{:S(2)}) async-start(), calls=%async_computation.20 | async-start | bytes 4456448 | tf_op jit(solution)/shard_map/all_gather | solution.py:75
  7.9 97.6 %all-gather.19.cloned.1.call-start = ((), (), s32[]{:S(2)}) async-start(), calls=%async_computation.23 | async-start | bytes 2228224 | tf_op jit(solution)/shard_map/all_gather | solution.py:70
  8.7 139.3 %all-gather.15.cloned.1.call-start = ((), (), s32[]{:S(2)}) async-start(), calls=%async_computation.21 | async-start | bytes 2228224 | tf_op jit(solution)/shard_map/all_gather | solution.py:71
  9.4 189.9 %all-gather.23.cloned.1.call-start = ((), (), s32[]{:S(2)}) async-start(), calls=%async_computation.25 | async-start | bytes 4456448 | tf_op jit(solution)/shard_map/all_gather | solution.py:76
  10.0 231.3 %all-gather.17.cloned.1.call-start = ((), (), s32[]{:S(2)}) async-start(), calls=%async_computation.22 | async-start | bytes 2228224 | tf_op jit(solution)/shard_map/all_gather | solution.py:69
  10.6 270.5 %all-gather.31.cloned.1.call-start = ((), (), s32[]{:S(2)}) async-start(), calls=%async_computation.48 | async-start | bytes 3932160 | tf_op jit(solution)/shard_map/all_gather | solution.py:112
  12.9 228.5 %copy-start.17 = (f32[640]{0:T(1024)}, f32[640]{0:T(1024)S(1)}, u32[]{:S(2)}) copy-start(f32[640]{0:T(1024)S(1)} %broadcast_multiply_fusion.1) | copy-start | bytes 7684
  13.9 227.4 %copy-start.21 = (f32[640]{0:T(1024)}, f32[640]{0:T(1024)S(1)}, u32[]{:S(2)}) copy-start(f32[640]{0:T(1024)S(1)} %fusion.77) | copy-start | bytes 7684
  14.1 185.3 %copy-start.23 = (f32[1,1024]{1,0:T(1,128)}, f32[1,1024]{1,0:T(1,128)S(1)}, u32[]{:S(2)}) copy-start(f32[1,1024]{1,0:T(1,128)S(1)} %fusion.79) | copy-start | bytes 12292
  67.4 173.9 %copy-start.19 = (f32[1,1024]{1,0:T(1,128)}, f32[1,1024]{1,0:T(1,128)S(1)}, u32[]{:S(2)}) copy-start(f32[1,1024]{1,0:T(1,128)S(1)} %get-tuple-element.87) | copy-start | bytes 12292
  67.4 173.9 %copy-start.27 = (f32[1,1024]{1,0:T(1,128)}, f32[1,1024]{1,0:T(1,128)S(1)}, u32[]{:S(2)}) copy-start(f32[1,1024]{1,0:T(1,128)S(1)} %get-tuple-element.88) | copy-start | bytes 12292
  109.8 214.2 %all-gather.29.cloned.1.call-start = ((), (), s32[]{:S(2)}) async-start(), calls=%async_computation.47 | async-start | bytes 3932160 | tf_op jit(solution)/shard_map/all_gather | solution.py:113
  152.2 213.7 %all-gather.21.cloned.1.call-start = ((), (), s32[]{:S(2)}) async-start(), calls=%async_computation.24 | async-start | bytes 2228224 | tf_op jit(solution)/shard_map/all_gather | solution.py:72
  153.0 288.8 %all-gather.25.cloned.1.call-start = ((), (), s32[]{:S(2)}) async-start(), calls=%async_computation.26 | async-start | bytes 8912896 | tf_op jit(solution)/shard_map/all_gather | solution.py:73
  153.7 363.3 %all-gather.27.cloned.1.call-start = ((), (), s32[]{:S(2)}) async-start(), calls=%async_computation.27 | async-start | bytes 8912896 | tf_op jit(solution)/shard_map/all_gather | solution.py:74
  154.3 549.7 %reduce-scatter.23.cloned.1.call-start = ((), (), s32[]{:S(2)}) async-start(), calls=%async_computation.28 | async-start | bytes 3932160 | tf_op jit(solution)/shard_map/reduce_scatter | solution.py:228
  284.1 23.1 %copy-start.2 = (bf16[1280,1024]{0,1:T(8,128)(2,1)}, bf16[1280,1024]{0,1:T(8,128)(2,1)S(1)}, u32[]{:S(2)}) copy-start(bf16[1280,1024]{0,1:T(8,128)(2,1)S(1)} %copy.60) | copy-start | bytes 7864324
  328.4 37.5 %copy-start.5 = (bf16[1,640,1024]{2,1,0:T(8,128)(2,1)S(1)}, bf16[1,640,1024]{2,1,0:T(8,128)(2,1)}, u32[]{:S(2)}) copy-start(bf16[1,640,1024]{2,1,0:T(8,128)(2,1)} %param.13) | copy-start | bytes 3932164
  348.6 20.6 %copy-start.32 = (bf16[16,64,640]{2,1,0:T(8,128)(2,1)}, bf16[16,64,640]{2,1,0:T(8,128)(2,1)S(1)}, u32[]{:S(2)}) copy-start(bf16[16,64,640]{2,1,0:T(8,128)(2,1)S(1)} %fusion.50) | copy-start | bytes 3932164
  441.8 75.2 %copy-start.12 = (bf16[1,640,1024]{2,1,0:T(8,128)(2,1)S(1)}, bf16[1,640,1024]{2,1,0:T(8,128)(2,1)}, u32[]{:S(2)}) copy-start(bf16[1,640,1024]{2,1,0:T(8,128)(2,1)} %param.14) | copy-start | bytes 3932164
  533.8 10.0 copy-start.7
  590.6 42.5 %copy-start.10 = (bf16[640,1024]{0,1:T(8,128)(2,1)S(1)}, bf16[640,1024]{0,1:T(8,128)(2,1)}, u32[]{:S(2)}) copy-start(bf16[640,1024]{0,1:T(8,128)(2,1)} %copy.59) | copy-start | bytes 3932164
  652.2 75.8 %reduce-scatter.25.cloned.1.call-start = ((), (), s32[]{:S(2)}) async-start(), calls=%async_computation.29 | async-start | bytes 3932160 | tf_op jit(solution)/shard_map/reduce_scatter | solution.py:231
  678.2 168.4 %reduce-scatter.59.cloned.1.call-start = ((), (), s32[]{:S(2)}) async-start(), calls=%async_computation.46 | async-start | bytes 24576 | tf_op jit(solution)/shard_map/reduce_scatter | solution.py:295
  704.0 24.0 %copy-start.18 = (f32[640]{0:T(1024)S(1)}, f32[640]{0:T(1024)}, u32[]{:S(2)}) copy-start(f32[640]{0:T(1024)} %copy-done.17) | copy-start | bytes 7684
  704.0 24.0 %copy-start.20 = (f32[1,1024]{1,0:T(1,128)S(1)}, f32[1,1024]{1,0:T(1,128)}, u32[]{:S(2)}) copy-start(f32[1,1024]{1,0:T(1,128)} %copy-done.19) | copy-start | bytes 12292
  708.4 25.4 %copy-start.26 = (f32[640]{0:T(1024)S(1)}, f32[640]{0:T(1024)}, u32[]{:S(2)}) copy-start(f32[640]{0:T(1024)} %copy-done.25) | copy-start | bytes 7684
  743.5 104.7 %reduce-scatter.39.cloned.1.call-start = ((), (), s32[]{:S(2)}) async-start(), calls=%async_computation.36 | async-start | bytes 3145728 | tf_op jit(solution)/shard_map/reduce_scatter | solution.py:280
  748.8 100.1 %reduce-scatter.35.cloned.1.call-start = ((), (), s32[]{:S(2)}) async-start(), calls=%async_computation.34 | async-start | bytes 3145728 | tf_op jit(solution)/shard_map/reduce_scatter | solution.py:277
  758.6 96.9 %reduce-scatter.27.cloned.1.call-start = ((), (), s32[]{:S(2)}) async-start(), calls=%async_computation.30 | async-start | bytes 3145728 | tf_op jit(solution)/shard_map/reduce_scatter | solution.py:271
  762.2 127.3 %reduce-scatter.31.cloned.1.call-start = ((), (), s32[]{:S(2)}) async-start(), calls=%async_computation.32 | async-start | bytes 3145728 | tf_op jit(solution)/shard_map/reduce_scatter | solution.py:274
  766.3 179.6 %reduce-scatter.55.cloned.1.call-start = ((), (), s32[]{:S(2)}) async-start(), calls=%async_computation.44 | async-start | bytes 6291456 | tf_op jit(solution)/shard_map/reduce_scatter | solution.py:292
  773.0 229.7 %reduce-scatter.51.cloned.1.call-start = ((), (), s32[]{:S(2)}) async-start(), calls=%async_computation.42 | async-start | bytes 6291456 | tf_op jit(solution)/shard_map/reduce_scatter | solution.py:289
  773.7 330.4 %reduce-scatter.43.cloned.1.call-start = ((), (), s32[]{:S(2)}) async-start(), calls=%async_computation.38 | async-start | bytes 12582912 | tf_op jit(solution)/shard_map/reduce_scatter | solution.py:283
  794.3 411.4 %reduce-scatter.47.cloned.1.call-start = ((), (), s32[]{:S(2)}) async-start(), calls=%async_computation.40 | async-start | bytes 12582912 | tf_op jit(solution)/shard_map/reduce_scatter | solution.py:286
  818.9 7.9 copy-start.13
  846.6 418.4 %reduce-scatter.61.cloned.1.call-start = ((), (), s32[]{:S(2)}) async-start(), calls=%async_computation.49 | async-start | bytes 139264
  848.2 476.9 %reduce-scatter.41.cloned.1.call-start = ((), (), s32[]{:S(2)}) async-start(), calls=%async_computation.37 | async-start | bytes 1114112 | tf_op jit(solution)/shard_map/reduce_scatter | solution.py:319
  848.9 536.6 %reduce-scatter.37.cloned.1.call-start = ((), (), s32[]{:S(2)}) async-start(), calls=%async_computation.35 | async-start | bytes 1114112 | tf_op jit(solution)/shard_map/reduce_scatter | solution.py:316
  849.5 596.1 %reduce-scatter.29.cloned.1.call-start = ((), (), s32[]{:S(2)}) async-start(), calls=%async_computation.31 | async-start | bytes 1114112 | tf_op jit(solution)/shard_map/reduce_scatter | solution.py:310
  855.4 650.4 %reduce-scatter.33.cloned.1.call-start = ((), (), s32[]{:S(2)}) async-start(), calls=%async_computation.33 | async-start | bytes 1114112 | tf_op jit(solution)/shard_map/reduce_scatter | solution.py:313
  889.5 680.6 %reduce-scatter.57.cloned.1.call-start = ((), (), s32[]{:S(2)}) async-start(), calls=%async_computation.45 | async-start | bytes 2228224 | tf_op jit(solution)/shard_map/reduce_scatter | solution.py:331
  946.0 688.9 %reduce-scatter.53.cloned.1.call-start = ((), (), s32[]{:S(2)}) async-start(), calls=%async_computation.43 | async-start | bytes 2228224 | tf_op jit(solution)/shard_map/reduce_scatter | solution.py:328
  1002.7 707.5 %reduce-scatter.45.cloned.1.call-start = ((), (), s32[]{:S(2)}) async-start(), calls=%async_computation.39 | async-start | bytes 4456448 | tf_op jit(solution)/shard_map/reduce_scatter | solution.py:322
  1104.1 101.7 %copy-start.8 = (f32[1,640,1024]{2,1,0:T(8,128)S(1)}, f32[1,640,1024]{2,1,0:T(8,128)}, u32[]{:S(2)}) copy-start(f32[1,640,1024]{2,1,0:T(8,128)} %copy-done.6) | copy-start | bytes 7864324
  1104.1 681.7 %reduce-scatter.49.cloned.1.call-start = ((), (), s32[]{:S(2)}) async-start(), calls=%async_computation.41 | async-start | bytes 4456448 | tf_op jit(solution)/shard_map/reduce_scatter | solution.py:325
  1205.8 581.8 %copy-start.1 = (bf16[8,1024]{1,0:T(8,128)(2,1)S(1)}, bf16[8,1024]{1,0:T(8,128)(2,1)}, u32[]{:S(2)}) copy-start(bf16[8,1024]{1,0:T(8,128)(2,1)} %param.17) | copy-start | bytes 49156
  (15 other events, 35.2 us)
Sparse Core Ops, SparseCore 0:
  10.2 53.2 all-gather.12
  65.7 39.8 all-gather.18
  107.7 40.1 all-gather.14
  150.0 49.3 all-gather.22
  201.3 39.9 all-gather.16
  243.3 37.7 all-gather.30
  283.2 39.0 all-gather.28
  324.5 41.4 all-gather.20
  368.1 73.6 all-gather.24
  443.8 73.1 all-gather.26
  652.3 35.8 reduce-scatter.22
  690.3 37.5 reduce-scatter.24
  743.6 9.7 reduce-scatter.58
  755.6 31.8 reduce-scatter.38
  789.6 31.8 reduce-scatter.34
  823.6 31.8 reduce-scatter.26
  857.6 31.8 reduce-scatter.30
  891.6 54.2 reduce-scatter.54
  948.3 54.3 reduce-scatter.50
  1004.8 99.2 reduce-scatter.42
  1106.5 99.2 reduce-scatter.46
  1209.8 55.1 reduce-scatter.60
  1268.6 56.4 reduce-scatter.40
  1329.0 56.3 reduce-scatter.36
  1389.1 56.4 reduce-scatter.28
  1449.4 56.3 reduce-scatter.32
  1509.4 60.5 reduce-scatter.56
  1574.3 60.5 reduce-scatter.52
  1638.7 71.4 reduce-scatter.44
  1714.4 71.3 reduce-scatter.48
where the time goes:
time: 1800 us; the launch traced here: 1790 us
  waiting for transfers between devices  1310 us (73%)
  matrix products  288 us (16%)
  other arithmetic  117 us (6%)
  local copies, waits for them, and re-layouts  60.5 us (3%)
    reduce_scatter x1, waiting for transfers between devices, shards(): lax.psum_scatter(part_up.astype(jnp.bfloat16), 'seq', scatter_dimension=0...  101 us
    reduce_scatter x1, waiting for transfers between devices, shards(): lax.psum_scatter(part_down.astype(jnp.bfloat16), 'seq', scatter_dimension...  101 us
    reduce_scatter x1, waiting for transfers between devices, shards(): lax.psum_scatter(seq_down.astype(jnp.bfloat16), 'items', scatter_dimensio...  73.8 us
    reduce_scatter x1, waiting for transfers between devices, shards(): lax.psum_scatter(seq_up.astype(jnp.bfloat16), 'items', scatter_dimension=...  73.7 us
    all_gather x1, waiting for transfers between devices, shards(): lax.all_gather(w_up, 'items', axis=0, tiled=True)  70.7 us
    reduce_scatter x1, waiting for transfers between devices, shards(): lax.psum_scatter(seq_ada_one.astype(jnp.bfloat16), 'items', scatter_dimen...  63.2 us
    reduce_scatter x1, waiting for transfers between devices, shards(): lax.psum_scatter(seq_ada_two.astype(jnp.bfloat16), 'items', scatter_dimen...  62.7 us
    reduce_scatter x1, waiting for transfers between devices, shards(): lax.psum_scatter(seq_value.astype(jnp.bfloat16), 'items', scatter_dimensi...  58.9 us
  transfers between devices with their start and end apart: 30, of which 25 were waited for; matrix products, arithmetic and copies ran while one was open for 17% of the time, Pallas kernels for 0%

commit v1 on v0

v1 whole, which is shorter than its diff:
```python
from functools import partial
import math

import jax
import jax.numpy as jnp
import numpy as np
from jax import lax
from jax.experimental import pallas as pl
from jax.experimental.pallas import tpu as pltpu
from jax.sharding import PartitionSpec as P

HEAD_DIM = 64
SCALE = 0.125
MASKED = -1e30
TILE = 128
LANES = 128

def row_ids(shape):
    return lax.broadcasted_iota(jnp.int32, shape, 0)
def lane_ids(shape):
    return lax.broadcasted_iota(jnp.int32, shape, 1)
def matmul(left, right):
    return jnp.dot(left, right, preferred_element_type=jnp.float32)
def twin_lanes(flipped):
    top = row_ids(flipped.shape) < HEAD_DIM
    return jnp.concatenate([jnp.where(top, flipped, 0.0), jnp.where(top, 0.0, flipped)], axis=1)
def twin_rows(block):
    first = lane_ids(block.shape) < HEAD_DIM
    return jnp.concatenate([jnp.where(first, block, 0.0), jnp.where(first, 0.0, block)], axis=0)
def untwin(wide):
    top = row_ids((LANES, LANES)) < HEAD_DIM
    return jnp.where(top, wide[:, :LANES], wide[:, LANES:]).T

def split3(value):
    high = value.astype(jnp.bfloat16).astype(jnp.float32)
    rest = value - high
    mid = rest.astype(jnp.bfloat16).astype(jnp.float32)
    return high, mid, rest - mid

def attend_kernel(place, q_ref, k_ref, v_ref, o_ref, lse_ref, keys_wide, values_t):
    half = q_ref.shape[0] // 2
    prompt = pl.multiple_of(place[0] * half, TILE)
    target = pl.multiple_of((1 - place[0]) * half, TILE)
    length = place[1]
    shape = (half, LANES)
    keys_wide[:half, :LANES] = k_ref[pl.ds(prompt, half), :]
    keys_wide[half:, :LANES] = k_ref[pl.ds(target, half), :]
    hidden = (lane_ids(shape) == 0) & (row_ids(shape) >= length)
    keys_wide[:half, LANES:] = jnp.where(hidden, MASKED, 0.0).astype(jnp.bfloat16)
    keys_wide[half:, LANES:] = jnp.zeros(shape, jnp.bfloat16)
    for piece in range(half // TILE):
        rows = slice(piece * TILE, (piece + 1) * TILE)
        values_t[:, rows] = v_ref[pl.ds(prompt + piece * TILE, TILE), :].astype(jnp.float32).T.astype(jnp.bfloat16)
        rows = slice(half + piece * TILE, half + (piece + 1) * TILE)
        values_t[:, rows] = v_ref[pl.ds(target + piece * TILE, TILE), :].astype(jnp.float32).T.astype(jnp.bfloat16)
    below = jnp.where(row_ids((LANES, 2 * TILE)) == 0, 1.0, 0.0)

    def score(start, seen):
        q_flip = (q_ref[pl.ds(start, TILE), :].astype(jnp.float32) * SCALE).T
        q_wide = jnp.concatenate([twin_lanes(q_flip), below], axis=0).astype(jnp.bfloat16)
        return matmul(keys_wide[:seen, :], q_wide)

    def tile(scores, start, seen, slot):
        peak = jnp.max(scores, axis=0, keepdims=True)
        expo = jnp.exp(scores - peak)
        total = jnp.sum(expo, axis=0, keepdims=True)
        out = matmul(values_t[:, :seen], expo.astype(jnp.bfloat16)) / total
        o_ref[pl.ds(start, TILE), :] = untwin(out).astype(jnp.bfloat16)
        lse_ref[0, pl.ds(slot, 1), :] = peak + jnp.log(total)

    tiles = half // TILE

    @pl.loop(0, tiles)
    def _(index):
        at_prompt = pl.multiple_of(prompt + index * TILE, TILE)
        at_target = pl.multiple_of(target + index * TILE, TILE)
        first = score(at_prompt, half)
        second = score(at_target, 2 * half)
        tile(first, at_prompt, half, index)
        tile(second, at_target, 2 * half, tiles + index)


def attend(qkv, place):
    rows = qkv.shape[0]
    width = qkv.shape[1] // 3
    pairs = width // LANES
    block = lambda shift: pl.BlockSpec((rows, LANES), lambda p, s, shift=shift: (0, shift * pairs + p))
    seen = rows * rows * 3 // 4
    return pl.pallas_call(
        attend_kernel,
        grid_spec=pltpu.PrefetchScalarGridSpec(
            num_scalar_prefetch=1, grid=(pairs,),
            in_specs=[block(0), block(1), block(2)],
            out_specs=[block(0), pl.BlockSpec((1, rows // TILE, 2 * TILE), lambda p, s: (p, 0, 0))],
            scratch_shapes=[pltpu.VMEM((rows, 2 * LANES), jnp.bfloat16), pltpu.VMEM((LANES, rows), jnp.bfloat16)],
        ),
        out_shape=[jax.ShapeDtypeStruct((rows, width), jnp.bfloat16),
                   jax.ShapeDtypeStruct((pairs, rows // TILE, 2 * TILE), jnp.float32)],
        compiler_params=pltpu.CompilerParams(vmem_limit_bytes=48 << 20),
        cost_estimate=pl.CostEstimate(flops=pairs * 2 * seen * 4 * HEAD_DIM * 4, transcendentals=pairs * 2 * seen, bytes_accessed=rows * width * 8),
        name="attend",
    )(place, qkv, qkv, qkv)


def attend_back_kernel(place, q_ref, k_ref, v_ref, o_ref, g_ref, lse_ref, out_ref, keys_wide, values_wide, keys_t, dq, dk, dv):
    half = q_ref.shape[0] // 2
    step = pl.program_id(1)
    prompt = pl.multiple_of(place[0] * half, TILE)
    target = pl.multiple_of((1 - place[0]) * half, TILE)
    length = place[1]

    @pl.when(step == 0)
    def _():
        shape = (half, LANES)
        lanes = lane_ids(shape)
        ones = jnp.where((lanes >= 1) & (lanes <= 3), 1.0, 0.0)
        hidden = (lanes == 0) & (row_ids(shape) >= length)
        keys_wide[:half, :LANES] = k_ref[pl.ds(prompt, half), :]
        keys_wide[half:, :LANES] = k_ref[pl.ds(target, half), :]
        keys_wide[:half, LANES:] = jnp.where(hidden, MASKED, ones).astype(jnp.bfloat16)
        keys_wide[half:, LANES:] = ones.astype(jnp.bfloat16)
        values_wide[:half, :LANES] = v_ref[pl.ds(prompt, half), :]
        values_wide[half:, :LANES] = v_ref[pl.ds(target, half), :]
        values_wide[:half, LANES:] = ones.astype(jnp.bfloat16)
        values_wide[half:, LANES:] = ones.astype(jnp.bfloat16)
        for piece in range(2 * half // TILE):
            rows = slice(piece * TILE, (piece + 1) * TILE)
            keys_t[:, rows] = keys_wide[rows, :LANES].astype(jnp.float32).T.astype(jnp.bfloat16)
        dk[...] = jnp.zeros_like(dk)
        dv[...] = jnp.zeros_like(dv)
        wide = (LANES, 2 * TILE)
        ids = row_ids(wide)

        def parts(value):
            high, mid, rest = split3(value)
            return jnp.where(ids == 1, -high, jnp.where(ids == 2, -mid, jnp.where(ids == 3, -rest, 0.0)))

        def tile(start, seen, slot):
            spot = pl.ds(start, TILE)
            q_here = q_ref[spot, :].astype(jnp.float32) * SCALE
            g_here = g_ref[spot, :].astype(jnp.float32)
            g_flip = g_here.T
            product = g_flip * o_ref[spot, :].astype(jnp.float32).T
            inner = jnp.concatenate(
                [jnp.sum(product[:HEAD_DIM], axis=0, keepdims=True), jnp.sum(product[HEAD_DIM:], axis=0, keepdims=True)], axis=1)
            lse = lse_ref[0, pl.ds(slot, 1), :]
            below = jnp.where(ids == 0, 1.0, parts(lse))
            q_wide = jnp.concatenate([twin_lanes(q_here.T), below], axis=0).astype(jnp.bfloat16)
            g_wide = jnp.concatenate([twin_lanes(g_flip), parts(inner)], axis=0).astype(jnp.bfloat16)
            probs = jnp.exp(matmul(keys_wide[:seen, :], q_wide))
            grads = matmul(values_wide[:seen, :], g_wide)
            scores = (probs * grads).astype(jnp.bfloat16)
            dk[:seen, :] += matmul(scores, twin_rows(q_here).astype(jnp.bfloat16))
            dv[:seen, :] += matmul(probs.astype(jnp.bfloat16), twin_rows(g_here).astype(jnp.bfloat16))
            dq[spot, :] = (untwin(matmul(keys_t[:, :seen], scores)) * SCALE).astype(jnp.bfloat16)

        tiles = half // TILE

        @pl.loop(0, tiles)
        def _(index):
            tile(pl.multiple_of(prompt + index * TILE, TILE), half, index)
            tile(pl.multiple_of(target + index * TILE, TILE), 2 * half, tiles + index)

        out_ref[...] = dq[...]

    for which, held in ((1, dk), (2, dv)):
        @pl.when(step == which)
        def _(held=held):
            out_ref[pl.ds(prompt, half), :] = held[:half, :].astype(jnp.bfloat16)
            out_ref[pl.ds(target, half), :] = held[half:, :].astype(jnp.bfloat16)


def attend_back(qkv, mixed, grad, lse, place):
    rows = qkv.shape[0]
    width = qkv.shape[1] // 3
    pairs = width // LANES
    block = lambda shift: pl.BlockSpec((rows, LANES), lambda p, j, s, shift=shift: (0, shift * pairs + p))
    seen = rows * rows * 3 // 4
    return pl.pallas_call(
        attend_back_kernel,
        grid_spec=pltpu.PrefetchScalarGridSpec(
            num_scalar_prefetch=1, grid=(pairs, 3),
            in_specs=[block(0), block(1), block(2), block(0), block(0), pl.BlockSpec((1, rows // TILE, 2 * TILE), lambda p, j, s: (p, 0, 0))],
            out_specs=pl.BlockSpec((rows, LANES), lambda p, j, s: (0, j * pairs + p)),
            scratch_shapes=[pltpu.VMEM((rows, 2 * LANES), jnp.bfloat16), pltpu.VMEM((rows, 2 * LANES), jnp.bfloat16), pltpu.VMEM((LANES, rows), jnp.bfloat16),
                pltpu.VMEM((rows, LANES), jnp.bfloat16), pltpu.VMEM((rows, LANES), jnp.float32), pltpu.VMEM((rows, LANES), jnp.float32)],
        ),
        out_shape=jax.ShapeDtypeStruct((rows, 3 * width), jnp.bfloat16),
        compiler_params=pltpu.CompilerParams(vmem_limit_bytes=48 << 20),
        cost_estimate=pl.CostEstimate(flops=pairs * 2 * seen * 10 * HEAD_DIM * 4, transcendentals=pairs * 2 * seen, bytes_accessed=rows * width * 20),
        name="attend_back",
    )(place, qkv, qkv, qkv, mixed, grad, lse)


HEADS = 16
EPSILON = 1e-05


def exact(left, right):
    return jnp.dot(left, right, precision=lax.Precision.HIGHEST)


def dot_rows(left, right):
    return lax.dot_general(
        left, right, (((0,), (0,)), ((), ())), preferred_element_type=jnp.float32
    )


def dot_last(left, right):
    return lax.dot_general(
        left, right, (((1,), (1,)), ((), ())), preferred_element_type=jnp.float32
    )


def standardise(values):
    centred = values - jnp.mean(values, axis=-1, keepdims=True)
    spread = jnp.mean(centred * centred, axis=-1, keepdims=True)
    inverse = lax.rsqrt(spread + EPSILON)
    return centred * inverse, inverse


def ada_norm(values, ada):
    width = values.shape[-1]
    normed, inverse = standardise(values)
    return (1.0 + ada[:width]) * normed + ada[width:], normed, inverse


def ada_norm_back(grad, normed, inverse, ada):
    width = normed.shape[-1]
    scaled = grad * (1.0 + ada[:width])
    inner = jnp.mean(scaled * normed, axis=-1, keepdims=True)
    values = inverse * (scaled - jnp.mean(scaled, axis=-1, keepdims=True) - normed * inner)
    return values, jnp.concatenate([jnp.sum(grad * normed, axis=0), jnp.sum(grad, axis=0)])


def ring_of(items_count):
    chips = items_count // 2
    outer = 4 if chips % 4 == 0 else chips
    inner = chips // outer
    order = [a * inner for a in range(outer)]
    for turn, a in enumerate(reversed(range(outer))):
        beside = list(range(1, inner))
        order += [a * inner + b for b in (beside if turn % 2 == 0 else beside[::-1])]
    return order


class Mover:
    def __init__(self, items_count, seq_count):
        self.items_count = items_count
        self.seq_count = seq_count
        self.chips = items_count // 2
        order = ring_of(items_count)
        self.forward = []
        self.backward = []
        table = np.zeros((items_count, self.chips), np.int32)
        for spot in range(self.chips):
            for core in range(2):
                here = 2 * order[spot] + core
                after = 2 * order[(spot + 1) % self.chips] + core
                self.forward.append((here, after))
                self.backward.append((after, here))
                for ahead in range(self.chips):
                    table[here, ahead] = order[(spot + ahead) % self.chips]
        self.item = lax.axis_index("items")
        self.core = self.item % 2
        self.seq = lax.axis_index("seq")
        row = lax.dynamic_index_in_dim(jnp.asarray(table), self.item, 0, keepdims=False)
        self.ahead = [row[j] for j in range(self.chips)]

    def flip(self, value, bit):
        pairs = [(i, i ^ bit) for i in range(self.items_count)]
        return lax.ppermute(value, "items", pairs)

    def across(self, value):
        return lax.ppermute(value, "seq", [(0, 1), (1, 0)])

    def sum_items(self, value):
        if self.items_count & (self.items_count - 1):
            return lax.psum(value, "items")
        bit = 1
        while bit < self.items_count:
            value = value + self.flip(value, bit)
            bit *= 2
        return value

    def sum_seq(self, value):
        if self.seq_count == 2:
            return value + self.across(value)
        return lax.psum(value, "seq")

    def frames(self, value):
        if self.seq_count == 2:
            return jnp.concatenate([value, self.across(value)], axis=0)
        return lax.all_gather(value, "seq", axis=0, tiled=True)

    def prompt_spot(self):
        return self.seq if self.seq_count == 2 else jnp.zeros((), jnp.int32)

    def to_rows(self, value):
        rows = value.shape[0] // self.seq_count
        if self.seq_count == 2:
            mine = value[:rows]
            other = self.across(value[rows:])
            return jnp.where(
                self.seq == 0,
                jnp.concatenate([mine, other], axis=1),
                jnp.concatenate([other, mine], axis=1),
            )
        return lax.all_to_all(value, "seq", split_axis=0, concat_axis=1, tiled=True)

    def to_heads(self, value):
        width = value.shape[1] // self.seq_count
        if self.seq_count == 2:
            sent = lax.dynamic_slice_in_dim(value, (1 - self.seq) * width, width, 1)
            held = lax.dynamic_slice_in_dim(value, self.seq * width, width, 1)
            return jnp.concatenate([held, self.across(sent)], axis=0)
        return lax.all_to_all(value, "seq", split_axis=1, concat_axis=0, tiled=True)

    def sum_frames(self, value):
        rows = value.shape[0] // self.seq_count
        if self.seq_count == 2:
            other = self.across(value[rows:].astype(jnp.bfloat16))
            return value[:rows] + other.astype(jnp.float32)
        return lax.psum_scatter(
            value.astype(jnp.bfloat16), "seq", scatter_dimension=0, tiled=True
        ).astype(jnp.float32)

    def reduce_items(self, total):
        chips = self.chips
        parts = total.astype(jnp.bfloat16).reshape(chips, 2, -1, total.shape[1])
        sent = lax.dynamic_index_in_dim(parts, 1 - self.core, 1, keepdims=False)
        kept = lax.dynamic_index_in_dim(parts, self.core, 1, keepdims=False)
        both = kept + self.flip(sent, 1)

        def block(ahead):
            return lax.dynamic_index_in_dim(both, self.ahead[ahead % chips], 0, keepdims=False)

        result = block(0).astype(jnp.float32)
        for pairs, sign, hops in (
            (self.forward, 1, chips // 2),
            (self.backward, -1, (chips - 1) // 2),
        ):
            moving = None
            for left in range(hops, 0, -1):
                piece = block(sign * left)
                moving = piece if moving is None else moving + piece
                moving = lax.ppermute(moving, "items", pairs)
            if moving is not None:
                result = result + moving.astype(jnp.float32)
        return result

    def reduce_seq(self, value):
        rows = value.shape[0] // self.seq_count
        if self.seq_count == 2:
            sent = lax.dynamic_slice_in_dim(value, (1 - self.seq) * rows, rows, 0)
            kept = lax.dynamic_slice_in_dim(value, self.seq * rows, rows, 0)
            return kept + self.across(sent.astype(jnp.bfloat16)).astype(jnp.float32)
        return lax.psum_scatter(
            value.astype(jnp.bfloat16), "seq", scatter_dimension=0, tiled=True
        ).astype(jnp.float32)

    def join_columns(self, value):
        rows = value.shape[0] // self.seq_count
        if self.seq_count == 2:
            sent = lax.dynamic_slice_in_dim(value, (1 - self.seq) * rows, rows, 0)
            kept = lax.dynamic_slice_in_dim(value, self.seq * rows, rows, 0)
            other = self.across(sent)
            return jnp.where(self.seq == 0, kept, other), jnp.where(self.seq == 0, other, kept)
        moved = lax.all_to_all(value, "seq", split_axis=0, concat_axis=0, tiled=True)
        return tuple(moved[j * rows : (j + 1) * rows] for j in range(self.seq_count))


def shards(
    tokens,
    cotangent,
    prompt_len,
    section_ids,
    section_table,
    w_query,
    w_key,
    w_value,
    w_out,
    w_up,
    w_down,
    w_ada_one,
    w_ada_two,
):
    items_count = lax.axis_size("items")
    seq_count = lax.axis_size("seq")
    mover = Mover(items_count, seq_count)
    batch, rows, width = tokens.shape
    hidden = w_up.shape[1]
    held = width // seq_count
    piece = w_query.shape[0]
    tokens = tokens.reshape(rows, width)
    grad_low = cotangent.reshape(rows, width)

    mine = [
        lax.dynamic_slice_in_dim(w, mover.seq * held, held, 1) for w in (w_query, w_key, w_value)
    ]
    qkv_w = lax.all_gather(jnp.concatenate(mine, axis=1), "items", axis=0, tiled=True)
    folds = hidden // width
    up_rows = jnp.concatenate([w_up[:, j * width : (j + 1) * width] for j in range(folds)], axis=0)
    rest = lax.all_gather(
        jnp.concatenate([w_out, up_rows, w_down], axis=0), "items", axis=0, tiled=False
    )
    out_w = rest[:, :piece].reshape(width, width)
    up_w = (
        rest[:, piece : piece + folds * piece]
        .reshape(items_count, folds, piece, width)
        .transpose(0, 2, 1, 3)
        .reshape(width, hidden)
    )
    down_w = rest[:, piece + folds * piece :].reshape(hidden, width)

    table = section_table.astype(jnp.float32)
    own_columns = lax.dynamic_slice_in_dim(section_table, mover.item * piece, piece, 1)
    ada_part = jnp.dot(
        own_columns,
        jnp.concatenate([w_ada_one, w_ada_two], axis=1),
        preferred_element_type=jnp.float32,
    )
    choose = (section_ids[0] == jnp.arange(section_table.shape[0])).astype(jnp.float32)
    ada_all = jnp.sum(choose[:, None] * mover.sum_items(ada_part), axis=0)
    ada_one = ada_all[: 2 * width]
    ada_two = ada_all[2 * width :]

    place = jnp.stack([mover.prompt_spot(), prompt_len[0]]).astype(jnp.int32)
    frames = mover.frames(tokens)
    normed_one, _, _ = ada_norm(frames.astype(jnp.float32), ada_one)
    low_one = normed_one.astype(jnp.bfloat16)
    qkv = jnp.dot(low_one, qkv_w, preferred_element_type=jnp.float32).astype(jnp.bfloat16)
    mixed_heads, lse = attend(qkv, place)
    mixed = mover.to_rows(mixed_heads)
    inputs = tokens.astype(jnp.float32)
    attended = inputs + jnp.dot(mixed, out_w, preferred_element_type=jnp.float32)
    normed_two, unit_two, inverse_two = ada_norm(attended, ada_two)
    low_two = normed_two.astype(jnp.bfloat16)
    upward = jnp.dot(low_two, up_w, preferred_element_type=jnp.float32)
    active, gelu_back = jax.vjp(partial(jax.nn.gelu, approximate=False), upward)
    active_low = active.astype(jnp.bfloat16)
    layer_out = (
        attended + jnp.dot(active_low, down_w, preferred_element_type=jnp.float32)
    ).astype(jnp.bfloat16)

    part_down = mover.reduce_items(dot_rows(active_low, grad_low))
    (grad_upward,) = gelu_back(dot_last(grad_low, down_w))
    upward_low = grad_upward.astype(jnp.bfloat16)
    part_up = mover.reduce_items(dot_rows(low_two, upward_low))
    grad_normed_two = dot_last(upward_low, up_w)
    back_mid, ada_two_rows = ada_norm_back(grad_normed_two, unit_two, inverse_two, ada_two)
    grad_attended = grad_low.astype(jnp.float32) + back_mid
    attended_low = grad_attended.astype(jnp.bfloat16)
    part_out = mover.reduce_items(dot_rows(mixed, attended_low))
    grad_mixed = dot_last(attended_low, out_w).astype(jnp.bfloat16)
    grad_heads = mover.to_heads(grad_mixed)
    grad_qkv = attend_back(qkv, mixed_heads, grad_heads, lse, place)
    part_qkv = mover.reduce_items(dot_rows(low_one, grad_qkv))
    grad_normed_one = mover.sum_frames(dot_last(grad_qkv, qkv_w))
    unit_one, inverse_one = standardise(inputs)
    back_in, ada_one_rows = ada_norm_back(grad_normed_one, unit_one, inverse_one, ada_one)
    input_grad = grad_attended + back_in

    ada_rows = jnp.concatenate([ada_one_rows, ada_two_rows])
    section_sums = mover.sum_items(mover.sum_seq(choose[:, None] * ada_rows[None, :]))
    out_piece = piece // seq_count
    first_row = mover.item * piece + mover.seq * out_piece
    table_rows = lax.dynamic_slice_in_dim(table, first_row, out_piece, 1)
    ada_grads = exact(table_rows.T, section_sums)
    grad_ada_one = ada_grads[:, : 2 * width]
    grad_ada_two = ada_grads[:, 2 * width :]
    own_ada = jnp.concatenate(
        [
            lax.dynamic_slice_in_dim(w, mover.seq * out_piece, out_piece, 0).astype(jnp.float32)
            for w in (w_ada_one, w_ada_two)
        ],
        axis=1,
    )
    grad_table = exact(section_sums, own_ada.T)

    grad_down = mover.reduce_seq(part_down)
    grad_up = mover.reduce_seq(part_up)
    grad_out = mover.reduce_seq(part_out)
    sides = mover.join_columns(part_qkv)
    grad_query, grad_key, grad_value = (
        jnp.concatenate([side[:, j * held : (j + 1) * held] for side in sides], axis=1)
        for j in range(3)
    )
    return (
        layer_out.reshape(batch, rows, width),
        input_grad.reshape(batch, rows, width),
        grad_query,
        grad_key,
        grad_value,
        grad_out,
        grad_up,
        grad_down,
        grad_ada_one,
        grad_ada_two,
        grad_table,
    )


def solution(mesh):
    return jax.shard_map(
        shards,
        mesh=mesh,
        in_specs=(
            P("items", "seq", None),
            P("items", "seq", None),
            P("items"),
            P("items"),
            P(),
            P("items", None),
            P("items", None),
            P("items", None),
            P("items", None),
            P("items", None),
            P("items", None),
            P("items", None),
            P("items", None),
        ),
        out_specs=(
            P("items", "seq", None),
            P("items", "seq", None),
            P(("items", "seq"), None),
            P(("items", "seq"), None),
            P(("items", "seq"), None),
            P(("items", "seq"), None),
            P(("items", "seq"), None),
            P(("items", "seq"), None),
            P(("items", "seq"), None),
            P(("items", "seq"), None),
            P(None, ("items", "seq")),
        ),
        check_vma=False,
    )
```

time: 1800 us -> 563 us (0.31)
  waiting for transfers between devices: 1310 us -> 204 us
  matrix products: 288 us -> 127 us
  other arithmetic: 117 us -> 20.6 us
  Pallas kernels: 0 us -> 69.2 us
  starting transfers between devices: 2.47 us -> 51.4 us
    reduce_scatter x19 -> x0, waiting for transfers between devices: 884 us -> none  [the longest x1 101 us: shards(): lax.psum_scatter(part_up.astype(jnp.bfloat16), 'seq', scatter_dimension=0...]
    all_gather x10 -> x2, waiting for transfers between devices: 373 us -> 66.5 us  [the longest x1 61.4 us: shards(): lax.all_gather(jnp.concatenate([w_out, up_rows, w_down], axis=0), 'items'...]
    dot_general x12 -> x5, matrix products: 193 us -> 54.3 us  [the longest x1 33.1 us: shards(): upward = jnp.dot(low_two, up_w, preferred_element_type=jnp.float32)]
    ppermute x0 -> x49, waiting for transfers between devices: none -> 137 us  [the longest x28 79.7 us: reduce_items(): moving = lax.ppermute(moving, 'items', pairs)]
    convert_element_type x14 -> x1, other arithmetic: 87.3 us -> 0.01 us  [shards(): (section_ids[0] == jnp.arange(section_table.shape[0])).astype(jnp.float32)]
    pallas_call x0 -> x2, Pallas kernels: none -> 69.2 us  [the longest x1 41.5 us: attend_back(): pl.pallas_call(attend_back_kernel, grid_spec=pltpu.PrefetchScalarGridSpec...]
    unnamed x31 -> x2, waiting for transfers between devices: 53.2 us -> 0.03 us
    ppermute x0 -> x49, starting transfers between devices: none -> 51.3 us  [the longest x28 29.1 us: reduce_items(): moving = lax.ppermute(moving, 'items', pairs)]
  transfers between devices with their start and end apart: 30 -> 51, of which waited for: 25 -> 25; matrix products, arithmetic and copies ran while one was open for 17% -> 12% of each run, Pallas kernels for 0% -> 12%
where the time goes in v1:
time: 563 us; the launch traced here: 554 us
  waiting for transfers between devices  204 us (36%)
  matrix products  127 us (23%)
  Pallas kernels  69.2 us (12%)
  local copies, waits for them, and re-layouts  51.4 us (9%)
  starting transfers between devices  51.4 us (9%)
  between operations  31.7 us (6%)
  other arithmetic  20.6 us (4%)
    ppermute x28, waiting for transfers between devices, reduce_items(): moving = lax.ppermute(moving, 'items', pairs)  79.7 us
    all_gather x1, waiting for transfers between devices, shards(): lax.all_gather(jnp.concatenate([w_out, up_rows, w_down], axis=0), 'items'...  61.4 us
    dot_general x4, matrix products, dot_last(): lax.dot_general(left, right, (((1,), (1,)), ((), ())), preferred_element_...  43.9 us
    pallas_call x1, Pallas kernels, attend_back(): pl.pallas_call(attend_back_kernel, grid_spec=pltpu.PrefetchScalarGridSpec...  41.5 us
    ppermute x9, waiting for transfers between devices, across(): return lax.ppermute(value, 'seq', [(0, 1), (1, 0)])  36 us
    dot_general x1, matrix products, shards(): upward = jnp.dot(low_two, up_w, preferred_element_type=jnp.float32)  33.1 us
    ppermute x28, starting transfers between devices, reduce_items(): moving = lax.ppermute(moving, 'items', pairs)  29.1 us
    pallas_call x1, Pallas kernels, attend(): pl.pallas_call(attend_kernel, grid_spec=pltpu.PrefetchScalarGridSpec(num_...  27.7 us
  transfers between devices with their start and end apart: 51, of which 25 were waited for; matrix products, arithmetic and copies ran while one was open for 12% of the time, Pallas kernels for 12%

profile of v1, /device:TPU:0, one launch (start us, length us, event | category | flops | bytes accessed | tf_op | source)
XLA Modules:
  0.0 554.5 jit_solution(2154014078668330198)
XLA Ops:
  17.9 2.6 collective-permute-start.4
  24.1 5.0 collective-permute-done.1
  32.8 3.9 collective-permute-done.2
  55.6 5.1 all-gather.4.cloned.1.call-done
  60.6 8.0 %convolution_convert_fusion.1.q_ref.k_ref.v_ref = bf16[1280,1536]{1,0:T(8,128)(2,1)S(1)} fusion(bf16[1024,1536]{1,0:T(8,128)(2,1)} %all-gather.4.cloned.1.call-done, f32[1024]{0:T(1024)S(1)} %get-tuple-element.67, f32[1280]{0:T(1024)S(1)} %add_rsqrt_fusion, f32[1280]{0:T(1024)S(1)} %broadcast_multiply_fusion.1, f32[1024]{0:T(1024)S(1)} %get-tuple-element.68, ...), kind=kOutput, calls=%fused_computation.26 | convolution fusion | flops 4040294400 | bytes 9717760 | tf_op jit(solution)/shard_map/dot_general | solution.py:432
  68.7 27.7 %attend.1 = (bf16[1280,512]{1,0:T(8,128)(2,1)S(1)}, f32[4,10,256]{2,1,0:T(8,128)S(1)}) custom-call(s32[2]{0:T(128)S(1)} %pad_add_fusion.place, bf16[1280,1536]{1,0:T(8,128)(2,1)S(1)} %convolution_convert_fusion.1.q_ref.k_ref.v_ref, bf16[1280,1536]{1,0:T(8,128)(2,1)S(1)} %convolution_convert_fusion.1.q_ref.k_ref.v_ref, ...), custom_call_target="tpu_custom_call" | custom-call | flops 10066329600 | bytes 5242880 | tf_op jit(solution)/shard_map/attend/pallas_call | solution.py:89
  99.2 61.4 %all-gather.6.cloned.1.call-done = bf16[9216,1024]{1,0:T(8,128)(2,1)} async-done(((bf16[576,1024]{1,0:T(8,128)(2,1)}), bf16[9216,1024]{1,0:T(8,128)(2,1)}) %all-gather.6.cloned.1.call-update) | async-done | bytes 18874384 | tf_op jit(solution)/shard_map/all_gather | solution.py:404
  160.6 9.6 %fusion.61 = (bf16[16,256,1024]{2,1,0:T(8,128)(2,1)}, bf16[16,256,1024]{2,1,0:T(8,128)(2,1)S(1)}) fusion(bf16[16,576,1024]{2,1,0:T(8,128)(2,1)} %bitcast.165), kind=kLoop, calls=%fused_computation.181 | loop fusion | bytes 33554432 | tf_op jit(solution)/shard_map/slice | solution.py:414
  174.1 7.8 %copy.27 = bf16[16,64,4,1024]{3,2,1,0:T(4,128)(2,1)} copy(bf16[16,64,4,1024]{3,1,2,0:T(8,128)(2,1)S(1)} %bitcast.164) | data formatting | bytes 16777216 | tf_op jit(solution)/shard_map/transpose | solution.py:411
  181.9 12.2 %copy.30 = bf16[128,8,4,1024]{3,1,2,0:T(8,128)(2,1)} copy(bf16[128,8,4,1024]{3,2,1,0:T(4,128)(2,1)} %bitcast.163) | data formatting | bytes 16777216
  194.2 33.1 %multiply_convert_fusion = (bf16[640,4096]{1,0:T(8,128)(2,1)}, f32[640,4096]{1,0:T(8,128)}, f32[640,4096]{1,0:T(8,128)}) fusion(bf16[1024,4096]{1,0:T(8,128)(2,1)} %bitcast.175, f32[640,1024]{1,0:T(8,128)S(1)} %get-tuple-element.78, f32[1024]{0:T(1024)S(1)} %get-tuple-element.66, f32[640]{0:T(1024)S(1)} %add_rsqrt_fusion.2, ...), kind=kOutput, calls=%fused_computation.11 | convolution fusion | flops 5542379520 | bytes 37237760 | tf_op jit(solution)/shard_map/dot_general | solution.py:439
  227.2 16.8 %fusion.6 = bf16[640,4096]{1,0:T(8,128)(2,1)} fusion(f32[640,4096]{1,0:T(8,128)} %get-tuple-element.24, f32[640,4096]{1,0:T(8,128)} %get-tuple-element.79, bf16[4096,1024]{1,0:T(8,128)(2,1)} %bitcast.177, bf16[1,640,1024]{2,1,0:T(8,128)(2,1)S(1)} %copy-done.13), kind=kOutput, calls=%fused_computation.9 | convolution fusion | flops 5405409280 | bytes 35913728 | tf_op jit(solution)/shard_map/dot_general | solution.py:210
  244.0 19.0 %multiply_reduce_fusion = (f32[1024]{0:T(1024)S(1)}, f32[640]{0:T(1024)S(1)}, f32[640]{0:T(1024)S(1)}, f32[1024]{0:T(1024)S(1)}, f32[640,1024]{1,0:T(8,128)S(1)}) fusion(f32[640,1024]{1,0:T(8,128)S(1)} %get-tuple-element.78, f32[640]{0:T(1024)S(1)} %add_rsqrt_fusion.2, f32[640]{0:T(1024)S(1)} %broadcast_multiply_fusion.7, f32[1024]{0:T(1024)S(1)} %get-tuple-element.65, ...), kind=kOutput, calls=%fused_computation.59 | convolution fusion | flops 5374604288 | bytes 18896896 | tf_op jit(solution)/shard_map/dot_general | solution.py:210
  263.1 9.7 %convolution_convert_fusion = bf16[1024,4096]{1,0:T(8,128)(2,1)} fusion(bf16[640,4096]{1,0:T(8,128)(2,1)S(1)} %copy-done.36, f32[640,1024]{1,0:T(8,128)S(1)} %get-tuple-element.78, f32[1024]{0:T(1024)S(1)} %get-tuple-element.66, f32[640]{0:T(1024)S(1)} %add_rsqrt_fusion.2, f32[640]{0:T(1024)S(1)} %broadcast_multiply_fusion.7, f32[1024]{0:T(1024)S(1)} %get-tuple-element.65), kind=kOutput, calls=%fused_computation.25 | convolution fusion | flops 5376180224 | bytes 16266240 | tf_op jit(solution)/shard_map/dot_general | solution.py:204
  272.8 9.6 %convolution_convert_fusion.2 = bf16[4096,1024]{1,0:T(8,128)(2,1)S(1)} fusion(bf16[640,4096]{1,0:T(8,128)(2,1)} %get-tuple-element.23, bf16[1,640,1024]{2,1,0:T(8,128)(2,1)S(1)} %copy-done.13), kind=kOutput, calls=%fused_computation.27 | convolution fusion | flops 5372903424 | bytes 14942208 | tf_op jit(solution)/shard_map/dot_general | solution.py:204
  282.5 10.7 %fusion.31 = bf16[1,640,1024]{2,1,0:T(8,128)(2,1)} fusion(f32[640,1024]{1,0:T(8,128)S(1)} %get-tuple-element.78, bf16[640,4096]{1,0:T(8,128)(2,1)} %get-tuple-element.23, bf16[4096,1024]{1,0:T(8,128)(2,1)S(1)} %bitcast.180), kind=kOutput, calls=%fused_computation.72 | convolution fusion | flops 5370019840 | bytes 17563648 | tf_op jit(solution)/shard_map/dot_general | solution.py:443
  300.0 2.5 dynamic-slice_bitcast_fusion
  302.5 2.6 dynamic-slice_bitcast_fusion.1
  308.6 6.9 %collective-permute-done.6 = bf16[640,512]{1,0:T(8,128)(2,1)S(1)} collective-permute-done((bf16[640,512]{1,0:T(8,128)(2,1)S(1)}, bf16[640,512]{1,0:T(8,128)(2,1)S(1)}, u32[]{:S(2)}, u32[]{:S(2)}) %collective-permute-start.6) | collective-permute-done | bytes 655392 | tf_op jit(solution)/shard_map/ppermute | solution.py:275
  317.7 41.5 %attend_back.1 = bf16[1280,1536]{1,0:T(8,128)(2,1)} custom-call(s32[2]{0:T(128)S(1)} %pad_add_fusion.place, bf16[1280,1536]{1,0:T(8,128)(2,1)} %copy-done.4, bf16[1280,1536]{1,0:T(8,128)(2,1)} %copy-done.4, bf16[1280,1536]{1,0:T(8,128)(2,1)} %copy-done.4, bf16[1280,512]{1,0:T(8,128)(2,1)S(1)} %copy-done.3, bf16[1280,512]{1,0:T(8,128)(2,1)S(1)} %pad_maximum_fusion.1.g_ref, ...), custom_call_target="tpu_custom_call" | custom-call | flops 25165824000 | bytes 13107200 | tf_op jit(solution)/shard_map/attend_back/pallas_call | solution.py:179
  361.3 6.5 %fusion.68 = f32[1280,1024]{1,0:T(8,128)S(1)} fusion(bf16[1280,1536]{1,0:T(8,128)(2,1)} %attend_back.1, bf16[1024,1536]{1,0:T(8,128)(2,1)S(1)} %copy-done.33), kind=kOutput, calls=%fused_computation.188 | convolution fusion | flops 4026531840 | bytes 12320768 | tf_op jit(solution)/shard_map/dot_general | solution.py:210
  371.8 5.0 convolution_convert_fusion.3
  377.8 20.7 %collective-permute-done.25 = bf16[32,1024]{1,0:T(8,128)(2,1)S(1)} collective-permute-done((bf16[32,1024]{1,0:T(8,128)(2,1)S(1)}, bf16[32,1024]{1,0:T(8,128)(2,1)S(1)}, u32[]{:S(2)}, u32[]{:S(2)}) %collective-permute-start.25) | collective-permute-done | bytes 65568 | tf_op jit(solution)/shard_map/ppermute | solution.py:275
  402.3 3.4 collective-permute-done.44
  410.4 3.3 collective-permute-done.46
  414.5 2.2 fusion.28
  422.0 6.8 %collective-permute-done.48 = f32[8,4096]{1,0:T(8,128)S(1)} collective-permute-done((f32[8,4096]{1,0:T(8,128)S(1)}, f32[8,4096]{1,0:T(8,128)S(1)}, u32[]{:S(2)}, u32[]{:S(2)}) %collective-permute-start.48) | collective-permute-done | bytes 131104 | tf_op jit(solution)/shard_map/ppermute | solution.py:272
  430.2 2.0 collective-permute-start.14
  433.0 2.8 collective-permute-done.11
  436.4 2.1 collective-permute-start.12
  439.4 2.7 collective-permute-done.12
  442.1 2.0 collective-permute-done.15
  445.8 3.9 bitcast_add_fusion.1
  451.5 2.0 collective-permute-start.36
  453.6 12.2 %collective-permute-done.27 = bf16[64,4096]{1,0:T(8,128)(2,1)S(1)} collective-permute-done((bf16[64,4096]{1,0:T(8,128)(2,1)}, bf16[64,4096]{1,0:T(8,128)(2,1)S(1)}, u32[]{:S(2)}, u32[]{:S(2)}) %collective-permute-start.27) | collective-permute-done | bytes 524320 | tf_op jit(solution)/shard_map/ppermute | solution.py:347
  466.1 2.0 collective-permute-start.40
  468.1 9.0 %collective-permute-done.36 = bf16[256,1024]{1,0:T(8,128)(2,1)S(1)} collective-permute-done((bf16[256,1024]{1,0:T(8,128)(2,1)S(1)}, bf16[256,1024]{1,0:T(8,128)(2,1)S(1)}, u32[]{:S(2)}, u32[]{:S(2)}) %collective-permute-start.36) | collective-permute-done | bytes 524320 | tf_op jit(solution)/shard_map/ppermute | solution.py:347
  477.3 11.0 %collective-permute-done.28 = bf16[64,4096]{1,0:T(8,128)(2,1)S(1)} collective-permute-done((bf16[64,4096]{1,0:T(8,128)(2,1)S(1)}, bf16[64,4096]{1,0:T(8,128)(2,1)S(1)}, u32[]{:S(2)}, u32[]{:S(2)}) %collective-permute-start.28) | collective-permute-done | bytes 524320 | tf_op jit(solution)/shard_map/ppermute | solution.py:347
  488.5 2.0 collective-permute-start.32
  490.5 9.0 %collective-permute-done.37 = bf16[256,1024]{1,0:T(8,128)(2,1)S(1)} collective-permute-done((bf16[256,1024]{1,0:T(8,128)(2,1)S(1)}, bf16[256,1024]{1,0:T(8,128)(2,1)S(1)}, u32[]{:S(2)}, u32[]{:S(2)}) %collective-permute-start.37) | collective-permute-done | bytes 524320 | tf_op jit(solution)/shard_map/ppermute | solution.py:347
  499.8 2.0 collective-permute-start.41
  501.7 9.0 %collective-permute-done.29 = bf16[64,4096]{1,0:T(8,128)(2,1)S(1)} collective-permute-done((bf16[64,4096]{1,0:T(8,128)(2,1)S(1)}, bf16[64,4096]{1,0:T(8,128)(2,1)S(1)}, u32[]{:S(2)}, u32[]{:S(2)}) %collective-permute-start.29) | collective-permute-done | bytes 524320 | tf_op jit(solution)/shard_map/ppermute | solution.py:347
  511.0 2.0 collective-permute-start.33
  514.9 7.0 %collective-permute-done.38 = bf16[256,1024]{1,0:T(8,128)(2,1)S(1)} collective-permute-done((bf16[256,1024]{1,0:T(8,128)(2,1)S(1)}, bf16[256,1024]{1,0:T(8,128)(2,1)S(1)}, u32[]{:S(2)}, u32[]{:S(2)}) %collective-permute-start.38) | collective-permute-done | bytes 524320 | tf_op jit(solution)/shard_map/ppermute | solution.py:347
  522.2 2.0 collective-permute-start.42
  524.2 9.0 %collective-permute-done.30 = bf16[64,4096]{1,0:T(8,128)(2,1)S(1)} collective-permute-done((bf16[64,4096]{1,0:T(8,128)(2,1)S(1)}, bf16[64,4096]{1,0:T(8,128)(2,1)S(1)}, u32[]{:S(2)}, u32[]{:S(2)}) %collective-permute-start.30) | collective-permute-done | bytes 524320 | tf_op jit(solution)/shard_map/ppermute | solution.py:347
  534.3 5.3 collective-permute-done.39
  542.9 3.4 collective-permute-done.43
  (257 shorter events, 76.7 us)
Async XLA Ops:
  7.2 53.4 %all-gather.4.cloned.1.call-start = ((), (), s32[]{:S(2)}) async-start(), calls=%async_computation | async-start | bytes 3342336 | tf_op jit(solution)/shard_map/all_gather | solution.py:401
  9.7 150.9 %all-gather.6.cloned.1.call-start = ((), (), s32[]{:S(2)}) async-start(), calls=%async_computation.1 | async-start | bytes 20054016 | tf_op jit(solution)/shard_map/all_gather | solution.py:404
  17.9 36.4 %collective-permute-start.4 = (bf16[640,1024]{1,0:T(8,128)(2,1)S(1)}, bf16[640,1024]{1,0:T(8,128)(2,1)S(1)}, u32[]{:S(2)}, u32[]{:S(2)}) collective-permute-start(bf16[640,1024]{1,0:T(8,128)(2,1)S(1)} %bitcast.158), channel_id=1, source_target_pairs={{0,1},{1,0},{2,3},{3,2},{4,5},{5,4},{6,7},{7,6},{8,9},{9,8},{10,11... | collective-permute-start | bytes 3932168 | tf_op jit(solution)/shard_map/ppermute | solution.py:275
  22.0 7.2 %collective-permute-start.1 = (f32[8,4096]{1,0:T(8,128)S(1)}, f32[8,4096]{1,0:T(8,128)S(1)}, u32[]{:S(2)}, u32[]{:S(2)}) collective-permute-start(f32[8,4096]{1,0:T(8,128)S(1)} %add.312), channel_id=1, source_target_pairs={{0,4},{2,6},{4,0},{6,2},{8,12},{10,14},{12,8},{14,10},{16,20},{18,... | collective-permute-start | bytes 393224 | tf_op jit(solution)/shard_map/ppermute | solution.py:272
  29.2 7.4 %collective-permute-start.2 = (f32[8,4096]{1,0:T(8,128)S(1)}, f32[8,4096]{1,0:T(8,128)S(1)}, u32[]{:S(2)}, u32[]{:S(2)}) collective-permute-start(f32[8,4096]{1,0:T(8,128)S(1)} %add.313), channel_id=1, source_target_pairs={{0,8},{2,10},{4,12},{6,14},{8,0},{10,2},{12,4},{14,6},{16,24},{18,... | collective-permute-start | bytes 393224 | tf_op jit(solution)/shard_map/ppermute | solution.py:272
  36.7 17.4 %collective-permute-start.3 = (f32[8,4096]{1,0:T(8,128)S(1)}, f32[8,4096]{1,0:T(8,128)S(1)}, u32[]{:S(2)}, u32[]{:S(2)}) collective-permute-start(f32[8,4096]{1,0:T(8,128)S(1)} %add.314), channel_id=1, source_target_pairs={{0,16},{2,18},{4,20},{6,22},{8,24},{10,26},{12,28},{14,30},{16,0},... | collective-permute-start | bytes 393224 | tf_op jit(solution)/shard_map/ppermute | solution.py:272
  97.7 74.3 %collective-permute-start.5 = (bf16[640,512]{1,0:T(8,128)(2,1)S(1)}, bf16[640,512]{1,0:T(8,128)(2,1)S(1)}, u32[]{:S(2)}, u32[]{:S(2)}) collective-permute-start(bf16[640,512]{1,0:T(8,128)(2,1)S(1)} %get-tuple-element.48), channel_id=1, source_target_pairs={{0,1},{1,0},{2,3},{3,2},{4,5},{5,4},{6,7},{7,6},{8,9},{9,8},{10,11... | collective-permute-start | bytes 1966088 | tf_op jit(solution)/shard_map/ppermute | solution.py:275
  296.4 9.2 %collective-permute-start.17 = (bf16[8,64,1024]{2,1,0:T(8,128)(2,1)S(1)}, bf16[8,64,1024]{2,1,0:T(8,128)(2,1)}, u32[]{:S(2)}, u32[]{:S(2)}) collective-permute-start(bf16[8,64,1024]{2,1,0:T(8,128)(2,1)S(1)} %dynamic-slice_bitcast_fusion.3), channel_id=1, source_target_pairs={{0,2},{2,0},{4,6},{6,4},{8,10},{10,8},{12,14},{14,12},{16,18},{18,... | collective-permute-start | bytes 3145736 | tf_op jit(solution)/shard_map/ppermute | solution.py:272
  298.5 17.0 %collective-permute-start.6 = (bf16[640,512]{1,0:T(8,128)(2,1)S(1)}, bf16[640,512]{1,0:T(8,128)(2,1)S(1)}, u32[]{:S(2)}, u32[]{:S(2)}) collective-permute-start(bf16[640,512]{1,0:T(8,128)(2,1)S(1)} %get-tuple-element.46), channel_id=1, source_target_pairs={{0,1},{1,0},{2,3},{3,2},{4,5},{5,4},{6,7},{7,6},{8,9},{9,8},{10,11... | collective-permute-start | bytes 1966088 | tf_op jit(solution)/shard_map/ppermute | solution.py:275
  302.5 148.3 %collective-permute-start.35 = (bf16[8,256,1024]{2,1,0:T(8,128)(2,1)}, bf16[8,256,1024]{2,1,0:T(8,128)(2,1)S(1)}, u32[]{:S(2)}, u32[]{:S(2)}) collective-permute-start(bf16[8,256,1024]{2,1,0:T(8,128)(2,1)} %dynamic-slice_bitcast_fusion), channel_id=1, source_target_pairs={{0,2},{2,0},{4,6},{6,4},{8,10},{10,8},{12,14},{14,12},{16,18},{18,... | collective-permute-start | bytes 12582920 | tf_op jit(solution)/shard_map/ppermute | solution.py:272
  305.1 140.7 %collective-permute-start.26 = (bf16[8,64,4096]{2,1,0:T(8,128)(2,1)}, bf16[8,64,4096]{2,1,0:T(8,128)(2,1)}, u32[]{:S(2)}, u32[]{:S(2)}) collective-permute-start(bf16[8,64,4096]{2,1,0:T(8,128)(2,1)} %dynamic-slice_bitcast_fusion.1), channel_id=1, source_target_pairs={{0,2},{2,0},{4,6},{6,4},{8,10},{10,8},{12,14},{14,12},{16,18},{18,... | collective-permute-start | bytes 12582920 | tf_op jit(solution)/shard_map/ppermute | solution.py:272
  307.0 9.8 %collective-permute-start.18 = (bf16[64,1024]{1,0:T(8,128)(2,1)S(1)}, bf16[64,1024]{1,0:T(8,128)(2,1)S(1)}, u32[]{:S(2)}, u32[]{:S(2)}) collective-permute-start(bf16[64,1024]{1,0:T(8,128)(2,1)S(1)} %get-tuple-element.53), channel_id=1, source_target_pairs={{0,8},{2,10},{8,16},{10,18},{16,24},{18,26},{24,28},{26,30},{28,20... | collective-permute-start | bytes 393224 | tf_op jit(solution)/shard_map/ppermute | solution.py:347
  315.5 43.6 %collective-permute-start.22 = (bf16[64,1024]{1,0:T(8,128)(2,1)S(1)}, bf16[64,1024]{1,0:T(8,128)(2,1)S(1)}, u32[]{:S(2)}, u32[]{:S(2)}) collective-permute-start(bf16[64,1024]{1,0:T(8,128)(2,1)S(1)} %get-tuple-element.54), channel_id=1, source_target_pairs={{8,0},{10,2},{16,8},{18,10},{24,16},{26,18},{28,24},{30,26},{20,28... | collective-permute-start | bytes 393224 | tf_op jit(solution)/shard_map/ppermute | solution.py:347
  316.9 42.3 %collective-permute-start.19 = (bf16[64,1024]{1,0:T(8,128)(2,1)S(1)}, bf16[64,1024]{1,0:T(8,128)(2,1)S(1)}, u32[]{:S(2)}, u32[]{:S(2)}) collective-permute-start(bf16[64,1024]{1,0:T(8,128)(2,1)S(1)} %bitcast_add_fusion.23), channel_id=1, source_target_pairs={{0,8},{2,10},{8,16},{10,18},{16,24},{18,26},{24,28},{26,30},{28,20... | collective-permute-start | bytes 393224 | tf_op jit(solution)/shard_map/ppermute | solution.py:347
  359.2 10.5 %collective-permute-start.20 = (bf16[64,1024]{1,0:T(8,128)(2,1)S(1)}, bf16[64,1024]{1,0:T(8,128)(2,1)S(1)}, u32[]{:S(2)}, u32[]{:S(2)}) collective-permute-start(bf16[64,1024]{1,0:T(8,128)(2,1)S(1)} %get-tuple-element.51), channel_id=1, source_target_pairs={{0,8},{2,10},{8,16},{10,18},{16,24},{18,26},{24,28},{26,30},{28,20... | collective-permute-start | bytes 393224 | tf_op jit(solution)/shard_map/ppermute | solution.py:347
  360.7 8.9 %collective-permute-start.23 = (bf16[64,1024]{1,0:T(8,128)(2,1)S(1)}, bf16[64,1024]{1,0:T(8,128)(2,1)S(1)}, u32[]{:S(2)}, u32[]{:S(2)}) collective-permute-start(bf16[64,1024]{1,0:T(8,128)(2,1)S(1)} %get-tuple-element.52), channel_id=1, source_target_pairs={{8,0},{10,2},{16,8},{18,10},{24,16},{26,18},{28,24},{30,26},{20,28... | collective-permute-start | bytes 393224 | tf_op jit(solution)/shard_map/ppermute | solution.py:347
  368.1 31.1 %collective-permute-start.7 = (bf16[640,1024]{1,0:T(8,128)(2,1)S(1)}, bf16[640,1024]{1,0:T(8,128)(2,1)S(1)}, u32[]{:S(2)}, u32[]{:S(2)}) collective-permute-start(bf16[640,1024]{1,0:T(8,128)(2,1)S(1)} %slice.176), channel_id=1, source_target_pairs={{0,1},{1,0},{2,3},{3,2},{4,5},{5,4},{6,7},{7,6},{8,9},{9,8},{10,11... | collective-permute-start | bytes 3932168 | tf_op jit(solution)/shard_map/ppermute | solution.py:275
  369.7 7.2 %collective-permute-start.21 = (bf16[64,1024]{1,0:T(8,128)(2,1)S(1)}, bf16[64,1024]{1,0:T(8,128)(2,1)S(1)}, u32[]{:S(2)}, u32[]{:S(2)}) collective-permute-start(bf16[64,1024]{1,0:T(8,128)(2,1)S(1)} %get-tuple-element.49), channel_id=1, source_target_pairs={{0,8},{2,10},{8,16},{10,18},{16,24},{18,26},{24,28},{26,30},{28,20... | collective-permute-start | bytes 393224 | tf_op jit(solution)/shard_map/ppermute | solution.py:347
  371.2 5.7 %collective-permute-start.24 = (bf16[64,1024]{1,0:T(8,128)(2,1)S(1)}, bf16[64,1024]{1,0:T(8,128)(2,1)S(1)}, u32[]{:S(2)}, u32[]{:S(2)}) collective-permute-start(bf16[64,1024]{1,0:T(8,128)(2,1)S(1)} %get-tuple-element.50), channel_id=1, source_target_pairs={{8,0},{10,2},{16,8},{18,10},{24,16},{26,18},{28,24},{30,26},{20,28... | collective-permute-start | bytes 393224 | tf_op jit(solution)/shard_map/ppermute | solution.py:347
  377.0 21.6 %collective-permute-start.25 = (bf16[32,1024]{1,0:T(8,128)(2,1)S(1)}, bf16[32,1024]{1,0:T(8,128)(2,1)S(1)}, u32[]{:S(2)}, u32[]{:S(2)}) collective-permute-start(bf16[32,1024]{1,0:T(8,128)(2,1)S(1)} %dynamic-slice_convert_fusion.2), channel_id=1, source_target_pairs={{0,1},{1,0},{2,3},{3,2},{4,5},{5,4},{6,7},{7,6},{8,9},{9,8},{10,11... | collective-permute-start | bytes 196616 | tf_op jit(solution)/shard_map/ppermute | solution.py:275
  377.8 30.9 %collective-permute-start.8 = (bf16[8,64,1536]{2,1,0:T(8,128)(2,1)S(1)}, bf16[8,64,1536]{2,1,0:T(8,128)(2,1)S(1)}, u32[]{:S(2)}, u32[]{:S(2)}) collective-permute-start(bf16[8,64,1536]{2,1,0:T(8,128)(2,1)S(1)} %dynamic-slice_bitcast_fusion.2), channel_id=1, source_target_pairs={{0,2},{2,0},{4,6},{6,4},{8,10},{10,8},{12,14},{14,12},{16,18},{18,... | collective-permute-start | bytes 4718600 | tf_op jit(solution)/shard_map/ppermute | solution.py:272
  407.3 6.4 %collective-permute-start.46 = (f32[8,4096]{1,0:T(8,128)S(1)}, f32[8,4096]{1,0:T(8,128)S(1)}, u32[]{:S(2)}, u32[]{:S(2)}) collective-permute-start(f32[8,4096]{1,0:T(8,128)S(1)} %fusion.83), channel_id=1, source_target_pairs={{0,4},{2,6},{4,0},{6,2},{8,12},{10,14},{12,8},{14,10},{16,20},{18,... | collective-permute-start | bytes 393224 | tf_op jit(solution)/shard_map/ppermute | solution.py:272
  408.9 11.5 %collective-permute-start.9 = (bf16[64,1536]{1,0:T(8,128)(2,1)S(1)}, bf16[64,1536]{1,0:T(8,128)(2,1)S(1)}, u32[]{:S(2)}, u32[]{:S(2)}) collective-permute-start(bf16[64,1536]{1,0:T(8,128)(2,1)S(1)} %get-tuple-element.43), channel_id=1, source_target_pairs={{0,8},{2,10},{8,16},{10,18},{16,24},{18,26},{24,28},{26,30},{28,20... | collective-permute-start | bytes 589832 | tf_op jit(solution)/shard_map/ppermute | solution.py:347
  413.8 5.4 collective-permute-start.47
  416.8 13.3 %collective-permute-start.13 = (bf16[64,1536]{1,0:T(8,128)(2,1)S(1)}, bf16[64,1536]{1,0:T(8,128)(2,1)S(1)}, u32[]{:S(2)}, u32[]{:S(2)}) collective-permute-start(bf16[64,1536]{1,0:T(8,128)(2,1)S(1)} %get-tuple-element.44), channel_id=1, source_target_pairs={{8,0},{10,2},{16,8},{18,10},{24,16},{26,18},{28,24},{30,26},{20,28... | collective-permute-start | bytes 589832 | tf_op jit(solution)/shard_map/ppermute | solution.py:347
  419.2 9.7 %collective-permute-start.48 = (f32[8,4096]{1,0:T(8,128)S(1)}, f32[8,4096]{1,0:T(8,128)S(1)}, u32[]{:S(2)}, u32[]{:S(2)}) collective-permute-start(f32[8,4096]{1,0:T(8,128)S(1)} %add.389), channel_id=1, source_target_pairs={{0,16},{2,18},{4,20},{6,22},{8,24},{10,26},{12,28},{14,30},{16,0},... | collective-permute-start | bytes 393224 | tf_op jit(solution)/shard_map/ppermute | solution.py:272
  420.5 9.6 %collective-permute-start.10 = (bf16[64,1536]{1,0:T(8,128)(2,1)S(1)}, bf16[64,1536]{1,0:T(8,128)(2,1)S(1)}, u32[]{:S(2)}, u32[]{:S(2)}) collective-permute-start(bf16[64,1536]{1,0:T(8,128)(2,1)S(1)} %bitcast_add_fusion.18), channel_id=1, source_target_pairs={{0,8},{2,10},{8,16},{10,18},{16,24},{18,26},{24,28},{26,30},{28,20... | collective-permute-start | bytes 589832 | tf_op jit(solution)/shard_map/ppermute | solution.py:347
  430.1 5.7 %collective-permute-start.11 = (bf16[64,1536]{1,0:T(8,128)(2,1)S(1)}, bf16[64,1536]{1,0:T(8,128)(2,1)S(1)}, u32[]{:S(2)}, u32[]{:S(2)}) collective-permute-start(bf16[64,1536]{1,0:T(8,128)(2,1)S(1)} %get-tuple-element.41), channel_id=1, source_target_pairs={{0,8},{2,10},{8,16},{10,18},{16,24},{18,26},{24,28},{26,30},{28,20... | collective-permute-start | bytes 589832 | tf_op jit(solution)/shard_map/ppermute | solution.py:347
  430.2 6.1 %collective-permute-start.14 = (bf16[64,1536]{1,0:T(8,128)(2,1)S(1)}, bf16[64,1536]{1,0:T(8,128)(2,1)S(1)}, u32[]{:S(2)}, u32[]{:S(2)}) collective-permute-start(bf16[64,1536]{1,0:T(8,128)(2,1)S(1)} %get-tuple-element.42), channel_id=1, source_target_pairs={{8,0},{10,2},{16,8},{18,10},{24,16},{26,18},{28,24},{30,26},{20,28... | collective-permute-start | bytes 589832 | tf_op jit(solution)/shard_map/ppermute | solution.py:347
  436.4 5.7 %collective-permute-start.12 = (bf16[64,1536]{1,0:T(8,128)(2,1)S(1)}, bf16[64,1536]{1,0:T(8,128)(2,1)S(1)}, u32[]{:S(2)}, u32[]{:S(2)}) collective-permute-start(bf16[64,1536]{1,0:T(8,128)(2,1)S(1)} %get-tuple-element.39), channel_id=1, source_target_pairs={{0,8},{2,10},{8,16},{10,18},{16,24},{18,26},{24,28},{26,30},{28,20... | collective-permute-start | bytes 589832 | tf_op jit(solution)/shard_map/ppermute | solution.py:347
  438.4 5.7 %collective-permute-start.15 = (bf16[64,1536]{1,0:T(8,128)(2,1)S(1)}, bf16[64,1536]{1,0:T(8,128)(2,1)S(1)}, u32[]{:S(2)}, u32[]{:S(2)}) collective-permute-start(bf16[64,1536]{1,0:T(8,128)(2,1)S(1)} %get-tuple-element.40), channel_id=1, source_target_pairs={{8,0},{10,2},{16,8},{18,10},{24,16},{26,18},{28,24},{30,26},{20,28... | collective-permute-start | bytes 589832 | tf_op jit(solution)/shard_map/ppermute | solution.py:347
  444.2 21.8 %collective-permute-start.16 = (f32[32,1536]{1,0:T(8,128)S(1)}, f32[32,1536]{1,0:T(8,128)S(1)}, u32[]{:S(2)}, u32[]{:S(2)}) collective-permute-start(f32[32,1536]{1,0:T(8,128)S(1)} %constant_dynamic-slice_fusion.3), channel_id=1, source_target_pairs={{0,1},{1,0},{2,3},{3,2},{4,5},{5,4},{6,7},{7,6},{8,9},{9,8},{10,11... | collective-permute-start | bytes 589832 | tf_op jit(solution)/shard_map/ppermute | solution.py:275
  450.7 15.1 %collective-permute-start.27 = (bf16[64,4096]{1,0:T(8,128)(2,1)}, bf16[64,4096]{1,0:T(8,128)(2,1)S(1)}, u32[]{:S(2)}, u32[]{:S(2)}) collective-permute-start(bf16[64,4096]{1,0:T(8,128)(2,1)} %get-tuple-element.37), channel_id=1, source_target_pairs={{0,8},{2,10},{8,16},{10,18},{16,24},{18,26},{24,28},{26,30},{28,20... | collective-permute-start | bytes 1572872 | tf_op jit(solution)/shard_map/ppermute | solution.py:347
  451.5 25.5 %collective-permute-start.36 = (bf16[256,1024]{1,0:T(8,128)(2,1)S(1)}, bf16[256,1024]{1,0:T(8,128)(2,1)S(1)}, u32[]{:S(2)}, u32[]{:S(2)}) collective-permute-start(bf16[256,1024]{1,0:T(8,128)(2,1)S(1)} %get-tuple-element.31), channel_id=1, source_target_pairs={{0,8},{2,10},{8,16},{10,18},{16,24},{18,26},{24,28},{26,30},{28,20... | collective-permute-start | bytes 1572872 | tf_op jit(solution)/shard_map/ppermute | solution.py:347
  453.5 23.7 %collective-permute-start.31 = (bf16[64,4096]{1,0:T(8,128)(2,1)}, bf16[64,4096]{1,0:T(8,128)(2,1)S(1)}, u32[]{:S(2)}, u32[]{:S(2)}) collective-permute-start(bf16[64,4096]{1,0:T(8,128)(2,1)} %get-tuple-element.38), channel_id=1, source_target_pairs={{8,0},{10,2},{16,8},{18,10},{24,16},{26,18},{28,24},{30,26},{20,28... | collective-permute-start | bytes 1572872 | tf_op jit(solution)/shard_map/ppermute | solution.py:347
  465.9 22.4 %collective-permute-start.28 = (bf16[64,4096]{1,0:T(8,128)(2,1)S(1)}, bf16[64,4096]{1,0:T(8,128)(2,1)S(1)}, u32[]{:S(2)}, u32[]{:S(2)}) collective-permute-start(bf16[64,4096]{1,0:T(8,128)(2,1)S(1)} %bitcast_add_fusion.13), channel_id=1, source_target_pairs={{0,8},{2,10},{8,16},{10,18},{16,24},{18,26},{24,28},{26,30},{28,20... | collective-permute-start | bytes 1572872 | tf_op jit(solution)/shard_map/ppermute | solution.py:347
  466.1 24.5 %collective-permute-start.40 = (bf16[256,1024]{1,0:T(8,128)(2,1)S(1)}, bf16[256,1024]{1,0:T(8,128)(2,1)S(1)}, u32[]{:S(2)}, u32[]{:S(2)}) collective-permute-start(bf16[256,1024]{1,0:T(8,128)(2,1)S(1)} %get-tuple-element.32), channel_id=1, source_target_pairs={{8,0},{10,2},{16,8},{18,10},{24,16},{26,18},{28,24},{30,26},{20,28... | collective-permute-start | bytes 1572872 | tf_op jit(solution)/shard_map/ppermute | solution.py:347
  477.1 22.4 %collective-permute-start.37 = (bf16[256,1024]{1,0:T(8,128)(2,1)S(1)}, bf16[256,1024]{1,0:T(8,128)(2,1)S(1)}, u32[]{:S(2)}, u32[]{:S(2)}) collective-permute-start(bf16[256,1024]{1,0:T(8,128)(2,1)S(1)} %bitcast_add_fusion.8), channel_id=1, source_target_pairs={{0,8},{2,10},{8,16},{10,18},{16,24},{18,26},{24,28},{26,30},{28,20... | collective-permute-start | bytes 1572872 | tf_op jit(solution)/shard_map/ppermute | solution.py:347
  488.4 22.4 %collective-permute-start.29 = (bf16[64,4096]{1,0:T(8,128)(2,1)S(1)}, bf16[64,4096]{1,0:T(8,128)(2,1)S(1)}, u32[]{:S(2)}, u32[]{:S(2)}) collective-permute-start(bf16[64,4096]{1,0:T(8,128)(2,1)S(1)} %get-tuple-element.35), channel_id=1, source_target_pairs={{0,8},{2,10},{8,16},{10,18},{16,24},{18,26},{24,28},{26,30},{28,20... | collective-permute-start | bytes 1572872 | tf_op jit(solution)/shard_map/ppermute | solution.py:347
  488.5 22.2 %collective-permute-start.32 = (bf16[64,4096]{1,0:T(8,128)(2,1)S(1)}, bf16[64,4096]{1,0:T(8,128)(2,1)S(1)}, u32[]{:S(2)}, u32[]{:S(2)}) collective-permute-start(bf16[64,4096]{1,0:T(8,128)(2,1)S(1)} %get-tuple-element.36), channel_id=1, source_target_pairs={{8,0},{10,2},{16,8},{18,10},{24,16},{26,18},{28,24},{30,26},{20,28... | collective-permute-start | bytes 1572872 | tf_op jit(solution)/shard_map/ppermute | solution.py:347
  499.6 22.4 %collective-permute-start.38 = (bf16[256,1024]{1,0:T(8,128)(2,1)S(1)}, bf16[256,1024]{1,0:T(8,128)(2,1)S(1)}, u32[]{:S(2)}, u32[]{:S(2)}) collective-permute-start(bf16[256,1024]{1,0:T(8,128)(2,1)S(1)} %get-tuple-element.29), channel_id=1, source_target_pairs={{0,8},{2,10},{8,16},{10,18},{16,24},{18,26},{24,28},{26,30},{28,20... | collective-permute-start | bytes 1572872 | tf_op jit(solution)/shard_map/ppermute | solution.py:347
  499.8 22.2 %collective-permute-start.41 = (bf16[256,1024]{1,0:T(8,128)(2,1)S(1)}, bf16[256,1024]{1,0:T(8,128)(2,1)S(1)}, u32[]{:S(2)}, u32[]{:S(2)}) collective-permute-start(bf16[256,1024]{1,0:T(8,128)(2,1)S(1)} %get-tuple-element.30), channel_id=1, source_target_pairs={{8,0},{10,2},{16,8},{18,10},{24,16},{26,18},{28,24},{30,26},{20,28... | collective-permute-start | bytes 1572872 | tf_op jit(solution)/shard_map/ppermute | solution.py:347
  510.9 22.4 %collective-permute-start.30 = (bf16[64,4096]{1,0:T(8,128)(2,1)S(1)}, bf16[64,4096]{1,0:T(8,128)(2,1)S(1)}, u32[]{:S(2)}, u32[]{:S(2)}) collective-permute-start(bf16[64,4096]{1,0:T(8,128)(2,1)S(1)} %get-tuple-element.33), channel_id=1, source_target_pairs={{0,8},{2,10},{8,16},{10,18},{16,24},{18,26},{24,28},{26,30},{28,20... | collective-permute-start | bytes 1572872 | tf_op jit(solution)/shard_map/ppermute | solution.py:347
  511.0 22.2 %collective-permute-start.33 = (bf16[64,4096]{1,0:T(8,128)(2,1)S(1)}, bf16[64,4096]{1,0:T(8,128)(2,1)S(1)}, u32[]{:S(2)}, u32[]{:S(2)}) collective-permute-start(bf16[64,4096]{1,0:T(8,128)(2,1)S(1)} %get-tuple-element.34), channel_id=1, source_target_pairs={{8,0},{10,2},{16,8},{18,10},{24,16},{26,18},{28,24},{30,26},{20,28... | collective-permute-start | bytes 1572872 | tf_op jit(solution)/shard_map/ppermute | solution.py:347
  522.1 17.5 %collective-permute-start.39 = (bf16[256,1024]{1,0:T(8,128)(2,1)S(1)}, bf16[256,1024]{1,0:T(8,128)(2,1)S(1)}, u32[]{:S(2)}, u32[]{:S(2)}) collective-permute-start(bf16[256,1024]{1,0:T(8,128)(2,1)S(1)} %get-tuple-element.27), channel_id=1, source_target_pairs={{0,8},{2,10},{8,16},{10,18},{16,24},{18,26},{24,28},{26,30},{28,20... | collective-permute-start | bytes 1572872 | tf_op jit(solution)/shard_map/ppermute | solution.py:347
  522.2 17.3 %collective-permute-start.42 = (bf16[256,1024]{1,0:T(8,128)(2,1)S(1)}, bf16[256,1024]{1,0:T(8,128)(2,1)S(1)}, u32[]{:S(2)}, u32[]{:S(2)}) collective-permute-start(bf16[256,1024]{1,0:T(8,128)(2,1)S(1)} %get-tuple-element.28), channel_id=1, source_target_pairs={{8,0},{10,2},{16,8},{18,10},{24,16},{26,18},{28,24},{30,26},{20,28... | collective-permute-start | bytes 1572872 | tf_op jit(solution)/shard_map/ppermute | solution.py:347
  533.5 8.6 %collective-permute-start.34 = (bf16[32,4096]{1,0:T(8,128)(2,1)S(1)}, bf16[32,4096]{1,0:T(8,128)(2,1)S(1)}, u32[]{:S(2)}, u32[]{:S(2)}) collective-permute-start(bf16[32,4096]{1,0:T(8,128)(2,1)S(1)} %dynamic-slice_convert_fusion.1), channel_id=1, source_target_pairs={{0,1},{1,0},{2,3},{3,2},{4,5},{5,4},{6,7},{7,6},{8,9},{9,8},{10,11... | collective-permute-start | bytes 786440 | tf_op jit(solution)/shard_map/ppermute | solution.py:275
  539.9 6.4 %collective-permute-start.43 = (bf16[128,1024]{1,0:T(8,128)(2,1)S(1)}, bf16[128,1024]{1,0:T(8,128)(2,1)S(1)}, u32[]{:S(2)}, u32[]{:S(2)}) collective-permute-start(bf16[128,1024]{1,0:T(8,128)(2,1)S(1)} %dynamic-slice_convert_fusion), channel_id=1, source_target_pairs={{0,1},{1,0},{2,3},{3,2},{4,5},{5,4},{6,7},{7,6},{8,9},{9,8},{10,11... | collective-permute-start | bytes 786440 | tf_op jit(solution)/shard_map/ppermute | solution.py:275
  (47 other events, 585.9 us)
Sparse Core Ops, SparseCore 0:
  10.9 49.6 all-gather.3
  62.8 97.7 all-gather.5

commit v2 on v1

v2 whole, which is shorter than its diff:
```python
from functools import partial
import math

import jax
import jax.numpy as jnp
import numpy as np
from jax import lax
from jax.experimental.layout import Layout, with_layout_constraint
from jax.experimental import pallas as pl
from jax.experimental.pallas import tpu as pltpu
from jax.sharding import PartitionSpec as P

HEAD_DIM = 64
SCALE = 0.125
MASKED = -1e30
COVER = 0.5
TILE = 128
LANES = 128

def row_ids(shape):
    return lax.broadcasted_iota(jnp.int32, shape, 0)
def lane_ids(shape):
    return lax.broadcasted_iota(jnp.int32, shape, 1)
def matmul(left, right):
    return jnp.dot(left, right, preferred_element_type=jnp.float32)
def twin_lanes(flipped):
    top = row_ids(flipped.shape) < HEAD_DIM
    return jnp.concatenate([jnp.where(top, flipped, 0.0), jnp.where(top, 0.0, flipped)], axis=1)
def twin_rows(block):
    first = lane_ids(block.shape) < HEAD_DIM
    return jnp.concatenate([jnp.where(first, block, 0.0), jnp.where(first, 0.0, block)], axis=0)
def untwin(wide):
    top = row_ids((LANES, LANES)) < HEAD_DIM
    return jnp.where(top, wide[:, :LANES], wide[:, LANES:]).T

def split3(value):
    high = value.astype(jnp.bfloat16).astype(jnp.float32)
    rest = value - high
    mid = rest.astype(jnp.bfloat16).astype(jnp.float32)
    return high, mid, rest - mid

def attend_kernel(place, q_ref, k_ref, v_ref, *refs):
    o_ref, lse_ref, keys_wide, values_t = refs[-4:]
    half = q_ref.shape[0] // 2
    prompt = pl.multiple_of(place[0] * half, TILE)
    target = pl.multiple_of((1 - place[0]) * half, TILE)
    length = place[1]
    shape = (half, LANES)
    keys_wide[:half, :LANES] = k_ref[pl.ds(prompt, half), :]
    keys_wide[half:, :LANES] = k_ref[pl.ds(target, half), :]
    hidden = (lane_ids(shape) == 0) & (row_ids(shape) >= length)
    keys_wide[:half, LANES:] = jnp.where(hidden, MASKED, 0.0).astype(jnp.bfloat16)
    keys_wide[half:, LANES:] = jnp.zeros(shape, jnp.bfloat16)
    for piece in range(half // TILE):
        rows = slice(piece * TILE, (piece + 1) * TILE)
        values_t[:, rows] = v_ref[pl.ds(prompt + piece * TILE, TILE), :].astype(jnp.float32).T.astype(jnp.bfloat16)
        rows = slice(half + piece * TILE, half + (piece + 1) * TILE)
        values_t[:, rows] = v_ref[pl.ds(target + piece * TILE, TILE), :].astype(jnp.float32).T.astype(jnp.bfloat16)
    below = jnp.where(row_ids((LANES, 2 * TILE)) == 0, 1.0, 0.0)

    def score(start, seen):
        q_flip = (q_ref[pl.ds(start, TILE), :].astype(jnp.float32) * SCALE).T
        q_wide = jnp.concatenate([twin_lanes(q_flip), below], axis=0).astype(jnp.bfloat16)
        return matmul(keys_wide[:seen, :], q_wide)

    def tile(scores, start, seen, slot):
        peak = jnp.max(scores, axis=0, keepdims=True)
        expo = jnp.exp(scores - peak)
        total = jnp.sum(expo, axis=0, keepdims=True)
        out = matmul(values_t[:, :seen], expo.astype(jnp.bfloat16)) / total
        o_ref[pl.ds(start, TILE), :] = untwin(out).astype(jnp.bfloat16)
        lse_ref[0, pl.ds(slot, 1), :] = peak + jnp.log(total)

    tiles = half // TILE

    @pl.loop(0, tiles)
    def _(index):
        at_prompt = pl.multiple_of(prompt + index * TILE, TILE)
        at_target = pl.multiple_of(target + index * TILE, TILE)
        first = score(at_prompt, half)
        second = score(at_target, 2 * half)
        tile(first, at_prompt, half, index)
        tile(second, at_target, 2 * half, tiles + index)


def attend(qkv, place, behind):
    rows = qkv.shape[0]
    width = qkv.shape[1] // 3
    pairs = width // LANES
    part = lambda shift: pl.BlockSpec((rows, LANES), lambda p, s, shift=shift: (0, 3 * p + shift))
    seen = rows * rows * 3 // 4
    return pl.pallas_call(
        attend_kernel,
        grid_spec=pltpu.PrefetchScalarGridSpec(
            num_scalar_prefetch=1, grid=(pairs,),
            in_specs=[part(0), part(1), part(2)] + [pl.BlockSpec(memory_space=pl.ANY)] * len(behind),
            out_specs=[pl.BlockSpec((rows, LANES), lambda p, s: (0, p)), pl.BlockSpec((1, rows // TILE, 2 * TILE), lambda p, s: (p, 0, 0))],
            scratch_shapes=[pltpu.VMEM((rows, 2 * LANES), jnp.bfloat16), pltpu.VMEM((LANES, rows), jnp.bfloat16)],
        ),
        out_shape=[jax.ShapeDtypeStruct((rows, width), jnp.bfloat16),
                   jax.ShapeDtypeStruct((pairs, rows // TILE, 2 * TILE), jnp.float32)],
        compiler_params=pltpu.CompilerParams(vmem_limit_bytes=48 << 20),
        cost_estimate=pl.CostEstimate(flops=int(COVER * pairs * 2 * seen * 4 * HEAD_DIM * 4), transcendentals=0, bytes_accessed=rows * width * 8),
        name="attend",
    )(place, qkv, qkv, qkv, *behind)


def attend_back_kernel(parts, place, q_ref, k_ref, v_ref, o_ref, lse_ref, *refs):
    g_refs = refs[:parts]
    out_ref, keys_wide, values_wide, keys_t, dq, dk, dv = refs[-7:]
    half = q_ref.shape[0] // 2
    step = pl.program_id(0)
    prompt = pl.multiple_of(place[0] * half, TILE)
    target = pl.multiple_of((1 - place[0]) * half, TILE)
    length = place[1]

    @pl.when(step == 0)
    def _():
        shape = (half, LANES)
        lanes = lane_ids(shape)
        ones = jnp.where((lanes >= 1) & (lanes <= 3), 1.0, 0.0)
        hidden = (lanes == 0) & (row_ids(shape) >= length)
        keys_wide[:half, :LANES] = k_ref[pl.ds(prompt, half), :]
        keys_wide[half:, :LANES] = k_ref[pl.ds(target, half), :]
        keys_wide[:half, LANES:] = jnp.where(hidden, MASKED, ones).astype(jnp.bfloat16)
        keys_wide[half:, LANES:] = ones.astype(jnp.bfloat16)
        values_wide[:half, :LANES] = v_ref[pl.ds(prompt, half), :]
        values_wide[half:, :LANES] = v_ref[pl.ds(target, half), :]
        values_wide[:half, LANES:] = ones.astype(jnp.bfloat16)
        values_wide[half:, LANES:] = ones.astype(jnp.bfloat16)
        for piece in range(2 * half // TILE):
            rows = slice(piece * TILE, (piece + 1) * TILE)
            keys_t[:, rows] = keys_wide[rows, :LANES].astype(jnp.float32).T.astype(jnp.bfloat16)
        dk[...] = jnp.zeros_like(dk)
        dv[...] = jnp.zeros_like(dv)
        wide = (LANES, 2 * TILE)
        ids = row_ids(wide)

        def lanes_of(value):
            high, mid, rest = split3(value)
            return jnp.where(ids == 1, -high, jnp.where(ids == 2, -mid, jnp.where(ids == 3, -rest, 0.0)))

        def g_tile(start):
            if parts == 1:
                return g_refs[0][pl.ds(start, TILE), :]
            inside = pl.multiple_of(jnp.where(start < half, start, start - half), TILE)
            first = g_refs[0][pl.ds(inside, TILE), :]
            return jnp.where(start < half, first, g_refs[1][pl.ds(inside, TILE), :])

        def tile(start, seen, slot):
            spot = pl.ds(start, TILE)
            q_here = q_ref[spot, :].astype(jnp.float32) * SCALE
            g_here = g_tile(start).astype(jnp.float32)
            g_flip = g_here.T
            product = g_flip * o_ref[spot, :].astype(jnp.float32).T
            inner = jnp.concatenate(
                [jnp.sum(product[:HEAD_DIM], axis=0, keepdims=True), jnp.sum(product[HEAD_DIM:], axis=0, keepdims=True)], axis=1)
            lse = lse_ref[0, pl.ds(slot, 1), :]
            below = jnp.where(ids == 0, 1.0, lanes_of(lse))
            q_wide = jnp.concatenate([twin_lanes(q_here.T), below], axis=0).astype(jnp.bfloat16)
            g_wide = jnp.concatenate([twin_lanes(g_flip), lanes_of(inner)], axis=0).astype(jnp.bfloat16)
            probs = jnp.exp(matmul(keys_wide[:seen, :], q_wide))
            grads = matmul(values_wide[:seen, :], g_wide)
            scores = (probs * grads).astype(jnp.bfloat16)
            dk[:seen, :] += matmul(scores, twin_rows(q_here).astype(jnp.bfloat16))
            dv[:seen, :] += matmul(probs.astype(jnp.bfloat16), twin_rows(g_here).astype(jnp.bfloat16))
            dq[spot, :] = (untwin(matmul(keys_t[:, :seen], scores)) * SCALE).astype(jnp.bfloat16)

        tiles = half // TILE

        @pl.loop(0, tiles)
        def _(index):
            tile(pl.multiple_of(prompt + index * TILE, TILE), half, index)
            tile(pl.multiple_of(target + index * TILE, TILE), 2 * half, tiles + index)

        out_ref[...] = dq[...]

    for which, held in ((1, dk), (2, dv)):
        @pl.when(step == which)
        def _(held=held):
            out_ref[pl.ds(prompt, half), :] = held[:half, :].astype(jnp.bfloat16)
            out_ref[pl.ds(target, half), :] = held[half:, :].astype(jnp.bfloat16)


def attend_back(place, qkv, mixed, grads, lse, held, behind):
    rows = qkv.shape[0]
    part = lambda shift: pl.BlockSpec((rows, LANES), lambda j, s, shift=shift: (0, 3 * s[2] + shift))
    block = pl.BlockSpec((rows, LANES), lambda j, s: (0, s[2]))
    lse_block = pl.BlockSpec((1, rows // TILE, 2 * TILE), lambda j, s: (s[2], 0, 0))
    seen = rows * rows * 3 // 4
    more = [] if held is None else [held]
    grad_blocks = [pl.BlockSpec((grad.shape[0], LANES), lambda j, s: (0, s[2])) for grad in grads]
    parts = len(grads)
    return pl.pallas_call(
        partial(attend_back_kernel, parts),
        grid_spec=pltpu.PrefetchScalarGridSpec(
            num_scalar_prefetch=1, grid=(3,),
            in_specs=[part(0), part(1), part(2), block, lse_block] + grad_blocks + [pl.BlockSpec(memory_space=pl.ANY)] * (len(more) + len(behind)),
            out_specs=pl.BlockSpec((rows, LANES), lambda j, s: (0, 3 * s[2] + j)),
            scratch_shapes=[pltpu.VMEM((rows, 2 * LANES), jnp.bfloat16), pltpu.VMEM((rows, 2 * LANES), jnp.bfloat16), pltpu.VMEM((LANES, rows), jnp.bfloat16),
                pltpu.VMEM((rows, LANES), jnp.bfloat16), pltpu.VMEM((rows, LANES), jnp.float32), pltpu.VMEM((rows, LANES), jnp.float32)],
        ),
        out_shape=jax.ShapeDtypeStruct(qkv.shape, jnp.bfloat16),
        input_output_aliases={6 + parts: 0} if more else {},
        compiler_params=pltpu.CompilerParams(vmem_limit_bytes=48 << 20),
        cost_estimate=pl.CostEstimate(flops=int(COVER * 2 * seen * 10 * HEAD_DIM * 4), transcendentals=0, bytes_accessed=rows * LANES * 20),
        name="attend_back",
    )(place, qkv, qkv, qkv, mixed, lse, *grads, *more, *behind)


EPSILON = 1e-05
ROOT_HALF = math.sqrt(0.5)
DENSITY = 1.0 / math.sqrt(2.0 * math.pi)
LATE_HOP = 2
BIG = pltpu.CompilerParams(vmem_limit_bytes=60 << 20)
ANYWHERE = pl.BlockSpec(memory_space=pl.ANY)


def cost(flops, moved, special=0):
    return pl.CostEstimate(
        flops=int(flops * COVER), bytes_accessed=int(moved * COVER), transcendentals=special
    )


def matmul_last(left, right):
    return lax.dot_general(
        left, right, (((1,), (1,)), ((), ())), preferred_element_type=jnp.float32
    )


def dot_rows(left, right):
    return lax.dot_general(
        left, right, (((0,), (0,)), ((), ())), preferred_element_type=jnp.float32
    )


def standardise(values):
    centred = values - jnp.mean(values, axis=-1, keepdims=True)
    spread = jnp.mean(centred * centred, axis=-1, keepdims=True)
    inverse = lax.rsqrt(spread + EPSILON)
    return centred * inverse, inverse


def add_rows(ref, scale, shift):
    step = pl.program_id(0)

    @pl.when(step == 0)
    def _():
        ref[0:1, :] = scale
        ref[1:2, :] = shift

    @pl.when(step > 0)
    def _():
        ref[0:1, :] += scale
        ref[1:2, :] += shift


def row_specs(parts, count):
    rows = sum(part.shape[0] for part in parts) // count
    specs = []
    first = 0
    for part in parts:
        steps = part.shape[0] // rows
        specs.append(
            pl.BlockSpec(
                (rows, part.shape[1]),
                lambda j, *s, first=first, steps=steps: (jnp.clip(j - first, 0, steps - 1), 0),
            )
        )
        first += steps
    return rows, specs


def current(refs, count):
    value = refs[0][...]
    for index, ref in enumerate(refs[1:], 1):
        value = jnp.where(pl.program_id(0) < index * count // len(refs), value, ref[...])
    return value


def first_kernel(parts, pieces, count, spots, *refs):
    frames = refs[:parts]
    ada = refs[parts]
    blocks = refs[parts + 1 : parts + 1 + pieces]
    low_ref, qkv_ref, weight_ref, sems = refs[-4:]
    rows = blocks[0].shape[0]

    @pl.when(pl.program_id(0) == 0)
    def _():
        copies = []
        for index, block in enumerate(blocks):
            start = pl.multiple_of(spots[index] * rows, rows)
            copy = pltpu.make_async_copy(
                block, weight_ref.at[pl.ds(start, rows), :], sems.at[index]
            )
            copy.start()
            copies.append(copy)
        for copy in copies:
            copy.wait()

    normed, _ = standardise(current(frames, count).astype(jnp.float32))
    low = ((1.0 + ada[0:1, :]) * normed + ada[1:2, :]).astype(jnp.bfloat16)
    low_ref[...] = low
    qkv_ref[...] = matmul(low, weight_ref[...]).astype(jnp.bfloat16)


def first_layer(frames, ada, blocks, spots):
    count = 4
    rows, specs = row_specs(frames, count)
    width = frames[0].shape[1]
    columns = blocks[0].shape[1]
    out = lambda size: pl.BlockSpec((rows, size), lambda j, s: (j, 0))
    shape = lambda *size: jax.ShapeDtypeStruct(size, jnp.bfloat16)
    return pl.pallas_call(
        partial(first_kernel, len(frames), len(blocks), count),
        grid_spec=pltpu.PrefetchScalarGridSpec(
            num_scalar_prefetch=1,
            grid=(count,),
            in_specs=specs
            + [pl.BlockSpec((2, width), lambda j, s: (0, 0))]
            + [ANYWHERE] * len(blocks),
            out_specs=[
                out(width),
                out(columns),
                pl.BlockSpec((width, columns), lambda j, s: (0, 0)),
            ],
            scratch_shapes=[pltpu.SemaphoreType.DMA((len(blocks),))],
        ),
        out_shape=[
            shape(rows * count, width),
            shape(rows * count, columns),
            shape(width, columns),
        ],
        compiler_params=BIG,
        cost_estimate=cost(
            2 * rows * count * width * columns, 4 * width * columns + 8 * rows * count * width
        ),
        name="first_layer",
    )(spots, *frames, ada, *blocks)


def second_kernel(pieces, spots, *refs):
    mixed = refs[:pieces]
    tokens, out_w, ada = refs[pieces : pieces + 3]
    attended_ref, low_ref = refs[-2:]
    weights = out_w.reshape(out_w.shape[0] * out_w.shape[2], out_w.shape[3])
    attended = tokens[...].astype(jnp.float32)
    for index, piece in enumerate(mixed):
        size = piece.shape[1]
        start = pl.multiple_of(spots[index] * size, size)
        attended = attended + matmul(piece[...], weights[pl.ds(start, size), :])
    attended_ref[...] = attended
    normed, _ = standardise(attended)
    low_ref[...] = ((1.0 + ada[0:1, :]) * normed + ada[1:2, :]).astype(jnp.bfloat16)


def second_layer(mixed, tokens, out_w, out_part, ada, spots):
    rows, width = tokens.shape
    count = 2
    block = lambda size: pl.BlockSpec((rows // count, size), lambda j, s: (j, 0))
    items, _, piece, _ = out_w.shape
    return pl.pallas_call(
        partial(second_kernel, len(mixed)),
        grid_spec=pltpu.PrefetchScalarGridSpec(
            num_scalar_prefetch=1,
            grid=(count,),
            in_specs=[block(part.shape[1]) for part in mixed]
            + [
                block(width),
                pl.BlockSpec((items, 1, piece, width), lambda j, s: (0, out_part, 0, 0)),
                pl.BlockSpec((2, width), lambda j, s: (0, 0)),
            ],
            out_specs=[block(width), block(width)],
        ),
        out_shape=[
            jax.ShapeDtypeStruct((rows, width), jnp.float32),
            jax.ShapeDtypeStruct((rows, width), jnp.bfloat16),
        ],
        compiler_params=BIG,
        cost_estimate=cost(2 * rows * width * width, 2 * width * width + 10 * rows * width),
        name="second_layer",
    )(spots, *mixed, tokens, out_w, ada)


class Weights:
    def __init__(self, up, up_first, down, down_parts, hidden, width):
        self.up = up
        self.down = down
        self.width = width
        self.hidden = hidden
        fold = up.shape[3]
        self.block = min(512, fold, hidden // 2)
        per_chip = down_parts * down.shape[3]
        per_fold = fold // self.block
        chips, _, _, piece, _ = down.shape
        self.steps = hidden // self.block
        per_core = self.steps // 2
        block = self.block
        self.up_spec = pl.BlockSpec(
            (up.shape[0], 1, up.shape[2], block),
            lambda j: (0, up_first + j // per_fold, 0, j % per_fold),
        )
        self.down_spec = pl.BlockSpec(
            (block // per_chip, 1, down_parts, piece, width),
            lambda j: (j % per_core, j // per_core, 0, 0, 0),
        )
        self.per_chip = per_chip
        self.bytes = 2 * hidden * width


def hidden_kernel(per_chip, x_ref, g_ref, up_ref, down_ref, *refs):
    active_ref, grad_ref = refs[-2:]
    columns = min(256, active_ref.shape[1])
    for start in range(0, active_ref.shape[1], columns):
        spot = slice(start, start + columns)
        upward = matmul(x_ref[...], up_ref[:, :, :, spot].reshape(-1, columns))
        chips = slice(start // per_chip, (start + columns) // per_chip)
        grad_active = matmul_last(g_ref[...], down_ref[chips].reshape(columns, -1))
        below = 0.5 * (1.0 + lax.erf(upward * ROOT_HALF))
        active_ref[:, spot] = (upward * below).astype(jnp.bfloat16)
        slope = below + upward * (DENSITY * jnp.exp(-0.5 * upward * upward))
        grad_ref[:, spot] = (grad_active * slope).astype(jnp.bfloat16)


def hidden_layer(x, grad, weights, total_rows, chunk, held=None):
    rows, width = x.shape
    whole = pl.BlockSpec((rows, width), lambda j: (0, 0))
    out = pl.BlockSpec((rows, weights.block), lambda j: (chunk, j))
    shape = jax.ShapeDtypeStruct((total_rows, weights.hidden), jnp.bfloat16)
    more = [] if held is None else list(held)
    return pl.pallas_call(
        partial(hidden_kernel, weights.per_chip),
        grid=(weights.steps,),
        in_specs=[whole, whole, weights.up_spec, weights.down_spec] + [ANYWHERE] * len(more),
        out_specs=[out, out],
        out_shape=[shape, shape],
        input_output_aliases={4: 0, 5: 1} if more else {},
        compiler_params=BIG,
        cost_estimate=cost(
            4 * rows * width * weights.hidden,
            2 * weights.bytes + 4 * rows * (width + weights.hidden),
        ),
        name="hidden_layer",
    )(x, grad, weights.up, weights.down, *more)


def accumulate(part, out_ref, total):
    step = pl.program_id(0)

    @pl.when(step == 0)
    def _():
        total[...] = part

    @pl.when(step > 0)
    def _():
        total[...] += part

    @pl.when(step == pl.num_programs(0) - 1)
    def _():
        out_ref[...] = total[...].astype(out_ref.dtype)


def down_kernel(a_ref, down_ref, *refs):
    out_ref, total = refs[-2:]
    accumulate(matmul(a_ref[...], down_ref[...].reshape(-1, out_ref.shape[1])), out_ref, total)


def up_back_kernel(g_ref, up_ref, *refs):
    out_ref, total = refs[-2:]
    weights = up_ref[...].reshape(out_ref.shape[1], -1)
    accumulate(matmul_last(g_ref[...], weights), out_ref, total)


def hidden_to_width(kernel, name, held, weights, spec, array, rows, chunk, dtype, behind):
    width = weights.width
    return pl.pallas_call(
        kernel,
        grid=(weights.steps,),
        in_specs=[pl.BlockSpec((rows, weights.block), lambda j: (chunk, j)), spec]
        + [ANYWHERE] * len(behind),
        out_specs=pl.BlockSpec((rows, width), lambda j: (0, 0)),
        out_shape=jax.ShapeDtypeStruct((rows, width), dtype),
        scratch_shapes=[pltpu.VMEM((rows, width), jnp.float32)],
        compiler_params=BIG,
        cost_estimate=cost(
            2 * rows * width * weights.hidden,
            weights.bytes + rows * (2 * weights.hidden + 4 * width),
        ),
        name=name,
    )(held, array, *behind)


def down_part(active, weights, rows, chunk, dtype, behind=()):
    return hidden_to_width(
        down_kernel,
        "down_part",
        active,
        weights,
        weights.down_spec,
        weights.down,
        rows,
        chunk,
        dtype,
        behind,
    )


def up_back(grad, weights, rows, chunk, dtype, behind=()):
    return hidden_to_width(
        up_back_kernel,
        "up_back",
        grad,
        weights,
        weights.up_spec,
        weights.up,
        rows,
        chunk,
        dtype,
        behind,
    )


def middle_back_kernel(pieces, spots, *refs):
    own_ref, other_ref, base_ref, top_ref, ada_ref, out_w = refs[:6]
    outs = refs[-3 - pieces :]
    grad_ref, low_ref, ada_grad_ref = outs[:3]
    grad = own_ref[...] + other_ref[...].astype(jnp.float32)
    normed, inverse = standardise(base_ref[...])
    scaled = grad * (1.0 + ada_ref[0:1, :])
    scale = jnp.sum(grad * normed, axis=0, keepdims=True)
    shift = jnp.sum(grad, axis=0, keepdims=True)
    inner = jnp.mean(scaled * normed, axis=-1, keepdims=True)
    shifted = scaled - jnp.mean(scaled, axis=-1, keepdims=True) - normed * inner
    out = top_ref[...].astype(jnp.float32) + inverse * shifted
    grad_ref[...] = out
    low = out.astype(jnp.bfloat16)
    low_ref[...] = low
    weights = out_w.reshape(out_w.shape[0] * out_w.shape[2], out_w.shape[3])
    for index, mixed_ref in enumerate(outs[3:]):
        size = mixed_ref.shape[1]
        start = pl.multiple_of(spots[index] * size, size)
        mixed_ref[...] = matmul_last(low, weights[pl.ds(start, size), :]).astype(jnp.bfloat16)
    add_rows(ada_grad_ref, scale, shift)


def middle_back(own, other, attended, cotangent, ada, out_w, out_part, spots, sizes, behind):
    rows, width = attended.shape
    count = 2
    block = lambda size: pl.BlockSpec((rows // count, size), lambda j, s: (j, 0))
    items, _, piece, _ = out_w.shape
    return pl.pallas_call(
        partial(middle_back_kernel, len(sizes)),
        grid_spec=pltpu.PrefetchScalarGridSpec(
            num_scalar_prefetch=1,
            grid=(count,),
            in_specs=[block(width)] * 4
            + [
                pl.BlockSpec((2, width), lambda j, s: (0, 0)),
                pl.BlockSpec((items, 1, piece, width), lambda j, s: (0, out_part, 0, 0)),
            ]
            + [ANYWHERE] * len(behind),
            out_specs=[block(width), block(width), pl.BlockSpec((2, width), lambda j, s: (0, 0))]
            + [block(size) for size in sizes],
        ),
        out_shape=[
            jax.ShapeDtypeStruct((rows, width), jnp.float32),
            jax.ShapeDtypeStruct((rows, width), jnp.bfloat16),
            jax.ShapeDtypeStruct((2, width), jnp.float32),
        ]
        + [jax.ShapeDtypeStruct((rows, size), jnp.bfloat16) for size in sizes],
        compiler_params=BIG,
        cost_estimate=cost(2 * rows * width * width, 2 * width * width + 20 * rows * width),
        name="middle_back",
    )(spots, own, other, attended, cotangent, ada, out_w, *behind)


def first_back_kernel(parts, count, grad_ref, weight_ref, *refs):
    frames = refs[:parts]
    out_ref, ada_grad_ref = refs[-2:]
    grad = matmul_last(grad_ref[...], weight_ref[...])
    normed, _ = standardise(current(frames, count).astype(jnp.float32))
    out_ref[...] = grad.astype(jnp.bfloat16)
    scale = jnp.sum(grad * normed, axis=0, keepdims=True)
    shift = jnp.sum(grad, axis=0, keepdims=True)
    add_rows(ada_grad_ref, scale, shift)


def first_back(grad, weights, frames, behind):
    width, columns = weights.shape
    count = 4
    rows, specs = row_specs(frames, count)
    block = pl.BlockSpec((rows, width), lambda j: (j, 0))
    return pl.pallas_call(
        partial(first_back_kernel, len(frames), count),
        grid=(count,),
        in_specs=[
            pl.BlockSpec((rows, columns), lambda j: (j, 0)),
            pl.BlockSpec((width, columns), lambda j: (0, 0)),
        ]
        + specs
        + [ANYWHERE] * len(behind),
        out_specs=[block, pl.BlockSpec((2, width), lambda j: (0, 0))],
        out_shape=[
            jax.ShapeDtypeStruct((rows * count, width), jnp.bfloat16),
            jax.ShapeDtypeStruct((2, width), jnp.float32),
        ],
        compiler_params=BIG,
        cost_estimate=cost(
            2 * rows * count * width * columns,
            2 * width * columns + 2 * rows * count * (2 * width + columns),
        ),
        name="first_back",
    )(grad, weights, *frames, *behind)


def stacked_dot(lefts, rights):
    total = None
    for left, right in zip(lefts, rights):
        part = dot_rows(left, right)
        total = part if total is None else total + part
    return total


def cut_rows(ref, count):
    rows = ref.shape[0] // count
    return [ref[j * rows : (j + 1) * rows, :] for j in range(count)]


def put_sum(out_ref, other_ref, value):
    if other_ref is not None:
        value = value + other_ref[...].astype(jnp.float32)
    out_ref[...] = value.astype(jnp.bfloat16)


def hidden_grads_kernel(count, more, core, *refs):
    active, upward = refs[:2]
    grads, lows = refs[2 : 2 + count], refs[2 + count : 2 + 2 * count]
    other = refs[2 + 2 * count] if more else None
    out_ref = refs[-1]
    step = pl.program_id(0)
    steps = pl.num_programs(0) // 2

    @pl.when(step < steps)
    def _():
        put_sum(
            out_ref, other, stacked_dot(cut_rows(active, count), [ref[...] for ref in grads])
        )

    @pl.when(step >= steps)
    def _():
        put_sum(out_ref, other, stacked_dot([ref[...] for ref in lows], cut_rows(upward, count)))


def hidden_grads(core, active, upward, grads, lows, other, behind):
    total, hidden = active.shape
    half = hidden // 2
    rows, width = lows[0].shape
    count = total // rows
    block = 512
    steps = half // block
    low = pl.BlockSpec((rows, width), lambda j, s: (0, 0))
    grad = pl.BlockSpec((rows, block), lambda j, s: (0, jnp.minimum(j, steps - 1)))
    out = pl.BlockSpec((width, block), lambda j, s: (0, j))
    more = [] if other is None else [other]
    return pl.pallas_call(
        partial(hidden_grads_kernel, count, bool(more)),
        grid_spec=pltpu.PrefetchScalarGridSpec(
            num_scalar_prefetch=1,
            grid=(2 * steps,),
            in_specs=[
                pl.BlockSpec((total, half), lambda j, s: (0, s[0])),
                pl.BlockSpec(
                    (total, block), lambda j, s: (0, s[0] * steps + jnp.maximum(j - steps, 0))
                ),
            ]
            + [grad] * count
            + [low] * count
            + [out] * len(more)
            + [ANYWHERE] * len(behind),
            out_specs=out,
        ),
        out_shape=jax.ShapeDtypeStruct((width, 2 * half), jnp.bfloat16),
        compiler_params=BIG,
        cost_estimate=cost(4 * total * half * width, 8 * total * half + 4 * width * half),
        name="hidden_grads",
    )(core, active, upward, *grads, *lows, *more, *behind)


def tail_grads_kernel(first, more, core, low, grad, mixed, attended, *refs):
    other = refs[0] if more else None
    out_ref = refs[-1]

    @pl.when(pl.program_id(0) < first)
    def _():
        put_sum(out_ref, other, dot_rows(low[...], grad[...]))

    @pl.when(pl.program_id(0) >= first)
    def _():
        put_sum(out_ref, other, dot_rows(mixed[...], attended[...]))


def tail_grads(core, low_one, grad_qkv, mixed, attended_low, other, behind):
    total, width = low_one.shape
    rows = mixed.shape[0]
    block = 256
    first = grad_qkv.shape[1] // 2 // block
    second = width // 2 // block
    out = pl.BlockSpec((width, block), lambda j, s: (0, j))
    more = [] if other is None else [other]
    return pl.pallas_call(
        partial(tail_grads_kernel, first, bool(more)),
        grid_spec=pltpu.PrefetchScalarGridSpec(
            num_scalar_prefetch=1,
            grid=(first + second,),
            in_specs=[
                pl.BlockSpec((total, width), lambda j, s: (0, 0)),
                pl.BlockSpec(
                    (total, block), lambda j, s: (0, s[0] * first + jnp.minimum(j, first - 1))
                ),
                pl.BlockSpec((rows, width), lambda j, s: (0, 0)),
                pl.BlockSpec(
                    (rows, block), lambda j, s: (0, s[0] * second + jnp.maximum(j - first, 0))
                ),
            ]
            + [out] * len(more)
            + [ANYWHERE] * len(behind),
            out_specs=out,
        ),
        out_shape=jax.ShapeDtypeStruct((width, (first + second) * block), jnp.bfloat16),
        compiler_params=BIG,
        cost_estimate=cost(
            2 * width * block * (total * first + rows * second), 8 * total * width
        ),
        name="tail_grads",
    )(core, low_one, grad_qkv, mixed, attended_low, *more, *behind)


def input_back_kernel(parts, tokens_ref, ada_ref, base_ref, *refs):
    out_ref = refs[-1]
    grad = refs[0][...].astype(jnp.float32)
    for ref in refs[1:parts]:
        grad = grad + ref[...].astype(jnp.float32)
    normed, inverse = standardise(tokens_ref[...].astype(jnp.float32))
    scaled = grad * (1.0 + ada_ref[0:1, :])
    inner = jnp.mean(scaled * normed, axis=-1, keepdims=True)
    shifted = scaled - jnp.mean(scaled, axis=-1, keepdims=True) - normed * inner
    out_ref[...] = base_ref[...] + inverse * shifted


def input_back(grads, tokens, ada, base):
    rows, width = tokens.shape
    count = 5 if rows % 80 == 0 else 1
    block = pl.BlockSpec((rows // count, width), lambda j: (j, 0))
    return pl.pallas_call(
        partial(input_back_kernel, len(grads)),
        grid=(count,),
        in_specs=[block, pl.BlockSpec((2, width), lambda j: (0, 0)), block] + [block] * len(grads),
        out_specs=block,
        out_shape=jax.ShapeDtypeStruct((rows, width), jnp.float32),
        compiler_params=BIG,
        cost_estimate=cost(20 * rows * width, 14 * rows * width),
        name="input_back",
    )(tokens, ada, base, *grads)


def exact(left, right):
    return jnp.dot(left, right, precision=lax.Precision.HIGHEST)


def rounded(total, other=None):
    if other is not None:
        total = total + other.astype(jnp.float32)
    return total.astype(jnp.bfloat16)


def tie(*values):
    return lax.optimization_barrier(values)


def cut(value, start, size, axis):
    return lax.dynamic_slice_in_dim(value, start, size, axis, allow_negative_indices=False)


def pick(value, index, axis):
    return lax.dynamic_index_in_dim(
        value, index, axis, keepdims=False, allow_negative_indices=False
    )


def ring_of(items_count):
    chips = items_count // 2
    outer = 4 if chips % 4 == 0 else chips
    inner = chips // outer
    order = [a * inner for a in range(outer)]
    for turn, a in enumerate(reversed(range(outer))):
        beside = list(range(1, inner))
        order += [a * inner + b for b in (beside if turn % 2 == 0 else beside[::-1])]
    return order


class Mover:
    def __init__(self, items_count, seq_count):
        self.items_count = items_count
        self.seq_count = seq_count
        self.pair = seq_count == 2
        self.chips = items_count // 2
        order = ring_of(items_count)
        self.forward = []
        self.backward = []
        table = np.zeros((items_count, self.chips + 2), np.int32)
        for spot in range(self.chips):
            for core in range(2):
                here = 2 * order[spot] + core
                next_one = 2 * order[(spot + 1) % self.chips] + core
                self.forward.append((here, next_one))
                self.backward.append((next_one, here))
                for ahead in range(self.chips):
                    table[here, ahead] = order[(spot + ahead) % self.chips]
                table[here, self.chips] = core
                table[here, self.chips + 1] = 1 - core
        self.item = lax.axis_index("items")
        row = pick(jnp.asarray(table), self.item, 0)
        self.ahead = [row[j] for j in range(self.chips)]
        self.core = row[self.chips]
        self.beside = row[self.chips + 1]
        self.core_spot = row[self.chips : self.chips + 1]
        self.beside_spot = row[self.chips + 1 :]
        self.spots = jnp.concatenate(
            [
                2 * row[: self.chips] + row[self.chips],
                2 * row[: self.chips] + row[self.chips + 1],
            ]
        )
        self.seq = lax.axis_index("seq")

    def flip(self, value, bit):
        pairs = [(i, i ^ bit) for i in range(self.items_count)]
        return lax.ppermute(value, "items", pairs)

    def across(self, value):
        return lax.ppermute(value, "seq", [(0, 1), (1, 0)])

    def gather_items(self, value, summed, late):
        bits = [1 << k for k in range(self.items_count.bit_length() - 1)]
        blocks = {0: value}
        moved = [value, value]
        for hop in range(1, self.chips // 2 + 1):
            ways = [self.forward, self.backward][: 2 if hop <= (self.chips - 1) // 2 else 1]
            moved = [lax.ppermute(v, "items", way) for v, way in zip(moved, ways)]
            if hop > 1 and bits:
                summed, moved = tie(summed, moved)
            if hop == LATE_HOP:
                late, moved = tie(late, moved)
            if bits:
                summed = summed + self.flip(summed, bits.pop(0))
            for v, sign in zip(moved, (-1, 1)):
                blocks[(sign * hop) % self.chips] = v
        while bits:
            summed = summed + self.flip(summed, bits.pop(0))
        mine = [blocks[ahead] for ahead in range(self.chips)]
        return mine + [self.flip(block, 1) for block in mine], summed, late

    def sum_seq(self, value):
        return value + self.across(value) if self.pair else lax.psum(value, "seq")

    def scatter_seq(self, value):
        rows = value.shape[0] // self.seq_count
        if self.pair:
            sent = cut(value, (1 - self.seq) * rows, rows, 0)
            kept = cut(value, self.seq * rows, rows, 0)
            return kept + self.across(sent.astype(jnp.bfloat16)).astype(jnp.float32)
        return lax.psum_scatter(
            value.astype(jnp.bfloat16), "seq", scatter_dimension=0, tiled=True
        ).astype(jnp.float32)

    def join_cores(self, value):
        parts = value.reshape(2, -1, value.shape[1])
        kept = pick(parts, self.core, 0)
        other = self.flip(pick(parts, self.beside, 0), 1)
        return jnp.where(self.core == 0, kept, other), jnp.where(self.core == 0, other, kept)

    def join_columns(self, value):
        rows = value.shape[0] // self.seq_count
        if self.pair:
            kept = cut(value, self.seq * rows, rows, 0)
            other = self.across(cut(value, (1 - self.seq) * rows, rows, 0))
            return jnp.where(self.seq == 0, kept, other), jnp.where(self.seq == 0, other, kept)
        moved = lax.all_to_all(value, "seq", split_axis=0, concat_axis=0, tiled=True)
        return tuple(moved[j * rows : (j + 1) * rows] for j in range(self.seq_count))


class RingSum:
    def __init__(self, mover, make, behind):
        self.mover = mover
        self.chips = mover.chips
        self.make = make
        self.flows = None
        self.sent = make(False, None, behind)
        self.arriving = [mover.flip(self.sent, 1)]

    def block(self, ahead):
        return pick(self.both, self.mover.ahead[ahead % self.chips], 0)

    def add_own(self, behind):
        self.both = self.make(True, self.arriving[0], behind)
        self.whole = self.both
        self.both = self.both.reshape(self.chips, -1, self.both.shape[1])
        self.result = self.block(0).astype(jnp.float32)
        flows = [
            (self.mover.forward, 1, self.chips // 2),
            (self.mover.backward, -1, (self.chips - 1) // 2),
        ]
        self.send([(flow, self.block(flow[1] * flow[2])) for flow in flows if flow[2]])

    def send(self, flows):
        self.arriving = [lax.ppermute(value, "items", flow[0]) for flow, value in flows]
        self.flows = [(pairs, sign, left - 1) for (pairs, sign, left), _ in flows]

    def advance(self):
        flows = []
        for flow, value in zip(self.flows, self.arriving):
            if flow[2]:
                flows.append((flow, self.block(flow[1] * flow[2]) + value))
            else:
                self.result = self.result + value.astype(jnp.float32)
        self.send(flows)

    def finish(self):
        while self.arriving:
            self.advance()
        return self.result


def in_rows(value):
    return with_layout_constraint(value, Layout((0, 1)))


def halves(value, core):
    half = value.shape[1] // 2
    return cut(value, core * half, half, 1)


def parted(value, at):
    return (None, None) if value is None else (value[:, :at], value[:, at:])


def shards(
    tokens,
    cotangent,
    prompt_len,
    section_ids,
    section_table,
    w_query,
    w_key,
    w_value,
    w_out,
    w_up,
    w_down,
    w_ada_one,
    w_ada_two,
):
    items_count = lax.axis_size("items")
    seq_count = lax.axis_size("seq")
    mover = Mover(items_count, seq_count)
    chips = mover.chips
    batch, rows, width = tokens.shape
    total_rows = rows * seq_count
    hidden = w_up.shape[1] // seq_count
    held = width // seq_count
    pairs = held // LANES
    piece = w_query.shape[0]
    units = w_down.shape[0] // seq_count
    tokens = tokens.reshape(rows, width)
    grad_low = cotangent.reshape(rows, width)

    def quarters(one, two):
        return jnp.stack([one[:, :width], one[:, width:], two[:, :width], two[:, width:]])

    up_shard = w_up.reshape(piece, chips, 2, seq_count, units).transpose(3, 0, 2, 1, 4)
    up_shard = pick(up_shard, mover.seq, 0).reshape(piece, hidden)
    down_shard = cut(w_down, mover.seq * units, units, 0)
    merged = hidden % width == 0 and units % piece == 0
    late = down_shard
    if merged:
        folds = hidden // width
        down_parts = units // piece
        up_rows = [up_shard[:, j * width : (j + 1) * width] for j in range(folds)]
        late = jnp.concatenate([down_shard] + up_rows + [w_out], axis=0)

    table_part = cut(section_table, mover.item * piece, piece, 1)
    ada_part = jnp.dot(
        table_part,
        jnp.concatenate([w_ada_one, w_ada_two], axis=1),
        preferred_element_type=jnp.float32,
    )
    ada_part = quarters(ada_part[:, : 2 * width], ada_part[:, 2 * width :])
    mine = [cut(w, mover.seq * held, held, 1) for w in (w_query, w_key, w_value)]
    mine = [w[:, p * LANES : (p + 1) * LANES] for p in range(pairs) for w in mine]
    blocks, ada_sum, late = mover.gather_items(jnp.concatenate(mine, axis=1), ada_part, late)

    def gathered(value):
        return lax.all_gather(value, "items", axis=0, tiled=False)

    if merged:
        rest = gathered(late)
        rest = rest.reshape(items_count, down_parts + folds + 1, piece, width)
        by_core = rest.reshape((chips, 2) + rest.shape[1:])
        weights = Weights(rest, down_parts, by_core, down_parts, hidden, width)
        out_w, out_part = rest, down_parts + folds
    else:
        by_core = gathered(late).reshape(chips, 2, 1, units, width)
        weights = Weights(gathered(up_shard)[:, None], 0, by_core, 1, hidden, width)
        out_w, out_part = gathered(w_out)[:, None], 0

    choose = (section_ids[0] == jnp.arange(section_table.shape[0])).astype(jnp.float32)
    ada = jnp.sum(choose[None, :, None] * ada_sum, axis=1)
    ada_one = ada[:2]
    ada_two = ada[2:]

    if mover.pair:
        prompt_at = mover.seq
        tokens_other = mover.across(tokens)
        grad_other = mover.across(grad_low)
        frames = [tokens, tokens_other]
        grads = [grad_low, grad_other]
        spots = jnp.stack([mover.seq, 1 - mover.seq])
        other_spots = jnp.stack([1 - mover.seq, mover.seq])
    else:
        prompt_at = jnp.zeros((), jnp.int32)
        frames = [lax.all_gather(tokens, "seq", axis=0, tiled=True)]
        grads = [lax.all_gather(grad_low, "seq", axis=0, tiled=True)]
        spots = other_spots = jnp.zeros((1,), jnp.int32)
    low_one, qkv, qkv_w = first_layer(frames, ada_one, blocks, mover.spots)
    length = prompt_len[0]
    mixed_heads, lse = attend(
        qkv, jnp.stack([prompt_at, length]).astype(jnp.int32), grads[1:]
    )
    if mover.pair:
        mixed_parts = [mixed_heads[:rows], mover.across(mixed_heads[rows:])]
        mixed = jnp.where(
            mover.seq == 0,
            jnp.concatenate(mixed_parts, axis=1),
            jnp.concatenate(mixed_parts[::-1], axis=1),
        )
    else:
        mixed = lax.all_to_all(mixed_heads, "seq", split_axis=0, concat_axis=1, tiled=True)
        mixed_parts = [mixed]
    attended, low_two = second_layer(mixed_parts, tokens, out_w, out_part, ada_two, spots)

    if mover.pair:
        low_other = mover.across(low_two)
        both = hidden_layer(low_two, grad_low, weights, total_rows, 0)
        active, upward = hidden_layer(low_other, grad_other, weights, total_rows, 1, both)
        lows = [low_two, low_other]
        for_other = up_back(upward, weights, rows, 1, jnp.bfloat16)
        from_other = mover.across(for_other)
        start = [for_other]
    else:
        lows = [lax.all_gather(low_two, "seq", axis=0, tiled=True)]
        active, upward = hidden_layer(lows[0], grads[0], weights, total_rows, 0)
        start = []

    down_columns = hidden // 2

    def hidden_parts(own, other, behind):
        spot = mover.core_spot if own else mover.beside_spot
        if down_columns == width:
            return hidden_grads(spot, active, upward, grads, lows, other, behind)
        core = mover.core if own else mover.beside
        first, second = parted(other, down_columns)
        down = dot_rows(halves(active, core), grads[0]).reshape(width, down_columns)
        up = dot_rows(lows[0], halves(upward, core))
        return in_rows(jnp.concatenate([rounded(down, first), rounded(up, second)], axis=1))

    ring = RingSum(mover, hidden_parts, start)
    if mover.pair:
        own = up_back(upward, weights, rows, 0, jnp.float32, [ring.sent])
        sizes = [held, held]
    else:
        own = lax.psum_scatter(
            up_back(upward, weights, total_rows, 0, jnp.bfloat16),
            "seq",
            scatter_dimension=0,
            tiled=True,
        ).astype(jnp.float32)
        from_other = jnp.zeros((rows, width), jnp.bfloat16)
        sizes = [width]
    ring.add_own([own])
    grad_attended, attended_low, ada_two_rows, *grad_mixed = middle_back(
        own,
        from_other,
        attended,
        grad_low,
        ada_two,
        out_w,
        out_part,
        other_spots,
        sizes,
        [ring.whole],
    )
    if mover.pair:
        out_other = down_part(active, weights, rows, 1, jnp.bfloat16, grad_mixed[:1])
        grad_heads = [grad_mixed[1], mover.across(grad_mixed[0])]
        filler = [out_other]
        out_other = mover.across(out_other)
    else:
        grad_heads = [
            lax.all_to_all(grad_mixed[0], "seq", split_axis=1, concat_axis=0, tiled=True)
        ]
        filler = []

    split = pairs // 2 if pairs % 2 == 0 else 0

    def tail_parts(own, other, behind):
        spot = mover.core_spot if own else mover.beside_spot
        if pairs % 4 == 0:
            return tail_grads(spot, low_one, grad_qkv, mixed, attended_low, other, behind)
        core = mover.core if own else mover.beside
        first, second = parted(other, grad_qkv.shape[1] // 2)
        qkv_part = rounded(dot_rows(low_one, halves(grad_qkv, core)), first)
        out_part = rounded(dot_rows(mixed, halves(attended_low, core)), second)
        return in_rows(jnp.concatenate([qkv_part, out_part], axis=1))

    tail = None
    grad_qkv = None
    for turn in range(pairs):
        behind = filler
        filler = []
        if turn != 1:
            behind = behind + ring.arriving
        pair = (mover.beside * split + turn) & (pairs - 1)
        place = jnp.stack([prompt_at, length, pair]).astype(jnp.int32)
        grad_qkv = attend_back(place, qkv, mixed_heads, grad_heads, lse, grad_qkv, behind)
        if turn != 1:
            ring.advance()
        if turn + 1 == split:
            tail = RingSum(mover, tail_parts, [])
            filler = [tail.sent]
    if tail is None:
        tail = RingSum(mover, tail_parts, [])
    tail.add_own([])
    grad_first, ada_one_rows = first_back(grad_qkv, qkv_w, frames, [tail.whole])
    ada_rows = jnp.concatenate([ada_one_rows, ada_two_rows])
    if mover.pair:
        grad_parts = [grad_first[:rows], mover.across(grad_first[rows:])]
        layer_sum = down_part(active, weights, rows, 0, jnp.float32, [ada_one_rows])
        layer_sum = layer_sum + out_other.astype(jnp.float32)
    else:
        grad_parts = [lax.psum_scatter(grad_first, "seq", scatter_dimension=0, tiled=True)]
        layer_sum = lax.psum_scatter(
            down_part(active, weights, total_rows, 0, jnp.bfloat16),
            "seq",
            scatter_dimension=0,
            tiled=True,
        ).astype(jnp.float32)
    layer_out = (attended + layer_sum).astype(jnp.bfloat16)
    input_grad = input_back(grad_parts, tokens, ada_one, grad_attended)

    sums = mover.sum_seq(choose[None, :, None] * ada_rows[:, None, :])
    bit = 1
    while bit < items_count:
        sums = sums + mover.flip(sums, bit)
        bit *= 2
    out_piece = piece // seq_count
    first_row = mover.item * piece + mover.seq * out_piece
    table_rows = cut(section_table, first_row, out_piece, 1).astype(jnp.float32)
    ada_grads = jnp.einsum("sr,ksd->krd", table_rows, sums, precision=lax.Precision.HIGHEST)
    grad_ada_one = jnp.concatenate([ada_grads[0], ada_grads[1]], axis=1)
    grad_ada_two = jnp.concatenate([ada_grads[2], ada_grads[3]], axis=1)
    own_ada = quarters(
        *(cut(w, mover.seq * out_piece, out_piece, 0) for w in (w_ada_one, w_ada_two))
    ).astype(jnp.float32)
    grad_table = jnp.einsum("ksd,krd->sr", sums, own_ada, precision=lax.Precision.HIGHEST)

    ring_total = ring.finish()
    grad_down = ring_total[:, :down_columns].reshape(units, width)
    up_sides = mover.join_columns(
        jnp.concatenate(mover.join_cores(ring_total[:, down_columns:]), axis=1)
    )
    grad_up = jnp.stack(
        [side.reshape(out_piece, 2, chips, units) for side in up_sides], axis=1
    )
    grad_up = grad_up.transpose(0, 3, 2, 1, 4).reshape(out_piece, hidden * seq_count)
    tail_total = tail.finish()
    cores = jnp.concatenate(mover.join_cores(tail_total), axis=1)
    half_qkv = 3 * held // 2
    half_all = cores.shape[1] // 2
    qkv_total = jnp.concatenate(
        [cores[:, :half_qkv], cores[:, half_all : half_all + half_qkv]], axis=1
    )
    out_total = jnp.concatenate([cores[:, half_qkv:half_all], cores[:, half_all + half_qkv :]], axis=1)
    sides = mover.join_columns(qkv_total)
    grad_out = mover.scatter_seq(out_total)
    grad_query, grad_key, grad_value = (
        jnp.concatenate(
            [
                side[:, (3 * p + j) * LANES : (3 * p + j + 1) * LANES]
                for side in sides
                for p in range(pairs)
            ],
            axis=1,
        )
        for j in range(3)
    )
    return (
        layer_out.reshape(batch, rows, width),
        input_grad.reshape(batch, rows, width),
        grad_query,
        grad_key,
        grad_value,
        grad_out,
        grad_up,
        grad_down,
        grad_ada_one,
        grad_ada_two,
        grad_table,
    )


def solution(mesh):
    return jax.shard_map(
        shards,
        mesh=mesh,
        in_specs=(
            P("items", "seq", None),
            P("items", "seq", None),
            P("items"),
            P("items"),
            P(),
            P("items", None),
            P("items", None),
            P("items", None),
            P("items", None),
            P("items", None),
            P("items", None),
            P("items", None),
            P("items", None),
        ),
        out_specs=(
            P("items", "seq", None),
            P("items", "seq", None),
            P(("items", "seq"), None),
            P(("items", "seq"), None),
            P(("items", "seq"), None),
            P(("items", "seq"), None),
            P(("items", "seq"), None),
            P(("items", "seq"), None),
            P(("items", "seq"), None),
            P(("items", "seq"), None),
            P(None, ("items", "seq")),
        ),
        check_vma=False,
    )
```

time: 563 us -> 461 us (0.82)
  Pallas kernels: 69.2 us -> 214 us
  matrix products: 127 us -> 3.36 us
  waiting for transfers between devices: 204 us -> 91.8 us
  local copies, waits for them, and re-layouts: 51.4 us -> 34.5 us
  other arithmetic: 20.6 us -> 36.1 us
  between operations: 31.7 us -> 17.7 us
  starting transfers between devices: 51.4 us -> 58.1 us
    pallas_call x1 -> x19, Pallas kernels: 41.5 us -> 185 us  [the longest x4 45.3 us: attend_back(): pl.pallas_call(partial(attend_back_kernel, parts), grid_spec=pltpu.Prefet...]
    dot_general x15 -> x3, matrix products: 127 us -> 3.36 us  [the longest x1 1.28 us: shards(): jnp.dot(table_part, jnp.concatenate([w_ada_one, w_ada_two], axis=1), pref...]
    all_gather x2 -> x1, waiting for transfers between devices: 66.5 us -> 0.01 us  [gathered(): return lax.all_gather(value, 'items', axis=0, tiled=False)]
    ppermute x28 -> x21, waiting for transfers between devices: 79.7 us -> 34 us  [the longest x14 22 us: send(): lax.ppermute(value, 'items', flow[0])]
    ppermute x12 -> x20, starting transfers between devices: 9.76 us -> 22 us  [flip(): return lax.ppermute(value, 'items', pairs)]
    add x32 -> x18, other arithmetic: 10.9 us -> 22.4 us  [the longest x7 16.6 us: advance(): flows.append((flow, self.block(flow[1] * flow[2]) + value))]
    unnamed x94 -> x105, local copies, waits for them, and re-layouts: 20.3 us -> 12.6 us
    transpose x1, local copies, waits for them, and re-layouts: 7.82 us -> 1.21 us  [shards(): grad_up.transpose(0, 3, 2, 1, 4).reshape(out_piece, hidden * seq_count)]
  transfers between devices with their start and end apart: 51 -> 54, of which waited for: 25 -> 24; matrix products, arithmetic and copies ran while one was open for 12% -> 13% of each run, Pallas kernels for 12% -> 39%
where the time goes in v2:
time: 461 us; the launch traced here: 455 us
  Pallas kernels  214 us (46%)
  waiting for transfers between devices  91.8 us (20%)
  starting transfers between devices  58.1 us (13%)
  other arithmetic  36.1 us (8%)
  local copies, waits for them, and re-layouts  34.5 us (7%)
  between operations  17.7 us (4%)
    pallas_call x4, Pallas kernels, attend_back(): pl.pallas_call(partial(attend_back_kernel, parts), grid_spec=pltpu.Prefet...  45.3 us
    ppermute x12, waiting for transfers between devices, across(): return lax.ppermute(value, 'seq', [(0, 1), (1, 0)])  39.3 us
    pallas_call x4, Pallas kernels, hidden_to_width(): pl.pallas_call(kernel, grid=(weights.steps,), in_specs=[pl.BlockSpec((row...  31 us
    pallas_call x1, Pallas kernels, attend(): pl.pallas_call(attend_kernel, grid_spec=pltpu.PrefetchScalarGridSpec(num_...  28.4 us
    pallas_call x2, Pallas kernels, hidden_grads(): pl.pallas_call(partial(hidden_grads_kernel, count, bool(more)), grid_spec...  26 us
    ppermute x14, waiting for transfers between devices, send(): lax.ppermute(value, 'items', flow[0])  22 us
    pallas_call x2, Pallas kernels, hidden_layer(): pl.pallas_call(partial(hidden_kernel, weights.per_chip), grid=(weights.st...  22 us
    ppermute x20, starting transfers between devices, flip(): return lax.ppermute(value, 'items', pairs)  22 us
  transfers between devices with their start and end apart: 54, of which 24 were waited for; matrix products, arithmetic and copies ran while one was open for 13% of the time, Pallas kernels for 39%

profile of v2, /device:TPU:0, one launch (start us, length us, event | category | flops | bytes accessed | tf_op | source)
XLA Modules:
  0.0 455.2 jit_solution(11214863627021726938)
XLA Ops:
  16.0 3.0 collective-permute-start.4
  26.1 5.3 %collective-permute-done.5.refs_5_ = bf16[64,1536]{1,0:T(8,128)(2,1)S(1)} collective-permute-done((bf16[64,1536]{1,0:T(8,128)(2,1)}, bf16[64,1536]{1,0:T(8,128)(2,1)S(1)}, u32[]{:S(2)}, u32[]{:S(2)}) %collective-permute-start.5) | collective-permute-done | bytes 196640 | tf_op jit(solution)/shard_map/ppermute | solution.py:849
  41.1 2.2 collective-permute-done.7.refs_8_
  47.0 9.4 %collective-permute-done.9 = f32[4,8,1024]{2,1,0:T(8,128)S(1)} collective-permute-done((f32[4,8,1024]{2,1,0:T(8,128)S(1)}, f32[4,8,1024]{2,1,0:T(8,128)S(1)}, u32[]{:S(2)}, u32[]{:S(2)}) %collective-permute-start.9) | collective-permute-done | bytes 131104 | tf_op jit(solution)/shard_map/ppermute | solution.py:838
  56.4 2.6 collective-permute-done.10.refs_7_
  59.0 11.3 %collective-permute-start.11 = (f32[4,8,1024]{2,1,0:T(8,128)S(1)}, f32[4,8,1024]{2,1,0:T(8,128)S(1)}, u32[]{:S(2)}, u32[]{:S(2)}) collective-permute-start(f32[4,8,1024]{2,1,0:T(8,128)S(1)} %add.116), channel_id=1, source_target_pairs={{0,16},{2,18},{4,20},{6,22},{8,24},{10,26},{12,28},{14,30},{16,0},... | collective-permute-start | bytes 393224 | tf_op jit(solution)/shard_map/ppermute | solution.py:838
  71.6 4.9 %collective-permute-done.11 = f32[4,8,1024]{2,1,0:T(8,128)S(1)} collective-permute-done((f32[4,8,1024]{2,1,0:T(8,128)S(1)}, f32[4,8,1024]{2,1,0:T(8,128)S(1)}, u32[]{:S(2)}, u32[]{:S(2)}) %collective-permute-start.11) | collective-permute-done | bytes 131104 | tf_op jit(solution)/shard_map/ppermute | solution.py:838
  80.3 11.3 %first_layer.1 = (bf16[1280,1024]{1,0:T(8,128)(2,1)}, bf16[1280,1536]{1,0:T(8,128)(2,1)}, bf16[1024,1536]{1,0:T(8,128)(2,1)}) custom-call(s32[16]{0:T(128)} %pad_add_fusion.2.spots, bf16[640,1024]{1,0:T(8,128)(2,1)} %bitcast.6.refs_0_.refs_2_.tokens_ref, bf16[640,1024]{1,0:T(8,128)(2,1)} %collective-permute-done.refs_1_, ...), custom_call_target="tpu_custom_call" | custom-call | flops 2013265920 | bytes 8388608 | tf_op jit(solution)/shard_map/first_layer/pallas_call | solution.py:314
  91.7 28.4 %attend.1 = (bf16[1280,512]{1,0:T(8,128)(2,1)S(1)}, f32[4,10,256]{2,1,0:T(8,128)S(1)}) custom-call(s32[2]{0:T(128)S(1)} %pad_add_fusion.1.place, bf16[1280,1536]{1,0:T(8,128)(2,1)} %get-tuple-element.50.q_ref.k_ref.v_ref, bf16[1280,1536]{1,0:T(8,128)(2,1)} %get-tuple-element.50.q_ref.k_ref.v_ref, bf16[1280,1536]{1,0:T(8,128)(2,1)} %get-tuple-element.50.q_ref.k_ref.v_ref, ...), custom_call_target="tpu_custom_call" | custom-call | flops 5033164800 | bytes 5242880 | tf_op jit(solution)/shard_map/attend/pallas_call | solution.py:92
  122.8 15.1 %collective-permute-done.21.refs_1_ = bf16[640,512]{1,0:T(8,128)(2,1)S(1)} collective-permute-done((bf16[640,512]{1,0:T(8,128)(2,1)S(1)}, bf16[640,512]{1,0:T(8,128)(2,1)S(1)}, u32[]{:S(2)}, u32[]{:S(2)}) %collective-permute-start.21) | collective-permute-done | bytes 655392 | tf_op jit(solution)/shard_map/ppermute | solution.py:841
  138.7 6.1 %second_layer.1 = (f32[640,1024]{1,0:T(8,128)}, bf16[640,1024]{1,0:T(8,128)(2,1)}) custom-call(s32[2]{0:T(128)} %pad_add_fusion.spots, bf16[640,512]{1,0:T(8,128)(2,1)} %get-tuple-element.84.refs_0_, bf16[640,512]{1,0:T(8,128)(2,1)} %copy-done.12, bf16[640,1024]{1,0:T(8,128)(2,1)} %bitcast.6.refs_0_.refs_2_.tokens_ref, bf16[16,5,64,1024]{3,2,1,0:T(8,128)(2,1)} %bitcast.127, ...), custom_call_target="tpu_custom_call" | custom-call | flops 671088640 | bytes 4325376 | tf_op jit(solution)/shard_map/second_layer/pallas_call | solution.py:362
  146.0 11.0 %hidden_layer.2 = (bf16[1280,2048]{1,0:T(8,128)(2,1)}, bf16[1280,2048]{1,0:T(8,128)(2,1)}) custom-call(bf16[640,1024]{1,0:T(8,128)(2,1)} %get-tuple-element.54.x_ref.refs_4_, bf16[640,1024]{1,0:T(8,128)(2,1)} %bitcast.148, bf16[16,5,64,1024]{3,2,1,0:T(8,128)(2,1)} %bitcast.128, bf16[8,2,5,64,1024]{4,3,2,1,0:T(8,128)(2,1)} %bitcast.129), custom_call_target="tpu_custom_call" | custom-call | flops 2684354560 | bytes 8126464 | tf_op jit(solution)/shard_map/hidden_layer/pallas_call | solution.py:431
  157.0 18.1 %collective-permute-done.22.x_ref.refs_5_ = bf16[640,1024]{1,0:T(8,128)(2,1)S(1)} collective-permute-done((bf16[640,1024]{1,0:T(8,128)(2,1)}, bf16[640,1024]{1,0:T(8,128)(2,1)S(1)}, u32[]{:S(2)}, u32[]{:S(2)}) %collective-permute-start.22) | collective-permute-done | bytes 1310752 | tf_op jit(solution)/shard_map/ppermute | solution.py:841
  176.2 11.0 %hidden_layer.3 = (bf16[1280,2048]{1,0:T(8,128)(2,1)}, bf16[1280,2048]{1,0:T(8,128)(2,1)}) custom-call(bf16[640,1024]{1,0:T(8,128)(2,1)} %copy-done.9, bf16[640,1024]{1,0:T(8,128)(2,1)} %copy-done.2, bf16[16,5,64,1024]{3,2,1,0:T(8,128)(2,1)} %bitcast.130, bf16[8,2,5,64,1024]{4,3,2,1,0:T(8,128)(2,1)} %bitcast.131, ...), custom_call_target="tpu_custom_call", output_to_operand_aliasing={{0}: (4, {}), {1}: (5, {})} | custom-call | flops 2684354560 | bytes 8126464 | tf_op jit(solution)/shard_map/hidden_layer/pallas_call | solution.py:431
  187.2 7.5 %up_back.2.refs_6_ = bf16[640,1024]{1,0:T(8,128)(2,1)} custom-call(bf16[1280,2048]{1,0:T(8,128)(2,1)} %get-tuple-element.59.g_ref.refs_1_, bf16[16,5,64,1024]{3,2,1,0:T(8,128)(2,1)} %bitcast.132), custom_call_target="tpu_custom_call" | custom-call | flops 1342177280 | bytes 4718592 | tf_op jit(solution)/shard_map/up_back/pallas_call | solution.py:476
  194.7 12.8 %hidden_grads.2.refs_0_ = bf16[1024,2048]{1,0:T(8,128)(2,1)} custom-call(s32[1]{0:T(128)} %bitcast.17.core, bf16[1280,2048]{1,0:T(8,128)(2,1)} %get-tuple-element.57.refs_0_.a_ref, bf16[1280,2048]{1,0:T(8,128)(2,1)} %get-tuple-element.59.g_ref.refs_1_, bf16[640,1024]{1,0:T(8,128)(2,1)} %bitcast.149, bf16[640,1024]{1,0:T(8,128)(2,1)} %copy-done.2, ...), custom_call_target="tpu_custom_call" | custom-call | flops 2684354560 | bytes 7340032 | tf_op jit(solution)/shard_map/hidden_grads/pallas_call | solution.py:665
  208.8 8.3 %up_back.3.refs_7_.refs_0_ = f32[640,1024]{1,0:T(8,128)} custom-call(bf16[1280,2048]{1,0:T(8,128)(2,1)} %get-tuple-element.59.g_ref.refs_1_, bf16[16,5,64,1024]{3,2,1,0:T(8,128)(2,1)} %bitcast.133, bf16[1024,2048]{1,0:T(8,128)(2,1)} %hidden_grads.2.refs_0_), custom_call_target="tpu_custom_call" | custom-call | flops 1342177280 | bytes 4718592 | tf_op jit(solution)/shard_map/up_back/pallas_call | solution.py:476
  217.2 13.1 %hidden_grads.3.refs_6_ = bf16[1024,2048]{1,0:T(8,128)(2,1)} custom-call(s32[1]{0:T(128)} %bitcast.18.core, bf16[1280,2048]{1,0:T(8,128)(2,1)} %get-tuple-element.57.refs_0_.a_ref, bf16[1280,2048]{1,0:T(8,128)(2,1)} %get-tuple-element.59.g_ref.refs_1_, bf16[640,1024]{1,0:T(8,128)(2,1)} %bitcast.150, bf16[640,1024]{1,0:T(8,128)(2,1)} %copy-done.2, ...), custom_call_target="tpu_custom_call" | custom-call | flops 2684354560 | bytes 7340032 | tf_op jit(solution)/shard_map/hidden_grads/pallas_call | solution.py:665
  230.3 3.5 dynamic-slice_bitcast_fusion
  237.6 11.1 %collective-permute-done.26.refs_3_ = bf16[128,2048]{1,0:T(8,128)(2,1)S(1)} collective-permute-done((bf16[128,2048]{1,0:T(8,128)(2,1)}, bf16[128,2048]{1,0:T(8,128)(2,1)S(1)}, u32[]{:S(2)}, u32[]{:S(2)}) %collective-permute-start.26) | collective-permute-done | bytes 524320 | tf_op jit(solution)/shard_map/ppermute | solution.py:916
  248.7 2.6 bitcast_add_fusion.4
  251.4 8.9 %middle_back.1 = (f32[640,1024]{1,0:T(8,128)}, bf16[640,1024]{1,0:T(8,128)(2,1)}, f32[2,1024]{1,0:T(2,128)}, bf16[640,512]{1,0:T(8,128)(2,1)}, bf16[640,512]{1,0:T(8,128)(2,1)}) custom-call(s32[2]{0:T(128)} %pad_add_fusion.5.spots, f32[640,1024]{1,0:T(8,128)} %up_back.3.refs_7_.refs_0_, bf16[640,1024]{1,0:T(8,128)(2,1)} %collective-permute-done.23.refs_1_, ...), custom_call_target="tpu_custom_call" | custom-call | flops 671088640 | bytes 7602176 | tf_op jit(solution)/shard_map/middle_back/pallas_call | solution.py:551
  261.0 2.8 maximum_select_fusion.mixed
  263.7 7.3 %down_part.2.refs_2_ = bf16[640,1024]{1,0:T(8,128)(2,1)} custom-call(bf16[1280,2048]{1,0:T(8,128)(2,1)} %get-tuple-element.57.refs_0_.a_ref, bf16[8,2,5,64,1024]{4,3,2,1,0:T(8,128)(2,1)} %bitcast.135, bf16[640,512]{1,0:T(8,128)(2,1)} %get-tuple-element.61.refs_0_), custom_call_target="tpu_custom_call" | custom-call | flops 1342177280 | bytes 4718592 | tf_op jit(solution)/shard_map/down_part/pallas_call | solution.py:476
  271.1 3.8 bitcast_add_fusion.2
  276.9 11.3 %attend_back.4.refs_2_ = bf16[1280,1536]{1,0:T(8,128)(2,1)} custom-call(s32[3]{0:T(128)S(1)} %get-tuple-element.69.place, bf16[1280,1536]{1,0:T(8,128)(2,1)} %get-tuple-element.50.q_ref.k_ref.v_ref, bf16[1280,1536]{1,0:T(8,128)(2,1)} %get-tuple-element.50.q_ref.k_ref.v_ref, bf16[1280,1536]{1,0:T(8,128)(2,1)} %get-tuple-element.50.q_ref.k_ref.v_ref, ...), custom_call_target="tpu_custom_call" | custom-call | flops 3145728000 | bytes 3276800 | tf_op jit(solution)/shard_map/attend_back/pallas_call | solution.py:194
  288.2 11.3 %attend_back.5.grad.refs_2_ = bf16[1280,1536]{1,0:T(8,128)(2,1)} custom-call(s32[3]{0:T(128)S(1)} %get-tuple-element.145.place, bf16[1280,1536]{1,0:T(8,128)(2,1)} %get-tuple-element.50.q_ref.k_ref.v_ref, bf16[1280,1536]{1,0:T(8,128)(2,1)} %get-tuple-element.50.q_ref.k_ref.v_ref, ...), custom_call_target="tpu_custom_call", output_to_operand_aliasing={{}: (8, {})} | custom-call | flops 3145728000 | bytes 3276800 | tf_op jit(solution)/shard_map/attend_back/pallas_call | solution.py:194
  299.6 8.9 %tail_grads.2.refs_3_ = bf16[1024,1280]{1,0:T(8,128)(2,1)} custom-call(s32[1]{0:T(128)} %bitcast.17.core, bf16[1280,1024]{1,0:T(8,128)(2,1)} %get-tuple-element.62.low, bf16[1280,1536]{1,0:T(8,128)(2,1)} %attend_back.5.grad.refs_2_, bf16[640,1024]{1,0:T(8,128)(2,1)} %maximum_select_fusion.mixed, bf16[640,1024]{1,0:T(8,128)(2,1)} %get-tuple-element.63.attended), custom_call_target="tpu_custom_call" | custom-call | flops 1342177280 | bytes 5242880 | tf_op jit(solution)/shard_map/tail_grads/pallas_call | solution.py:710
  308.6 4.0 bitcast_add_fusion
  318.2 11.5 %attend_back.6.refs_2_ = bf16[1280,1536]{1,0:T(8,128)(2,1)} custom-call(s32[3]{0:T(128)S(1)} %get-tuple-element.146.place, bf16[1280,1536]{1,0:T(8,128)(2,1)} %get-tuple-element.50.q_ref.k_ref.v_ref, bf16[1280,1536]{1,0:T(8,128)(2,1)} %get-tuple-element.50.q_ref.k_ref.v_ref, ...), custom_call_target="tpu_custom_call", output_to_operand_aliasing={{}: (8, {})} | custom-call | flops 3145728000 | bytes 3276800 | tf_op jit(solution)/shard_map/attend_back/pallas_call | solution.py:194
  329.7 2.2 fusion.1
  333.5 11.2 %attend_back.7.grad.grad_ref = bf16[1280,1536]{1,0:T(8,128)(2,1)} custom-call(s32[3]{0:T(128)S(1)} %get-tuple-element.147.place, bf16[1280,1536]{1,0:T(8,128)(2,1)} %get-tuple-element.50.q_ref.k_ref.v_ref, bf16[1280,1536]{1,0:T(8,128)(2,1)} %get-tuple-element.50.q_ref.k_ref.v_ref, ...), custom_call_target="tpu_custom_call", output_to_operand_aliasing={{}: (8, {})} | custom-call | flops 3145728000 | bytes 3276800 | tf_op jit(solution)/shard_map/attend_back/pallas_call | solution.py:194
  346.3 9.4 %tail_grads.3.refs_2_ = bf16[1024,1280]{1,0:T(8,128)(2,1)} custom-call(s32[1]{0:T(128)} %bitcast.18.core, bf16[1280,1024]{1,0:T(8,128)(2,1)} %get-tuple-element.62.low, bf16[1280,1536]{1,0:T(8,128)(2,1)} %attend_back.7.grad.grad_ref, bf16[640,1024]{1,0:T(8,128)(2,1)} %maximum_select_fusion.mixed, bf16[640,1024]{1,0:T(8,128)(2,1)} %get-tuple-element.63.attended, ...), custom_call_target="tpu_custom_call" | custom-call | flops 1342177280 | bytes 5242880 | tf_op jit(solution)/shard_map/tail_grads/pallas_call | solution.py:710
  355.7 9.4 %first_back.1 = (bf16[1280,1024]{1,0:T(8,128)(2,1)}, f32[2,1024]{1,0:T(2,128)}) custom-call(bf16[1280,1536]{1,0:T(8,128)(2,1)} %attend_back.7.grad.grad_ref, bf16[1024,1536]{1,0:T(8,128)(2,1)} %get-tuple-element.64.weight_ref, bf16[640,1024]{1,0:T(8,128)(2,1)} %bitcast.6.refs_0_.refs_2_.tokens_ref, bf16[640,1024]{1,0:T(8,128)(2,1)} %collective-permute-done.refs_1_, ...), custom_call_target="tpu_custom_call" | custom-call | flops 2013265920 | bytes 6160384 | tf_op jit(solution)/shard_map/first_back/pallas_call | solution.py:593
  371.9 7.0 %collective-permute-done.35 = bf16[128,1280]{1,0:T(8,128)(2,1)S(1)} collective-permute-done((bf16[128,1280]{1,0:T(8,128)(2,1)S(1)}, bf16[128,1280]{1,0:T(8,128)(2,1)S(1)}, u32[]{:S(2)}, u32[]{:S(2)}) %collective-permute-start.35) | collective-permute-done | bytes 327712 | tf_op jit(solution)/shard_map/ppermute | solution.py:916
  380.4 2.0 collective-permute-start.36
  383.6 2.3 reshape.107
  388.4 2.1 collective-permute-done.36
  390.5 2.5 bitcast_add_fusion.9
  394.3 3.5 fusion.30
  398.5 7.8 %down_part.3 = f32[640,1024]{1,0:T(8,128)} custom-call(bf16[1280,2048]{1,0:T(8,128)(2,1)} %get-tuple-element.57.refs_0_.a_ref, bf16[8,2,5,64,1024]{4,3,2,1,0:T(8,128)(2,1)} %bitcast.136, f32[2,1024]{1,0:T(2,128)} %get-tuple-element.65.refs_0_), custom_call_target="tpu_custom_call" | custom-call | flops 1342177280 | bytes 4718592 | tf_op jit(solution)/shard_map/down_part/pallas_call | solution.py:476
  410.3 4.7 %fusion = bf16[1,640,1024]{2,1,0:T(8,128)(2,1)} fusion(f32[640,1024]{1,0:T(8,128)} %get-tuple-element.53.refs_2_, f32[640,1024]{1,0:T(8,128)} %down_part.3, bf16[640,1024]{1,0:T(8,128)(2,1)} %collective-permute-done.33), kind=kLoop, calls=%fused_computation.1 | loop fusion | flops 2621440 | bytes 7864320 | tf_op jit(solution)/shard_map/reshape | solution.py:1206
  415.1 2.6 collective-permute-start.52
  418.8 2.5 collective-permute-start.41
  421.3 2.5 collective-permute-done.52
  430.8 6.8 %input_back.1 = f32[640,1024]{1,0:T(8,128)} custom-call(bf16[640,1024]{1,0:T(8,128)(2,1)} %bitcast.6.refs_0_.refs_2_.tokens_ref, f32[2,1024]{1,0:T(2,128)} %get-tuple-element.134.refs_2_.ada_ref, f32[640,1024]{1,0:T(8,128)} %get-tuple-element.66.base_ref, bf16[640,1024]{1,0:T(8,128)(2,1)} %get-tuple-element.82.refs_0_, ...), custom_call_target="tpu_custom_call" | custom-call | flops 6553600 | bytes 4587520 | tf_op jit(solution)/shard_map/input_back/pallas_call | solution.py:754
  440.6 2.7 collective-permute-done.44
  444.0 3.2 collective-permute-done.43
  (256 shorter events, 84.6 us)
Async XLA Ops:
  7.2 130.7 %all-gather.3.cloned.1.call-start = ((), (), s32[]{:S(2)}) async-start(), calls=%async_computation | async-start | bytes 11141120 | tf_op jit(solution)/shard_map/all_gather | solution.py:1002
  16.0 8.0 %collective-permute-start.4 = (bf16[64,1536]{1,0:T(8,128)(2,1)S(1)}, bf16[64,1536]{1,0:T(8,128)(2,1)}, u32[]{:S(2)}, u32[]{:S(2)}) collective-permute-start(bf16[64,1536]{1,0:T(8,128)(2,1)S(1)} %constant_dynamic-update-slice_fusion.refs_3_), channel_id=1, source_target_pairs={{8,0},{10,2},{16,8},{18,10},{24,16},{26,18},{28,24},{30,26},{20,28... | collective-permute-start | bytes 589832 | tf_op jit(solution)/shard_map/ppermute | solution.py:849
  19.0 6.8 %collective-permute-start.2 = (bf16[64,1536]{1,0:T(8,128)(2,1)S(1)}, bf16[64,1536]{1,0:T(8,128)(2,1)S(1)}, u32[]{:S(2)}, u32[]{:S(2)}) collective-permute-start(bf16[64,1536]{1,0:T(8,128)(2,1)S(1)} %constant_dynamic-update-slice_fusion.refs_3_), channel_id=1, source_target_pairs={{0,8},{2,10},{8,16},{10,18},{16,24},{18,26},{24,28},{26,30},{28,20... | collective-permute-start | bytes 589832 | tf_op jit(solution)/shard_map/ppermute | solution.py:849
  24.0 7.3 %collective-permute-start.5 = (bf16[64,1536]{1,0:T(8,128)(2,1)}, bf16[64,1536]{1,0:T(8,128)(2,1)S(1)}, u32[]{:S(2)}, u32[]{:S(2)}) collective-permute-start(bf16[64,1536]{1,0:T(8,128)(2,1)} %collective-permute-done.4.refs_4_), channel_id=1, source_target_pairs={{8,0},{10,2},{16,8},{18,10},{24,16},{26,18},{28,24},{30,26},{20,28... | collective-permute-start | bytes 589832 | tf_op jit(solution)/shard_map/ppermute | solution.py:849
  25.7 6.8 %collective-permute-start.3 = (bf16[64,1536]{1,0:T(8,128)(2,1)S(1)}, bf16[64,1536]{1,0:T(8,128)(2,1)S(1)}, u32[]{:S(2)}, u32[]{:S(2)}) collective-permute-start(bf16[64,1536]{1,0:T(8,128)(2,1)S(1)} %collective-permute-done.2.refs_10_), channel_id=1, source_target_pairs={{0,8},{2,10},{8,16},{10,18},{16,24},{18,26},{24,28},{26,30},{28,20... | collective-permute-start | bytes 589832 | tf_op jit(solution)/shard_map/ppermute | solution.py:849
  32.6 47.0 %collective-permute-start = (bf16[640,1024]{1,0:T(8,128)(2,1)}, bf16[640,1024]{1,0:T(8,128)(2,1)}, u32[]{:S(2)}, u32[]{:S(2)}) collective-permute-start(bf16[640,1024]{1,0:T(8,128)(2,1)} %bitcast.6.refs_0_.refs_2_.tokens_ref), channel_id=1, source_target_pairs={{0,1},{1,0},{2,3},{3,2},{4,5},{5,4},{6,7},{7,6},{8,9},{9,8},{10,11... | collective-permute-start | bytes 3932168 | tf_op jit(solution)/shard_map/ppermute | solution.py:841
  34.2 57.5 %collective-permute-start.20 = (bf16[640,1024]{1,0:T(8,128)(2,1)S(1)}, bf16[640,1024]{1,0:T(8,128)(2,1)S(1)}, u32[]{:S(2)}, u32[]{:S(2)}) collective-permute-start(bf16[640,1024]{1,0:T(8,128)(2,1)S(1)} %bitcast.152), channel_id=1, source_target_pairs={{0,1},{1,0},{2,3},{3,2},{4,5},{5,4},{6,7},{7,6},{8,9},{9,8},{10,11... | collective-permute-start | bytes 3932168 | tf_op jit(solution)/shard_map/ppermute | solution.py:841
  34.8 6.3 %collective-permute-start.6 = (f32[4,8,1024]{2,1,0:T(8,128)S(1)}, f32[4,8,1024]{2,1,0:T(8,128)S(1)}, u32[]{:S(2)}, u32[]{:S(2)}) collective-permute-start(f32[4,8,1024]{2,1,0:T(8,128)S(1)} %fusion.29), channel_id=1, source_target_pairs={{0,4},{2,6},{4,0},{6,2},{8,12},{10,14},{12,8},{14,10},{16,20},{18,... | collective-permute-start | bytes 393224 | tf_op jit(solution)/shard_map/ppermute | solution.py:838
  36.3 7.0 %collective-permute-start.7 = (bf16[64,1536]{1,0:T(8,128)(2,1)}, bf16[64,1536]{1,0:T(8,128)(2,1)S(1)}, u32[]{:S(2)}, u32[]{:S(2)}) collective-permute-start(bf16[64,1536]{1,0:T(8,128)(2,1)} %copy-done.30), channel_id=1, source_target_pairs={{0,8},{2,10},{8,16},{10,18},{16,24},{18,26},{24,28},{26,30},{28,20... | collective-permute-start | bytes 589832 | tf_op jit(solution)/shard_map/ppermute | solution.py:849
  37.9 5.7 %collective-permute-start.8 = (bf16[64,1536]{1,0:T(8,128)(2,1)S(1)}, bf16[64,1536]{1,0:T(8,128)(2,1)S(1)}, u32[]{:S(2)}, u32[]{:S(2)}) collective-permute-start(bf16[64,1536]{1,0:T(8,128)(2,1)S(1)} %collective-permute-done.5.refs_5_), channel_id=1, source_target_pairs={{8,0},{10,2},{16,8},{18,10},{24,16},{26,18},{28,24},{30,26},{20,28... | collective-permute-start | bytes 589832 | tf_op jit(solution)/shard_map/ppermute | solution.py:849
  41.1 30.0 %collective-permute-start.12 = (bf16[64,1536]{1,0:T(8,128)(2,1)S(1)}, bf16[64,1536]{1,0:T(8,128)(2,1)S(1)}, u32[]{:S(2)}, u32[]{:S(2)}) collective-permute-start(bf16[64,1536]{1,0:T(8,128)(2,1)S(1)} %constant_dynamic-update-slice_fusion.refs_3_), channel_id=1, source_target_pairs={{0,2},{2,0},{4,6},{6,4},{8,10},{10,8},{12,14},{14,12},{16,18},{18,... | collective-permute-start | bytes 589832 | tf_op jit(solution)/shard_map/ppermute | solution.py:838
  43.6 12.8 %collective-permute-start.9 = (f32[4,8,1024]{2,1,0:T(8,128)S(1)}, f32[4,8,1024]{2,1,0:T(8,128)S(1)}, u32[]{:S(2)}, u32[]{:S(2)}) collective-permute-start(f32[4,8,1024]{2,1,0:T(8,128)S(1)} %add.115), channel_id=1, source_target_pairs={{0,8},{2,10},{4,12},{6,14},{8,0},{10,2},{12,4},{14,6},{16,24},{18,... | collective-permute-start | bytes 393224 | tf_op jit(solution)/shard_map/ppermute | solution.py:838
  45.1 13.8 %collective-permute-start.10 = (bf16[64,1536]{1,0:T(8,128)(2,1)S(1)}, bf16[64,1536]{1,0:T(8,128)(2,1)S(1)}, u32[]{:S(2)}, u32[]{:S(2)}) collective-permute-start(bf16[64,1536]{1,0:T(8,128)(2,1)S(1)} %collective-permute-done.7.refs_8_), channel_id=1, source_target_pairs={{0,8},{2,10},{8,16},{10,18},{16,24},{18,26},{24,28},{26,30},{28,20... | collective-permute-start | bytes 589832 | tf_op jit(solution)/shard_map/ppermute | solution.py:849
  56.4 14.7 %collective-permute-start.13 = (bf16[64,1536]{1,0:T(8,128)(2,1)}, bf16[64,1536]{1,0:T(8,128)(2,1)S(1)}, u32[]{:S(2)}, u32[]{:S(2)}) collective-permute-start(bf16[64,1536]{1,0:T(8,128)(2,1)} %collective-permute-done.4.refs_4_), channel_id=1, source_target_pairs={{0,2},{2,0},{4,6},{6,4},{8,10},{10,8},{12,14},{14,12},{16,18},{18,... | collective-permute-start | bytes 589832 | tf_op jit(solution)/shard_map/ppermute | solution.py:838
  59.0 17.5 %collective-permute-start.11 = (f32[4,8,1024]{2,1,0:T(8,128)S(1)}, f32[4,8,1024]{2,1,0:T(8,128)S(1)}, u32[]{:S(2)}, u32[]{:S(2)}) collective-permute-start(f32[4,8,1024]{2,1,0:T(8,128)S(1)} %add.116), channel_id=1, source_target_pairs={{0,16},{2,18},{4,20},{6,22},{8,24},{10,26},{12,28},{14,30},{16,0},... | collective-permute-start | bytes 393224 | tf_op jit(solution)/shard_map/ppermute | solution.py:838
  71.1 6.2 %collective-permute-start.19 = (bf16[64,1536]{1,0:T(8,128)(2,1)}, bf16[64,1536]{1,0:T(8,128)(2,1)S(1)}, u32[]{:S(2)}, u32[]{:S(2)}) collective-permute-start(bf16[64,1536]{1,0:T(8,128)(2,1)} %copy-done.28), channel_id=1, source_target_pairs={{0,2},{2,0},{4,6},{6,4},{8,10},{10,8},{12,14},{14,12},{16,18},{18,... | collective-permute-start | bytes 589832 | tf_op jit(solution)/shard_map/ppermute | solution.py:838
  71.1 6.7 %collective-permute-start.18 = (bf16[64,1536]{1,0:T(8,128)(2,1)}, bf16[64,1536]{1,0:T(8,128)(2,1)S(1)}, u32[]{:S(2)}, u32[]{:S(2)}) collective-permute-start(bf16[64,1536]{1,0:T(8,128)(2,1)} %copy-done.30), channel_id=1, source_target_pairs={{0,2},{2,0},{4,6},{6,4},{8,10},{10,8},{12,14},{14,12},{16,18},{18,... | collective-permute-start | bytes 589832 | tf_op jit(solution)/shard_map/ppermute | solution.py:838
  121.0 16.8 %collective-permute-start.21 = (bf16[640,512]{1,0:T(8,128)(2,1)S(1)}, bf16[640,512]{1,0:T(8,128)(2,1)S(1)}, u32[]{:S(2)}, u32[]{:S(2)}) collective-permute-start(bf16[640,512]{1,0:T(8,128)(2,1)S(1)} %get-tuple-element.83), channel_id=1, source_target_pairs={{0,1},{1,0},{2,3},{3,2},{4,5},{5,4},{6,7},{7,6},{8,9},{9,8},{10,11... | collective-permute-start | bytes 1966088 | tf_op jit(solution)/shard_map/ppermute | solution.py:841
  144.8 30.3 %collective-permute-start.22 = (bf16[640,1024]{1,0:T(8,128)(2,1)}, bf16[640,1024]{1,0:T(8,128)(2,1)S(1)}, u32[]{:S(2)}, u32[]{:S(2)}) collective-permute-start(bf16[640,1024]{1,0:T(8,128)(2,1)} %get-tuple-element.54.x_ref.refs_4_), channel_id=1, source_target_pairs={{0,1},{1,0},{2,3},{3,2},{4,5},{5,4},{6,7},{7,6},{8,9},{9,8},{10,11... | collective-permute-start | bytes 3932168 | tf_op jit(solution)/shard_map/ppermute | solution.py:841
  207.6 9.6 %collective-permute-start.24 = (bf16[1024,2048]{1,0:T(8,128)(2,1)}, bf16[1024,2048]{1,0:T(8,128)(2,1)}, u32[]{:S(2)}, u32[]{:S(2)}) collective-permute-start(bf16[1024,2048]{1,0:T(8,128)(2,1)} %hidden_grads.2.refs_0_), channel_id=1, source_target_pairs={{0,2},{2,0},{4,6},{6,4},{8,10},{10,8},{12,14},{14,12},{16,18},{18,... | collective-permute-start | bytes 12582920 | tf_op jit(solution)/shard_map/ppermute | solution.py:838
  207.6 43.8 %collective-permute-start.23 = (bf16[640,1024]{1,0:T(8,128)(2,1)S(1)}, bf16[640,1024]{1,0:T(8,128)(2,1)}, u32[]{:S(2)}, u32[]{:S(2)}) collective-permute-start(bf16[640,1024]{1,0:T(8,128)(2,1)S(1)} %copy-done.11), channel_id=1, source_target_pairs={{0,1},{1,0},{2,3},{3,2},{4,5},{5,4},{6,7},{7,6},{8,9},{9,8},{10,11... | collective-permute-start | bytes 3932168 | tf_op jit(solution)/shard_map/ppermute | solution.py:841
  233.8 15.0 %collective-permute-start.26 = (bf16[128,2048]{1,0:T(8,128)(2,1)}, bf16[128,2048]{1,0:T(8,128)(2,1)S(1)}, u32[]{:S(2)}, u32[]{:S(2)}) collective-permute-start(bf16[128,2048]{1,0:T(8,128)(2,1)} %get-tuple-element.76), channel_id=1, source_target_pairs={{0,8},{2,10},{8,16},{10,18},{16,24},{18,26},{24,28},{26,30},{28,20... | collective-permute-start | bytes 1572872 | tf_op jit(solution)/shard_map/ppermute | solution.py:916
  235.8 35.3 %collective-permute-start.27 = (bf16[128,2048]{1,0:T(8,128)(2,1)}, bf16[128,2048]{1,0:T(8,128)(2,1)}, u32[]{:S(2)}, u32[]{:S(2)}) collective-permute-start(bf16[128,2048]{1,0:T(8,128)(2,1)} %get-tuple-element.75), channel_id=1, source_target_pairs={{8,0},{10,2},{16,8},{18,10},{24,16},{26,18},{28,24},{30,26},{20,28... | collective-permute-start | bytes 1572872 | tf_op jit(solution)/shard_map/ppermute | solution.py:916
  251.3 19.8 %collective-permute-start.28 = (bf16[128,2048]{1,0:T(8,128)(2,1)}, bf16[128,2048]{1,0:T(8,128)(2,1)S(1)}, u32[]{:S(2)}, u32[]{:S(2)}) collective-permute-start(bf16[128,2048]{1,0:T(8,128)(2,1)} %bitcast_add_fusion.4), channel_id=1, source_target_pairs={{0,8},{2,10},{8,16},{10,18},{16,24},{18,26},{24,28},{26,30},{28,20... | collective-permute-start | bytes 1572872 | tf_op jit(solution)/shard_map/ppermute | solution.py:916
  260.2 16.7 %collective-permute-start.25 = (bf16[640,512]{1,0:T(8,128)(2,1)}, bf16[640,512]{1,0:T(8,128)(2,1)S(1)}, u32[]{:S(2)}, u32[]{:S(2)}) collective-permute-start(bf16[640,512]{1,0:T(8,128)(2,1)} %get-tuple-element.61.refs_0_), channel_id=1, source_target_pairs={{0,1},{1,0},{2,3},{3,2},{4,5},{5,4},{6,7},{7,6},{8,9},{9,8},{10,11... | collective-permute-start | bytes 1966088 | tf_op jit(solution)/shard_map/ppermute | solution.py:841
  274.9 33.7 %collective-permute-start.30 = (bf16[128,2048]{1,0:T(8,128)(2,1)}, bf16[128,2048]{1,0:T(8,128)(2,1)}, u32[]{:S(2)}, u32[]{:S(2)}) collective-permute-start(bf16[128,2048]{1,0:T(8,128)(2,1)} %get-tuple-element.73), channel_id=1, source_target_pairs={{0,8},{2,10},{8,16},{10,18},{16,24},{18,26},{24,28},{26,30},{28,20... | collective-permute-start | bytes 1572872 | tf_op jit(solution)/shard_map/ppermute | solution.py:916
  276.1 32.4 %collective-permute-start.29 = (bf16[128,2048]{1,0:T(8,128)(2,1)}, bf16[128,2048]{1,0:T(8,128)(2,1)}, u32[]{:S(2)}, u32[]{:S(2)}) collective-permute-start(bf16[128,2048]{1,0:T(8,128)(2,1)} %get-tuple-element.74), channel_id=1, source_target_pairs={{8,0},{10,2},{16,8},{18,10},{24,16},{26,18},{28,24},{30,26},{20,28... | collective-permute-start | bytes 1572872 | tf_op jit(solution)/shard_map/ppermute | solution.py:916
  308.5 37.8 %collective-permute-start.32 = (bf16[1024,1280]{1,0:T(8,128)(2,1)}, bf16[1024,1280]{1,0:T(8,128)(2,1)}, u32[]{:S(2)}, u32[]{:S(2)}) collective-permute-start(bf16[1024,1280]{1,0:T(8,128)(2,1)} %tail_grads.2.refs_3_), channel_id=1, source_target_pairs={{0,2},{2,0},{4,6},{6,4},{8,10},{10,8},{12,14},{14,12},{16,18},{18,... | collective-permute-start | bytes 7864328 | tf_op jit(solution)/shard_map/ppermute | solution.py:838
  312.6 17.1 %collective-permute-start.45 = (bf16[128,2048]{1,0:T(8,128)(2,1)}, bf16[128,2048]{1,0:T(8,128)(2,1)}, u32[]{:S(2)}, u32[]{:S(2)}) collective-permute-start(bf16[128,2048]{1,0:T(8,128)(2,1)} %get-tuple-element.71), channel_id=1, source_target_pairs={{0,8},{2,10},{8,16},{10,18},{16,24},{18,26},{24,28},{26,30},{28,20... | collective-permute-start | bytes 1572872 | tf_op jit(solution)/shard_map/ppermute | solution.py:916
  314.2 15.5 %collective-permute-start.31 = (bf16[128,2048]{1,0:T(8,128)(2,1)}, bf16[128,2048]{1,0:T(8,128)(2,1)}, u32[]{:S(2)}, u32[]{:S(2)}) collective-permute-start(bf16[128,2048]{1,0:T(8,128)(2,1)} %get-tuple-element.72), channel_id=1, source_target_pairs={{8,0},{10,2},{16,8},{18,10},{24,16},{26,18},{28,24},{30,26},{20,28... | collective-permute-start | bytes 1572872 | tf_op jit(solution)/shard_map/ppermute | solution.py:916
  316.9 93.4 %collective-permute-start.33 = (bf16[640,1024]{1,0:T(8,128)(2,1)}, bf16[640,1024]{1,0:T(8,128)(2,1)}, u32[]{:S(2)}, u32[]{:S(2)}) collective-permute-start(bf16[640,1024]{1,0:T(8,128)(2,1)} %down_part.2.refs_2_), channel_id=1, source_target_pairs={{0,1},{1,0},{2,3},{3,2},{4,5},{5,4},{6,7},{7,6},{8,9},{9,8},{10,11... | collective-permute-start | bytes 3932168 | tf_op jit(solution)/shard_map/ppermute | solution.py:841
  333.4 11.3 %collective-permute-start.46 = (f32[64,1024]{1,0:T(8,128)S(1)}, f32[64,1024]{1,0:T(8,128)S(1)}, u32[]{:S(2)}, u32[]{:S(2)}) collective-permute-start(f32[64,1024]{1,0:T(8,128)S(1)} %dynamic-slice_bitcast_fusion.5), channel_id=1, source_target_pairs={{0,2},{2,0},{4,6},{6,4},{8,10},{10,8},{12,14},{14,12},{16,18},{18,... | collective-permute-start | bytes 786440 | tf_op jit(solution)/shard_map/ppermute | solution.py:838
  345.5 25.8 %collective-permute-start.47 = (f32[32,2048]{1,0:T(8,128)S(1)}, f32[32,2048]{1,0:T(8,128)S(1)}, u32[]{:S(2)}, u32[]{:S(2)}) collective-permute-start(f32[32,2048]{1,0:T(8,128)S(1)} %fusion.7), channel_id=1, source_target_pairs={{0,1},{1,0},{2,3},{3,2},{4,5},{5,4},{6,7},{7,6},{8,9},{9,8},{10,11... | collective-permute-start | bytes 786440 | tf_op jit(solution)/shard_map/ppermute | solution.py:841
  366.0 5.8 %collective-permute-start.48 = (f32[4,8,1024]{2,1,0:T(8,128)S(1)}, f32[4,8,1024]{2,1,0:T(8,128)S(1)}, u32[]{:S(2)}, u32[]{:S(2)}) collective-permute-start(f32[4,8,1024]{2,1,0:T(8,128)S(1)} %broadcast_multiply_fusion), channel_id=1, source_target_pairs={{0,1},{1,0},{2,3},{3,2},{4,5},{5,4},{6,7},{7,6},{8,9},{9,8},{10,11... | collective-permute-start | bytes 393224 | tf_op jit(solution)/shard_map/ppermute | solution.py:841
  369.3 9.7 %collective-permute-start.35 = (bf16[128,1280]{1,0:T(8,128)(2,1)S(1)}, bf16[128,1280]{1,0:T(8,128)(2,1)S(1)}, u32[]{:S(2)}, u32[]{:S(2)}) collective-permute-start(bf16[128,1280]{1,0:T(8,128)(2,1)S(1)} %get-tuple-element.79), channel_id=1, source_target_pairs={{8,0},{10,2},{16,8},{18,10},{24,16},{26,18},{28,24},{30,26},{20,28... | collective-permute-start | bytes 983048 | tf_op jit(solution)/shard_map/ppermute | solution.py:916
  371.5 17.0 %collective-permute-start.38 = (bf16[128,1280]{1,0:T(8,128)(2,1)}, bf16[128,1280]{1,0:T(8,128)(2,1)}, u32[]{:S(2)}, u32[]{:S(2)}) collective-permute-start(bf16[128,1280]{1,0:T(8,128)(2,1)} %get-tuple-element.80), channel_id=1, source_target_pairs={{0,8},{2,10},{8,16},{10,18},{16,24},{18,26},{24,28},{26,30},{28,20... | collective-permute-start | bytes 983048 | tf_op jit(solution)/shard_map/ppermute | solution.py:916
  371.8 14.0 %collective-permute-start.49 = (f32[4,8,1024]{2,1,0:T(8,128)S(1)}, f32[4,8,1024]{2,1,0:T(8,128)S(1)}, u32[]{:S(2)}, u32[]{:S(2)}) collective-permute-start(f32[4,8,1024]{2,1,0:T(8,128)S(1)} %fusion.24), channel_id=1, source_target_pairs={{0,2},{2,0},{4,6},{6,4},{8,10},{10,8},{12,14},{14,12},{16,18},{18,... | collective-permute-start | bytes 393224 | tf_op jit(solution)/shard_map/ppermute | solution.py:838
  380.4 10.1 %collective-permute-start.36 = (bf16[128,1280]{1,0:T(8,128)(2,1)}, bf16[128,1280]{1,0:T(8,128)(2,1)}, u32[]{:S(2)}, u32[]{:S(2)}) collective-permute-start(bf16[128,1280]{1,0:T(8,128)(2,1)} %bitcast_add_fusion.8), channel_id=1, source_target_pairs={{8,0},{10,2},{16,8},{18,10},{24,16},{26,18},{28,24},{30,26},{20,28... | collective-permute-start | bytes 983048 | tf_op jit(solution)/shard_map/ppermute | solution.py:916
  386.6 19.7 %collective-permute-start.50 = (f32[4,8,1024]{2,1,0:T(8,128)S(1)}, f32[4,8,1024]{2,1,0:T(8,128)S(1)}, u32[]{:S(2)}, u32[]{:S(2)}) collective-permute-start(f32[4,8,1024]{2,1,0:T(8,128)S(1)} %fusion.36), channel_id=1, source_target_pairs={{0,4},{2,6},{4,0},{6,2},{8,12},{10,14},{12,8},{14,10},{16,20},{18,... | collective-permute-start | bytes 393224 | tf_op jit(solution)/shard_map/ppermute | solution.py:838
  393.0 14.9 %collective-permute-start.39 = (bf16[128,1280]{1,0:T(8,128)(2,1)S(1)}, bf16[128,1280]{1,0:T(8,128)(2,1)}, u32[]{:S(2)}, u32[]{:S(2)}) collective-permute-start(bf16[128,1280]{1,0:T(8,128)(2,1)S(1)} %get-tuple-element.78), channel_id=1, source_target_pairs={{0,8},{2,10},{8,16},{10,18},{16,24},{18,26},{24,28},{26,30},{28,20... | collective-permute-start | bytes 983048 | tf_op jit(solution)/shard_map/ppermute | solution.py:916
  397.8 33.0 %collective-permute-start.34 = (bf16[640,1024]{1,0:T(8,128)(2,1)}, bf16[640,1024]{1,0:T(8,128)(2,1)}, u32[]{:S(2)}, u32[]{:S(2)}) collective-permute-start(bf16[640,1024]{1,0:T(8,128)(2,1)} %get-tuple-element.81), channel_id=1, source_target_pairs={{0,1},{1,0},{2,3},{3,2},{4,5},{5,4},{6,7},{7,6},{8,9},{9,8},{10,11... | collective-permute-start | bytes 3932168 | tf_op jit(solution)/shard_map/ppermute | solution.py:841
  406.3 8.7 %collective-permute-start.51 = (f32[4,8,1024]{2,1,0:T(8,128)S(1)}, f32[4,8,1024]{2,1,0:T(8,128)S(1)}, u32[]{:S(2)}, u32[]{:S(2)}) collective-permute-start(f32[4,8,1024]{2,1,0:T(8,128)S(1)} %add.140), channel_id=1, source_target_pairs={{0,8},{2,10},{4,12},{6,14},{8,0},{10,2},{12,4},{14,6},{16,24},{18,... | collective-permute-start | bytes 393224 | tf_op jit(solution)/shard_map/ppermute | solution.py:838
  409.4 8.7 %collective-permute-start.40 = (bf16[128,1280]{1,0:T(8,128)(2,1)S(1)}, bf16[128,1280]{1,0:T(8,128)(2,1)S(1)}, u32[]{:S(2)}, u32[]{:S(2)}) collective-permute-start(bf16[128,1280]{1,0:T(8,128)(2,1)S(1)} %bitcast_add_fusion.6), channel_id=1, source_target_pairs={{0,8},{2,10},{8,16},{10,18},{16,24},{18,26},{24,28},{26,30},{28,20... | collective-permute-start | bytes 983048 | tf_op jit(solution)/shard_map/ppermute | solution.py:916
  415.1 8.8 %collective-permute-start.52 = (f32[4,8,1024]{2,1,0:T(8,128)S(1)}, f32[4,8,1024]{2,1,0:T(8,128)S(1)}, u32[]{:S(2)}, u32[]{:S(2)}) collective-permute-start(f32[4,8,1024]{2,1,0:T(8,128)S(1)} %add.141), channel_id=1, source_target_pairs={{0,16},{2,18},{4,20},{6,22},{8,24},{10,26},{12,28},{14,30},{16,0},... | collective-permute-start | bytes 393224 | tf_op jit(solution)/shard_map/ppermute | solution.py:838
  417.7 8.2 %collective-permute-start.37 = (bf16[128,1280]{1,0:T(8,128)(2,1)S(1)}, bf16[128,1280]{1,0:T(8,128)(2,1)S(1)}, u32[]{:S(2)}, u32[]{:S(2)}) collective-permute-start(bf16[128,1280]{1,0:T(8,128)(2,1)S(1)} %get-tuple-element.77), channel_id=1, source_target_pairs={{8,0},{10,2},{16,8},{18,10},{24,16},{26,18},{28,24},{30,26},{20,28... | collective-permute-start | bytes 983048 | tf_op jit(solution)/shard_map/ppermute | solution.py:916
  418.8 7.9 %collective-permute-start.41 = (bf16[128,1280]{1,0:T(8,128)(2,1)S(1)}, bf16[128,1280]{1,0:T(8,128)(2,1)S(1)}, u32[]{:S(2)}, u32[]{:S(2)}) collective-permute-start(bf16[128,1280]{1,0:T(8,128)(2,1)S(1)} %bitcast_add_fusion.7), channel_id=1, source_target_pairs={{0,8},{2,10},{8,16},{10,18},{16,24},{18,26},{24,28},{26,30},{28,20... | collective-permute-start | bytes 983048 | tf_op jit(solution)/shard_map/ppermute | solution.py:916
  428.9 8.7 %collective-permute-start.42 = (f32[64,1280]{1,0:T(8,128)S(1)}, f32[64,1280]{1,0:T(8,128)S(1)}, u32[]{:S(2)}, u32[]{:S(2)}) collective-permute-start(f32[64,1280]{1,0:T(8,128)S(1)} %dynamic-slice_bitcast_fusion.2), channel_id=1, source_target_pairs={{0,2},{2,0},{4,6},{6,4},{8,10},{10,8},{12,14},{14,12},{16,18},{18,... | collective-permute-start | bytes 983048 | tf_op jit(solution)/shard_map/ppermute | solution.py:838
  439.8 7.4 %collective-permute-start.43 = (f32[32,1536]{1,0:T(8,128)S(1)}, f32[32,1536]{1,0:T(8,128)S(1)}, u32[]{:S(2)}, u32[]{:S(2)}) collective-permute-start(f32[32,1536]{1,0:T(8,128)S(1)} %fusion.16), channel_id=1, source_target_pairs={{0,1},{1,0},{2,3},{3,2},{4,5},{5,4},{6,7},{7,6},{8,9},{9,8},{10,11... | collective-permute-start | bytes 589832 | tf_op jit(solution)/shard_map/ppermute | solution.py:841
  (48 other events, 720.1 us)
Sparse Core Ops, SparseCore 0:
  32.7 97.1 all-gather.2

commit v3 on v2

--- a/solution.py
+++ b/solution.py
@@ -83,11 +83,10 @@
         tile(second, at_target, 2 * half, tiles + index)
 
 
-def attend(qkv, place, behind):
+def attend(qkv, place, first, pairs, behind):
     rows = qkv.shape[0]
-    width = qkv.shape[1] // 3
-    pairs = width // LANES
-    part = lambda shift: pl.BlockSpec((rows, LANES), lambda p, s, shift=shift: (0, 3 * p + shift))
+    width = pairs * LANES
+    part = lambda shift: pl.BlockSpec((rows, LANES), lambda p, s, shift=shift: (0, 3 * (first + p) + shift))
     seen = rows * rows * 3 // 4
     return pl.pallas_call(
         attend_kernel,
@@ -99,14 +98,15 @@
         ),
         out_shape=[jax.ShapeDtypeStruct((rows, width), jnp.bfloat16),
                    jax.ShapeDtypeStruct((pairs, rows // TILE, 2 * TILE), jnp.float32)],
-        compiler_params=pltpu.CompilerParams(vmem_limit_bytes=48 << 20),
+        compiler_params=pltpu.CompilerParams(vmem_limit_bytes=60 << 20),
         cost_estimate=pl.CostEstimate(flops=int(COVER * pairs * 2 * seen * 4 * HEAD_DIM * 4), transcendentals=0, bytes_accessed=rows * width * 8),
         name="attend",
     )(place, qkv, qkv, qkv, *behind)
 
 
-def attend_back_kernel(parts, place, q_ref, k_ref, v_ref, o_ref, lse_ref, *refs):
-    g_refs = refs[:parts]
+def attend_back_kernel(parts, calls, place, q_ref, k_ref, v_ref, *refs):
+    o_refs, lse_refs, g_refs = refs[:calls], refs[calls:2 * calls], refs[2 * calls:2 * calls + parts]
+    per = place[3]
     out_ref, keys_wide, values_wide, keys_t, dq, dk, dv = refs[-7:]
     half = q_ref.shape[0] // 2
     step = pl.program_id(0)
@@ -147,15 +147,22 @@
             first = g_refs[0][pl.ds(inside, TILE), :]
             return jnp.where(start < half, first, g_refs[1][pl.ds(inside, TILE), :])
 
+        def of_call(values):
+            value = values[0]
+            for call, later in enumerate(values[1:], 1):
+                value = jnp.where(place[2] < call * per, value, later)
+            return value
+
         def tile(start, seen, slot):
             spot = pl.ds(start, TILE)
             q_here = q_ref[spot, :].astype(jnp.float32) * SCALE
             g_here = g_tile(start).astype(jnp.float32)
             g_flip = g_here.T
-            product = g_flip * o_ref[spot, :].astype(jnp.float32).T
+            o_here = of_call([ref[spot, :].astype(jnp.float32) for ref in o_refs])
+            product = g_flip * o_here.T
             inner = jnp.concatenate(
                 [jnp.sum(product[:HEAD_DIM], axis=0, keepdims=True), jnp.sum(product[HEAD_DIM:], axis=0, keepdims=True)], axis=1)
-            lse = lse_ref[0, pl.ds(slot, 1), :]
+            lse = of_call([ref[0, pl.ds(slot, 1), :] for ref in lse_refs])
             below = jnp.where(ids == 0, 1.0, lanes_of(lse))
             q_wide = jnp.concatenate([twin_lanes(q_here.T), below], axis=0).astype(jnp.bfloat16)
             g_wide = jnp.concatenate([twin_lanes(g_flip), lanes_of(inner)], axis=0).astype(jnp.bfloat16)
@@ -185,27 +192,28 @@
 def attend_back(place, qkv, mixed, grads, lse, held, behind):
     rows = qkv.shape[0]
     part = lambda shift: pl.BlockSpec((rows, LANES), lambda j, s, shift=shift: (0, 3 * s[2] + shift))
-    block = pl.BlockSpec((rows, LANES), lambda j, s: (0, s[2]))
-    lse_block = pl.BlockSpec((1, rows // TILE, 2 * TILE), lambda j, s: (s[2], 0, 0))
+    calls = len(mixed)
+    parts = len(grads)
+    block = pl.BlockSpec((rows, LANES), lambda j, s: (0, s[2] & (s[3] - 1)))
+    lse_block = pl.BlockSpec((1, rows // TILE, 2 * TILE), lambda j, s: (s[2] & (s[3] - 1), 0, 0))
+    grad_blocks = [pl.BlockSpec((grad.shape[0], LANES), lambda j, s: (0, s[2])) for grad in grads]
     seen = rows * rows * 3 // 4
     more = [] if held is None else [held]
-    grad_blocks = [pl.BlockSpec((grad.shape[0], LANES), lambda j, s: (0, s[2])) for grad in grads]
-    parts = len(grads)
     return pl.pallas_call(
-        partial(attend_back_kernel, parts),
+        partial(attend_back_kernel, parts, calls),
         grid_spec=pltpu.PrefetchScalarGridSpec(
             num_scalar_prefetch=1, grid=(3,),
-            in_specs=[part(0), part(1), part(2), block, lse_block] + grad_blocks + [pl.BlockSpec(memory_space=pl.ANY)] * (len(more) + len(behind)),
+            in_specs=[part(0), part(1), part(2)] + [block] * calls + [lse_block] * calls + grad_blocks + [pl.BlockSpec(memory_space=pl.ANY)] * (len(more) + len(behind)),
             out_specs=pl.BlockSpec((rows, LANES), lambda j, s: (0, 3 * s[2] + j)),
             scratch_shapes=[pltpu.VMEM((rows, 2 * LANES), jnp.bfloat16), pltpu.VMEM((rows, 2 * LANES), jnp.bfloat16), pltpu.VMEM((LANES, rows), jnp.bfloat16),
                 pltpu.VMEM((rows, LANES), jnp.bfloat16), pltpu.VMEM((rows, LANES), jnp.float32), pltpu.VMEM((rows, LANES), jnp.float32)],
         ),
         out_shape=jax.ShapeDtypeStruct(qkv.shape, jnp.bfloat16),
-        input_output_aliases={6 + parts: 0} if more else {},
-        compiler_params=pltpu.CompilerParams(vmem_limit_bytes=48 << 20),
+        input_output_aliases={4 + 2 * calls + parts: 0} if more else {},
+        compiler_params=pltpu.CompilerParams(vmem_limit_bytes=60 << 20),
         cost_estimate=pl.CostEstimate(flops=int(COVER * 2 * seen * 10 * HEAD_DIM * 4), transcendentals=0, bytes_accessed=rows * LANES * 20),
         name="attend_back",
-    )(place, qkv, qkv, qkv, mixed, lse, *grads, *more, *behind)
+    )(place, qkv, qkv, qkv, *mixed, *lse, *grads, *more, *behind)
 
 
 EPSILON = 1e-05
@@ -276,6 +284,29 @@
     for index, ref in enumerate(refs[1:], 1):
         value = jnp.where(pl.program_id(0) < index * count // len(refs), value, ref[...])
     return value
+
+
+def pack_kernel(place, query_ref, key_ref, value_ref, out_ref):
+    for pair in range(query_ref.shape[1] // LANES):
+        for which, ref in enumerate((query_ref, key_ref, value_ref)):
+            start = (3 * pair + which) * LANES
+            out_ref[:, start : start + LANES] = ref[:, pair * LANES : (pair + 1) * LANES]
+
+
+def pack_columns(query, key, value, held, place):
+    rows = query.shape[0]
+    return pl.pallas_call(
+        pack_kernel,
+        grid_spec=pltpu.PrefetchScalarGridSpec(
+            num_scalar_prefetch=1,
+            grid=(1,),
+            in_specs=[pl.BlockSpec((rows, held), lambda j, s: (0, s[0]))] * 3,
+            out_specs=pl.BlockSpec((rows, 3 * held), lambda j, s: (0, 0)),
+        ),
+        out_shape=jax.ShapeDtypeStruct((rows, 3 * held), query.dtype),
+        cost_estimate=cost(0, 12 * rows * held),
+        name="pack_columns",
+    )(place, query, key, value)
 
 
 def first_kernel(parts, pieces, count, spots, *refs):
@@ -339,12 +370,13 @@
     )(spots, *frames, ada, *blocks)
 
 
-def second_kernel(pieces, spots, *refs):
+def second_kernel(pieces, parts, count, spots, *refs):
     mixed = refs[:pieces]
-    tokens, out_w, ada = refs[pieces : pieces + 3]
+    tokens = refs[pieces : pieces + parts]
+    out_w, ada = refs[pieces + parts : pieces + parts + 2]
     attended_ref, low_ref = refs[-2:]
     weights = out_w.reshape(out_w.shape[0] * out_w.shape[2], out_w.shape[3])
-    attended = tokens[...].astype(jnp.float32)
+    attended = current(tokens, count).astype(jnp.float32)
     for index, piece in enumerate(mixed):
         size = piece.shape[1]
         start = pl.multiple_of(spots[index] * size, size)
@@ -354,32 +386,39 @@
     low_ref[...] = ((1.0 + ada[0:1, :]) * normed + ada[1:2, :]).astype(jnp.bfloat16)
 
 
-def second_layer(mixed, tokens, out_w, out_part, ada, spots):
-    rows, width = tokens.shape
-    count = 2
-    block = lambda size: pl.BlockSpec((rows // count, size), lambda j, s: (j, 0))
+def second_layer(mixed, swapped, tokens, out_w, out_part, ada, spots):
+    rows, width = tokens[-1].shape
+    parts = len(tokens)
+    count = 2 * parts
+    size, token_specs = row_specs(tokens, count)
+    later = count - 2
+    block = lambda columns, order: pl.BlockSpec((size, columns), lambda j, s: (order(j), 0))
+    first = lambda j: (j + later) % count
     items, _, piece, _ = out_w.shape
     return pl.pallas_call(
-        partial(second_kernel, len(mixed)),
+        partial(second_kernel, len(mixed) + len(swapped), parts, count),
         grid_spec=pltpu.PrefetchScalarGridSpec(
             num_scalar_prefetch=1,
             grid=(count,),
-            in_specs=[block(part.shape[1]) for part in mixed]
+            in_specs=[block(part.shape[1], first) for part in mixed]
+            + [block(part.shape[1], lambda j: j) for part in swapped]
+            + token_specs
             + [
-                block(width),
                 pl.BlockSpec((items, 1, piece, width), lambda j, s: (0, out_part, 0, 0)),
                 pl.BlockSpec((2, width), lambda j, s: (0, 0)),
             ],
-            out_specs=[block(width), block(width)],
+            out_specs=[block(width, lambda j: jnp.maximum(j - later, 0)), block(width, first)],
         ),
         out_shape=[
             jax.ShapeDtypeStruct((rows, width), jnp.float32),
-            jax.ShapeDtypeStruct((rows, width), jnp.bfloat16),
+            jax.ShapeDtypeStruct((rows * parts, width), jnp.bfloat16),
         ],
         compiler_params=BIG,
-        cost_estimate=cost(2 * rows * width * width, 2 * width * width + 10 * rows * width),
+        cost_estimate=cost(
+            2 * rows * parts * width * width, 2 * width * width + 10 * rows * parts * width
+        ),
         name="second_layer",
-    )(spots, *mixed, tokens, out_w, ada)
+    )(spots, *mixed, *swapped, *tokens, out_w, ada)
 
 
 class Weights:
@@ -408,40 +447,48 @@
         self.bytes = 2 * hidden * width
 
 
-def hidden_kernel(per_chip, x_ref, g_ref, up_ref, down_ref, *refs):
+def hidden_kernel(per_chip, parts, x_ref, up_ref, down_ref, *refs):
+    g_refs = refs[:parts]
     active_ref, grad_ref = refs[-2:]
     columns = min(256, active_ref.shape[1])
+    size = x_ref.shape[0] // parts
     for start in range(0, active_ref.shape[1], columns):
         spot = slice(start, start + columns)
-        upward = matmul(x_ref[...], up_ref[:, :, :, spot].reshape(-1, columns))
+        up = up_ref[:, :, :, spot].reshape(-1, columns)
         chips = slice(start // per_chip, (start + columns) // per_chip)
-        grad_active = matmul_last(g_ref[...], down_ref[chips].reshape(columns, -1))
-        below = 0.5 * (1.0 + lax.erf(upward * ROOT_HALF))
-        active_ref[:, spot] = (upward * below).astype(jnp.bfloat16)
-        slope = below + upward * (DENSITY * jnp.exp(-0.5 * upward * upward))
-        grad_ref[:, spot] = (grad_active * slope).astype(jnp.bfloat16)
-
-
-def hidden_layer(x, grad, weights, total_rows, chunk, held=None):
+        down = down_ref[chips].reshape(columns, -1)
+        for index, g_ref in enumerate(g_refs):
+            rows = slice(index * size, (index + 1) * size)
+            upward = matmul(x_ref[rows, :], up)
+            grad_active = matmul_last(g_ref[...], down)
+            below = 0.5 * (1.0 + lax.erf(upward * ROOT_HALF))
+            active_ref[rows, spot] = (upward * below).astype(jnp.bfloat16)
+            slope = below + upward * (DENSITY * jnp.exp(-0.5 * upward * upward))
+            grad_ref[rows, spot] = (grad_active * slope).astype(jnp.bfloat16)
+
+
+def hidden_layer(x, grads, weights):
     rows, width = x.shape
-    whole = pl.BlockSpec((rows, width), lambda j: (0, 0))
-    out = pl.BlockSpec((rows, weights.block), lambda j: (chunk, j))
-    shape = jax.ShapeDtypeStruct((total_rows, weights.hidden), jnp.bfloat16)
-    more = [] if held is None else list(held)
+    out = pl.BlockSpec((rows, weights.block), lambda j: (0, j))
+    shape = jax.ShapeDtypeStruct((rows, weights.hidden), jnp.bfloat16)
     return pl.pallas_call(
-        partial(hidden_kernel, weights.per_chip),
+        partial(hidden_kernel, weights.per_chip, len(grads)),
         grid=(weights.steps,),
-        in_specs=[whole, whole, weights.up_spec, weights.down_spec] + [ANYWHERE] * len(more),
+        in_specs=[
+            pl.BlockSpec((rows, width), lambda j: (0, 0)),
+            weights.up_spec,
+            weights.down_spec,
+        ]
+        + [pl.BlockSpec(grad.shape, lambda j: (0, 0)) for grad in grads],
         out_specs=[out, out],
         out_shape=[shape, shape],
-        input_output_aliases={4: 0, 5: 1} if more else {},
         compiler_params=BIG,
         cost_estimate=cost(
             4 * rows * width * weights.hidden,
             2 * weights.bytes + 4 * rows * (width + weights.hidden),
         ),
         name="hidden_layer",
-    )(x, grad, weights.up, weights.down, *more)
+    )(x, weights.up, weights.down, *grads)
 
 
 def accumulate(part, out_ref, total):
@@ -520,11 +567,12 @@
     )
 
 
-def middle_back_kernel(pieces, spots, *refs):
-    own_ref, other_ref, base_ref, top_ref, ada_ref, out_w = refs[:6]
+def middle_back_kernel(pieces, parts, spots, *refs):
+    own_ref, base_ref, top_ref, ada_ref, out_w = refs[:5]
+    others = refs[5 : 5 + parts]
     outs = refs[-3 - pieces :]
     grad_ref, low_ref, ada_grad_ref = outs[:3]
-    grad = own_ref[...] + other_ref[...].astype(jnp.float32)
+    grad = own_ref[...] + current(others, 2).astype(jnp.float32)
     normed, inverse = standardise(base_ref[...])
     scaled = grad * (1.0 + ada_ref[0:1, :])
     scale = jnp.sum(grad * normed, axis=0, keepdims=True)
@@ -548,16 +596,18 @@
     count = 2
     block = lambda size: pl.BlockSpec((rows // count, size), lambda j, s: (j, 0))
     items, _, piece, _ = out_w.shape
+    _, other_specs = row_specs(other, count)
     return pl.pallas_call(
-        partial(middle_back_kernel, len(sizes)),
+        partial(middle_back_kernel, len(sizes), len(other)),
         grid_spec=pltpu.PrefetchScalarGridSpec(
             num_scalar_prefetch=1,
             grid=(count,),
-            in_specs=[block(width)] * 4
+            in_specs=[block(width)] * 3
             + [
                 pl.BlockSpec((2, width), lambda j, s: (0, 0)),
                 pl.BlockSpec((items, 1, piece, width), lambda j, s: (0, out_part, 0, 0)),
             ]
+            + other_specs
             + [ANYWHERE] * len(behind),
             out_specs=[block(width), block(width), pl.BlockSpec((2, width), lambda j, s: (0, 0))]
             + [block(size) for size in sizes],
@@ -571,33 +621,32 @@
         compiler_params=BIG,
         cost_estimate=cost(2 * rows * width * width, 2 * width * width + 20 * rows * width),
         name="middle_back",
-    )(spots, own, other, attended, cotangent, ada, out_w, *behind)
-
-
-def first_back_kernel(parts, count, grad_ref, weight_ref, *refs):
-    frames = refs[:parts]
+    )(spots, own, attended, cotangent, ada, out_w, *other, *behind)
+
+
+def first_back_kernel(grad_ref, weight_ref, frames, *refs):
     out_ref, ada_grad_ref = refs[-2:]
     grad = matmul_last(grad_ref[...], weight_ref[...])
-    normed, _ = standardise(current(frames, count).astype(jnp.float32))
+    normed, _ = standardise(frames[...].astype(jnp.float32))
     out_ref[...] = grad.astype(jnp.bfloat16)
     scale = jnp.sum(grad * normed, axis=0, keepdims=True)
     shift = jnp.sum(grad, axis=0, keepdims=True)
     add_rows(ada_grad_ref, scale, shift)
 
 
-def first_back(grad, weights, frames, behind):
+def first_back(grad, weights, frames, part, behind):
     width, columns = weights.shape
-    count = 4
-    rows, specs = row_specs(frames, count)
+    count = 2
+    rows = frames.shape[0] // count
     block = pl.BlockSpec((rows, width), lambda j: (j, 0))
     return pl.pallas_call(
-        partial(first_back_kernel, len(frames), count),
+        first_back_kernel,
         grid=(count,),
         in_specs=[
-            pl.BlockSpec((rows, columns), lambda j: (j, 0)),
+            pl.BlockSpec((rows, columns), lambda j: (part * count + j, 0)),
             pl.BlockSpec((width, columns), lambda j: (0, 0)),
+            block,
         ]
-        + specs
         + [ANYWHERE] * len(behind),
         out_specs=[block, pl.BlockSpec((2, width), lambda j: (0, 0))],
         out_shape=[
@@ -610,7 +659,7 @@
             2 * width * columns + 2 * rows * count * (2 * width + columns),
         ),
         name="first_back",
-    )(grad, weights, *frames, *behind)
+    )(grad, weights, frames, *behind)
 
 
 def stacked_dot(lefts, rights):
@@ -634,8 +683,8 @@
 
 def hidden_grads_kernel(count, more, core, *refs):
     active, upward = refs[:2]
-    grads, lows = refs[2 : 2 + count], refs[2 + count : 2 + 2 * count]
-    other = refs[2 + 2 * count] if more else None
+    grads, low = refs[2 : 2 + count], refs[2 + count]
+    other = refs[3 + count] if more else None
     out_ref = refs[-1]
     step = pl.program_id(0)
     steps = pl.num_programs(0) // 2
@@ -648,17 +697,17 @@
 
     @pl.when(step >= steps)
     def _():
-        put_sum(out_ref, other, stacked_dot([ref[...] for ref in lows], cut_rows(upward, count)))
-
-
-def hidden_grads(core, active, upward, grads, lows, other, behind):
+        put_sum(out_ref, other, dot_rows(low[...], upward[...]))
+
+
+def hidden_grads(core, active, upward, grads, low, other, behind):
     total, hidden = active.shape
     half = hidden // 2
-    rows, width = lows[0].shape
-    count = total // rows
+    rows, width = grads[0].shape
+    count = len(grads)
     block = 512
     steps = half // block
-    low = pl.BlockSpec((rows, width), lambda j, s: (0, 0))
+    whole = pl.BlockSpec((total, width), lambda j, s: (0, 0))
     grad = pl.BlockSpec((rows, block), lambda j, s: (0, jnp.minimum(j, steps - 1)))
     out = pl.BlockSpec((width, block), lambda j, s: (0, j))
     more = [] if other is None else [other]
@@ -674,7 +723,7 @@
                 ),
             ]
             + [grad] * count
-            + [low] * count
+            + [whole]
             + [out] * len(more)
             + [ANYWHERE] * len(behind),
             out_specs=out,
@@ -683,11 +732,12 @@
         compiler_params=BIG,
         cost_estimate=cost(4 * total * half * width, 8 * total * half + 4 * width * half),
         name="hidden_grads",
-    )(core, active, upward, *grads, *lows, *more, *behind)
-
-
-def tail_grads_kernel(first, more, core, low, grad, mixed, attended, *refs):
-    other = refs[0] if more else None
+    )(core, active, upward, *grads, low, *more, *behind)
+
+
+def tail_grads_kernel(first, more, pieces, place, low, grad, attended, *refs):
+    mixed = refs[:pieces]
+    other = refs[pieces] if more else None
     out_ref = refs[-1]
 
     @pl.when(pl.program_id(0) < first)
@@ -696,19 +746,25 @@
 
     @pl.when(pl.program_id(0) >= first)
     def _():
-        put_sum(out_ref, other, dot_rows(mixed[...], attended[...]))
-
-
-def tail_grads(core, low_one, grad_qkv, mixed, attended_low, other, behind):
+        for index, piece in enumerate(mixed):
+            size = piece.shape[1]
+            rows = pl.ds(pl.multiple_of(place[1 + index] * size, size), size)
+            value = dot_rows(piece[...], attended[...])
+            if more:
+                value = value + other[rows, :].astype(jnp.float32)
+            out_ref[rows, :] = value.astype(jnp.bfloat16)
+
+
+def tail_grads(place, low_one, grad_qkv, mixed, swapped, attended_low, other, behind):
     total, width = low_one.shape
-    rows = mixed.shape[0]
+    rows = attended_low.shape[0]
     block = 256
     first = grad_qkv.shape[1] // 2 // block
     second = width // 2 // block
     out = pl.BlockSpec((width, block), lambda j, s: (0, j))
     more = [] if other is None else [other]
     return pl.pallas_call(
-        partial(tail_grads_kernel, first, bool(more)),
+        partial(tail_grads_kernel, first, bool(more), len(mixed) + len(swapped)),
         grid_spec=pltpu.PrefetchScalarGridSpec(
             num_scalar_prefetch=1,
             grid=(first + second,),
@@ -717,11 +773,12 @@
                 pl.BlockSpec(
                     (total, block), lambda j, s: (0, s[0] * first + jnp.minimum(j, first - 1))
                 ),
-                pl.BlockSpec((rows, width), lambda j, s: (0, 0)),
                 pl.BlockSpec(
                     (rows, block), lambda j, s: (0, s[0] * second + jnp.maximum(j - first, 0))
                 ),
             ]
+            + [pl.BlockSpec((rows, part.shape[1]), lambda j, s: (0, 0)) for part in mixed]
+            + [pl.BlockSpec((rows, part.shape[1]), lambda j, s: (1, 0)) for part in swapped]
             + [out] * len(more)
             + [ANYWHERE] * len(behind),
             out_specs=out,
@@ -732,14 +789,12 @@
             2 * width * block * (total * first + rows * second), 8 * total * width
         ),
         name="tail_grads",
-    )(core, low_one, grad_qkv, mixed, attended_low, *more, *behind)
-
-
-def input_back_kernel(parts, tokens_ref, ada_ref, base_ref, *refs):
+    )(place, low_one, grad_qkv, attended_low, *mixed, *swapped, *more, *behind)
+
+
+def input_back_kernel(parts, count, own_ref, tokens_ref, ada_ref, base_ref, *refs):
     out_ref = refs[-1]
-    grad = refs[0][...].astype(jnp.float32)
-    for ref in refs[1:parts]:
-        grad = grad + ref[...].astype(jnp.float32)
+    grad = own_ref[...].astype(jnp.float32) + current(refs[:parts], count).astype(jnp.float32)
     normed, inverse = standardise(tokens_ref[...].astype(jnp.float32))
     scaled = grad * (1.0 + ada_ref[0:1, :])
     inner = jnp.mean(scaled * normed, axis=-1, keepdims=True)
@@ -747,20 +802,21 @@
     out_ref[...] = base_ref[...] + inverse * shifted
 
 
-def input_back(grads, tokens, ada, base):
+def input_back(own, others, tokens, ada, base):
     rows, width = tokens.shape
-    count = 5 if rows % 80 == 0 else 1
+    count = 4
     block = pl.BlockSpec((rows // count, width), lambda j: (j, 0))
+    _, specs = row_specs(others, count)
     return pl.pallas_call(
-        partial(input_back_kernel, len(grads)),
+        partial(input_back_kernel, len(others), count),
         grid=(count,),
-        in_specs=[block, pl.BlockSpec((2, width), lambda j: (0, 0)), block] + [block] * len(grads),
+        in_specs=[block, block, pl.BlockSpec((2, width), lambda j: (0, 0)), block] + specs,
         out_specs=block,
         out_shape=jax.ShapeDtypeStruct((rows, width), jnp.float32),
         compiler_params=BIG,
         cost_estimate=cost(20 * rows * width, 14 * rows * width),
         name="input_back",
-    )(tokens, ada, base, *grads)
+    )(own, tokens, ada, base, *others)
 
 
 def exact(left, right):
@@ -807,7 +863,9 @@
         order = ring_of(items_count)
         self.forward = []
         self.backward = []
-        table = np.zeros((items_count, self.chips + 2), np.int32)
+        chips = self.chips
+        table = np.zeros((items_count, 2 * chips + 2), np.int32)
+        hops = list(range(chips // 2 + 1)) + [-hop for hop in range(1, (chips + 1) // 2)]
         for spot in range(self.chips):
             for core in range(2):
                 here = 2 * order[spot] + core
@@ -816,21 +874,21 @@
                 self.backward.append((next_one, here))
                 for ahead in range(self.chips):
                     table[here, ahead] = order[(spot + ahead) % self.chips]
-                table[here, self.chips] = core
-                table[here, self.chips + 1] = 1 - core
+                table[here, chips] = core
+                table[here, chips + 1] = 1 - core
+                for spot_of, hop in enumerate(hops):
+                    ahead = hop if core == 1 else -hop
+                    table[here, chips + 2 + spot_of] = order[(spot + ahead) % chips]
+        self.both_ways = [p for p in self.forward if p[0] % 2 == 0]
+        self.both_ways += [p for p in self.backward if p[0] % 2 == 1]
         self.item = lax.axis_index("items")
         row = pick(jnp.asarray(table), self.item, 0)
         self.ahead = [row[j] for j in range(self.chips)]
         self.core = row[self.chips]
         self.beside = row[self.chips + 1]
         self.core_spot = row[self.chips : self.chips + 1]
-        self.beside_spot = row[self.chips + 1 :]
-        self.spots = jnp.concatenate(
-            [
-                2 * row[: self.chips] + row[self.chips],
-                2 * row[: self.chips] + row[self.chips + 1],
-            ]
-        )
+        self.beside_spot = row[self.chips + 1 : self.chips + 2]
+        self.spots = row[self.chips + 2 :]
         self.seq = lax.axis_index("seq")
 
     def flip(self, value, bit):
@@ -840,25 +898,23 @@
     def across(self, value):
         return lax.ppermute(value, "seq", [(0, 1), (1, 0)])
 
-    def gather_items(self, value, summed, late):
-        bits = [1 << k for k in range(self.items_count.bit_length() - 1)]
-        blocks = {0: value}
-        moved = [value, value]
+    def gather_items(self, value, summed, early, late):
+        for bit in [1 << k for k in range(self.items_count.bit_length() - 1)]:
+            summed = summed + self.flip(summed, bit)
+        beside = self.flip(value, 1)
+        block = jnp.where(
+            self.core == 0,
+            jnp.concatenate([value, beside], axis=0),
+            jnp.concatenate([beside, value], axis=0),
+        )
+        direct = [block]
         for hop in range(1, self.chips // 2 + 1):
-            ways = [self.forward, self.backward][: 2 if hop <= (self.chips - 1) // 2 else 1]
-            moved = [lax.ppermute(v, "items", way) for v, way in zip(moved, ways)]
-            if hop > 1 and bits:
-                summed, moved = tie(summed, moved)
-            if hop == LATE_HOP:
-                late, moved = tie(late, moved)
-            if bits:
-                summed = summed + self.flip(summed, bits.pop(0))
-            for v, sign in zip(moved, (-1, 1)):
-                blocks[(sign * hop) % self.chips] = v
-        while bits:
-            summed = summed + self.flip(summed, bits.pop(0))
-        mine = [blocks[ahead] for ahead in range(self.chips)]
-        return mine + [self.flip(block, 1) for block in mine], summed, late
+            moved = lax.ppermute(direct[-1], "items", self.both_ways)
+            if hop == min(LATE_HOP, self.chips // 2):
+                late, summed, moved, early = tie(late, summed, moved, early)
+            direct.append(moved)
+        beside = [self.flip(moved, 1) for moved in direct[1 : (self.chips + 1) // 2]]
+        return direct + beside, summed, early, late
 
     def sum_seq(self, value):
         return value + self.across(value) if self.pair else lax.psum(value, "seq")
@@ -890,13 +946,14 @@
 
 
 class RingSum:
-    def __init__(self, mover, make, behind):
+    def __init__(self, mover, make, behind, ready=()):
         self.mover = mover
         self.chips = mover.chips
         self.make = make
         self.flows = None
-        self.sent = make(False, None, behind)
-        self.arriving = [mover.flip(self.sent, 1)]
+        sent, self.ready = tie(make(False, None, behind), list(ready))
+        self.sent = sent
+        self.arriving = [mover.flip(sent, 1)]
 
     def block(self, ahead):
         return pick(self.both, self.mover.ahead[ahead % self.chips], 0)
@@ -916,14 +973,17 @@
         self.arriving = [lax.ppermute(value, "items", flow[0]) for flow, value in flows]
         self.flows = [(pairs, sign, left - 1) for (pairs, sign, left), _ in flows]
 
-    def advance(self):
+    def advance(self, anchor=None):
         flows = []
+        if anchor is not None:
+            self.arriving, anchor = tie(self.arriving, anchor)
         for flow, value in zip(self.flows, self.arriving):
             if flow[2]:
                 flows.append((flow, self.block(flow[1] * flow[2]) + value))
             else:
                 self.result = self.result + value.astype(jnp.float32)
         self.send(flows)
+        return anchor
 
     def finish(self):
         while self.arriving:
@@ -994,9 +1054,12 @@
         preferred_element_type=jnp.float32,
     )
     ada_part = quarters(ada_part[:, : 2 * width], ada_part[:, 2 * width :])
-    mine = [cut(w, mover.seq * held, held, 1) for w in (w_query, w_key, w_value)]
-    mine = [w[:, p * LANES : (p + 1) * LANES] for p in range(pairs) for w in mine]
-    blocks, ada_sum, late = mover.gather_items(jnp.concatenate(mine, axis=1), ada_part, late)
+    seq_place = jnp.reshape(mover.seq, (1,)).astype(jnp.int32)
+    mine = pack_columns(w_query, w_key, w_value, held, seq_place)
+    early = [mover.across(tokens)] if mover.pair else []
+    blocks, ada_sum, early, late = mover.gather_items(
+        mine, ada_part, early, late
+    )
 
     def gathered(value):
         return lax.all_gather(value, "items", axis=0, tiled=False)
@@ -1019,46 +1082,58 @@
 
     if mover.pair:
         prompt_at = mover.seq
-        tokens_other = mover.across(tokens)
-        grad_other = mover.across(grad_low)
+        tokens_other, grad_sent = tie(early[0], grad_low)
+        grad_other = mover.across(grad_sent)
         frames = [tokens, tokens_other]
         grads = [grad_low, grad_other]
-        spots = jnp.stack([mover.seq, 1 - mover.seq])
+        calls = 2 if pairs % 2 == 0 else 1
+        own_spots = [mover.seq * calls + call for call in range(calls)]
+        far_spots = [(1 - mover.seq) * calls + call for call in range(calls)]
+        spots = jnp.stack(own_spots + far_spots)
         other_spots = jnp.stack([1 - mover.seq, mover.seq])
     else:
         prompt_at = jnp.zeros((), jnp.int32)
         frames = [lax.all_gather(tokens, "seq", axis=0, tiled=True)]
         grads = [lax.all_gather(grad_low, "seq", axis=0, tiled=True)]
+        calls = 1
         spots = other_spots = jnp.zeros((1,), jnp.int32)
     low_one, qkv, qkv_w = first_layer(frames, ada_one, blocks, mover.spots)
     length = prompt_len[0]
-    mixed_heads, lse = attend(
-        qkv, jnp.stack([prompt_at, length]).astype(jnp.int32), grads[1:]
-    )
+    per_call = pairs // calls
+    mixed_heads = []
+    lse = []
+    for call in range(calls):
+        place = jnp.stack([prompt_at, length]).astype(jnp.int32)
+        behind = grads[1:] + mixed_heads
+        out = attend(qkv, place, call * per_call, per_call, behind)
+        mixed_heads.append(out[0])
+        lse.append(out[1])
     if mover.pair:
-        mixed_parts = [mixed_heads[:rows], mover.across(mixed_heads[rows:])]
-        mixed = jnp.where(
-            mover.seq == 0,
-            jnp.concatenate(mixed_parts, axis=1),
-            jnp.concatenate(mixed_parts[::-1], axis=1),
+        mixed_far = []
+        for call in range(calls):
+            sent = mixed_heads[call]
+            if mixed_far:
+                sent, mixed_far[-1] = tie(sent, mixed_far[-1])
+            mixed_far.append(mover.across(sent))
+        attended, low_two = second_layer(
+            mixed_heads, mixed_far, frames[::-1], out_w, out_part, ada_two, spots
         )
+        lows = low_two
+        active, upward = hidden_layer(lows, grads, weights)
+        for_other = up_back(upward, weights, rows, 1, jnp.bfloat16)
+        half = rows // 2
+        first_half, last_half = for_other[:half], for_other[half:]
+        start = [for_other]
+        ready = [mover.across(first_half), last_half]
     else:
-        mixed = lax.all_to_all(mixed_heads, "seq", split_axis=0, concat_axis=1, tiled=True)
-        mixed_parts = [mixed]
-    attended, low_two = second_layer(mixed_parts, tokens, out_w, out_part, ada_two, spots)
-
-    if mover.pair:
-        low_other = mover.across(low_two)
-        both = hidden_layer(low_two, grad_low, weights, total_rows, 0)
-        active, upward = hidden_layer(low_other, grad_other, weights, total_rows, 1, both)
-        lows = [low_two, low_other]
-        for_other = up_back(upward, weights, rows, 1, jnp.bfloat16)
-        from_other = mover.across(for_other)
-        start = [for_other]
-    else:
-        lows = [lax.all_gather(low_two, "seq", axis=0, tiled=True)]
-        active, upward = hidden_layer(lows[0], grads[0], weights, total_rows, 0)
+        mixed = lax.all_to_all(mixed_heads[0], "seq", split_axis=0, concat_axis=1, tiled=True)
+        attended, low_two = second_layer(
+            [mixed], [], [tokens], out_w, out_part, ada_two, spots
+        )
+        lows = lax.all_gather(low_two, "seq", axis=0, tiled=True)
+        active, upward = hidden_layer(lows, grads, weights)
         start = []
+        ready = []
 
     down_columns = hidden // 2
 
@@ -1069,12 +1144,13 @@
         core = mover.core if own else mover.beside
         first, second = parted(other, down_columns)
         down = dot_rows(halves(active, core), grads[0]).reshape(width, down_columns)
-        up = dot_rows(lows[0], halves(upward, core))
+        up = dot_rows(lows, halves(upward, core))
         return in_rows(jnp.concatenate([rounded(down, first), rounded(up, second)], axis=1))
 
-    ring = RingSum(mover, hidden_parts, start)
+    ring = RingSum(mover, hidden_parts, start, ready)
     if mover.pair:
         own = up_back(upward, weights, rows, 0, jnp.float32, [ring.sent])
+        from_other = [ring.ready[0], mover.across(ring.ready[1])]
         sizes = [held, held]
     else:
         own = lax.psum_scatter(
@@ -1083,7 +1159,7 @@
             scatter_dimension=0,
             tiled=True,
         ).astype(jnp.float32)
-        from_other = jnp.zeros((rows, width), jnp.bfloat16)
+        from_other = [jnp.zeros((rows, width), jnp.bfloat16)]
         sizes = [width]
     ring.add_own([own])
     grad_attended, attended_low, ada_two_rows, *grad_mixed = middle_back(
@@ -1101,7 +1177,9 @@
     if mover.pair:
         out_other = down_part(active, weights, rows, 1, jnp.bfloat16, grad_mixed[:1])
         grad_heads = [grad_mixed[1], mover.across(grad_mixed[0])]
-        filler = [out_other]
+        out_other = ring.advance(out_other)
+        out_own = down_part(active, weights, rows, 0, jnp.float32, [out_other])
+        filler = [out_own]
         out_other = mover.across(out_other)
     else:
         grad_heads = [
@@ -1113,8 +1191,17 @@
 
     def tail_parts(own, other, behind):
         spot = mover.core_spot if own else mover.beside_spot
-        if pairs % 4 == 0:
-            return tail_grads(spot, low_one, grad_qkv, mixed, attended_low, other, behind)
+        if mover.pair:
+            return tail_grads(
+                jnp.concatenate([spot, spots.astype(jnp.int32)]),
+                low_one,
+                grad_qkv,
+                mixed_heads,
+                mixed_far,
+                attended_low,
+                other,
+                behind,
+            )
         core = mover.core if own else mover.beside
         first, second = parted(other, grad_qkv.shape[1] // 2)
         qkv_part = rounded(dot_rows(low_one, halves(grad_qkv, core)), first)
@@ -1126,27 +1213,36 @@
     for turn in range(pairs):
         behind = filler
         filler = []
-        if turn != 1:
-            behind = behind + ring.arriving
         pair = (mover.beside * split + turn) & (pairs - 1)
-        place = jnp.stack([prompt_at, length, pair]).astype(jnp.int32)
+        place = jnp.stack([prompt_at, length, pair, per_call]).astype(jnp.int32)
         grad_qkv = attend_back(place, qkv, mixed_heads, grad_heads, lse, grad_qkv, behind)
-        if turn != 1:
-            ring.advance()
+        grad_qkv = ring.advance(grad_qkv)
         if turn + 1 == split:
             tail = RingSum(mover, tail_parts, [])
             filler = [tail.sent]
     if tail is None:
         tail = RingSum(mover, tail_parts, [])
     tail.add_own([])
-    grad_first, ada_one_rows = first_back(grad_qkv, qkv_w, frames, [tail.whole])
-    ada_rows = jnp.concatenate([ada_one_rows, ada_two_rows])
     if mover.pair:
-        grad_parts = [grad_first[:rows], mover.across(grad_first[rows:])]
-        layer_sum = down_part(active, weights, rows, 0, jnp.float32, [ada_one_rows])
-        layer_sum = layer_sum + out_other.astype(jnp.float32)
+        far_first, far_rows = first_back(grad_qkv, qkv_w, frames[1], 1, [tail.whole])
+        far_first = tail.advance(far_first)
+        half = rows // 2
+        near_half, last_half = far_first[:half], far_first[half:]
+        near_half = mover.across(near_half)
+        own_first, own_rows = first_back(grad_qkv, qkv_w, frames[0], 0, [far_first])
+        ada_rows = jnp.concatenate([own_rows + far_rows, ada_two_rows])
+        ada_other = mover.across(ada_rows)
+        near_half, last_half, ada_other, out_other = tail.advance(
+            [near_half, last_half, ada_other, out_other]
+        )
+        ada_rows = ada_rows + ada_other
+        far_parts = [near_half, mover.across(last_half)]
+        layer_sum = out_own + out_other.astype(jnp.float32)
     else:
-        grad_parts = [lax.psum_scatter(grad_first, "seq", scatter_dimension=0, tiled=True)]
+        grad_first, ada_one_rows = first_back(grad_qkv, qkv_w, frames[0], 0, [tail.whole])
+        ada_rows = lax.psum(jnp.concatenate([ada_one_rows, ada_two_rows]), "seq")
+        own_first = lax.psum_scatter(grad_first, "seq", scatter_dimension=0, tiled=True)
+        far_parts = [jnp.zeros((rows, width), jnp.bfloat16)]
         layer_sum = lax.psum_scatter(
             down_part(active, weights, total_rows, 0, jnp.bfloat16),
             "seq",
@@ -1154,13 +1250,12 @@
             tiled=True,
         ).astype(jnp.float32)
     layer_out = (attended + layer_sum).astype(jnp.bfloat16)
-    input_grad = input_back(grad_parts, tokens, ada_one, grad_attended)
-
-    sums = mover.sum_seq(choose[None, :, None] * ada_rows[:, None, :])
-    bit = 1
-    while bit < items_count:
+    sums = choose[None, :, None] * ada_rows[:, None, :]
+    for bit in [1 << k for k in range(items_count.bit_length() - 1)]:
         sums = sums + mover.flip(sums, bit)
-        bit *= 2
+        if bit == 2:
+            sums = tail.advance(sums)
+    input_grad = input_back(own_first, far_parts, tokens, ada_one, grad_attended)
     out_piece = piece // seq_count
     first_row = mover.item * piece + mover.seq * out_piece
     table_rows = cut(section_table, first_row, out_piece, 1).astype(jnp.float32)

time: 461 us -> 437 us (0.948)
  starting transfers between devices: 58.1 us -> 41.9 us
  waiting for transfers between devices: 91.8 us -> 78.1 us
  Pallas kernels: 214 us -> 221 us
    ppermute x20 -> x16, starting transfers between devices: 22 us -> 7.68 us  [flip(): return lax.ppermute(value, 'items', pairs)]
    ppermute x14, waiting for transfers between devices: 22 us -> 8.9 us  [send(): lax.ppermute(value, 'items', flow[0])]
    ppermute x12 -> x14, waiting for transfers between devices: 39.3 us -> 30.9 us  [across(): return lax.ppermute(value, 'seq', [(0, 1), (1, 0)])]
    pallas_call x12 -> x13, Pallas kernels: 117 us -> 122 us  [the longest x4 47.6 us: attend_back(): pl.pallas_call(partial(attend_back_kernel, parts, calls), grid_spec=pltpu...]
    unnamed x105 -> x94, local copies, waits for them, and re-layouts: 12.6 us -> 7.24 us
    ppermute x7 -> x4, waiting for transfers between devices: 12 us -> 16.8 us  [gather_items(): moved = lax.ppermute(direct[-1], 'items', self.both_ways)]
    pallas_call x1 -> x2, Pallas kernels: 28.4 us -> 31.6 us  [attend(): pl.pallas_call(attend_kernel, grid_spec=pltpu.PrefetchScalarGridSpec(num_...]
    ppermute x12 -> x14, starting transfers between devices: 12.9 us -> 14.5 us  [across(): return lax.ppermute(value, 'seq', [(0, 1), (1, 0)])]
  transfers between devices with their start and end apart: 54 -> 49, of which waited for: 24 -> 19; matrix products, arithmetic and copies ran while one was open for 13% -> 14% of each run, Pallas kernels for 39% -> 41%
where the time goes in v3:
time: 437 us; the launch traced here: 432 us
  Pallas kernels  221 us (51%)
  waiting for transfers between devices  78.1 us (18%)
  starting transfers between devices  41.9 us (10%)
  other arithmetic  38.8 us (9%)
  local copies, waits for them, and re-layouts  30.9 us (7%)
  between operations  17.5 us (4%)
    pallas_call x4, Pallas kernels, attend_back(): pl.pallas_call(partial(attend_back_kernel, parts, calls), grid_spec=pltpu...  47.6 us
    pallas_call x2, Pallas kernels, attend(): pl.pallas_call(attend_kernel, grid_spec=pltpu.PrefetchScalarGridSpec(num_...  31.6 us
    ppermute x14, waiting for transfers between devices, across(): return lax.ppermute(value, 'seq', [(0, 1), (1, 0)])  30.9 us
    pallas_call x4, Pallas kernels, hidden_to_width(): pl.pallas_call(kernel, grid=(weights.steps,), in_specs=[pl.BlockSpec((row...  30.6 us
    pallas_call x2, Pallas kernels, hidden_grads(): pl.pallas_call(partial(hidden_grads_kernel, count, bool(more)), grid_spec...  25.2 us
    pallas_call x1, Pallas kernels, hidden_layer(): pl.pallas_call(partial(hidden_kernel, weights.per_chip, len(grads)), grid...  18.5 us
    pallas_call x2, Pallas kernels, tail_grads(): pl.pallas_call(partial(tail_grads_kernel, first, bool(more), len(mixed) +...  18.3 us
    ppermute x16, waiting for transfers between devices, flip(): return lax.ppermute(value, 'items', pairs)  17.6 us
  transfers between devices with their start and end apart: 49, of which 19 were waited for; matrix products, arithmetic and copies ran while one was open for 14% of the time, Pallas kernels for 41%

profile of v3, /device:TPU:0, one launch (start us, length us, event | category | flops | bytes accessed | tf_op | source)
XLA Modules:
  0.0 431.8 jit_solution(44040434846855314)
XLA Ops:
  10.9 2.9 collective-permute-start.7
  22.3 6.3 %collective-permute-done.1 = f32[4,8,1024]{2,1,0:T(8,128)} collective-permute-done((f32[4,8,1024]{2,1,0:T(8,128)}, f32[4,8,1024]{2,1,0:T(8,128)}, u32[]{:S(2)}, u32[]{:S(2)}) %collective-permute-start.1) | collective-permute-done | bytes 131104 | tf_op jit(solution)/shard_map/ppermute | solution.py:896
  32.7 3.4 collective-permute-done.2
  38.8 5.3 %collective-permute-done.3 = f32[4,8,1024]{2,1,0:T(8,128)S(1)} collective-permute-done((f32[4,8,1024]{2,1,0:T(8,128)S(1)}, f32[4,8,1024]{2,1,0:T(8,128)S(1)}, u32[]{:S(2)}, u32[]{:S(2)}) %collective-permute-start.3) | collective-permute-done | bytes 131104 | tf_op jit(solution)/shard_map/ppermute | solution.py:896
  50.4 3.8 collective-permute-done.8.refs_6_
  56.2 12.9 %collective-permute-done.9.refs_7_ = bf16[128,1536]{1,0:T(8,128)(2,1)S(1)} collective-permute-done((bf16[128,1536]{1,0:T(8,128)(2,1)S(1)}, bf16[128,1536]{1,0:T(8,128)(2,1)S(1)}, u32[]{:S(2)}, u32[]{:S(2)}) %collective-permute-start.9) | collective-permute-done | bytes 393248 | tf_op jit(solution)/shard_map/ppermute | solution.py:912
  70.6 11.3 %first_layer.1 = (bf16[1280,1024]{1,0:T(8,128)(2,1)}, bf16[1280,1536]{1,0:T(8,128)(2,1)}, bf16[1024,1536]{1,0:T(8,128)(2,1)}) custom-call(s32[8]{0:T(128)} %slice_bitcast_fusion.8.spots, bf16[640,1024]{1,0:T(8,128)(2,1)} %bitcast.153, bf16[640,1024]{1,0:T(8,128)(2,1)} %copy-done.9, f32[2,1024]{1,0:T(2,128)} %get-tuple-element.186.refs_2_.ada_ref, ...), custom_call_target="tpu_custom_call" | custom-call | flops 2013265920 | bytes 8388608 | tf_op jit(solution)/shard_map/first_layer/pallas_call | solution.py:345
  83.0 15.8 %attend.2 = (bf16[1280,256]{1,0:T(8,128)(2,1)}, f32[2,10,256]{2,1,0:T(8,128)}) custom-call(s32[2]{0:T(128)} %pad_add_fusion.5.place, bf16[1280,1536]{1,0:T(8,128)(2,1)} %get-tuple-element.69.q_ref.k_ref.v_ref, bf16[1280,1536]{1,0:T(8,128)(2,1)} %get-tuple-element.69.q_ref.k_ref.v_ref, bf16[1280,1536]{1,0:T(8,128)(2,1)} %get-tuple-element.69.q_ref.k_ref.v_ref, ...), custom_call_target="tpu_custom_call" | custom-call | flops 2516582400 | bytes 2621440 | tf_op jit(solution)/shard_map/attend/pallas_call | solution.py:91
  99.2 15.8 %attend.3 = (bf16[1280,256]{1,0:T(8,128)(2,1)}, f32[2,10,256]{2,1,0:T(8,128)}) custom-call(s32[2]{0:T(128)} %pad_add_fusion.5.place, bf16[1280,1536]{1,0:T(8,128)(2,1)} %get-tuple-element.69.q_ref.k_ref.v_ref, bf16[1280,1536]{1,0:T(8,128)(2,1)} %get-tuple-element.69.q_ref.k_ref.v_ref, bf16[1280,1536]{1,0:T(8,128)(2,1)} %get-tuple-element.69.q_ref.k_ref.v_ref, ...), custom_call_target="tpu_custom_call" | custom-call | flops 2516582400 | bytes 2621440 | tf_op jit(solution)/shard_map/attend/pallas_call | solution.py:91
  117.4 15.5 %collective-permute-done.15.refs_3_ = bf16[1280,256]{1,0:T(8,128)(2,1)S(1)} collective-permute-done((bf16[1280,256]{1,0:T(8,128)(2,1)}, bf16[1280,256]{1,0:T(8,128)(2,1)S(1)}, u32[]{:S(2)}, u32[]{:S(2)}) %collective-permute-start.15) | collective-permute-done | bytes 655392 | tf_op jit(solution)/shard_map/ppermute | solution.py:899
  132.8 4.0 all-gather.3.cloned.1.call-done
  136.8 9.3 %second_layer.1 = (f32[640,1024]{1,0:T(8,128)}, bf16[1280,1024]{1,0:T(8,128)(2,1)}) custom-call(s32[4]{0:T(128)} %pad_add_fusion.4.spots, bf16[1280,256]{1,0:T(8,128)(2,1)} %get-tuple-element.71.refs_1_.refs_0_, bf16[1280,256]{1,0:T(8,128)(2,1)} %get-tuple-element.74.refs_1_, bf16[1280,256]{1,0:T(8,128)(2,1)} %copy-done.6, bf16[1280,256]{1,0:T(8,128)(2,1)} %copy-done.7, ...), custom_call_target="tpu_custom_call" | custom-call | flops 1342177280 | bytes 7602176 | tf_op jit(solution)/shard_map/second_layer/pallas_call | solution.py:398
  146.1 18.5 %hidden_layer.1 = (bf16[1280,2048]{1,0:T(8,128)(2,1)}, bf16[1280,2048]{1,0:T(8,128)(2,1)}) custom-call(bf16[1280,1024]{1,0:T(8,128)(2,1)} %get-tuple-element.77.x_ref.refs_4_, bf16[16,5,64,1024]{3,2,1,0:T(8,128)(2,1)} %bitcast.130, bf16[8,2,5,64,1024]{4,3,2,1,0:T(8,128)(2,1)} %bitcast.131, bf16[640,1024]{1,0:T(8,128)(2,1)} %bitcast.147, ...), custom_call_target="tpu_custom_call" | custom-call | flops 5368709120 | bytes 12058624 | tf_op jit(solution)/shard_map/hidden_layer/pallas_call | solution.py:474
  164.6 7.5 %up_back.2.refs_5_ = bf16[640,1024]{1,0:T(8,128)(2,1)} custom-call(bf16[1280,2048]{1,0:T(8,128)(2,1)} %get-tuple-element.79.g_ref.refs_1_, bf16[16,5,64,1024]{3,2,1,0:T(8,128)(2,1)} %bitcast.132), custom_call_target="tpu_custom_call" | custom-call | flops 1342177280 | bytes 4718592 | tf_op jit(solution)/shard_map/up_back/pallas_call | solution.py:523
  175.1 12.3 %hidden_grads.2.refs_0_ = bf16[1024,2048]{1,0:T(8,128)(2,1)} custom-call(s32[1]{0:T(128)} %bitcast.18.core, bf16[1280,2048]{1,0:T(8,128)(2,1)} %get-tuple-element.78.refs_0_.a_ref, bf16[1280,2048]{1,0:T(8,128)(2,1)} %get-tuple-element.79.g_ref.refs_1_, bf16[640,1024]{1,0:T(8,128)(2,1)} %bitcast.148, bf16[640,1024]{1,0:T(8,128)(2,1)} %copy-done.2, ...), custom_call_target="tpu_custom_call" | custom-call | flops 2684354560 | bytes 7340032 | tf_op jit(solution)/shard_map/hidden_grads/pallas_call | solution.py:714
  187.4 3.1 collective-permute-done.16.refs_5_
  192.0 7.9 %up_back.3.refs_6_.refs_0_ = f32[640,1024]{1,0:T(8,128)} custom-call(bf16[1280,2048]{1,0:T(8,128)(2,1)} %get-tuple-element.79.g_ref.refs_1_, bf16[16,5,64,1024]{3,2,1,0:T(8,128)(2,1)} %bitcast.133, bf16[1024,2048]{1,0:T(8,128)(2,1)} %hidden_grads.2.refs_0_), custom_call_target="tpu_custom_call" | custom-call | flops 1342177280 | bytes 4718592 | tf_op jit(solution)/shard_map/up_back/pallas_call | solution.py:523
  199.9 12.9 %hidden_grads.3.refs_7_ = bf16[1024,2048]{1,0:T(8,128)(2,1)} custom-call(s32[1]{0:T(128)} %bitcast.17.core, bf16[1280,2048]{1,0:T(8,128)(2,1)} %get-tuple-element.78.refs_0_.a_ref, bf16[1280,2048]{1,0:T(8,128)(2,1)} %get-tuple-element.79.g_ref.refs_1_, bf16[640,1024]{1,0:T(8,128)(2,1)} %bitcast.149, bf16[640,1024]{1,0:T(8,128)(2,1)} %copy-done.2, ...), custom_call_target="tpu_custom_call" | custom-call | flops 2684354560 | bytes 7340032 | tf_op jit(solution)/shard_map/hidden_grads/pallas_call | solution.py:714
  212.7 2.6 dynamic-slice_bitcast_fusion
  220.1 8.9 %middle_back.1 = (f32[640,1024]{1,0:T(8,128)}, bf16[640,1024]{1,0:T(8,128)(2,1)}, f32[2,1024]{1,0:T(2,128)}, bf16[640,512]{1,0:T(8,128)(2,1)}, bf16[640,512]{1,0:T(8,128)(2,1)}) custom-call(s32[2]{0:T(128)} %pad_add_fusion.6.spots, f32[640,1024]{1,0:T(8,128)} %up_back.3.refs_6_.refs_0_, f32[640,1024]{1,0:T(8,128)} %get-tuple-element.76.refs_1_, ...), custom_call_target="tpu_custom_call" | custom-call | flops 671088640 | bytes 7602176 | tf_op jit(solution)/shard_map/middle_back/pallas_call | solution.py:600
  229.6 7.4 %down_part.2.refs_0_ = bf16[640,1024]{1,0:T(8,128)(2,1)} custom-call(bf16[1280,2048]{1,0:T(8,128)(2,1)} %get-tuple-element.78.refs_0_.a_ref, bf16[8,2,5,64,1024]{4,3,2,1,0:T(8,128)(2,1)} %bitcast.135, bf16[640,512]{1,0:T(8,128)(2,1)} %get-tuple-element.83.refs_0_), custom_call_target="tpu_custom_call" | custom-call | flops 1342177280 | bytes 4718592 | tf_op jit(solution)/shard_map/down_part/pallas_call | solution.py:523
  237.0 2.6 bitcast_add_fusion.1
  242.3 7.8 %down_part.3.refs_6_ = f32[640,1024]{1,0:T(8,128)} custom-call(bf16[1280,2048]{1,0:T(8,128)(2,1)} %get-tuple-element.78.refs_0_.a_ref, bf16[8,2,5,64,1024]{4,3,2,1,0:T(8,128)(2,1)} %bitcast.136, bf16[640,1024]{1,0:T(8,128)(2,1)} %down_part.2.refs_0_), custom_call_target="tpu_custom_call" | custom-call | flops 1342177280 | bytes 4718592 | tf_op jit(solution)/shard_map/down_part/pallas_call | solution.py:523
  250.9 11.7 %attend_back.4.refs_6_ = bf16[1280,1536]{1,0:T(8,128)(2,1)} custom-call(s32[4]{0:T(128)} %get-tuple-element.198.place, bf16[1280,1536]{1,0:T(8,128)(2,1)} %get-tuple-element.69.q_ref.k_ref.v_ref, bf16[1280,1536]{1,0:T(8,128)(2,1)} %get-tuple-element.69.q_ref.k_ref.v_ref, bf16[1280,1536]{1,0:T(8,128)(2,1)} %get-tuple-element.69.q_ref.k_ref.v_ref, ...), custom_call_target="tpu_custom_call" | custom-call | flops 3145728000 | bytes 3276800 | tf_op jit(solution)/shard_map/attend_back/pallas_call | solution.py:202
  262.7 2.6 bitcast_add_fusion
  268.5 12.2 %attend_back.5.grad.refs_6_ = bf16[1280,1536]{1,0:T(8,128)(2,1)} custom-call(s32[4]{0:T(128)} %get-tuple-element.197.place, bf16[1280,1536]{1,0:T(8,128)(2,1)} %get-tuple-element.69.q_ref.k_ref.v_ref, bf16[1280,1536]{1,0:T(8,128)(2,1)} %get-tuple-element.69.q_ref.k_ref.v_ref, ...), custom_call_target="tpu_custom_call", output_to_operand_aliasing={{}: (10, {})} | custom-call | flops 3145728000 | bytes 3276800 | tf_op jit(solution)/shard_map/attend_back/pallas_call | solution.py:202
  280.8 9.0 %tail_grads.2.refs_7_ = bf16[1024,1280]{1,0:T(8,128)(2,1)} custom-call(s32[5]{0:T(128)} %concatenate.52.place, bf16[1280,1024]{1,0:T(8,128)(2,1)} %get-tuple-element.85.low, bf16[1280,1536]{1,0:T(8,128)(2,1)} %attend_back.5.grad.refs_6_, bf16[640,1024]{1,0:T(8,128)(2,1)} %get-tuple-element.96.attended, bf16[1280,256]{1,0:T(8,128)(2,1)} %get-tuple-element.71.refs_1_.refs_0_, ...), custom_call_target="tpu_custom_call" | custom-call | flops 1342177280 | bytes 5242880 | tf_op jit(solution)/shard_map/tail_grads/pallas_call | solution.py:766
  295.4 11.8 %attend_back.6.refs_6_ = bf16[1280,1536]{1,0:T(8,128)(2,1)} custom-call(s32[4]{0:T(128)} %get-tuple-element.119.place, bf16[1280,1536]{1,0:T(8,128)(2,1)} %get-tuple-element.69.q_ref.k_ref.v_ref, bf16[1280,1536]{1,0:T(8,128)(2,1)} %get-tuple-element.69.q_ref.k_ref.v_ref, ...), custom_call_target="tpu_custom_call", output_to_operand_aliasing={{}: (10, {})} | custom-call | flops 3145728000 | bytes 3276800 | tf_op jit(solution)/shard_map/attend_back/pallas_call | solution.py:202
  307.2 11.9 %attend_back.7.grad.grad_ref = bf16[1280,1536]{1,0:T(8,128)(2,1)} custom-call(s32[4]{0:T(128)} %get-tuple-element.199.place, bf16[1280,1536]{1,0:T(8,128)(2,1)} %get-tuple-element.69.q_ref.k_ref.v_ref, bf16[1280,1536]{1,0:T(8,128)(2,1)} %get-tuple-element.69.q_ref.k_ref.v_ref, ...), custom_call_target="tpu_custom_call", output_to_operand_aliasing={{}: (10, {})} | custom-call | flops 3145728000 | bytes 3276800 | tf_op jit(solution)/shard_map/attend_back/pallas_call | solution.py:202
  319.1 2.0 fusion.1
  322.7 9.3 %tail_grads.3.refs_0_ = bf16[1024,1280]{1,0:T(8,128)(2,1)} custom-call(s32[5]{0:T(128)} %concatenate.51.place, bf16[1280,1024]{1,0:T(8,128)(2,1)} %get-tuple-element.85.low, bf16[1280,1536]{1,0:T(8,128)(2,1)} %attend_back.7.grad.grad_ref, bf16[640,1024]{1,0:T(8,128)(2,1)} %get-tuple-element.96.attended, bf16[1280,256]{1,0:T(8,128)(2,1)} %get-tuple-element.71.refs_1_.refs_0_, ...), custom_call_target="tpu_custom_call" | custom-call | flops 1342177280 | bytes 5242880 | tf_op jit(solution)/shard_map/tail_grads/pallas_call | solution.py:766
  332.0 3.3 dynamic-slice_bitcast_fusion.3
  338.9 5.9 %first_back.2 = (bf16[640,1024]{1,0:T(8,128)(2,1)}, f32[2,1024]{1,0:T(2,128)}) custom-call(bf16[1280,1536]{1,0:T(8,128)(2,1)} %attend_back.7.grad.grad_ref, bf16[1024,1536]{1,0:T(8,128)(2,1)} %get-tuple-element.98.weight_ref, bf16[640,1024]{1,0:T(8,128)(2,1)} %copy-done.9, bf16[1024,1280]{1,0:T(8,128)(2,1)} %tail_grads.3.refs_0_), custom_call_target="tpu_custom_call" | custom-call | flops 1006632960 | bytes 3866624 | tf_op jit(solution)/shard_map/first_back/pallas_call | solution.py:642
  347.0 2.5 fusion.31
  350.0 3.4 bitcast_add_fusion.8
  355.4 6.4 %first_back.3 = (bf16[640,1024]{1,0:T(8,128)(2,1)}, f32[2,1024]{1,0:T(2,128)}) custom-call(bf16[1280,1536]{1,0:T(8,128)(2,1)} %attend_back.7.grad.grad_ref, bf16[1024,1536]{1,0:T(8,128)(2,1)} %get-tuple-element.98.weight_ref, bf16[640,1024]{1,0:T(8,128)(2,1)} %bitcast.155, bf16[640,1024]{1,0:T(8,128)(2,1)} %get-tuple-element.102.refs_0_), custom_call_target="tpu_custom_call" | custom-call | flops 1006632960 | bytes 3866624 | tf_op jit(solution)/shard_map/first_back/pallas_call | solution.py:642
  364.7 2.3 collective-permute-done.33
  368.7 3.0 collective-permute-done.45
  373.1 3.6 bitcast_add_fusion.6
  380.0 2.3 reshape.102
  382.3 2.6 collective-permute-done.36
  387.7 3.9 fusion
  391.8 2.8 collective-permute-start.47
  396.7 2.4 collective-permute-done.47
  400.4 3.0 collective-permute-done.40
  408.5 5.8 %input_back.1 = f32[640,1024]{1,0:T(8,128)} custom-call(bf16[640,1024]{1,0:T(8,128)(2,1)} %get-tuple-element.107.own_ref, bf16[640,1024]{1,0:T(8,128)(2,1)} %bitcast.156, f32[2,1024]{1,0:T(2,128)} %get-tuple-element.186.refs_2_.ada_ref, f32[640,1024]{1,0:T(8,128)} %get-tuple-element.108.base_ref, bf16[320,1024]{1,0:T(8,128)(2,1)} %collective-permute-done.32.refs_0_, ...), custom_call_target="tpu_custom_call" | custom-call | flops 6553600 | bytes 4587520 | tf_op jit(solution)/shard_map/input_back/pallas_call | solution.py:810
  417.2 2.8 collective-permute-done.43
  420.7 3.1 collective-permute-done.42
  (238 shorter events, 86.6 us)
Async XLA Ops:
  7.2 129.6 %all-gather.3.cloned.1.call-start = ((), (), s32[]{:S(2)}) async-start(), calls=%async_computation | async-start | bytes 11141120 | tf_op jit(solution)/shard_map/all_gather | solution.py:1065
  8.7 10.6 %collective-permute-start = (f32[4,8,1024]{2,1,0:T(8,128)S(1)}, f32[4,8,1024]{2,1,0:T(8,128)S(1)}, u32[]{:S(2)}, u32[]{:S(2)}) collective-permute-start(f32[4,8,1024]{2,1,0:T(8,128)S(1)} %pad_maximum_fusion.3), channel_id=1, source_target_pairs={{0,2},{2,0},{4,6},{6,4},{8,10},{10,8},{12,14},{14,12},{16,18},{18,... | collective-permute-start | bytes 393224 | tf_op jit(solution)/shard_map/ppermute | solution.py:896
  10.9 5.0 %collective-permute-start.4 = (bf16[64,1536]{1,0:T(8,128)(2,1)}, bf16[64,1536]{1,0:T(8,128)(2,1)S(1)}, u32[]{:S(2)}, u32[]{:S(2)}) collective-permute-start(bf16[64,1536]{1,0:T(8,128)(2,1)} %pack_columns.1), channel_id=1, source_target_pairs={{0,2},{2,0},{4,6},{6,4},{8,10},{10,8},{12,14},{14,12},{16,18},{18,... | collective-permute-start | bytes 589832 | tf_op jit(solution)/shard_map/ppermute | solution.py:896
  10.9 33.3 %collective-permute-start.7 = (bf16[640,1024]{1,0:T(8,128)(2,1)}, bf16[640,1024]{1,0:T(8,128)(2,1)S(1)}, u32[]{:S(2)}, u32[]{:S(2)}) collective-permute-start(bf16[640,1024]{1,0:T(8,128)(2,1)} %bitcast.152), channel_id=1, source_target_pairs={{0,1},{1,0},{2,3},{3,2},{4,5},{5,4},{6,7},{7,6},{8,9},{9,8},{10,11... | collective-permute-start | bytes 3932168 | tf_op jit(solution)/shard_map/ppermute | solution.py:899
  17.7 12.0 %collective-permute-start.5 = (bf16[128,1536]{1,0:T(8,128)(2,1)}, bf16[128,1536]{1,0:T(8,128)(2,1)}, u32[]{:S(2)}, u32[]{:S(2)}) collective-permute-start(bf16[128,1536]{1,0:T(8,128)(2,1)} %maximum_select_fusion.refs_3_), channel_id=1, source_target_pairs={{0,8},{8,16},{16,24},{24,28},{28,20},{20,12},{12,4},{4,0},{10,2},{... | collective-permute-start | bytes 1179656 | tf_op jit(solution)/shard_map/ppermute | solution.py:912
  20.0 8.6 %collective-permute-start.1 = (f32[4,8,1024]{2,1,0:T(8,128)}, f32[4,8,1024]{2,1,0:T(8,128)}, u32[]{:S(2)}, u32[]{:S(2)}) collective-permute-start(f32[4,8,1024]{2,1,0:T(8,128)} %fusion.30), channel_id=1, source_target_pairs={{0,4},{2,6},{4,0},{6,2},{8,12},{10,14},{12,8},{14,10},{16,20},{18,... | collective-permute-start | bytes 393224 | tf_op jit(solution)/shard_map/ppermute | solution.py:896
  29.6 6.5 %collective-permute-start.2 = (f32[4,8,1024]{2,1,0:T(8,128)S(1)}, f32[4,8,1024]{2,1,0:T(8,128)S(1)}, u32[]{:S(2)}, u32[]{:S(2)}) collective-permute-start(f32[4,8,1024]{2,1,0:T(8,128)S(1)} %fusion.38), channel_id=1, source_target_pairs={{0,8},{2,10},{4,12},{6,14},{8,0},{10,2},{12,4},{14,6},{16,24},{18,... | collective-permute-start | bytes 393224 | tf_op jit(solution)/shard_map/ppermute | solution.py:896
  29.7 14.5 %collective-permute-start.6 = (bf16[128,1536]{1,0:T(8,128)(2,1)}, bf16[128,1536]{1,0:T(8,128)(2,1)}, u32[]{:S(2)}, u32[]{:S(2)}) collective-permute-start(bf16[128,1536]{1,0:T(8,128)(2,1)} %collective-permute-done.5.refs_4_), channel_id=1, source_target_pairs={{0,8},{8,16},{16,24},{24,28},{28,20},{20,12},{12,4},{4,0},{10,2},{... | collective-permute-start | bytes 1179656 | tf_op jit(solution)/shard_map/ppermute | solution.py:912
  36.1 8.0 %collective-permute-start.3 = (f32[4,8,1024]{2,1,0:T(8,128)S(1)}, f32[4,8,1024]{2,1,0:T(8,128)S(1)}, u32[]{:S(2)}, u32[]{:S(2)}) collective-permute-start(f32[4,8,1024]{2,1,0:T(8,128)S(1)} %add.103), channel_id=1, source_target_pairs={{0,16},{2,18},{4,20},{6,22},{8,24},{10,26},{12,28},{14,30},{16,0},... | collective-permute-start | bytes 393224 | tf_op jit(solution)/shard_map/ppermute | solution.py:896
  45.2 36.7 %collective-permute-start.13 = (bf16[640,1024]{1,0:T(8,128)(2,1)S(1)}, bf16[640,1024]{1,0:T(8,128)(2,1)S(1)}, u32[]{:S(2)}, u32[]{:S(2)}) collective-permute-start(bf16[640,1024]{1,0:T(8,128)(2,1)S(1)} %bitcast.151), channel_id=1, source_target_pairs={{0,1},{1,0},{2,3},{3,2},{4,5},{5,4},{6,7},{7,6},{8,9},{9,8},{10,11... | collective-permute-start | bytes 3932168 | tf_op jit(solution)/shard_map/ppermute | solution.py:899
  45.8 8.4 %collective-permute-start.8 = (bf16[128,1536]{1,0:T(8,128)(2,1)}, bf16[128,1536]{1,0:T(8,128)(2,1)S(1)}, u32[]{:S(2)}, u32[]{:S(2)}) collective-permute-start(bf16[128,1536]{1,0:T(8,128)(2,1)} %collective-permute-done.6.refs_5_), channel_id=1, source_target_pairs={{0,8},{8,16},{16,24},{24,28},{28,20},{20,12},{12,4},{4,0},{10,2},{... | collective-permute-start | bytes 1179656 | tf_op jit(solution)/shard_map/ppermute | solution.py:912
  49.9 6.3 %collective-permute-start.10 = (bf16[128,1536]{1,0:T(8,128)(2,1)}, bf16[128,1536]{1,0:T(8,128)(2,1)S(1)}, u32[]{:S(2)}, u32[]{:S(2)}) collective-permute-start(bf16[128,1536]{1,0:T(8,128)(2,1)} %collective-permute-done.5.refs_4_), channel_id=1, source_target_pairs={{0,2},{2,0},{4,6},{6,4},{8,10},{10,8},{12,14},{14,12},{16,18},{18,... | collective-permute-start | bytes 1179656 | tf_op jit(solution)/shard_map/ppermute | solution.py:896
  49.9 6.3 %collective-permute-start.11 = (bf16[128,1536]{1,0:T(8,128)(2,1)}, bf16[128,1536]{1,0:T(8,128)(2,1)S(1)}, u32[]{:S(2)}, u32[]{:S(2)}) collective-permute-start(bf16[128,1536]{1,0:T(8,128)(2,1)} %collective-permute-done.6.refs_5_), channel_id=1, source_target_pairs={{0,2},{2,0},{4,6},{6,4},{8,10},{10,8},{12,14},{14,12},{16,18},{18,... | collective-permute-start | bytes 1179656 | tf_op jit(solution)/shard_map/ppermute | solution.py:896
  54.2 14.9 %collective-permute-start.9 = (bf16[128,1536]{1,0:T(8,128)(2,1)S(1)}, bf16[128,1536]{1,0:T(8,128)(2,1)S(1)}, u32[]{:S(2)}, u32[]{:S(2)}) collective-permute-start(bf16[128,1536]{1,0:T(8,128)(2,1)S(1)} %collective-permute-done.8.refs_6_), channel_id=1, source_target_pairs={{0,8},{8,16},{16,24},{24,28},{28,20},{20,12},{12,4},{4,0},{10,2},{... | collective-permute-start | bytes 1179656 | tf_op jit(solution)/shard_map/ppermute | solution.py:912
  55.4 13.7 %collective-permute-start.12 = (bf16[128,1536]{1,0:T(8,128)(2,1)S(1)}, bf16[128,1536]{1,0:T(8,128)(2,1)S(1)}, u32[]{:S(2)}, u32[]{:S(2)}) collective-permute-start(bf16[128,1536]{1,0:T(8,128)(2,1)S(1)} %collective-permute-done.8.refs_6_), channel_id=1, source_target_pairs={{0,2},{2,0},{4,6},{6,4},{8,10},{10,8},{12,14},{14,12},{16,18},{18,... | collective-permute-start | bytes 1179656 | tf_op jit(solution)/shard_map/ppermute | solution.py:896
  98.8 17.3 %collective-permute-start.14 = (bf16[1280,256]{1,0:T(8,128)(2,1)}, bf16[1280,256]{1,0:T(8,128)(2,1)S(1)}, u32[]{:S(2)}, u32[]{:S(2)}) collective-permute-start(bf16[1280,256]{1,0:T(8,128)(2,1)} %get-tuple-element.71.refs_1_.refs_0_), channel_id=1, source_target_pairs={{0,1},{1,0},{2,3},{3,2},{4,5},{5,4},{6,7},{7,6},{8,9},{9,8},{10,11... | collective-permute-start | bytes 1966088 | tf_op jit(solution)/shard_map/ppermute | solution.py:899
  116.2 16.7 %collective-permute-start.15 = (bf16[1280,256]{1,0:T(8,128)(2,1)}, bf16[1280,256]{1,0:T(8,128)(2,1)S(1)}, u32[]{:S(2)}, u32[]{:S(2)}) collective-permute-start(bf16[1280,256]{1,0:T(8,128)(2,1)} %get-tuple-element.74.refs_1_), channel_id=1, source_target_pairs={{0,1},{1,0},{2,3},{3,2},{4,5},{5,4},{6,7},{7,6},{8,9},{9,8},{10,11... | collective-permute-start | bytes 1966088 | tf_op jit(solution)/shard_map/ppermute | solution.py:899
  173.5 17.0 %collective-permute-start.16 = (bf16[320,1024]{1,0:T(8,128)(2,1)S(1)}, bf16[320,1024]{1,0:T(8,128)(2,1)S(1)}, u32[]{:S(2)}, u32[]{:S(2)}) collective-permute-start(bf16[320,1024]{1,0:T(8,128)(2,1)S(1)} %get-tuple-element.136), channel_id=1, source_target_pairs={{0,1},{1,0},{2,3},{3,2},{4,5},{5,4},{6,7},{7,6},{8,9},{9,8},{10,11... | collective-permute-start | bytes 1966088 | tf_op jit(solution)/shard_map/ppermute | solution.py:899
  190.5 9.4 %collective-permute-start.17 = (bf16[1024,2048]{1,0:T(8,128)(2,1)}, bf16[1024,2048]{1,0:T(8,128)(2,1)}, u32[]{:S(2)}, u32[]{:S(2)}) collective-permute-start(bf16[1024,2048]{1,0:T(8,128)(2,1)} %hidden_grads.2.refs_0_), channel_id=1, source_target_pairs={{0,2},{2,0},{4,6},{6,4},{8,10},{10,8},{12,14},{14,12},{16,18},{18,... | collective-permute-start | bytes 12582920 | tf_op jit(solution)/shard_map/ppermute | solution.py:896
  190.5 28.7 %collective-permute-start.20 = (bf16[320,1024]{1,0:T(8,128)(2,1)S(1)}, bf16[320,1024]{1,0:T(8,128)(2,1)S(1)}, u32[]{:S(2)}, u32[]{:S(2)}) collective-permute-start(bf16[320,1024]{1,0:T(8,128)(2,1)S(1)} %get-tuple-element.82), channel_id=1, source_target_pairs={{0,1},{1,0},{2,3},{3,2},{4,5},{5,4},{6,7},{7,6},{8,9},{9,8},{10,11... | collective-permute-start | bytes 1966088 | tf_op jit(solution)/shard_map/ppermute | solution.py:899
  215.3 21.7 %collective-permute-start.18 = (bf16[128,2048]{1,0:T(8,128)(2,1)S(1)}, bf16[128,2048]{1,0:T(8,128)(2,1)S(1)}, u32[]{:S(2)}, u32[]{:S(2)}) collective-permute-start(bf16[128,2048]{1,0:T(8,128)(2,1)S(1)} %get-tuple-element.126), channel_id=1, source_target_pairs={{0,8},{2,10},{8,16},{10,18},{16,24},{18,26},{24,28},{26,30},{28,20... | collective-permute-start | bytes 1572872 | tf_op jit(solution)/shard_map/ppermute | solution.py:973
  215.9 21.1 %collective-permute-start.19 = (bf16[128,2048]{1,0:T(8,128)(2,1)S(1)}, bf16[128,2048]{1,0:T(8,128)(2,1)S(1)}, u32[]{:S(2)}, u32[]{:S(2)}) collective-permute-start(bf16[128,2048]{1,0:T(8,128)(2,1)S(1)} %get-tuple-element.125), channel_id=1, source_target_pairs={{8,0},{10,2},{16,8},{18,10},{24,16},{26,18},{28,24},{30,26},{20,28... | collective-permute-start | bytes 1572872 | tf_op jit(solution)/shard_map/ppermute | solution.py:973
  229.0 21.1 %collective-permute-start.21 = (bf16[640,512]{1,0:T(8,128)(2,1)}, bf16[640,512]{1,0:T(8,128)(2,1)S(1)}, u32[]{:S(2)}, u32[]{:S(2)}) collective-permute-start(bf16[640,512]{1,0:T(8,128)(2,1)} %get-tuple-element.83.refs_0_), channel_id=1, source_target_pairs={{0,1},{1,0},{2,3},{3,2},{4,5},{5,4},{6,7},{7,6},{8,9},{9,8},{10,11... | collective-permute-start | bytes 1966088 | tf_op jit(solution)/shard_map/ppermute | solution.py:899
  239.6 23.1 %collective-permute-start.22 = (bf16[128,2048]{1,0:T(8,128)(2,1)S(1)}, bf16[128,2048]{1,0:T(8,128)(2,1)S(1)}, u32[]{:S(2)}, u32[]{:S(2)}) collective-permute-start(bf16[128,2048]{1,0:T(8,128)(2,1)S(1)} %get-tuple-element.124), channel_id=1, source_target_pairs={{0,8},{2,10},{8,16},{10,18},{16,24},{18,26},{24,28},{26,30},{28,20... | collective-permute-start | bytes 1572872 | tf_op jit(solution)/shard_map/ppermute | solution.py:973
  240.2 22.5 %collective-permute-start.23 = (bf16[128,2048]{1,0:T(8,128)(2,1)S(1)}, bf16[128,2048]{1,0:T(8,128)(2,1)S(1)}, u32[]{:S(2)}, u32[]{:S(2)}) collective-permute-start(bf16[128,2048]{1,0:T(8,128)(2,1)S(1)} %get-tuple-element.123), channel_id=1, source_target_pairs={{8,0},{10,2},{16,8},{18,10},{24,16},{26,18},{28,24},{30,26},{20,28... | collective-permute-start | bytes 1572872 | tf_op jit(solution)/shard_map/ppermute | solution.py:973
  265.3 15.4 %collective-permute-start.24 = (bf16[128,2048]{1,0:T(8,128)(2,1)S(1)}, bf16[128,2048]{1,0:T(8,128)(2,1)S(1)}, u32[]{:S(2)}, u32[]{:S(2)}) collective-permute-start(bf16[128,2048]{1,0:T(8,128)(2,1)S(1)} %get-tuple-element.122), channel_id=1, source_target_pairs={{0,8},{2,10},{8,16},{10,18},{16,24},{18,26},{24,28},{26,30},{28,20... | collective-permute-start | bytes 1572872 | tf_op jit(solution)/shard_map/ppermute | solution.py:973
  265.9 14.8 %collective-permute-start.25 = (bf16[128,2048]{1,0:T(8,128)(2,1)S(1)}, bf16[128,2048]{1,0:T(8,128)(2,1)S(1)}, u32[]{:S(2)}, u32[]{:S(2)}) collective-permute-start(bf16[128,2048]{1,0:T(8,128)(2,1)S(1)} %get-tuple-element.121), channel_id=1, source_target_pairs={{8,0},{10,2},{16,8},{18,10},{24,16},{26,18},{28,24},{30,26},{20,28... | collective-permute-start | bytes 1572872 | tf_op jit(solution)/shard_map/ppermute | solution.py:973
  289.8 32.9 %collective-permute-start.27 = (bf16[1024,1280]{1,0:T(8,128)(2,1)}, bf16[1024,1280]{1,0:T(8,128)(2,1)}, u32[]{:S(2)}, u32[]{:S(2)}) collective-permute-start(bf16[1024,1280]{1,0:T(8,128)(2,1)} %tail_grads.2.refs_7_), channel_id=1, source_target_pairs={{0,2},{2,0},{4,6},{6,4},{8,10},{10,8},{12,14},{14,12},{16,18},{18,... | collective-permute-start | bytes 7864328 | tf_op jit(solution)/shard_map/ppermute | solution.py:896
  291.5 15.7 %collective-permute-start.26 = (bf16[128,2048]{1,0:T(8,128)(2,1)S(1)}, bf16[128,2048]{1,0:T(8,128)(2,1)}, u32[]{:S(2)}, u32[]{:S(2)}) collective-permute-start(bf16[128,2048]{1,0:T(8,128)(2,1)S(1)} %bitcast_add_fusion.4), channel_id=1, source_target_pairs={{0,8},{2,10},{8,16},{10,18},{16,24},{18,26},{24,28},{26,30},{28,20... | collective-permute-start | bytes 1572872 | tf_op jit(solution)/shard_map/ppermute | solution.py:973
  294.0 70.1 %collective-permute-start.34 = (bf16[640,1024]{1,0:T(8,128)(2,1)S(1)}, bf16[640,1024]{1,0:T(8,128)(2,1)S(1)}, u32[]{:S(2)}, u32[]{:S(2)}) collective-permute-start(bf16[640,1024]{1,0:T(8,128)(2,1)S(1)} %copy-done.8), channel_id=1, source_target_pairs={{0,1},{1,0},{2,3},{3,2},{4,5},{5,4},{6,7},{7,6},{8,9},{9,8},{10,11... | collective-permute-start | bytes 3932168 | tf_op jit(solution)/shard_map/ppermute | solution.py:899
  322.6 14.7 %collective-permute-start.44 = (f32[64,1024]{1,0:T(8,128)S(1)}, f32[64,1024]{1,0:T(8,128)}, u32[]{:S(2)}, u32[]{:S(2)}) collective-permute-start(f32[64,1024]{1,0:T(8,128)S(1)} %dynamic-slice_bitcast_fusion.5), channel_id=1, source_target_pairs={{0,2},{2,0},{4,6},{6,4},{8,10},{10,8},{12,14},{14,12},{16,18},{18,... | collective-permute-start | bytes 786440 | tf_op jit(solution)/shard_map/ppermute | solution.py:896
  335.3 10.3 %collective-permute-start.28 = (bf16[128,1280]{1,0:T(8,128)(2,1)}, bf16[128,1280]{1,0:T(8,128)(2,1)S(1)}, u32[]{:S(2)}, u32[]{:S(2)}) collective-permute-start(bf16[128,1280]{1,0:T(8,128)(2,1)} %get-tuple-element.132), channel_id=1, source_target_pairs={{0,8},{2,10},{8,16},{10,18},{16,24},{18,26},{24,28},{26,30},{28,20... | collective-permute-start | bytes 983048 | tf_op jit(solution)/shard_map/ppermute | solution.py:973
  336.9 10.1 %collective-permute-start.29 = (bf16[128,1280]{1,0:T(8,128)(2,1)}, bf16[128,1280]{1,0:T(8,128)(2,1)}, u32[]{:S(2)}, u32[]{:S(2)}) collective-permute-start(bf16[128,1280]{1,0:T(8,128)(2,1)} %get-tuple-element.131), channel_id=1, source_target_pairs={{8,0},{10,2},{16,8},{18,10},{24,16},{26,18},{28,24},{30,26},{20,28... | collective-permute-start | bytes 983048 | tf_op jit(solution)/shard_map/ppermute | solution.py:973
  349.5 17.6 %collective-permute-start.32 = (bf16[320,1024]{1,0:T(8,128)(2,1)}, bf16[320,1024]{1,0:T(8,128)(2,1)}, u32[]{:S(2)}, u32[]{:S(2)}) collective-permute-start(bf16[320,1024]{1,0:T(8,128)(2,1)} %get-tuple-element.134), channel_id=1, source_target_pairs={{0,1},{1,0},{2,3},{3,2},{4,5},{5,4},{6,7},{7,6},{8,9},{9,8},{10,11... | collective-permute-start | bytes 1966088 | tf_op jit(solution)/shard_map/ppermute | solution.py:899
  353.4 13.7 %collective-permute-start.30 = (bf16[128,1280]{1,0:T(8,128)(2,1)}, bf16[128,1280]{1,0:T(8,128)(2,1)S(1)}, u32[]{:S(2)}, u32[]{:S(2)}) collective-permute-start(bf16[128,1280]{1,0:T(8,128)(2,1)} %get-tuple-element.130), channel_id=1, source_target_pairs={{0,8},{2,10},{8,16},{10,18},{16,24},{18,26},{24,28},{26,30},{28,20... | collective-permute-start | bytes 983048 | tf_op jit(solution)/shard_map/ppermute | solution.py:973
  353.9 13.2 %collective-permute-start.31 = (bf16[128,1280]{1,0:T(8,128)(2,1)}, bf16[128,1280]{1,0:T(8,128)(2,1)S(1)}, u32[]{:S(2)}, u32[]{:S(2)}) collective-permute-start(bf16[128,1280]{1,0:T(8,128)(2,1)} %get-tuple-element.129), channel_id=1, source_target_pairs={{8,0},{10,2},{16,8},{18,10},{24,16},{26,18},{28,24},{30,26},{20,28... | collective-permute-start | bytes 983048 | tf_op jit(solution)/shard_map/ppermute | solution.py:973
  362.5 4.5 %collective-permute-start.33 = (f32[4,1024]{1,0:T(4,128)S(1)}, f32[4,1024]{1,0:T(4,128)S(1)}, u32[]{:S(2)}, u32[]{:S(2)}) collective-permute-start(f32[4,1024]{1,0:T(4,128)S(1)} %pad_maximum_fusion.4), channel_id=1, source_target_pairs={{0,1},{1,0},{2,3},{3,2},{4,5},{5,4},{6,7},{7,6},{8,9},{9,8},{10,11... | collective-permute-start | bytes 49160 | tf_op jit(solution)/shard_map/ppermute | solution.py:899
  364.1 7.6 %collective-permute-start.45 = (f32[32,2048]{1,0:T(8,128)S(1)}, f32[32,2048]{1,0:T(8,128)S(1)}, u32[]{:S(2)}, u32[]{:S(2)}) collective-permute-start(f32[32,2048]{1,0:T(8,128)S(1)} %fusion.7), channel_id=1, source_target_pairs={{0,1},{1,0},{2,3},{3,2},{4,5},{5,4},{6,7},{7,6},{8,9},{9,8},{10,11... | collective-permute-start | bytes 786440 | tf_op jit(solution)/shard_map/ppermute | solution.py:899
  372.6 9.6 %collective-permute-start.39 = (f32[4,8,1024]{2,1,0:T(8,128)}, f32[4,8,1024]{2,1,0:T(8,128)S(1)}, u32[]{:S(2)}, u32[]{:S(2)}) collective-permute-start(f32[4,8,1024]{2,1,0:T(8,128)} %fusion.24), channel_id=1, source_target_pairs={{0,4},{2,6},{4,0},{6,2},{8,12},{10,14},{12,8},{14,10},{16,20},{18,... | collective-permute-start | bytes 393224 | tf_op jit(solution)/shard_map/ppermute | solution.py:896
  376.7 8.2 %collective-permute-start.36 = (bf16[128,1280]{1,0:T(8,128)(2,1)}, bf16[128,1280]{1,0:T(8,128)(2,1)}, u32[]{:S(2)}, u32[]{:S(2)}) collective-permute-start(bf16[128,1280]{1,0:T(8,128)(2,1)} %get-tuple-element.128), channel_id=1, source_target_pairs={{0,8},{2,10},{8,16},{10,18},{16,24},{18,26},{24,28},{26,30},{28,20... | collective-permute-start | bytes 983048 | tf_op jit(solution)/shard_map/ppermute | solution.py:973
  377.9 8.1 %collective-permute-start.37 = (bf16[128,1280]{1,0:T(8,128)(2,1)}, bf16[128,1280]{1,0:T(8,128)(2,1)}, u32[]{:S(2)}, u32[]{:S(2)}) collective-permute-start(bf16[128,1280]{1,0:T(8,128)(2,1)} %get-tuple-element.127), channel_id=1, source_target_pairs={{8,0},{10,2},{16,8},{18,10},{24,16},{26,18},{28,24},{30,26},{20,28... | collective-permute-start | bytes 983048 | tf_op jit(solution)/shard_map/ppermute | solution.py:973
  386.0 5.8 %collective-permute-start.46 = (f32[4,8,1024]{2,1,0:T(8,128)S(1)}, f32[4,8,1024]{2,1,0:T(8,128)S(1)}, u32[]{:S(2)}, u32[]{:S(2)}) collective-permute-start(f32[4,8,1024]{2,1,0:T(8,128)S(1)} %fusion.37), channel_id=1, source_target_pairs={{0,8},{2,10},{4,12},{6,14},{8,0},{10,2},{12,4},{14,6},{16,24},{18,... | collective-permute-start | bytes 393224 | tf_op jit(solution)/shard_map/ppermute | solution.py:896
  391.6 16.0 %collective-permute-start.35 = (bf16[320,1024]{1,0:T(8,128)(2,1)S(1)}, bf16[320,1024]{1,0:T(8,128)(2,1)S(1)}, u32[]{:S(2)}, u32[]{:S(2)}) collective-permute-start(bf16[320,1024]{1,0:T(8,128)(2,1)S(1)} %copy-done.13), channel_id=1, source_target_pairs={{0,1},{1,0},{2,3},{3,2},{4,5},{5,4},{6,7},{7,6},{8,9},{9,8},{10,11... | collective-permute-start | bytes 1966088 | tf_op jit(solution)/shard_map/ppermute | solution.py:899
  391.8 7.3 %collective-permute-start.47 = (f32[4,8,1024]{2,1,0:T(8,128)S(1)}, f32[4,8,1024]{2,1,0:T(8,128)S(1)}, u32[]{:S(2)}, u32[]{:S(2)}) collective-permute-start(f32[4,8,1024]{2,1,0:T(8,128)S(1)} %add.129), channel_id=1, source_target_pairs={{0,16},{2,18},{4,20},{6,22},{8,24},{10,26},{12,28},{14,30},{16,0},... | collective-permute-start | bytes 393224 | tf_op jit(solution)/shard_map/ppermute | solution.py:896
  396.3 7.1 %collective-permute-start.40 = (bf16[128,1280]{1,0:T(8,128)(2,1)S(1)}, bf16[128,1280]{1,0:T(8,128)(2,1)S(1)}, u32[]{:S(2)}, u32[]{:S(2)}) collective-permute-start(bf16[128,1280]{1,0:T(8,128)(2,1)S(1)} %bitcast_add_fusion.5), channel_id=1, source_target_pairs={{0,8},{2,10},{8,16},{10,18},{16,24},{18,26},{24,28},{26,30},{28,20... | collective-permute-start | bytes 983048 | tf_op jit(solution)/shard_map/ppermute | solution.py:973
  405.8 8.5 %collective-permute-start.41 = (f32[64,1280]{1,0:T(8,128)S(1)}, f32[64,1280]{1,0:T(8,128)S(1)}, u32[]{:S(2)}, u32[]{:S(2)}) collective-permute-start(f32[64,1280]{1,0:T(8,128)S(1)} %dynamic-slice_bitcast_fusion.2), channel_id=1, source_target_pairs={{0,2},{2,0},{4,6},{6,4},{8,10},{10,8},{12,14},{14,12},{16,18},{18,... | collective-permute-start | bytes 983048 | tf_op jit(solution)/shard_map/ppermute | solution.py:896
  415.1 5.0 %collective-permute-start.43 = (bf16[32,1024]{1,0:T(8,128)(2,1)S(1)}, bf16[32,1024]{1,0:T(8,128)(2,1)S(1)}, u32[]{:S(2)}, u32[]{:S(2)}) collective-permute-start(bf16[32,1024]{1,0:T(8,128)(2,1)S(1)} %fusion.19), channel_id=1, source_target_pairs={{0,1},{1,0},{2,3},{3,2},{4,5},{5,4},{6,7},{7,6},{8,9},{9,8},{10,11... | collective-permute-start | bytes 196616 | tf_op jit(solution)/shard_map/ppermute | solution.py:899
  416.2 7.7 %collective-permute-start.42 = (f32[32,1536]{1,0:T(8,128)S(1)}, f32[32,1536]{1,0:T(8,128)S(1)}, u32[]{:S(2)}, u32[]{:S(2)}) collective-permute-start(f32[32,1536]{1,0:T(8,128)S(1)} %fusion.16), channel_id=1, source_target_pairs={{0,1},{1,0},{2,3},{3,2},{4,5},{5,4},{6,7},{7,6},{8,9},{9,8},{10,11... | collective-permute-start | bytes 589832 | tf_op jit(solution)/shard_map/ppermute | solution.py:899
  (43 other events, 425.0 us)
Sparse Core Ops, SparseCore 0:
  44.3 92.4 all-gather.2

commit v4 on v3

--- a/solution.py
+++ b/solution.py
@@ -104,9 +104,8 @@
     )(place, qkv, qkv, qkv, *behind)
 
 
-def attend_back_kernel(parts, calls, place, q_ref, k_ref, v_ref, *refs):
+def attend_back_kernel(parts, calls, per, at, place, q_ref, k_ref, v_ref, *refs):
     o_refs, lse_refs, g_refs = refs[:calls], refs[calls:2 * calls], refs[2 * calls:2 * calls + parts]
-    per = place[3]
     out_ref, keys_wide, values_wide, keys_t, dq, dk, dv = refs[-7:]
     half = q_ref.shape[0] // 2
     step = pl.program_id(0)
@@ -150,7 +149,7 @@
         def of_call(values):
             value = values[0]
             for call, later in enumerate(values[1:], 1):
-                value = jnp.where(place[2] < call * per, value, later)
+                value = jnp.where(at(place) < call * per, value, later)
             return value
 
         def tile(start, seen, slot):
@@ -189,22 +188,25 @@
             out_ref[pl.ds(target, half), :] = held[half:, :].astype(jnp.bfloat16)
 
 
-def attend_back(place, qkv, mixed, grads, lse, held, behind):
+def attend_back(place, turn, pairs, qkv, mixed, grads, lse, held, behind):
     rows = qkv.shape[0]
-    part = lambda shift: pl.BlockSpec((rows, LANES), lambda j, s, shift=shift: (0, 3 * s[2] + shift))
+    part = lambda shift: pl.BlockSpec((rows, LANES), lambda j, s, shift=shift: (0, 3 * at(s) + shift))
     calls = len(mixed)
+    per = pairs // calls
+    split = pairs // 2 if pairs % 2 == 0 else 0
+    at = lambda s: (s[3] * split + turn) & (pairs - 1)
     parts = len(grads)
-    block = pl.BlockSpec((rows, LANES), lambda j, s: (0, s[2] & (s[3] - 1)))
-    lse_block = pl.BlockSpec((1, rows // TILE, 2 * TILE), lambda j, s: (s[2] & (s[3] - 1), 0, 0))
-    grad_blocks = [pl.BlockSpec((grad.shape[0], LANES), lambda j, s: (0, s[2])) for grad in grads]
+    block = pl.BlockSpec((rows, LANES), lambda j, s: (0, at(s) & (per - 1)))
+    lse_block = pl.BlockSpec((1, rows // TILE, 2 * TILE), lambda j, s: (at(s) & (per - 1), 0, 0))
+    grad_blocks = [pl.BlockSpec((grad.shape[0], LANES), lambda j, s: (0, at(s))) for grad in grads]
     seen = rows * rows * 3 // 4
     more = [] if held is None else [held]
     return pl.pallas_call(
-        partial(attend_back_kernel, parts, calls),
+        partial(attend_back_kernel, parts, calls, per, at),
         grid_spec=pltpu.PrefetchScalarGridSpec(
             num_scalar_prefetch=1, grid=(3,),
             in_specs=[part(0), part(1), part(2)] + [block] * calls + [lse_block] * calls + grad_blocks + [pl.BlockSpec(memory_space=pl.ANY)] * (len(more) + len(behind)),
-            out_specs=pl.BlockSpec((rows, LANES), lambda j, s: (0, 3 * s[2] + j)),
+            out_specs=pl.BlockSpec((rows, LANES), lambda j, s: (0, 3 * at(s) + j)),
             scratch_shapes=[pltpu.VMEM((rows, 2 * LANES), jnp.bfloat16), pltpu.VMEM((rows, 2 * LANES), jnp.bfloat16), pltpu.VMEM((LANES, rows), jnp.bfloat16),
                 pltpu.VMEM((rows, LANES), jnp.bfloat16), pltpu.VMEM((rows, LANES), jnp.float32), pltpu.VMEM((rows, LANES), jnp.float32)],
         ),
@@ -300,7 +302,7 @@
         grid_spec=pltpu.PrefetchScalarGridSpec(
             num_scalar_prefetch=1,
             grid=(1,),
-            in_specs=[pl.BlockSpec((rows, held), lambda j, s: (0, s[0]))] * 3,
+            in_specs=[pl.BlockSpec((rows, held), lambda j, s: (0, s[4]))] * 3,
             out_specs=pl.BlockSpec((rows, 3 * held), lambda j, s: (0, 0)),
         ),
         out_shape=jax.ShapeDtypeStruct((rows, 3 * held), query.dtype),
@@ -370,12 +372,13 @@
     )(spots, *frames, ada, *blocks)
 
 
-def second_kernel(pieces, parts, count, spots, *refs):
+def second_kernel(pieces, calls, parts, count, place, *refs):
     mixed = refs[:pieces]
     tokens = refs[pieces : pieces + parts]
     out_w, ada = refs[pieces + parts : pieces + parts + 2]
     attended_ref, low_ref = refs[-2:]
     weights = out_w.reshape(out_w.shape[0] * out_w.shape[2], out_w.shape[3])
+    spots = head_spots(place[4], calls, pieces)
     attended = current(tokens, count).astype(jnp.float32)
     for index, piece in enumerate(mixed):
         size = piece.shape[1]
@@ -396,7 +399,7 @@
     first = lambda j: (j + later) % count
     items, _, piece, _ = out_w.shape
     return pl.pallas_call(
-        partial(second_kernel, len(mixed) + len(swapped), parts, count),
+        partial(second_kernel, len(mixed) + len(swapped), len(mixed), parts, count),
         grid_spec=pltpu.PrefetchScalarGridSpec(
             num_scalar_prefetch=1,
             grid=(count,),
@@ -419,6 +422,13 @@
         ),
         name="second_layer",
     )(spots, *mixed, *swapped, *tokens, out_w, ada)
+
+
+def head_spots(seq, calls, pieces):
+    if pieces == 1:
+        return [0]
+    own = [seq * calls + call for call in range(calls)]
+    return own + [(1 - seq) * calls + call for call in range(pieces - calls)]
 
 
 class Weights:
@@ -567,7 +577,7 @@
     )
 
 
-def middle_back_kernel(pieces, parts, spots, *refs):
+def middle_back_kernel(pieces, parts, place, *refs):
     own_ref, base_ref, top_ref, ada_ref, out_w = refs[:5]
     others = refs[5 : 5 + parts]
     outs = refs[-3 - pieces :]
@@ -584,6 +594,7 @@
     low = out.astype(jnp.bfloat16)
     low_ref[...] = low
     weights = out_w.reshape(out_w.shape[0] * out_w.shape[2], out_w.shape[3])
+    spots = head_spots(1 - place[4], 1, pieces)
     for index, mixed_ref in enumerate(outs[3:]):
         size = mixed_ref.shape[1]
         start = pl.multiple_of(spots[index] * size, size)
@@ -681,7 +692,7 @@
     out_ref[...] = value.astype(jnp.bfloat16)
 
 
-def hidden_grads_kernel(count, more, core, *refs):
+def hidden_grads_kernel(count, more, place, *refs):
     active, upward = refs[:2]
     grads, low = refs[2 : 2 + count], refs[2 + count]
     other = refs[3 + count] if more else None
@@ -700,7 +711,7 @@
         put_sum(out_ref, other, dot_rows(low[...], upward[...]))
 
 
-def hidden_grads(core, active, upward, grads, low, other, behind):
+def hidden_grads(place, who, active, upward, grads, low, other, behind):
     total, hidden = active.shape
     half = hidden // 2
     rows, width = grads[0].shape
@@ -717,9 +728,9 @@
             num_scalar_prefetch=1,
             grid=(2 * steps,),
             in_specs=[
-                pl.BlockSpec((total, half), lambda j, s: (0, s[0])),
+                pl.BlockSpec((total, half), lambda j, s: (0, s[who])),
                 pl.BlockSpec(
-                    (total, block), lambda j, s: (0, s[0] * steps + jnp.maximum(j - steps, 0))
+                    (total, block), lambda j, s: (0, s[who] * steps + jnp.maximum(j - steps, 0))
                 ),
             ]
             + [grad] * count
@@ -732,10 +743,10 @@
         compiler_params=BIG,
         cost_estimate=cost(4 * total * half * width, 8 * total * half + 4 * width * half),
         name="hidden_grads",
-    )(core, active, upward, *grads, low, *more, *behind)
-
-
-def tail_grads_kernel(first, more, pieces, place, low, grad, attended, *refs):
+    )(place, active, upward, *grads, low, *more, *behind)
+
+
+def tail_grads_kernel(first, more, pieces, calls, place, low, grad, attended, *refs):
     mixed = refs[:pieces]
     other = refs[pieces] if more else None
     out_ref = refs[-1]
@@ -746,16 +757,17 @@
 
     @pl.when(pl.program_id(0) >= first)
     def _():
+        spots = head_spots(place[4], calls, pieces)
         for index, piece in enumerate(mixed):
             size = piece.shape[1]
-            rows = pl.ds(pl.multiple_of(place[1 + index] * size, size), size)
+            rows = pl.ds(pl.multiple_of(spots[index] * size, size), size)
             value = dot_rows(piece[...], attended[...])
             if more:
                 value = value + other[rows, :].astype(jnp.float32)
             out_ref[rows, :] = value.astype(jnp.bfloat16)
 
 
-def tail_grads(place, low_one, grad_qkv, mixed, swapped, attended_low, other, behind):
+def tail_grads(place, who, low_one, grad_qkv, mixed, swapped, attended_low, other, behind):
     total, width = low_one.shape
     rows = attended_low.shape[0]
     block = 256
@@ -764,17 +776,19 @@
     out = pl.BlockSpec((width, block), lambda j, s: (0, j))
     more = [] if other is None else [other]
     return pl.pallas_call(
-        partial(tail_grads_kernel, first, bool(more), len(mixed) + len(swapped)),
+        partial(
+            tail_grads_kernel, first, bool(more), len(mixed) + len(swapped), len(mixed)
+        ),
         grid_spec=pltpu.PrefetchScalarGridSpec(
             num_scalar_prefetch=1,
             grid=(first + second,),
             in_specs=[
                 pl.BlockSpec((total, width), lambda j, s: (0, 0)),
                 pl.BlockSpec(
-                    (total, block), lambda j, s: (0, s[0] * first + jnp.minimum(j, first - 1))
+                    (total, block), lambda j, s: (0, s[who] * first + jnp.minimum(j, first - 1))
                 ),
                 pl.BlockSpec(
-                    (rows, block), lambda j, s: (0, s[0] * second + jnp.maximum(j - first, 0))
+                    (rows, block), lambda j, s: (0, s[who] * second + jnp.maximum(j - first, 0))
                 ),
             ]
             + [pl.BlockSpec((rows, part.shape[1]), lambda j, s: (0, 0)) for part in mixed]
@@ -886,8 +900,6 @@
         self.ahead = [row[j] for j in range(self.chips)]
         self.core = row[self.chips]
         self.beside = row[self.chips + 1]
-        self.core_spot = row[self.chips : self.chips + 1]
-        self.beside_spot = row[self.chips + 1 : self.chips + 2]
         self.spots = row[self.chips + 2 :]
         self.seq = lax.axis_index("seq")
 
@@ -1054,8 +1066,9 @@
         preferred_element_type=jnp.float32,
     )
     ada_part = quarters(ada_part[:, : 2 * width], ada_part[:, 2 * width :])
-    seq_place = jnp.reshape(mover.seq, (1,)).astype(jnp.int32)
-    mine = pack_columns(w_query, w_key, w_value, held, seq_place)
+    prompt_at = mover.seq if mover.pair else jnp.zeros((), jnp.int32)
+    place = jnp.stack([prompt_at, prompt_len[0], mover.core, mover.beside, mover.seq])
+    mine = pack_columns(w_query, w_key, w_value, held, place)
     early = [mover.across(tokens)] if mover.pair else []
     blocks, ada_sum, early, late = mover.gather_items(
         mine, ada_part, early, late
@@ -1081,29 +1094,20 @@
     ada_two = ada[2:]
 
     if mover.pair:
-        prompt_at = mover.seq
         tokens_other, grad_sent = tie(early[0], grad_low)
         grad_other = mover.across(grad_sent)
         frames = [tokens, tokens_other]
         grads = [grad_low, grad_other]
         calls = 2 if pairs % 2 == 0 else 1
-        own_spots = [mover.seq * calls + call for call in range(calls)]
-        far_spots = [(1 - mover.seq) * calls + call for call in range(calls)]
-        spots = jnp.stack(own_spots + far_spots)
-        other_spots = jnp.stack([1 - mover.seq, mover.seq])
     else:
-        prompt_at = jnp.zeros((), jnp.int32)
         frames = [lax.all_gather(tokens, "seq", axis=0, tiled=True)]
         grads = [lax.all_gather(grad_low, "seq", axis=0, tiled=True)]
         calls = 1
-        spots = other_spots = jnp.zeros((1,), jnp.int32)
     low_one, qkv, qkv_w = first_layer(frames, ada_one, blocks, mover.spots)
-    length = prompt_len[0]
     per_call = pairs // calls
     mixed_heads = []
     lse = []
     for call in range(calls):
-        place = jnp.stack([prompt_at, length]).astype(jnp.int32)
         behind = grads[1:] + mixed_heads
         out = attend(qkv, place, call * per_call, per_call, behind)
         mixed_heads.append(out[0])
@@ -1116,7 +1120,7 @@
                 sent, mixed_far[-1] = tie(sent, mixed_far[-1])
             mixed_far.append(mover.across(sent))
         attended, low_two = second_layer(
-            mixed_heads, mixed_far, frames[::-1], out_w, out_part, ada_two, spots
+            mixed_heads, mixed_far, frames[::-1], out_w, out_part, ada_two, place
         )
         lows = low_two
         active, upward = hidden_layer(lows, grads, weights)
@@ -1128,7 +1132,7 @@
     else:
         mixed = lax.all_to_all(mixed_heads[0], "seq", split_axis=0, concat_axis=1, tiled=True)
         attended, low_two = second_layer(
-            [mixed], [], [tokens], out_w, out_part, ada_two, spots
+            [mixed], [], [tokens], out_w, out_part, ada_two, place
         )
         lows = lax.all_gather(low_two, "seq", axis=0, tiled=True)
         active, upward = hidden_layer(lows, grads, weights)
@@ -1138,9 +1142,9 @@
     down_columns = hidden // 2
 
     def hidden_parts(own, other, behind):
-        spot = mover.core_spot if own else mover.beside_spot
+        who = 2 if own else 3
         if down_columns == width:
-            return hidden_grads(spot, active, upward, grads, lows, other, behind)
+            return hidden_grads(place, who, active, upward, grads, lows, other, behind)
         core = mover.core if own else mover.beside
         first, second = parted(other, down_columns)
         down = dot_rows(halves(active, core), grads[0]).reshape(width, down_columns)
@@ -1170,7 +1174,7 @@
         ada_two,
         out_w,
         out_part,
-        other_spots,
+        place,
         sizes,
         [ring.whole],
     )
@@ -1190,10 +1194,10 @@
     split = pairs // 2 if pairs % 2 == 0 else 0
 
     def tail_parts(own, other, behind):
-        spot = mover.core_spot if own else mover.beside_spot
         if mover.pair:
             return tail_grads(
-                jnp.concatenate([spot, spots.astype(jnp.int32)]),
+                place,
+                2 if own else 3,
                 low_one,
                 grad_qkv,
                 mixed_heads,
@@ -1213,9 +1217,9 @@
     for turn in range(pairs):
         behind = filler
         filler = []
-        pair = (mover.beside * split + turn) & (pairs - 1)
-        place = jnp.stack([prompt_at, length, pair, per_call]).astype(jnp.int32)
-        grad_qkv = attend_back(place, qkv, mixed_heads, grad_heads, lse, grad_qkv, behind)
+        grad_qkv = attend_back(
+            place, turn, pairs, qkv, mixed_heads, grad_heads, lse, grad_qkv, behind
+        )
         grad_qkv = ring.advance(grad_qkv)
         if turn + 1 == split:
             tail = RingSum(mover, tail_parts, [])

time: 437 us -> 436 us (level)
  transfers between devices with their start and end apart: 49 -> 49, of which waited for: 19 -> 20; matrix products, arithmetic and copies ran while one was open for 14% -> 12% of each run, Pallas kernels for 41% -> 41%
where the time goes in v4:
time: 436 us; the launch traced here: 431 us
  Pallas kernels  222 us (51%)
  waiting for transfers between devices  79 us (18%)
  starting transfers between devices  43.5 us (10%)
  other arithmetic  35.6 us (8%)
  local copies, waits for them, and re-layouts  30.6 us (7%)
  between operations  17.1 us (4%)
    pallas_call x4, Pallas kernels, attend_back(): pl.pallas_call(partial(attend_back_kernel, parts, calls, per, at), grid_s...  47.7 us
    ppermute x14, waiting for transfers between devices, across(): return lax.ppermute(value, 'seq', [(0, 1), (1, 0)])  32.6 us
    pallas_call x2, Pallas kernels, attend(): pl.pallas_call(attend_kernel, grid_spec=pltpu.PrefetchScalarGridSpec(num_...  31.6 us
    pallas_call x4, Pallas kernels, hidden_to_width(): pl.pallas_call(kernel, grid=(weights.steps,), in_specs=[pl.BlockSpec((row...  30.5 us
    pallas_call x2, Pallas kernels, hidden_grads(): pl.pallas_call(partial(hidden_grads_kernel, count, bool(more)), grid_spec...  25.3 us
    pallas_call x1, Pallas kernels, hidden_layer(): pl.pallas_call(partial(hidden_kernel, weights.per_chip, len(grads)), grid...  18.5 us
    pallas_call x2, Pallas kernels, tail_grads(): pl.pallas_call(partial(tail_grads_kernel, first, bool(more), len(mixed) +...  18.4 us
    ppermute x4, waiting for transfers between devices, gather_items(): moved = lax.ppermute(direct[-1], 'items', self.both_ways)  17.6 us
  transfers between devices with their start and end apart: 49, of which 20 were waited for; matrix products, arithmetic and copies ran while one was open for 12% of the time, Pallas kernels for 41%

profile of v4, /device:TPU:0, one launch (start us, length us, event | category | flops | bytes accessed | tf_op | source)
XLA Modules:
  0.0 431.1 jit_solution(3899861607617345842)
XLA Ops:
  11.3 2.3 pack_columns.1
  15.5 2.9 collective-permute-start.7
  25.6 6.3 %collective-permute-done.1 = f32[4,8,1024]{2,1,0:T(8,128)} collective-permute-done((f32[4,8,1024]{2,1,0:T(8,128)}, f32[4,8,1024]{2,1,0:T(8,128)}, u32[]{:S(2)}, u32[]{:S(2)}) %collective-permute-start.1) | collective-permute-done | bytes 131104 | tf_op jit(solution)/shard_map/ppermute | solution.py:908
  36.0 3.4 collective-permute-done.2
  42.1 5.4 %collective-permute-done.3 = f32[4,8,1024]{2,1,0:T(8,128)S(1)} collective-permute-done((f32[4,8,1024]{2,1,0:T(8,128)S(1)}, f32[4,8,1024]{2,1,0:T(8,128)S(1)}, u32[]{:S(2)}, u32[]{:S(2)}) %collective-permute-start.3) | collective-permute-done | bytes 131104 | tf_op jit(solution)/shard_map/ppermute | solution.py:908
  53.8 4.7 %collective-permute-done.8.refs_6_ = bf16[128,1536]{1,0:T(8,128)(2,1)S(1)} collective-permute-done((bf16[128,1536]{1,0:T(8,128)(2,1)}, bf16[128,1536]{1,0:T(8,128)(2,1)S(1)}, u32[]{:S(2)}, u32[]{:S(2)}) %collective-permute-start.8) | collective-permute-done | bytes 393248 | tf_op jit(solution)/shard_map/ppermute | solution.py:924
  60.8 12.9 %collective-permute-done.9.refs_7_ = bf16[128,1536]{1,0:T(8,128)(2,1)S(1)} collective-permute-done((bf16[128,1536]{1,0:T(8,128)(2,1)S(1)}, bf16[128,1536]{1,0:T(8,128)(2,1)S(1)}, u32[]{:S(2)}, u32[]{:S(2)}) %collective-permute-start.9) | collective-permute-done | bytes 393248 | tf_op jit(solution)/shard_map/ppermute | solution.py:924
  75.3 11.3 %first_layer.1 = (bf16[1280,1024]{1,0:T(8,128)(2,1)}, bf16[1280,1536]{1,0:T(8,128)(2,1)}, bf16[1024,1536]{1,0:T(8,128)(2,1)}) custom-call(s32[8]{0:T(128)} %slice_bitcast_fusion.8.spots, bf16[640,1024]{1,0:T(8,128)(2,1)} %bitcast.144, bf16[640,1024]{1,0:T(8,128)(2,1)} %copy-done.9, f32[2,1024]{1,0:T(2,128)} %get-tuple-element.184.refs_2_.ada_ref, ...), custom_call_target="tpu_custom_call" | custom-call | flops 2013265920 | bytes 8388608 | tf_op jit(solution)/shard_map/first_layer/pallas_call | solution.py:347
  87.7 15.8 %attend.2 = (bf16[1280,256]{1,0:T(8,128)(2,1)}, f32[2,10,256]{2,1,0:T(8,128)}) custom-call(s32[5]{0:T(128)} %stack.41.place, bf16[1280,1536]{1,0:T(8,128)(2,1)} %get-tuple-element.69.q_ref.k_ref.v_ref, bf16[1280,1536]{1,0:T(8,128)(2,1)} %get-tuple-element.69.q_ref.k_ref.v_ref, bf16[1280,1536]{1,0:T(8,128)(2,1)} %get-tuple-element.69.q_ref.k_ref.v_ref, ...), custom_call_target="tpu_custom_call" | custom-call | flops 2516582400 | bytes 2621440 | tf_op jit(solution)/shard_map/attend/pallas_call | solution.py:91
  103.9 15.8 %attend.3 = (bf16[1280,256]{1,0:T(8,128)(2,1)}, f32[2,10,256]{2,1,0:T(8,128)}) custom-call(s32[5]{0:T(128)} %stack.41.place, bf16[1280,1536]{1,0:T(8,128)(2,1)} %get-tuple-element.69.q_ref.k_ref.v_ref, bf16[1280,1536]{1,0:T(8,128)(2,1)} %get-tuple-element.69.q_ref.k_ref.v_ref, bf16[1280,1536]{1,0:T(8,128)(2,1)} %get-tuple-element.69.q_ref.k_ref.v_ref, ...), custom_call_target="tpu_custom_call" | custom-call | flops 2516582400 | bytes 2621440 | tf_op jit(solution)/shard_map/attend/pallas_call | solution.py:91
  121.6 16.7 %collective-permute-done.15.refs_3_ = bf16[1280,256]{1,0:T(8,128)(2,1)S(1)} collective-permute-done((bf16[1280,256]{1,0:T(8,128)(2,1)}, bf16[1280,256]{1,0:T(8,128)(2,1)S(1)}, u32[]{:S(2)}, u32[]{:S(2)}) %collective-permute-start.15) | collective-permute-done | bytes 655392 | tf_op jit(solution)/shard_map/ppermute | solution.py:911
  138.3 3.2 all-gather.3.cloned.1.call-done
  141.5 9.3 %second_layer.1 = (f32[640,1024]{1,0:T(8,128)}, bf16[1280,1024]{1,0:T(8,128)(2,1)}) custom-call(s32[5]{0:T(128)} %stack.41.place, bf16[1280,256]{1,0:T(8,128)(2,1)} %get-tuple-element.71.refs_1_.refs_0_, bf16[1280,256]{1,0:T(8,128)(2,1)} %get-tuple-element.74.refs_1_, bf16[1280,256]{1,0:T(8,128)(2,1)} %copy-done.6, bf16[1280,256]{1,0:T(8,128)(2,1)} %copy-done.7, ...), custom_call_target="tpu_custom_call" | custom-call | flops 1342177280 | bytes 7602176 | tf_op jit(solution)/shard_map/second_layer/pallas_call | solution.py:401
  150.8 18.5 %hidden_layer.1 = (bf16[1280,2048]{1,0:T(8,128)(2,1)}, bf16[1280,2048]{1,0:T(8,128)(2,1)}) custom-call(bf16[1280,1024]{1,0:T(8,128)(2,1)} %get-tuple-element.77.x_ref.refs_4_, bf16[16,5,64,1024]{3,2,1,0:T(8,128)(2,1)} %bitcast.121, bf16[8,2,5,64,1024]{4,3,2,1,0:T(8,128)(2,1)} %bitcast.122, bf16[640,1024]{1,0:T(8,128)(2,1)} %bitcast.138, ...), custom_call_target="tpu_custom_call" | custom-call | flops 5368709120 | bytes 12058624 | tf_op jit(solution)/shard_map/hidden_layer/pallas_call | solution.py:484
  169.3 7.4 %up_back.2.refs_5_ = bf16[640,1024]{1,0:T(8,128)(2,1)} custom-call(bf16[1280,2048]{1,0:T(8,128)(2,1)} %get-tuple-element.79.g_ref.refs_1_, bf16[16,5,64,1024]{3,2,1,0:T(8,128)(2,1)} %bitcast.123), custom_call_target="tpu_custom_call" | custom-call | flops 1342177280 | bytes 4718592 | tf_op jit(solution)/shard_map/up_back/pallas_call | solution.py:533
  179.7 12.4 %hidden_grads.2.refs_0_ = bf16[1024,2048]{1,0:T(8,128)(2,1)} custom-call(s32[5]{0:T(128)} %stack.41.place, bf16[1280,2048]{1,0:T(8,128)(2,1)} %get-tuple-element.78.refs_0_.a_ref, bf16[1280,2048]{1,0:T(8,128)(2,1)} %get-tuple-element.79.g_ref.refs_1_, bf16[640,1024]{1,0:T(8,128)(2,1)} %bitcast.139, bf16[640,1024]{1,0:T(8,128)(2,1)} %copy-done.2, ...), custom_call_target="tpu_custom_call" | custom-call | flops 2684354560 | bytes 7340032 | tf_op jit(solution)/shard_map/hidden_grads/pallas_call | solution.py:725
  192.1 3.0 collective-permute-done.16.refs_5_
  196.6 7.9 %up_back.3.refs_6_.refs_0_ = f32[640,1024]{1,0:T(8,128)} custom-call(bf16[1280,2048]{1,0:T(8,128)(2,1)} %get-tuple-element.79.g_ref.refs_1_, bf16[16,5,64,1024]{3,2,1,0:T(8,128)(2,1)} %bitcast.124, bf16[1024,2048]{1,0:T(8,128)(2,1)} %hidden_grads.2.refs_0_), custom_call_target="tpu_custom_call" | custom-call | flops 1342177280 | bytes 4718592 | tf_op jit(solution)/shard_map/up_back/pallas_call | solution.py:533
  204.5 12.9 %hidden_grads.3.refs_7_ = bf16[1024,2048]{1,0:T(8,128)(2,1)} custom-call(s32[5]{0:T(128)} %stack.41.place, bf16[1280,2048]{1,0:T(8,128)(2,1)} %get-tuple-element.78.refs_0_.a_ref, bf16[1280,2048]{1,0:T(8,128)(2,1)} %get-tuple-element.79.g_ref.refs_1_, bf16[640,1024]{1,0:T(8,128)(2,1)} %bitcast.140, bf16[640,1024]{1,0:T(8,128)(2,1)} %copy-done.2, ...), custom_call_target="tpu_custom_call" | custom-call | flops 2684354560 | bytes 7340032 | tf_op jit(solution)/shard_map/hidden_grads/pallas_call | solution.py:725
  217.4 2.7 dynamic-slice_bitcast_fusion
  223.0 8.9 %middle_back.1 = (f32[640,1024]{1,0:T(8,128)}, bf16[640,1024]{1,0:T(8,128)(2,1)}, f32[2,1024]{1,0:T(2,128)}, bf16[640,512]{1,0:T(8,128)(2,1)}, bf16[640,512]{1,0:T(8,128)(2,1)}) custom-call(s32[5]{0:T(128)} %stack.41.place, f32[640,1024]{1,0:T(8,128)} %up_back.3.refs_6_.refs_0_, f32[640,1024]{1,0:T(8,128)} %get-tuple-element.76.refs_1_, ...), custom_call_target="tpu_custom_call" | custom-call | flops 671088640 | bytes 7602176 | tf_op jit(solution)/shard_map/middle_back/pallas_call | solution.py:611
  232.5 7.3 %down_part.2.refs_0_ = bf16[640,1024]{1,0:T(8,128)(2,1)} custom-call(bf16[1280,2048]{1,0:T(8,128)(2,1)} %get-tuple-element.78.refs_0_.a_ref, bf16[8,2,5,64,1024]{4,3,2,1,0:T(8,128)(2,1)} %bitcast.126, bf16[640,512]{1,0:T(8,128)(2,1)} %get-tuple-element.83.refs_0_), custom_call_target="tpu_custom_call" | custom-call | flops 1342177280 | bytes 4718592 | tf_op jit(solution)/shard_map/down_part/pallas_call | solution.py:533
  239.8 2.6 bitcast_add_fusion.1
  244.5 7.8 %down_part.3.refs_6_ = f32[640,1024]{1,0:T(8,128)} custom-call(bf16[1280,2048]{1,0:T(8,128)(2,1)} %get-tuple-element.78.refs_0_.a_ref, bf16[8,2,5,64,1024]{4,3,2,1,0:T(8,128)(2,1)} %bitcast.127, bf16[640,1024]{1,0:T(8,128)(2,1)} %down_part.2.refs_0_), custom_call_target="tpu_custom_call" | custom-call | flops 1342177280 | bytes 4718592 | tf_op jit(solution)/shard_map/down_part/pallas_call | solution.py:533
  253.2 11.7 %attend_back.4.refs_6_ = bf16[1280,1536]{1,0:T(8,128)(2,1)} custom-call(s32[5]{0:T(128)} %stack.41.place, bf16[1280,1536]{1,0:T(8,128)(2,1)} %get-tuple-element.69.q_ref.k_ref.v_ref, bf16[1280,1536]{1,0:T(8,128)(2,1)} %get-tuple-element.69.q_ref.k_ref.v_ref, bf16[1280,1536]{1,0:T(8,128)(2,1)} %get-tuple-element.69.q_ref.k_ref.v_ref, ...), custom_call_target="tpu_custom_call" | custom-call | flops 3145728000 | bytes 3276800 | tf_op jit(solution)/shard_map/attend_back/pallas_call | solution.py:204
  265.0 2.5 bitcast_add_fusion
  269.6 12.3 %attend_back.5.grad.refs_6_ = bf16[1280,1536]{1,0:T(8,128)(2,1)} custom-call(s32[5]{0:T(128)} %stack.41.place, bf16[1280,1536]{1,0:T(8,128)(2,1)} %get-tuple-element.69.q_ref.k_ref.v_ref, bf16[1280,1536]{1,0:T(8,128)(2,1)} %get-tuple-element.69.q_ref.k_ref.v_ref, ...), custom_call_target="tpu_custom_call", output_to_operand_aliasing={{}: (10, {})} | custom-call | flops 3145728000 | bytes 3276800 | tf_op jit(solution)/shard_map/attend_back/pallas_call | solution.py:204
  281.9 9.0 %tail_grads.2.refs_7_ = bf16[1024,1280]{1,0:T(8,128)(2,1)} custom-call(s32[5]{0:T(128)} %stack.41.place, bf16[1280,1024]{1,0:T(8,128)(2,1)} %get-tuple-element.85.low, bf16[1280,1536]{1,0:T(8,128)(2,1)} %attend_back.5.grad.refs_6_, bf16[640,1024]{1,0:T(8,128)(2,1)} %get-tuple-element.96.attended, bf16[1280,256]{1,0:T(8,128)(2,1)} %get-tuple-element.71.refs_1_.refs_0_, ...), custom_call_target="tpu_custom_call" | custom-call | flops 1342177280 | bytes 5242880 | tf_op jit(solution)/shard_map/tail_grads/pallas_call | solution.py:778
  295.3 11.8 %attend_back.6.refs_6_ = bf16[1280,1536]{1,0:T(8,128)(2,1)} custom-call(s32[5]{0:T(128)} %stack.41.place, bf16[1280,1536]{1,0:T(8,128)(2,1)} %get-tuple-element.69.q_ref.k_ref.v_ref, bf16[1280,1536]{1,0:T(8,128)(2,1)} %get-tuple-element.69.q_ref.k_ref.v_ref, bf16[1280,1536]{1,0:T(8,128)(2,1)} %get-tuple-element.69.q_ref.k_ref.v_ref, ...), custom_call_target="tpu_custom_call", output_to_operand_aliasing={{}: (10, {})} | custom-call | flops 3145728000 | bytes 3276800 | tf_op jit(solution)/shard_map/attend_back/pallas_call | solution.py:204
  307.1 11.9 %attend_back.7.grad.grad_ref = bf16[1280,1536]{1,0:T(8,128)(2,1)} custom-call(s32[5]{0:T(128)} %stack.41.place, bf16[1280,1536]{1,0:T(8,128)(2,1)} %get-tuple-element.69.q_ref.k_ref.v_ref, bf16[1280,1536]{1,0:T(8,128)(2,1)} %get-tuple-element.69.q_ref.k_ref.v_ref, ...), custom_call_target="tpu_custom_call", output_to_operand_aliasing={{}: (10, {})} | custom-call | flops 3145728000 | bytes 3276800 | tf_op jit(solution)/shard_map/attend_back/pallas_call | solution.py:204
  319.0 2.0 fusion.1
  322.6 9.4 %tail_grads.3.refs_0_ = bf16[1024,1280]{1,0:T(8,128)(2,1)} custom-call(s32[5]{0:T(128)} %stack.41.place, bf16[1280,1024]{1,0:T(8,128)(2,1)} %get-tuple-element.85.low, bf16[1280,1536]{1,0:T(8,128)(2,1)} %attend_back.7.grad.grad_ref, bf16[640,1024]{1,0:T(8,128)(2,1)} %get-tuple-element.96.attended, bf16[1280,256]{1,0:T(8,128)(2,1)} %get-tuple-element.71.refs_1_.refs_0_, ...), custom_call_target="tpu_custom_call" | custom-call | flops 1342177280 | bytes 5242880 | tf_op jit(solution)/shard_map/tail_grads/pallas_call | solution.py:778
  332.0 3.3 dynamic-slice_bitcast_fusion.3
  339.0 5.9 %first_back.2 = (bf16[640,1024]{1,0:T(8,128)(2,1)}, f32[2,1024]{1,0:T(2,128)}) custom-call(bf16[1280,1536]{1,0:T(8,128)(2,1)} %attend_back.7.grad.grad_ref, bf16[1024,1536]{1,0:T(8,128)(2,1)} %get-tuple-element.98.weight_ref, bf16[640,1024]{1,0:T(8,128)(2,1)} %copy-done.9, bf16[1024,1280]{1,0:T(8,128)(2,1)} %tail_grads.3.refs_0_), custom_call_target="tpu_custom_call" | custom-call | flops 1006632960 | bytes 3866624 | tf_op jit(solution)/shard_map/first_back/pallas_call | solution.py:653
  347.0 2.5 fusion.31
  350.0 3.4 bitcast_add_fusion.8
  355.4 6.3 %first_back.3 = (bf16[640,1024]{1,0:T(8,128)(2,1)}, f32[2,1024]{1,0:T(2,128)}) custom-call(bf16[1280,1536]{1,0:T(8,128)(2,1)} %attend_back.7.grad.grad_ref, bf16[1024,1536]{1,0:T(8,128)(2,1)} %get-tuple-element.98.weight_ref, bf16[640,1024]{1,0:T(8,128)(2,1)} %bitcast.146, bf16[640,1024]{1,0:T(8,128)(2,1)} %get-tuple-element.102.refs_0_), custom_call_target="tpu_custom_call" | custom-call | flops 1006632960 | bytes 3866624 | tf_op jit(solution)/shard_map/first_back/pallas_call | solution.py:653
  364.7 2.3 collective-permute-done.33
  368.6 3.1 collective-permute-done.45
  373.2 3.4 bitcast_add_fusion.6
  379.8 2.3 reshape.101
  382.2 2.7 collective-permute-done.36
  386.8 3.9 fusion
  396.8 2.4 collective-permute-done.47
  400.4 2.2 collective-permute-done.40
  407.8 5.8 %input_back.1 = f32[640,1024]{1,0:T(8,128)} custom-call(bf16[640,1024]{1,0:T(8,128)(2,1)} %get-tuple-element.107.own_ref, bf16[640,1024]{1,0:T(8,128)(2,1)} %bitcast.147, f32[2,1024]{1,0:T(2,128)} %get-tuple-element.184.refs_2_.ada_ref, f32[640,1024]{1,0:T(8,128)} %get-tuple-element.108.base_ref, bf16[320,1024]{1,0:T(8,128)(2,1)} %collective-permute-done.32.refs_0_, ...), custom_call_target="tpu_custom_call" | custom-call | flops 6553600 | bytes 4587520 | tf_op jit(solution)/shard_map/input_back/pallas_call | solution.py:824
  416.6 2.8 collective-permute-done.43
  420.0 3.1 collective-permute-done.42
  (232 shorter events, 86.3 us)
Async XLA Ops:
  7.2 134.3 %all-gather.3.cloned.1.call-start = ((), (), s32[]{:S(2)}) async-start(), calls=%async_computation | async-start | bytes 11141120 | tf_op jit(solution)/shard_map/all_gather | solution.py:1078
  13.6 5.6 %collective-permute-start.4 = (bf16[64,1536]{1,0:T(8,128)(2,1)}, bf16[64,1536]{1,0:T(8,128)(2,1)S(1)}, u32[]{:S(2)}, u32[]{:S(2)}) collective-permute-start(bf16[64,1536]{1,0:T(8,128)(2,1)} %pack_columns.1), channel_id=1, source_target_pairs={{0,2},{2,0},{4,6},{6,4},{8,10},{10,8},{12,14},{14,12},{16,18},{18,... | collective-permute-start | bytes 589832 | tf_op jit(solution)/shard_map/ppermute | solution.py:908
  15.4 7.2 %collective-permute-start = (f32[4,8,1024]{2,1,0:T(8,128)S(1)}, f32[4,8,1024]{2,1,0:T(8,128)S(1)}, u32[]{:S(2)}, u32[]{:S(2)}) collective-permute-start(f32[4,8,1024]{2,1,0:T(8,128)S(1)} %pad_maximum_fusion.3), channel_id=1, source_target_pairs={{0,2},{2,0},{4,6},{6,4},{8,10},{10,8},{12,14},{14,12},{16,18},{18,... | collective-permute-start | bytes 393224 | tf_op jit(solution)/shard_map/ppermute | solution.py:908
  15.5 32.2 %collective-permute-start.7 = (bf16[640,1024]{1,0:T(8,128)(2,1)}, bf16[640,1024]{1,0:T(8,128)(2,1)S(1)}, u32[]{:S(2)}, u32[]{:S(2)}) collective-permute-start(bf16[640,1024]{1,0:T(8,128)(2,1)} %bitcast.143), channel_id=1, source_target_pairs={{0,1},{1,0},{2,3},{3,2},{4,5},{5,4},{6,7},{7,6},{8,9},{9,8},{10,11... | collective-permute-start | bytes 3932168 | tf_op jit(solution)/shard_map/ppermute | solution.py:911
  21.0 12.0 %collective-permute-start.5 = (bf16[128,1536]{1,0:T(8,128)(2,1)}, bf16[128,1536]{1,0:T(8,128)(2,1)}, u32[]{:S(2)}, u32[]{:S(2)}) collective-permute-start(bf16[128,1536]{1,0:T(8,128)(2,1)} %maximum_select_fusion.refs_3_), channel_id=1, source_target_pairs={{0,8},{8,16},{16,24},{24,28},{28,20},{20,12},{12,4},{4,0},{10,2},{... | collective-permute-start | bytes 1179656 | tf_op jit(solution)/shard_map/ppermute | solution.py:924
  23.3 8.6 %collective-permute-start.1 = (f32[4,8,1024]{2,1,0:T(8,128)}, f32[4,8,1024]{2,1,0:T(8,128)}, u32[]{:S(2)}, u32[]{:S(2)}) collective-permute-start(f32[4,8,1024]{2,1,0:T(8,128)} %fusion.30), channel_id=1, source_target_pairs={{0,4},{2,6},{4,0},{6,2},{8,12},{10,14},{12,8},{14,10},{16,20},{18,... | collective-permute-start | bytes 393224 | tf_op jit(solution)/shard_map/ppermute | solution.py:908
  32.9 6.5 %collective-permute-start.2 = (f32[4,8,1024]{2,1,0:T(8,128)S(1)}, f32[4,8,1024]{2,1,0:T(8,128)S(1)}, u32[]{:S(2)}, u32[]{:S(2)}) collective-permute-start(f32[4,8,1024]{2,1,0:T(8,128)S(1)} %fusion.38), channel_id=1, source_target_pairs={{0,8},{2,10},{4,12},{6,14},{8,0},{10,2},{12,4},{14,6},{16,24},{18,... | collective-permute-start | bytes 393224 | tf_op jit(solution)/shard_map/ppermute | solution.py:908
  33.0 14.5 %collective-permute-start.6 = (bf16[128,1536]{1,0:T(8,128)(2,1)}, bf16[128,1536]{1,0:T(8,128)(2,1)}, u32[]{:S(2)}, u32[]{:S(2)}) collective-permute-start(bf16[128,1536]{1,0:T(8,128)(2,1)} %collective-permute-done.5.refs_4_), channel_id=1, source_target_pairs={{0,8},{8,16},{16,24},{24,28},{28,20},{20,12},{12,4},{4,0},{10,2},{... | collective-permute-start | bytes 1179656 | tf_op jit(solution)/shard_map/ppermute | solution.py:924
  39.4 8.1 %collective-permute-start.3 = (f32[4,8,1024]{2,1,0:T(8,128)S(1)}, f32[4,8,1024]{2,1,0:T(8,128)S(1)}, u32[]{:S(2)}, u32[]{:S(2)}) collective-permute-start(f32[4,8,1024]{2,1,0:T(8,128)S(1)} %add.86), channel_id=1, source_target_pairs={{0,16},{2,18},{4,20},{6,22},{8,24},{10,26},{12,28},{14,30},{16,0},... | collective-permute-start | bytes 393224 | tf_op jit(solution)/shard_map/ppermute | solution.py:908
  48.8 37.9 %collective-permute-start.13 = (bf16[640,1024]{1,0:T(8,128)(2,1)S(1)}, bf16[640,1024]{1,0:T(8,128)(2,1)S(1)}, u32[]{:S(2)}, u32[]{:S(2)}) collective-permute-start(bf16[640,1024]{1,0:T(8,128)(2,1)S(1)} %bitcast.142), channel_id=1, source_target_pairs={{0,1},{1,0},{2,3},{3,2},{4,5},{5,4},{6,7},{7,6},{8,9},{9,8},{10,11... | collective-permute-start | bytes 3932168 | tf_op jit(solution)/shard_map/ppermute | solution.py:911
  50.5 8.0 %collective-permute-start.8 = (bf16[128,1536]{1,0:T(8,128)(2,1)}, bf16[128,1536]{1,0:T(8,128)(2,1)S(1)}, u32[]{:S(2)}, u32[]{:S(2)}) collective-permute-start(bf16[128,1536]{1,0:T(8,128)(2,1)} %collective-permute-done.6.refs_5_), channel_id=1, source_target_pairs={{0,8},{8,16},{16,24},{24,28},{28,20},{20,12},{12,4},{4,0},{10,2},{... | collective-permute-start | bytes 1179656 | tf_op jit(solution)/shard_map/ppermute | solution.py:924
  53.3 7.5 %collective-permute-start.10 = (bf16[128,1536]{1,0:T(8,128)(2,1)}, bf16[128,1536]{1,0:T(8,128)(2,1)S(1)}, u32[]{:S(2)}, u32[]{:S(2)}) collective-permute-start(bf16[128,1536]{1,0:T(8,128)(2,1)} %collective-permute-done.5.refs_4_), channel_id=1, source_target_pairs={{0,2},{2,0},{4,6},{6,4},{8,10},{10,8},{12,14},{14,12},{16,18},{18,... | collective-permute-start | bytes 1179656 | tf_op jit(solution)/shard_map/ppermute | solution.py:908
  53.3 7.5 %collective-permute-start.11 = (bf16[128,1536]{1,0:T(8,128)(2,1)}, bf16[128,1536]{1,0:T(8,128)(2,1)S(1)}, u32[]{:S(2)}, u32[]{:S(2)}) collective-permute-start(bf16[128,1536]{1,0:T(8,128)(2,1)} %collective-permute-done.6.refs_5_), channel_id=1, source_target_pairs={{0,2},{2,0},{4,6},{6,4},{8,10},{10,8},{12,14},{14,12},{16,18},{18,... | collective-permute-start | bytes 1179656 | tf_op jit(solution)/shard_map/ppermute | solution.py:908
  58.5 15.3 %collective-permute-start.9 = (bf16[128,1536]{1,0:T(8,128)(2,1)S(1)}, bf16[128,1536]{1,0:T(8,128)(2,1)S(1)}, u32[]{:S(2)}, u32[]{:S(2)}) collective-permute-start(bf16[128,1536]{1,0:T(8,128)(2,1)S(1)} %collective-permute-done.8.refs_6_), channel_id=1, source_target_pairs={{0,8},{8,16},{16,24},{24,28},{28,20},{20,12},{12,4},{4,0},{10,2},{... | collective-permute-start | bytes 1179656 | tf_op jit(solution)/shard_map/ppermute | solution.py:924
  60.1 13.7 %collective-permute-start.12 = (bf16[128,1536]{1,0:T(8,128)(2,1)S(1)}, bf16[128,1536]{1,0:T(8,128)(2,1)S(1)}, u32[]{:S(2)}, u32[]{:S(2)}) collective-permute-start(bf16[128,1536]{1,0:T(8,128)(2,1)S(1)} %collective-permute-done.8.refs_6_), channel_id=1, source_target_pairs={{0,2},{2,0},{4,6},{6,4},{8,10},{10,8},{12,14},{14,12},{16,18},{18,... | collective-permute-start | bytes 1179656 | tf_op jit(solution)/shard_map/ppermute | solution.py:908
  103.5 17.8 %collective-permute-start.14 = (bf16[1280,256]{1,0:T(8,128)(2,1)}, bf16[1280,256]{1,0:T(8,128)(2,1)S(1)}, u32[]{:S(2)}, u32[]{:S(2)}) collective-permute-start(bf16[1280,256]{1,0:T(8,128)(2,1)} %get-tuple-element.71.refs_1_.refs_0_), channel_id=1, source_target_pairs={{0,1},{1,0},{2,3},{3,2},{4,5},{5,4},{6,7},{7,6},{8,9},{9,8},{10,11... | collective-permute-start | bytes 1966088 | tf_op jit(solution)/shard_map/ppermute | solution.py:911
  121.3 17.0 %collective-permute-start.15 = (bf16[1280,256]{1,0:T(8,128)(2,1)}, bf16[1280,256]{1,0:T(8,128)(2,1)S(1)}, u32[]{:S(2)}, u32[]{:S(2)}) collective-permute-start(bf16[1280,256]{1,0:T(8,128)(2,1)} %get-tuple-element.74.refs_1_), channel_id=1, source_target_pairs={{0,1},{1,0},{2,3},{3,2},{4,5},{5,4},{6,7},{7,6},{8,9},{9,8},{10,11... | collective-permute-start | bytes 1966088 | tf_op jit(solution)/shard_map/ppermute | solution.py:911
  178.1 17.0 %collective-permute-start.16 = (bf16[320,1024]{1,0:T(8,128)(2,1)S(1)}, bf16[320,1024]{1,0:T(8,128)(2,1)S(1)}, u32[]{:S(2)}, u32[]{:S(2)}) collective-permute-start(bf16[320,1024]{1,0:T(8,128)(2,1)S(1)} %get-tuple-element.134), channel_id=1, source_target_pairs={{0,1},{1,0},{2,3},{3,2},{4,5},{5,4},{6,7},{7,6},{8,9},{9,8},{10,11... | collective-permute-start | bytes 1966088 | tf_op jit(solution)/shard_map/ppermute | solution.py:911
  195.1 9.4 %collective-permute-start.17 = (bf16[1024,2048]{1,0:T(8,128)(2,1)}, bf16[1024,2048]{1,0:T(8,128)(2,1)}, u32[]{:S(2)}, u32[]{:S(2)}) collective-permute-start(bf16[1024,2048]{1,0:T(8,128)(2,1)} %hidden_grads.2.refs_0_), channel_id=1, source_target_pairs={{0,2},{2,0},{4,6},{6,4},{8,10},{10,8},{12,14},{14,12},{16,18},{18,... | collective-permute-start | bytes 12582920 | tf_op jit(solution)/shard_map/ppermute | solution.py:908
  195.1 27.0 %collective-permute-start.20 = (bf16[320,1024]{1,0:T(8,128)(2,1)S(1)}, bf16[320,1024]{1,0:T(8,128)(2,1)S(1)}, u32[]{:S(2)}, u32[]{:S(2)}) collective-permute-start(bf16[320,1024]{1,0:T(8,128)(2,1)S(1)} %get-tuple-element.82), channel_id=1, source_target_pairs={{0,1},{1,0},{2,3},{3,2},{4,5},{5,4},{6,7},{7,6},{8,9},{9,8},{10,11... | collective-permute-start | bytes 1966088 | tf_op jit(solution)/shard_map/ppermute | solution.py:911
  220.0 19.8 %collective-permute-start.18 = (bf16[128,2048]{1,0:T(8,128)(2,1)S(1)}, bf16[128,2048]{1,0:T(8,128)(2,1)S(1)}, u32[]{:S(2)}, u32[]{:S(2)}) collective-permute-start(bf16[128,2048]{1,0:T(8,128)(2,1)S(1)} %get-tuple-element.124), channel_id=1, source_target_pairs={{0,8},{2,10},{8,16},{10,18},{16,24},{18,26},{24,28},{26,30},{28,20... | collective-permute-start | bytes 1572872 | tf_op jit(solution)/shard_map/ppermute | solution.py:985
  220.6 19.3 %collective-permute-start.19 = (bf16[128,2048]{1,0:T(8,128)(2,1)S(1)}, bf16[128,2048]{1,0:T(8,128)(2,1)S(1)}, u32[]{:S(2)}, u32[]{:S(2)}) collective-permute-start(bf16[128,2048]{1,0:T(8,128)(2,1)S(1)} %get-tuple-element.123), channel_id=1, source_target_pairs={{8,0},{10,2},{16,8},{18,10},{24,16},{26,18},{28,24},{30,26},{20,28... | collective-permute-start | bytes 1572872 | tf_op jit(solution)/shard_map/ppermute | solution.py:985
  231.9 20.5 %collective-permute-start.21 = (bf16[640,512]{1,0:T(8,128)(2,1)}, bf16[640,512]{1,0:T(8,128)(2,1)S(1)}, u32[]{:S(2)}, u32[]{:S(2)}) collective-permute-start(bf16[640,512]{1,0:T(8,128)(2,1)} %get-tuple-element.83.refs_0_), channel_id=1, source_target_pairs={{0,1},{1,0},{2,3},{3,2},{4,5},{5,4},{6,7},{7,6},{8,9},{9,8},{10,11... | collective-permute-start | bytes 1966088 | tf_op jit(solution)/shard_map/ppermute | solution.py:911
  242.5 22.5 %collective-permute-start.22 = (bf16[128,2048]{1,0:T(8,128)(2,1)S(1)}, bf16[128,2048]{1,0:T(8,128)(2,1)S(1)}, u32[]{:S(2)}, u32[]{:S(2)}) collective-permute-start(bf16[128,2048]{1,0:T(8,128)(2,1)S(1)} %get-tuple-element.122), channel_id=1, source_target_pairs={{0,8},{2,10},{8,16},{10,18},{16,24},{18,26},{24,28},{26,30},{28,20... | collective-permute-start | bytes 1572872 | tf_op jit(solution)/shard_map/ppermute | solution.py:985
  243.0 22.0 %collective-permute-start.23 = (bf16[128,2048]{1,0:T(8,128)(2,1)S(1)}, bf16[128,2048]{1,0:T(8,128)(2,1)S(1)}, u32[]{:S(2)}, u32[]{:S(2)}) collective-permute-start(bf16[128,2048]{1,0:T(8,128)(2,1)S(1)} %get-tuple-element.121), channel_id=1, source_target_pairs={{8,0},{10,2},{16,8},{18,10},{24,16},{26,18},{28,24},{30,26},{20,28... | collective-permute-start | bytes 1572872 | tf_op jit(solution)/shard_map/ppermute | solution.py:985
  267.5 14.3 %collective-permute-start.24 = (bf16[128,2048]{1,0:T(8,128)(2,1)S(1)}, bf16[128,2048]{1,0:T(8,128)(2,1)S(1)}, u32[]{:S(2)}, u32[]{:S(2)}) collective-permute-start(bf16[128,2048]{1,0:T(8,128)(2,1)S(1)} %get-tuple-element.120), channel_id=1, source_target_pairs={{0,8},{2,10},{8,16},{10,18},{16,24},{18,26},{24,28},{26,30},{28,20... | collective-permute-start | bytes 1572872 | tf_op jit(solution)/shard_map/ppermute | solution.py:985
  268.0 13.8 %collective-permute-start.25 = (bf16[128,2048]{1,0:T(8,128)(2,1)S(1)}, bf16[128,2048]{1,0:T(8,128)(2,1)S(1)}, u32[]{:S(2)}, u32[]{:S(2)}) collective-permute-start(bf16[128,2048]{1,0:T(8,128)(2,1)S(1)} %get-tuple-element.119), channel_id=1, source_target_pairs={{8,0},{10,2},{16,8},{18,10},{24,16},{26,18},{28,24},{30,26},{20,28... | collective-permute-start | bytes 1572872 | tf_op jit(solution)/shard_map/ppermute | solution.py:985
  290.9 31.6 %collective-permute-start.27 = (bf16[1024,1280]{1,0:T(8,128)(2,1)}, bf16[1024,1280]{1,0:T(8,128)(2,1)}, u32[]{:S(2)}, u32[]{:S(2)}) collective-permute-start(bf16[1024,1280]{1,0:T(8,128)(2,1)} %tail_grads.2.refs_7_), channel_id=1, source_target_pairs={{0,2},{2,0},{4,6},{6,4},{8,10},{10,8},{12,14},{14,12},{16,18},{18,... | collective-permute-start | bytes 7864328 | tf_op jit(solution)/shard_map/ppermute | solution.py:908
  292.6 14.5 %collective-permute-start.26 = (bf16[128,2048]{1,0:T(8,128)(2,1)S(1)}, bf16[128,2048]{1,0:T(8,128)(2,1)}, u32[]{:S(2)}, u32[]{:S(2)}) collective-permute-start(bf16[128,2048]{1,0:T(8,128)(2,1)S(1)} %bitcast_add_fusion.4), channel_id=1, source_target_pairs={{0,8},{2,10},{8,16},{10,18},{16,24},{18,26},{24,28},{26,30},{28,20... | collective-permute-start | bytes 1572872 | tf_op jit(solution)/shard_map/ppermute | solution.py:985
  293.8 70.2 %collective-permute-start.34 = (bf16[640,1024]{1,0:T(8,128)(2,1)S(1)}, bf16[640,1024]{1,0:T(8,128)(2,1)S(1)}, u32[]{:S(2)}, u32[]{:S(2)}) collective-permute-start(bf16[640,1024]{1,0:T(8,128)(2,1)S(1)} %copy-done.8), channel_id=1, source_target_pairs={{0,1},{1,0},{2,3},{3,2},{4,5},{5,4},{6,7},{7,6},{8,9},{9,8},{10,11... | collective-permute-start | bytes 3932168 | tf_op jit(solution)/shard_map/ppermute | solution.py:911
  322.5 14.8 %collective-permute-start.44 = (f32[64,1024]{1,0:T(8,128)S(1)}, f32[64,1024]{1,0:T(8,128)}, u32[]{:S(2)}, u32[]{:S(2)}) collective-permute-start(f32[64,1024]{1,0:T(8,128)S(1)} %dynamic-slice_bitcast_fusion.5), channel_id=1, source_target_pairs={{0,2},{2,0},{4,6},{6,4},{8,10},{10,8},{12,14},{14,12},{16,18},{18,... | collective-permute-start | bytes 786440 | tf_op jit(solution)/shard_map/ppermute | solution.py:908
  335.3 10.3 %collective-permute-start.28 = (bf16[128,1280]{1,0:T(8,128)(2,1)}, bf16[128,1280]{1,0:T(8,128)(2,1)S(1)}, u32[]{:S(2)}, u32[]{:S(2)}) collective-permute-start(bf16[128,1280]{1,0:T(8,128)(2,1)} %get-tuple-element.130), channel_id=1, source_target_pairs={{0,8},{2,10},{8,16},{10,18},{16,24},{18,26},{24,28},{26,30},{28,20... | collective-permute-start | bytes 983048 | tf_op jit(solution)/shard_map/ppermute | solution.py:985
  336.9 10.1 %collective-permute-start.29 = (bf16[128,1280]{1,0:T(8,128)(2,1)}, bf16[128,1280]{1,0:T(8,128)(2,1)}, u32[]{:S(2)}, u32[]{:S(2)}) collective-permute-start(bf16[128,1280]{1,0:T(8,128)(2,1)} %get-tuple-element.129), channel_id=1, source_target_pairs={{8,0},{10,2},{16,8},{18,10},{24,16},{26,18},{28,24},{30,26},{20,28... | collective-permute-start | bytes 983048 | tf_op jit(solution)/shard_map/ppermute | solution.py:985
  349.5 17.5 %collective-permute-start.32 = (bf16[320,1024]{1,0:T(8,128)(2,1)}, bf16[320,1024]{1,0:T(8,128)(2,1)}, u32[]{:S(2)}, u32[]{:S(2)}) collective-permute-start(bf16[320,1024]{1,0:T(8,128)(2,1)} %get-tuple-element.132), channel_id=1, source_target_pairs={{0,1},{1,0},{2,3},{3,2},{4,5},{5,4},{6,7},{7,6},{8,9},{9,8},{10,11... | collective-permute-start | bytes 1966088 | tf_op jit(solution)/shard_map/ppermute | solution.py:911
  353.4 13.6 %collective-permute-start.30 = (bf16[128,1280]{1,0:T(8,128)(2,1)}, bf16[128,1280]{1,0:T(8,128)(2,1)S(1)}, u32[]{:S(2)}, u32[]{:S(2)}) collective-permute-start(bf16[128,1280]{1,0:T(8,128)(2,1)} %get-tuple-element.128), channel_id=1, source_target_pairs={{0,8},{2,10},{8,16},{10,18},{16,24},{18,26},{24,28},{26,30},{28,20... | collective-permute-start | bytes 983048 | tf_op jit(solution)/shard_map/ppermute | solution.py:985
  354.6 12.4 %collective-permute-start.31 = (bf16[128,1280]{1,0:T(8,128)(2,1)}, bf16[128,1280]{1,0:T(8,128)(2,1)S(1)}, u32[]{:S(2)}, u32[]{:S(2)}) collective-permute-start(bf16[128,1280]{1,0:T(8,128)(2,1)} %get-tuple-element.127), channel_id=1, source_target_pairs={{8,0},{10,2},{16,8},{18,10},{24,16},{26,18},{28,24},{30,26},{20,28... | collective-permute-start | bytes 983048 | tf_op jit(solution)/shard_map/ppermute | solution.py:985
  362.5 4.5 %collective-permute-start.33 = (f32[4,1024]{1,0:T(4,128)S(1)}, f32[4,1024]{1,0:T(4,128)S(1)}, u32[]{:S(2)}, u32[]{:S(2)}) collective-permute-start(f32[4,1024]{1,0:T(4,128)S(1)} %pad_maximum_fusion.4), channel_id=1, source_target_pairs={{0,1},{1,0},{2,3},{3,2},{4,5},{5,4},{6,7},{7,6},{8,9},{9,8},{10,11... | collective-permute-start | bytes 49160 | tf_op jit(solution)/shard_map/ppermute | solution.py:911
  364.1 7.6 %collective-permute-start.45 = (f32[32,2048]{1,0:T(8,128)S(1)}, f32[32,2048]{1,0:T(8,128)S(1)}, u32[]{:S(2)}, u32[]{:S(2)}) collective-permute-start(f32[32,2048]{1,0:T(8,128)S(1)} %fusion.7), channel_id=1, source_target_pairs={{0,1},{1,0},{2,3},{3,2},{4,5},{5,4},{6,7},{7,6},{8,9},{9,8},{10,11... | collective-permute-start | bytes 786440 | tf_op jit(solution)/shard_map/ppermute | solution.py:911
  372.6 9.5 %collective-permute-start.39 = (f32[4,8,1024]{2,1,0:T(8,128)}, f32[4,8,1024]{2,1,0:T(8,128)S(1)}, u32[]{:S(2)}, u32[]{:S(2)}) collective-permute-start(f32[4,8,1024]{2,1,0:T(8,128)} %fusion.24), channel_id=1, source_target_pairs={{0,4},{2,6},{4,0},{6,2},{8,12},{10,14},{12,8},{14,10},{16,20},{18,... | collective-permute-start | bytes 393224 | tf_op jit(solution)/shard_map/ppermute | solution.py:908
  376.6 8.3 %collective-permute-start.36 = (bf16[128,1280]{1,0:T(8,128)(2,1)}, bf16[128,1280]{1,0:T(8,128)(2,1)}, u32[]{:S(2)}, u32[]{:S(2)}) collective-permute-start(bf16[128,1280]{1,0:T(8,128)(2,1)} %get-tuple-element.126), channel_id=1, source_target_pairs={{0,8},{2,10},{8,16},{10,18},{16,24},{18,26},{24,28},{26,30},{28,20... | collective-permute-start | bytes 983048 | tf_op jit(solution)/shard_map/ppermute | solution.py:985
  377.8 8.1 %collective-permute-start.37 = (bf16[128,1280]{1,0:T(8,128)(2,1)}, bf16[128,1280]{1,0:T(8,128)(2,1)}, u32[]{:S(2)}, u32[]{:S(2)}) collective-permute-start(bf16[128,1280]{1,0:T(8,128)(2,1)} %get-tuple-element.125), channel_id=1, source_target_pairs={{8,0},{10,2},{16,8},{18,10},{24,16},{26,18},{28,24},{30,26},{20,28... | collective-permute-start | bytes 983048 | tf_op jit(solution)/shard_map/ppermute | solution.py:985
  385.9 6.2 %collective-permute-start.46 = (f32[4,8,1024]{2,1,0:T(8,128)S(1)}, f32[4,8,1024]{2,1,0:T(8,128)S(1)}, u32[]{:S(2)}, u32[]{:S(2)}) collective-permute-start(f32[4,8,1024]{2,1,0:T(8,128)S(1)} %fusion.37), channel_id=1, source_target_pairs={{0,8},{2,10},{4,12},{6,14},{8,0},{10,2},{12,4},{14,6},{16,24},{18,... | collective-permute-start | bytes 393224 | tf_op jit(solution)/shard_map/ppermute | solution.py:908
  390.7 16.2 %collective-permute-start.35 = (bf16[320,1024]{1,0:T(8,128)(2,1)S(1)}, bf16[320,1024]{1,0:T(8,128)(2,1)S(1)}, u32[]{:S(2)}, u32[]{:S(2)}) collective-permute-start(bf16[320,1024]{1,0:T(8,128)(2,1)S(1)} %copy-done.13), channel_id=1, source_target_pairs={{0,1},{1,0},{2,3},{3,2},{4,5},{5,4},{6,7},{7,6},{8,9},{9,8},{10,11... | collective-permute-start | bytes 1966088 | tf_op jit(solution)/shard_map/ppermute | solution.py:911
  392.1 7.1 %collective-permute-start.47 = (f32[4,8,1024]{2,1,0:T(8,128)S(1)}, f32[4,8,1024]{2,1,0:T(8,128)S(1)}, u32[]{:S(2)}, u32[]{:S(2)}) collective-permute-start(f32[4,8,1024]{2,1,0:T(8,128)S(1)} %add.109), channel_id=1, source_target_pairs={{0,16},{2,18},{4,20},{6,22},{8,24},{10,26},{12,28},{14,30},{16,0},... | collective-permute-start | bytes 393224 | tf_op jit(solution)/shard_map/ppermute | solution.py:908
  395.5 7.1 %collective-permute-start.40 = (bf16[128,1280]{1,0:T(8,128)(2,1)S(1)}, bf16[128,1280]{1,0:T(8,128)(2,1)S(1)}, u32[]{:S(2)}, u32[]{:S(2)}) collective-permute-start(bf16[128,1280]{1,0:T(8,128)(2,1)S(1)} %bitcast_add_fusion.5), channel_id=1, source_target_pairs={{0,8},{2,10},{8,16},{10,18},{16,24},{18,26},{24,28},{26,30},{28,20... | collective-permute-start | bytes 983048 | tf_op jit(solution)/shard_map/ppermute | solution.py:985
  405.0 8.5 %collective-permute-start.41 = (f32[64,1280]{1,0:T(8,128)S(1)}, f32[64,1280]{1,0:T(8,128)S(1)}, u32[]{:S(2)}, u32[]{:S(2)}) collective-permute-start(f32[64,1280]{1,0:T(8,128)S(1)} %dynamic-slice_bitcast_fusion.2), channel_id=1, source_target_pairs={{0,2},{2,0},{4,6},{6,4},{8,10},{10,8},{12,14},{14,12},{16,18},{18,... | collective-permute-start | bytes 983048 | tf_op jit(solution)/shard_map/ppermute | solution.py:908
  414.4 5.0 %collective-permute-start.43 = (bf16[32,1024]{1,0:T(8,128)(2,1)S(1)}, bf16[32,1024]{1,0:T(8,128)(2,1)S(1)}, u32[]{:S(2)}, u32[]{:S(2)}) collective-permute-start(bf16[32,1024]{1,0:T(8,128)(2,1)S(1)} %fusion.19), channel_id=1, source_target_pairs={{0,1},{1,0},{2,3},{3,2},{4,5},{5,4},{6,7},{7,6},{8,9},{9,8},{10,11... | collective-permute-start | bytes 196616 | tf_op jit(solution)/shard_map/ppermute | solution.py:911
  415.6 7.5 %collective-permute-start.42 = (f32[32,1536]{1,0:T(8,128)S(1)}, f32[32,1536]{1,0:T(8,128)S(1)}, u32[]{:S(2)}, u32[]{:S(2)}) collective-permute-start(f32[32,1536]{1,0:T(8,128)S(1)} %fusion.16), channel_id=1, source_target_pairs={{0,1},{1,0},{2,3},{3,2},{4,5},{5,4},{6,7},{7,6},{8,9},{9,8},{10,11... | collective-permute-start | bytes 589832 | tf_op jit(solution)/shard_map/ppermute | solution.py:911
  (43 other events, 407.5 us)
Sparse Core Ops, SparseCore 0:
  47.9 93.5 all-gather.2

commit v5 on v4

--- a/solution.py
+++ b/solution.py
@@ -302,7 +302,7 @@
         grid_spec=pltpu.PrefetchScalarGridSpec(
             num_scalar_prefetch=1,
             grid=(1,),
-            in_specs=[pl.BlockSpec((rows, held), lambda j, s: (0, s[4]))] * 3,
+            in_specs=[pl.BlockSpec((rows, held), lambda j, s: (0, s[0]))] * 3,
             out_specs=pl.BlockSpec((rows, 3 * held), lambda j, s: (0, 0)),
         ),
         out_shape=jax.ShapeDtypeStruct((rows, 3 * held), query.dtype),
@@ -501,7 +501,7 @@
     )(x, weights.up, weights.down, *grads)
 
 
-def accumulate(part, out_ref, total):
+def accumulate(part, outs, total):
     step = pl.program_id(0)
 
     @pl.when(step == 0)
@@ -514,29 +514,33 @@
 
     @pl.when(step == pl.num_programs(0) - 1)
     def _():
-        out_ref[...] = total[...].astype(out_ref.dtype)
-
-
-def down_kernel(a_ref, down_ref, *refs):
-    out_ref, total = refs[-2:]
-    accumulate(matmul(a_ref[...], down_ref[...].reshape(-1, out_ref.shape[1])), out_ref, total)
-
-
-def up_back_kernel(g_ref, up_ref, *refs):
-    out_ref, total = refs[-2:]
-    weights = up_ref[...].reshape(out_ref.shape[1], -1)
-    accumulate(matmul_last(g_ref[...], weights), out_ref, total)
-
-
-def hidden_to_width(kernel, name, held, weights, spec, array, rows, chunk, dtype, behind):
+        rows = total.shape[0] // len(outs)
+        for index, out_ref in enumerate(outs):
+            value = total[index * rows : (index + 1) * rows, :]
+            out_ref[...] = value.astype(out_ref.dtype)
+
+
+def down_kernel(splits, a_ref, down_ref, *refs):
+    total = refs[-1]
+    part = matmul(a_ref[...], down_ref[...].reshape(-1, total.shape[1]))
+    accumulate(part, refs[-1 - splits : -1], total)
+
+
+def up_back_kernel(splits, g_ref, up_ref, *refs):
+    total = refs[-1]
+    weights = up_ref[...].reshape(total.shape[1], -1)
+    accumulate(matmul_last(g_ref[...], weights), refs[-1 - splits : -1], total)
+
+
+def hidden_to_width(kernel, name, held, weights, spec, array, rows, chunk, dtype, behind, splits=1):
     width = weights.width
-    return pl.pallas_call(
-        kernel,
+    outs = pl.pallas_call(
+        partial(kernel, splits),
         grid=(weights.steps,),
         in_specs=[pl.BlockSpec((rows, weights.block), lambda j: (chunk, j)), spec]
         + [ANYWHERE] * len(behind),
-        out_specs=pl.BlockSpec((rows, width), lambda j: (0, 0)),
-        out_shape=jax.ShapeDtypeStruct((rows, width), dtype),
+        out_specs=[pl.BlockSpec((rows // splits, width), lambda j: (0, 0))] * splits,
+        out_shape=[jax.ShapeDtypeStruct((rows // splits, width), dtype)] * splits,
         scratch_shapes=[pltpu.VMEM((rows, width), jnp.float32)],
         compiler_params=BIG,
         cost_estimate=cost(
@@ -545,6 +549,7 @@
         ),
         name=name,
     )(held, array, *behind)
+    return outs[0] if splits == 1 else outs
 
 
 def down_part(active, weights, rows, chunk, dtype, behind=()):
@@ -562,7 +567,7 @@
     )
 
 
-def up_back(grad, weights, rows, chunk, dtype, behind=()):
+def up_back(grad, weights, rows, chunk, dtype, behind=(), splits=1):
     return hidden_to_width(
         up_back_kernel,
         "up_back",
@@ -574,6 +579,7 @@
         chunk,
         dtype,
         behind,
+        splits,
     )
 
 
@@ -635,23 +641,29 @@
     )(spots, own, attended, cotangent, ada, out_w, *other, *behind)
 
 
-def first_back_kernel(grad_ref, weight_ref, frames, *refs):
-    out_ref, ada_grad_ref = refs[-2:]
+def first_back_kernel(splits, grad_ref, weight_ref, frames, *refs):
+    outs, ada_grad_ref = refs[-1 - splits : -1], refs[-1]
     grad = matmul_last(grad_ref[...], weight_ref[...])
     normed, _ = standardise(frames[...].astype(jnp.float32))
-    out_ref[...] = grad.astype(jnp.bfloat16)
+    for index, out_ref in enumerate(outs):
+
+        @pl.when((pl.program_id(0) == index) | (splits == 1))
+        def _(out_ref=out_ref):
+            out_ref[...] = grad.astype(jnp.bfloat16)
+
     scale = jnp.sum(grad * normed, axis=0, keepdims=True)
     shift = jnp.sum(grad, axis=0, keepdims=True)
     add_rows(ada_grad_ref, scale, shift)
 
 
-def first_back(grad, weights, frames, part, behind):
+def first_back(grad, weights, frames, part, behind, splits=1):
     width, columns = weights.shape
     count = 2
     rows = frames.shape[0] // count
     block = pl.BlockSpec((rows, width), lambda j: (j, 0))
+    out = block if splits == 1 else pl.BlockSpec((rows, width), lambda j: (0, 0))
     return pl.pallas_call(
-        first_back_kernel,
+        partial(first_back_kernel, splits),
         grid=(count,),
         in_specs=[
             pl.BlockSpec((rows, columns), lambda j: (part * count + j, 0)),
@@ -659,11 +671,9 @@
             block,
         ]
         + [ANYWHERE] * len(behind),
-        out_specs=[block, pl.BlockSpec((2, width), lambda j: (0, 0))],
-        out_shape=[
-            jax.ShapeDtypeStruct((rows * count, width), jnp.bfloat16),
-            jax.ShapeDtypeStruct((2, width), jnp.float32),
-        ],
+        out_specs=[out] * splits + [pl.BlockSpec((2, width), lambda j: (0, 0))],
+        out_shape=[jax.ShapeDtypeStruct((rows * count // splits, width), jnp.bfloat16)] * splits
+        + [jax.ShapeDtypeStruct((2, width), jnp.float32)],
         compiler_params=BIG,
         cost_estimate=cost(
             2 * rows * count * width * columns,
@@ -974,7 +984,7 @@
         self.both = self.make(True, self.arriving[0], behind)
         self.whole = self.both
         self.both = self.both.reshape(self.chips, -1, self.both.shape[1])
-        self.result = self.block(0).astype(jnp.float32)
+        self.arrived = []
         flows = [
             (self.mover.forward, 1, self.chips // 2),
             (self.mover.backward, -1, (self.chips - 1) // 2),
@@ -993,14 +1003,19 @@
             if flow[2]:
                 flows.append((flow, self.block(flow[1] * flow[2]) + value))
             else:
-                self.result = self.result + value.astype(jnp.float32)
+                self.arrived.append(value)
         self.send(flows)
         return anchor
 
-    def finish(self):
+    def finish(self, anchor=None):
         while self.arriving:
             self.advance()
-        return self.result
+        if anchor is not None:
+            self.arrived, anchor = tie(self.arrived, anchor)
+        result = self.block(0).astype(jnp.float32)
+        for value in self.arrived:
+            result = result + value.astype(jnp.float32)
+        return result if anchor is None else (result, anchor)
 
 
 def in_rows(value):
@@ -1068,7 +1083,8 @@
     ada_part = quarters(ada_part[:, : 2 * width], ada_part[:, 2 * width :])
     prompt_at = mover.seq if mover.pair else jnp.zeros((), jnp.int32)
     place = jnp.stack([prompt_at, prompt_len[0], mover.core, mover.beside, mover.seq])
-    mine = pack_columns(w_query, w_key, w_value, held, place)
+    seq_place = jnp.reshape(mover.seq, (1,)).astype(jnp.int32)
+    mine = pack_columns(w_query, w_key, w_value, held, seq_place)
     early = [mover.across(tokens)] if mover.pair else []
     blocks, ada_sum, early, late = mover.gather_items(
         mine, ada_part, early, late
@@ -1124,10 +1140,8 @@
         )
         lows = low_two
         active, upward = hidden_layer(lows, grads, weights)
-        for_other = up_back(upward, weights, rows, 1, jnp.bfloat16)
-        half = rows // 2
-        first_half, last_half = for_other[:half], for_other[half:]
-        start = [for_other]
+        first_half, last_half = up_back(upward, weights, rows, 1, jnp.bfloat16, (), 2)
+        start = [first_half]
         ready = [mover.across(first_half), last_half]
     else:
         mixed = lax.all_to_all(mixed_heads[0], "seq", split_axis=0, concat_axis=1, tiled=True)
@@ -1228,25 +1242,24 @@
         tail = RingSum(mover, tail_parts, [])
     tail.add_own([])
     if mover.pair:
-        far_first, far_rows = first_back(grad_qkv, qkv_w, frames[1], 1, [tail.whole])
-        far_first = tail.advance(far_first)
-        half = rows // 2
-        near_half, last_half = far_first[:half], far_first[half:]
+        near_half, last_half, far_rows = first_back(
+            grad_qkv, qkv_w, frames[1], 1, [tail.whole, out_other], 2
+        )
         near_half = mover.across(near_half)
-        own_first, own_rows = first_back(grad_qkv, qkv_w, frames[0], 0, [far_first])
+        last_half = tail.advance(last_half)
+        hidden_total, last_half = ring.finish(last_half)
+        own_first, own_rows = first_back(grad_qkv, qkv_w, frames[0], 0, [last_half])
+        own_rows, near_half, last_half = tail.advance([own_rows, near_half, last_half])
+        far_parts = [near_half, mover.across(last_half)]
         ada_rows = jnp.concatenate([own_rows + far_rows, ada_two_rows])
-        ada_other = mover.across(ada_rows)
-        near_half, last_half, ada_other, out_other = tail.advance(
-            [near_half, last_half, ada_other, out_other]
-        )
-        ada_rows = ada_rows + ada_other
-        far_parts = [near_half, mover.across(last_half)]
+        ada_rows = ada_rows + mover.across(ada_rows)
         layer_sum = out_own + out_other.astype(jnp.float32)
     else:
         grad_first, ada_one_rows = first_back(grad_qkv, qkv_w, frames[0], 0, [tail.whole])
         ada_rows = lax.psum(jnp.concatenate([ada_one_rows, ada_two_rows]), "seq")
         own_first = lax.psum_scatter(grad_first, "seq", scatter_dimension=0, tiled=True)
         far_parts = [jnp.zeros((rows, width), jnp.bfloat16)]
+        hidden_total = ring.finish()
         layer_sum = lax.psum_scatter(
             down_part(active, weights, total_rows, 0, jnp.bfloat16),
             "seq",
@@ -1258,7 +1271,7 @@
     for bit in [1 << k for k in range(items_count.bit_length() - 1)]:
         sums = sums + mover.flip(sums, bit)
         if bit == 2:
-            sums = tail.advance(sums)
+            sums, far_parts = tail.advance([sums, far_parts])
     input_grad = input_back(own_first, far_parts, tokens, ada_one, grad_attended)
     out_piece = piece // seq_count
     first_row = mover.item * piece + mover.seq * out_piece
@@ -1271,10 +1284,9 @@
     ).astype(jnp.float32)
     grad_table = jnp.einsum("ksd,krd->sr", sums, own_ada, precision=lax.Precision.HIGHEST)
 
-    ring_total = ring.finish()
-    grad_down = ring_total[:, :down_columns].reshape(units, width)
+    grad_down = hidden_total[:, :down_columns].reshape(units, width)
     up_sides = mover.join_columns(
-        jnp.concatenate(mover.join_cores(ring_total[:, down_columns:]), axis=1)
+        jnp.concatenate(mover.join_cores(hidden_total[:, down_columns:]), axis=1)
     )
     grad_up = jnp.stack(
         [side.reshape(out_piece, 2, chips, units) for side in up_sides], axis=1

time: 436 us -> 425 us (0.975)
  local copies, waits for them, and re-layouts: 30.6 us -> 25.8 us
    ppermute x14, waiting for transfers between devices: 7.96 us -> 0.74 us  [send(): lax.ppermute(value, 'items', flow[0])]
  transfers between devices with their start and end apart: 49 -> 49, of which waited for: 20 -> 16; matrix products, arithmetic and copies ran while one was open for 12% -> 11% of each run, Pallas kernels for 41% -> 42%
where the time goes in v5:
time: 425 us; the launch traced here: 420 us
  Pallas kernels  222 us (52%)
  waiting for transfers between devices  75.7 us (18%)
  starting transfers between devices  43.5 us (10%)
  other arithmetic  32.2 us (8%)
  local copies, waits for them, and re-layouts  25.8 us (6%)
  between operations  17 us (4%)
    pallas_call x4, Pallas kernels, attend_back(): pl.pallas_call(partial(attend_back_kernel, parts, calls, per, at), grid_s...  47.6 us
    ppermute x14, waiting for transfers between devices, across(): return lax.ppermute(value, 'seq', [(0, 1), (1, 0)])  33.8 us
    pallas_call x2, Pallas kernels, attend(): pl.pallas_call(attend_kernel, grid_spec=pltpu.PrefetchScalarGridSpec(num_...  31.7 us
    pallas_call x4, Pallas kernels, hidden_to_width(): pl.pallas_call(partial(kernel, splits), grid=(weights.steps,), in_specs=[...  30.8 us
    pallas_call x2, Pallas kernels, hidden_grads(): pl.pallas_call(partial(hidden_grads_kernel, count, bool(more)), grid_spec...  25.3 us
    ppermute x16, waiting for transfers between devices, flip(): return lax.ppermute(value, 'items', pairs)  20.2 us
    pallas_call x1, Pallas kernels, hidden_layer(): pl.pallas_call(partial(hidden_kernel, weights.per_chip, len(grads)), grid...  18.5 us
    pallas_call x2, Pallas kernels, tail_grads(): pl.pallas_call(partial(tail_grads_kernel, first, bool(more), len(mixed) +...  18.4 us
  transfers between devices with their start and end apart: 49, of which 16 were waited for; matrix products, arithmetic and copies ran while one was open for 11% of the time, Pallas kernels for 42%

profile of v5, /device:TPU:0, one launch (start us, length us, event | category | flops | bytes accessed | tf_op | source)
XLA Modules:
  0.0 420.0 jit_solution(5007759402429824041)
XLA Ops:
  10.9 2.9 collective-permute-start.7
  15.9 1.8 maximum_select_fusion.refs_3_
  22.3 6.3 %collective-permute-done.1 = f32[4,8,1024]{2,1,0:T(8,128)} collective-permute-done((f32[4,8,1024]{2,1,0:T(8,128)}, f32[4,8,1024]{2,1,0:T(8,128)}, u32[]{:S(2)}, u32[]{:S(2)}) %collective-permute-start.1) | collective-permute-done | bytes 131104 | tf_op jit(solution)/shard_map/ppermute | solution.py:918
  29.7 2.0 collective-permute-start.6
  32.7 3.4 collective-permute-done.2
  38.8 5.4 %collective-permute-done.3 = f32[4,8,1024]{2,1,0:T(8,128)S(1)} collective-permute-done((f32[4,8,1024]{2,1,0:T(8,128)S(1)}, f32[4,8,1024]{2,1,0:T(8,128)S(1)}, u32[]{:S(2)}, u32[]{:S(2)}) %collective-permute-start.3) | collective-permute-done | bytes 131104 | tf_op jit(solution)/shard_map/ppermute | solution.py:918
  49.1 5.0 %collective-permute-done.8.refs_6_ = bf16[128,1536]{1,0:T(8,128)(2,1)S(1)} collective-permute-done((bf16[128,1536]{1,0:T(8,128)(2,1)}, bf16[128,1536]{1,0:T(8,128)(2,1)S(1)}, u32[]{:S(2)}, u32[]{:S(2)}) %collective-permute-start.8) | collective-permute-done | bytes 393248 | tf_op jit(solution)/shard_map/ppermute | solution.py:934
  56.1 1.8 stack.41.place
  58.6 10.5 %collective-permute-done.9.refs_7_ = bf16[128,1536]{1,0:T(8,128)(2,1)} collective-permute-done((bf16[128,1536]{1,0:T(8,128)(2,1)S(1)}, bf16[128,1536]{1,0:T(8,128)(2,1)}, u32[]{:S(2)}, u32[]{:S(2)}) %collective-permute-start.9) | collective-permute-done | bytes 393248 | tf_op jit(solution)/shard_map/ppermute | solution.py:934
  69.1 11.3 %first_layer.1 = (bf16[1280,1024]{1,0:T(8,128)(2,1)}, bf16[1280,1536]{1,0:T(8,128)(2,1)}, bf16[1024,1536]{1,0:T(8,128)(2,1)}) custom-call(s32[8]{0:T(128)} %slice_bitcast_fusion.8.spots, bf16[640,1024]{1,0:T(8,128)(2,1)} %bitcast.144, bf16[640,1024]{1,0:T(8,128)(2,1)} %copy-done.10, f32[2,1024]{1,0:T(2,128)} %get-tuple-element.194.refs_2_.ada_ref, ...), custom_call_target="tpu_custom_call" | custom-call | flops 2013265920 | bytes 8388608 | tf_op jit(solution)/shard_map/first_layer/pallas_call | solution.py:347
  81.5 15.8 %attend.2 = (bf16[1280,256]{1,0:T(8,128)(2,1)}, f32[2,10,256]{2,1,0:T(8,128)}) custom-call(s32[5]{0:T(128)} %stack.41.place, bf16[1280,1536]{1,0:T(8,128)(2,1)} %get-tuple-element.76.q_ref.k_ref.v_ref, bf16[1280,1536]{1,0:T(8,128)(2,1)} %get-tuple-element.76.q_ref.k_ref.v_ref, bf16[1280,1536]{1,0:T(8,128)(2,1)} %get-tuple-element.76.q_ref.k_ref.v_ref, ...), custom_call_target="tpu_custom_call" | custom-call | flops 2516582400 | bytes 2621440 | tf_op jit(solution)/shard_map/attend/pallas_call | solution.py:91
  97.8 15.8 %attend.3 = (bf16[1280,256]{1,0:T(8,128)(2,1)}, f32[2,10,256]{2,1,0:T(8,128)}) custom-call(s32[5]{0:T(128)} %stack.41.place, bf16[1280,1536]{1,0:T(8,128)(2,1)} %get-tuple-element.76.q_ref.k_ref.v_ref, bf16[1280,1536]{1,0:T(8,128)(2,1)} %get-tuple-element.76.q_ref.k_ref.v_ref, bf16[1280,1536]{1,0:T(8,128)(2,1)} %get-tuple-element.76.q_ref.k_ref.v_ref, ...), custom_call_target="tpu_custom_call" | custom-call | flops 2516582400 | bytes 2621440 | tf_op jit(solution)/shard_map/attend/pallas_call | solution.py:91
  115.3 16.0 %collective-permute-done.15.refs_3_ = bf16[1280,256]{1,0:T(8,128)(2,1)S(1)} collective-permute-done((bf16[1280,256]{1,0:T(8,128)(2,1)}, bf16[1280,256]{1,0:T(8,128)(2,1)S(1)}, u32[]{:S(2)}, u32[]{:S(2)}) %collective-permute-start.15) | collective-permute-done | bytes 655392 | tf_op jit(solution)/shard_map/ppermute | solution.py:921
  131.3 5.5 %all-gather.3.cloned.1.call-done = bf16[5120,1024]{1,0:T(8,128)(2,1)} async-done(((bf16[320,1024]{1,0:T(8,128)(2,1)}), bf16[5120,1024]{1,0:T(8,128)(2,1)}) %all-gather.3.cloned.1.call-update) | async-done | bytes 10485776 | tf_op jit(solution)/shard_map/all_gather | solution.py:1094
  136.8 9.3 %second_layer.1 = (f32[640,1024]{1,0:T(8,128)}, bf16[1280,1024]{1,0:T(8,128)(2,1)}) custom-call(s32[5]{0:T(128)} %stack.41.place, bf16[1280,256]{1,0:T(8,128)(2,1)} %get-tuple-element.78.refs_1_.refs_0_, bf16[1280,256]{1,0:T(8,128)(2,1)} %get-tuple-element.81.refs_1_, bf16[1280,256]{1,0:T(8,128)(2,1)} %copy-done.7, bf16[1280,256]{1,0:T(8,128)(2,1)} %copy-done.8, ...), custom_call_target="tpu_custom_call" | custom-call | flops 1342177280 | bytes 7602176 | tf_op jit(solution)/shard_map/second_layer/pallas_call | solution.py:401
  146.1 18.5 %hidden_layer.1 = (bf16[1280,2048]{1,0:T(8,128)(2,1)}, bf16[1280,2048]{1,0:T(8,128)(2,1)}) custom-call(bf16[1280,1024]{1,0:T(8,128)(2,1)} %get-tuple-element.84.x_ref.refs_4_, bf16[16,5,64,1024]{3,2,1,0:T(8,128)(2,1)} %bitcast.121, bf16[8,2,5,64,1024]{4,3,2,1,0:T(8,128)(2,1)} %bitcast.122, bf16[640,1024]{1,0:T(8,128)(2,1)} %bitcast.138, ...), custom_call_target="tpu_custom_call" | custom-call | flops 5368709120 | bytes 12058624 | tf_op jit(solution)/shard_map/hidden_layer/pallas_call | solution.py:484
  164.6 7.5 %up_back.2 = (bf16[320,1024]{1,0:T(8,128)(2,1)}, bf16[320,1024]{1,0:T(8,128)(2,1)}) custom-call(bf16[1280,2048]{1,0:T(8,128)(2,1)} %get-tuple-element.86.g_ref.refs_1_, bf16[16,5,64,1024]{3,2,1,0:T(8,128)(2,1)} %bitcast.123), custom_call_target="tpu_custom_call" | custom-call | flops 1342177280 | bytes 4718592 | tf_op jit(solution)/shard_map/up_back/pallas_call | solution.py:537
  173.6 12.4 %hidden_grads.2.refs_0_ = bf16[1024,2048]{1,0:T(8,128)(2,1)} custom-call(s32[5]{0:T(128)} %stack.41.place, bf16[1280,2048]{1,0:T(8,128)(2,1)} %get-tuple-element.85.refs_0_.a_ref, bf16[1280,2048]{1,0:T(8,128)(2,1)} %get-tuple-element.86.g_ref.refs_1_, bf16[640,1024]{1,0:T(8,128)(2,1)} %bitcast.139, bf16[640,1024]{1,0:T(8,128)(2,1)} %copy-done.2, ...), custom_call_target="tpu_custom_call" | custom-call | flops 2684354560 | bytes 7340032 | tf_op jit(solution)/shard_map/hidden_grads/pallas_call | solution.py:735
  186.0 3.2 collective-permute-done.16.refs_5_
  190.8 8.1 %up_back.3.refs_6_.refs_0_ = f32[640,1024]{1,0:T(8,128)} custom-call(bf16[1280,2048]{1,0:T(8,128)(2,1)} %get-tuple-element.86.g_ref.refs_1_, bf16[16,5,64,1024]{3,2,1,0:T(8,128)(2,1)} %bitcast.124, bf16[1024,2048]{1,0:T(8,128)(2,1)} %hidden_grads.2.refs_0_), custom_call_target="tpu_custom_call" | custom-call | flops 1342177280 | bytes 4718592 | tf_op jit(solution)/shard_map/up_back/pallas_call | solution.py:537
  198.9 12.9 %hidden_grads.3.refs_7_ = bf16[1024,2048]{1,0:T(8,128)(2,1)} custom-call(s32[5]{0:T(128)} %stack.41.place, bf16[1280,2048]{1,0:T(8,128)(2,1)} %get-tuple-element.85.refs_0_.a_ref, bf16[1280,2048]{1,0:T(8,128)(2,1)} %get-tuple-element.86.g_ref.refs_1_, bf16[640,1024]{1,0:T(8,128)(2,1)} %bitcast.140, bf16[640,1024]{1,0:T(8,128)(2,1)} %copy-done.2, ...), custom_call_target="tpu_custom_call" | custom-call | flops 2684354560 | bytes 7340032 | tf_op jit(solution)/shard_map/hidden_grads/pallas_call | solution.py:735
  211.8 2.5 dynamic-slice_bitcast_fusion
  217.2 8.9 %middle_back.1 = (f32[640,1024]{1,0:T(8,128)}, bf16[640,1024]{1,0:T(8,128)(2,1)}, f32[2,1024]{1,0:T(2,128)}, bf16[640,512]{1,0:T(8,128)(2,1)}, bf16[640,512]{1,0:T(8,128)(2,1)}) custom-call(s32[5]{0:T(128)} %stack.41.place, f32[640,1024]{1,0:T(8,128)} %up_back.3.refs_6_.refs_0_, f32[640,1024]{1,0:T(8,128)} %get-tuple-element.83.refs_1_, ...), custom_call_target="tpu_custom_call" | custom-call | flops 671088640 | bytes 7602176 | tf_op jit(solution)/shard_map/middle_back/pallas_call | solution.py:617
  226.8 7.4 %down_part.2.refs_0_ = bf16[640,1024]{1,0:T(8,128)(2,1)} custom-call(bf16[1280,2048]{1,0:T(8,128)(2,1)} %get-tuple-element.85.refs_0_.a_ref, bf16[8,2,5,64,1024]{4,3,2,1,0:T(8,128)(2,1)} %bitcast.126, bf16[640,512]{1,0:T(8,128)(2,1)} %get-tuple-element.92.refs_0_), custom_call_target="tpu_custom_call" | custom-call | flops 1342177280 | bytes 4718592 | tf_op jit(solution)/shard_map/down_part/pallas_call | solution.py:537
  234.2 2.5 bitcast_add_fusion.1
  238.7 7.8 %down_part.3.refs_6_ = f32[640,1024]{1,0:T(8,128)} custom-call(bf16[1280,2048]{1,0:T(8,128)(2,1)} %get-tuple-element.85.refs_0_.a_ref, bf16[8,2,5,64,1024]{4,3,2,1,0:T(8,128)(2,1)} %bitcast.127, bf16[640,1024]{1,0:T(8,128)(2,1)} %down_part.2.refs_0_), custom_call_target="tpu_custom_call" | custom-call | flops 1342177280 | bytes 4718592 | tf_op jit(solution)/shard_map/down_part/pallas_call | solution.py:537
  247.4 11.8 %attend_back.4.refs_6_ = bf16[1280,1536]{1,0:T(8,128)(2,1)} custom-call(s32[5]{0:T(128)} %stack.41.place, bf16[1280,1536]{1,0:T(8,128)(2,1)} %get-tuple-element.76.q_ref.k_ref.v_ref, bf16[1280,1536]{1,0:T(8,128)(2,1)} %get-tuple-element.76.q_ref.k_ref.v_ref, bf16[1280,1536]{1,0:T(8,128)(2,1)} %get-tuple-element.76.q_ref.k_ref.v_ref, ...), custom_call_target="tpu_custom_call" | custom-call | flops 3145728000 | bytes 3276800 | tf_op jit(solution)/shard_map/attend_back/pallas_call | solution.py:204
  259.2 2.5 bitcast_add_fusion
  263.8 12.1 %attend_back.5.grad.refs_6_ = bf16[1280,1536]{1,0:T(8,128)(2,1)} custom-call(s32[5]{0:T(128)} %stack.41.place, bf16[1280,1536]{1,0:T(8,128)(2,1)} %get-tuple-element.76.q_ref.k_ref.v_ref, bf16[1280,1536]{1,0:T(8,128)(2,1)} %get-tuple-element.76.q_ref.k_ref.v_ref, ...), custom_call_target="tpu_custom_call", output_to_operand_aliasing={{}: (10, {})} | custom-call | flops 3145728000 | bytes 3276800 | tf_op jit(solution)/shard_map/attend_back/pallas_call | solution.py:204
  276.0 9.0 %tail_grads.2.refs_7_ = bf16[1024,1280]{1,0:T(8,128)(2,1)} custom-call(s32[5]{0:T(128)} %stack.41.place, bf16[1280,1024]{1,0:T(8,128)(2,1)} %get-tuple-element.104.low, bf16[1280,1536]{1,0:T(8,128)(2,1)} %attend_back.5.grad.refs_6_, bf16[640,1024]{1,0:T(8,128)(2,1)} %get-tuple-element.105.attended, bf16[1280,256]{1,0:T(8,128)(2,1)} %get-tuple-element.78.refs_1_.refs_0_, ...), custom_call_target="tpu_custom_call" | custom-call | flops 1342177280 | bytes 5242880 | tf_op jit(solution)/shard_map/tail_grads/pallas_call | solution.py:788
  288.8 11.7 %attend_back.6.refs_6_ = bf16[1280,1536]{1,0:T(8,128)(2,1)} custom-call(s32[5]{0:T(128)} %stack.41.place, bf16[1280,1536]{1,0:T(8,128)(2,1)} %get-tuple-element.76.q_ref.k_ref.v_ref, bf16[1280,1536]{1,0:T(8,128)(2,1)} %get-tuple-element.76.q_ref.k_ref.v_ref, bf16[1280,1536]{1,0:T(8,128)(2,1)} %get-tuple-element.76.q_ref.k_ref.v_ref, ...), custom_call_target="tpu_custom_call", output_to_operand_aliasing={{}: (10, {})} | custom-call | flops 3145728000 | bytes 3276800 | tf_op jit(solution)/shard_map/attend_back/pallas_call | solution.py:204
  301.2 11.9 %attend_back.7.grad.grad_ref = bf16[1280,1536]{1,0:T(8,128)(2,1)} custom-call(s32[5]{0:T(128)} %stack.41.place, bf16[1280,1536]{1,0:T(8,128)(2,1)} %get-tuple-element.76.q_ref.k_ref.v_ref, bf16[1280,1536]{1,0:T(8,128)(2,1)} %get-tuple-element.76.q_ref.k_ref.v_ref, ...), custom_call_target="tpu_custom_call", output_to_operand_aliasing={{}: (10, {})} | custom-call | flops 3145728000 | bytes 3276800 | tf_op jit(solution)/shard_map/attend_back/pallas_call | solution.py:204
  313.1 9.4 %tail_grads.3.refs_0_ = bf16[1024,1280]{1,0:T(8,128)(2,1)} custom-call(s32[5]{0:T(128)} %stack.41.place, bf16[1280,1024]{1,0:T(8,128)(2,1)} %get-tuple-element.104.low, bf16[1280,1536]{1,0:T(8,128)(2,1)} %attend_back.7.grad.grad_ref, bf16[640,1024]{1,0:T(8,128)(2,1)} %get-tuple-element.105.attended, bf16[1280,256]{1,0:T(8,128)(2,1)} %get-tuple-element.78.refs_1_.refs_0_, ...), custom_call_target="tpu_custom_call" | custom-call | flops 1342177280 | bytes 5242880 | tf_op jit(solution)/shard_map/tail_grads/pallas_call | solution.py:788
  322.5 3.2 dynamic-slice_bitcast_fusion.3
  329.4 6.8 %first_back.2 = (bf16[320,1024]{1,0:T(8,128)(2,1)}, bf16[320,1024]{1,0:T(8,128)(2,1)}, f32[2,1024]{1,0:T(2,128)}) custom-call(bf16[1280,1536]{1,0:T(8,128)(2,1)} %attend_back.7.grad.grad_ref, bf16[1024,1536]{1,0:T(8,128)(2,1)} %get-tuple-element.107.weight_ref, bf16[640,1024]{1,0:T(8,128)(2,1)} %copy-done.10, bf16[1024,1280]{1,0:T(8,128)(2,1)} %tail_grads.3.refs_0_, ...), custom_call_target="tpu_custom_call" | custom-call | flops 1006632960 | bytes 3866624 | tf_op jit(solution)/shard_map/first_back/pallas_call | solution.py:665
  337.8 2.1 fusion.1
  341.5 3.1 bitcast_add_fusion.7
  346.5 6.3 %first_back.3 = (bf16[640,1024]{1,0:T(8,128)(2,1)}, f32[2,1024]{1,0:T(2,128)}) custom-call(bf16[1280,1536]{1,0:T(8,128)(2,1)} %attend_back.7.grad.grad_ref, bf16[1024,1536]{1,0:T(8,128)(2,1)} %get-tuple-element.107.weight_ref, bf16[640,1024]{1,0:T(8,128)(2,1)} %bitcast.146, bf16[320,1024]{1,0:T(8,128)(2,1)} %get-tuple-element.125.refs_0_), custom_call_target="tpu_custom_call" | custom-call | flops 1006632960 | bytes 3866624 | tf_op jit(solution)/shard_map/first_back/pallas_call | solution.py:665
  352.9 2.2 bitcast_select_fusion.2
  360.0 2.2 bitcast_add_fusion.6
  366.6 3.6 fusion
  370.2 5.0 %collective-permute-done.38 = f32[4,8,1024]{2,1,0:T(8,128)S(1)} collective-permute-done((f32[4,8,1024]{2,1,0:T(8,128)S(1)}, f32[4,8,1024]{2,1,0:T(8,128)S(1)}, u32[]{:S(2)}, u32[]{:S(2)}) %collective-permute-start.38) | collective-permute-done | bytes 131104 | tf_op jit(solution)/shard_map/ppermute | solution.py:918
  375.3 5.8 %collective-permute-done.39.refs_1_ = bf16[320,1024]{1,0:T(8,128)(2,1)S(1)} collective-permute-done((bf16[320,1024]{1,0:T(8,128)(2,1)}, bf16[320,1024]{1,0:T(8,128)(2,1)S(1)}, u32[]{:S(2)}, u32[]{:S(2)}) %collective-permute-start.39) | collective-permute-done | bytes 655392 | tf_op jit(solution)/shard_map/ppermute | solution.py:921
  384.2 2.3 reshape.102
  390.5 5.7 %input_back.1 = f32[640,1024]{1,0:T(8,128)} custom-call(bf16[640,1024]{1,0:T(8,128)(2,1)} %get-tuple-element.113.own_ref, bf16[640,1024]{1,0:T(8,128)(2,1)} %bitcast.147, f32[2,1024]{1,0:T(2,128)} %get-tuple-element.194.refs_2_.ada_ref, f32[640,1024]{1,0:T(8,128)} %get-tuple-element.114.base_ref, bf16[320,1024]{1,0:T(8,128)(2,1)} %collective-permute-done.33.refs_0_, ...), custom_call_target="tpu_custom_call" | custom-call | flops 6553600 | bytes 4587520 | tf_op jit(solution)/shard_map/input_back/pallas_call | solution.py:834
  398.2 1.9 fusion.2
  405.5 2.8 collective-permute-done.43
  409.0 3.1 collective-permute-done.42
  (228 shorter events, 73.8 us)
Async XLA Ops:
  7.2 129.6 %all-gather.3.cloned.1.call-start = ((), (), s32[]{:S(2)}) async-start(), calls=%async_computation | async-start | bytes 11141120 | tf_op jit(solution)/shard_map/all_gather | solution.py:1094
  8.7 10.6 %collective-permute-start = (f32[4,8,1024]{2,1,0:T(8,128)S(1)}, f32[4,8,1024]{2,1,0:T(8,128)S(1)}, u32[]{:S(2)}, u32[]{:S(2)}) collective-permute-start(f32[4,8,1024]{2,1,0:T(8,128)S(1)} %pad_maximum_fusion.3), channel_id=1, source_target_pairs={{0,2},{2,0},{4,6},{6,4},{8,10},{10,8},{12,14},{14,12},{16,18},{18,... | collective-permute-start | bytes 393224 | tf_op jit(solution)/shard_map/ppermute | solution.py:918
  10.9 5.0 %collective-permute-start.4 = (bf16[64,1536]{1,0:T(8,128)(2,1)}, bf16[64,1536]{1,0:T(8,128)(2,1)S(1)}, u32[]{:S(2)}, u32[]{:S(2)}) collective-permute-start(bf16[64,1536]{1,0:T(8,128)(2,1)} %pack_columns.1), channel_id=1, source_target_pairs={{0,2},{2,0},{4,6},{6,4},{8,10},{10,8},{12,14},{14,12},{16,18},{18,... | collective-permute-start | bytes 589832 | tf_op jit(solution)/shard_map/ppermute | solution.py:918
  10.9 33.2 %collective-permute-start.7 = (bf16[640,1024]{1,0:T(8,128)(2,1)}, bf16[640,1024]{1,0:T(8,128)(2,1)S(1)}, u32[]{:S(2)}, u32[]{:S(2)}) collective-permute-start(bf16[640,1024]{1,0:T(8,128)(2,1)} %bitcast.143), channel_id=1, source_target_pairs={{0,1},{1,0},{2,3},{3,2},{4,5},{5,4},{6,7},{7,6},{8,9},{9,8},{10,11... | collective-permute-start | bytes 3932168 | tf_op jit(solution)/shard_map/ppermute | solution.py:921
  17.7 12.0 %collective-permute-start.5 = (bf16[128,1536]{1,0:T(8,128)(2,1)}, bf16[128,1536]{1,0:T(8,128)(2,1)}, u32[]{:S(2)}, u32[]{:S(2)}) collective-permute-start(bf16[128,1536]{1,0:T(8,128)(2,1)} %maximum_select_fusion.refs_3_), channel_id=1, source_target_pairs={{0,8},{8,16},{16,24},{24,28},{28,20},{20,12},{12,4},{4,0},{10,2},{... | collective-permute-start | bytes 1179656 | tf_op jit(solution)/shard_map/ppermute | solution.py:934
  20.0 8.6 %collective-permute-start.1 = (f32[4,8,1024]{2,1,0:T(8,128)}, f32[4,8,1024]{2,1,0:T(8,128)}, u32[]{:S(2)}, u32[]{:S(2)}) collective-permute-start(f32[4,8,1024]{2,1,0:T(8,128)} %fusion.30), channel_id=1, source_target_pairs={{0,4},{2,6},{4,0},{6,2},{8,12},{10,14},{12,8},{14,10},{16,20},{18,... | collective-permute-start | bytes 393224 | tf_op jit(solution)/shard_map/ppermute | solution.py:918
  29.6 6.5 %collective-permute-start.2 = (f32[4,8,1024]{2,1,0:T(8,128)S(1)}, f32[4,8,1024]{2,1,0:T(8,128)S(1)}, u32[]{:S(2)}, u32[]{:S(2)}) collective-permute-start(f32[4,8,1024]{2,1,0:T(8,128)S(1)} %fusion.36), channel_id=1, source_target_pairs={{0,8},{2,10},{4,12},{6,14},{8,0},{10,2},{12,4},{14,6},{16,24},{18,... | collective-permute-start | bytes 393224 | tf_op jit(solution)/shard_map/ppermute | solution.py:918
  29.7 14.5 %collective-permute-start.6 = (bf16[128,1536]{1,0:T(8,128)(2,1)}, bf16[128,1536]{1,0:T(8,128)(2,1)}, u32[]{:S(2)}, u32[]{:S(2)}) collective-permute-start(bf16[128,1536]{1,0:T(8,128)(2,1)} %collective-permute-done.5.refs_4_), channel_id=1, source_target_pairs={{0,8},{8,16},{16,24},{24,28},{28,20},{20,12},{12,4},{4,0},{10,2},{... | collective-permute-start | bytes 1179656 | tf_op jit(solution)/shard_map/ppermute | solution.py:934
  36.1 8.0 %collective-permute-start.3 = (f32[4,8,1024]{2,1,0:T(8,128)S(1)}, f32[4,8,1024]{2,1,0:T(8,128)S(1)}, u32[]{:S(2)}, u32[]{:S(2)}) collective-permute-start(f32[4,8,1024]{2,1,0:T(8,128)S(1)} %add.86), channel_id=1, source_target_pairs={{0,16},{2,18},{4,20},{6,22},{8,24},{10,26},{12,28},{14,30},{16,0},... | collective-permute-start | bytes 393224 | tf_op jit(solution)/shard_map/ppermute | solution.py:918
  45.2 35.2 %collective-permute-start.13 = (bf16[640,1024]{1,0:T(8,128)(2,1)S(1)}, bf16[640,1024]{1,0:T(8,128)(2,1)S(1)}, u32[]{:S(2)}, u32[]{:S(2)}) collective-permute-start(bf16[640,1024]{1,0:T(8,128)(2,1)S(1)} %bitcast.142), channel_id=1, source_target_pairs={{0,1},{1,0},{2,3},{3,2},{4,5},{5,4},{6,7},{7,6},{8,9},{9,8},{10,11... | collective-permute-start | bytes 3932168 | tf_op jit(solution)/shard_map/ppermute | solution.py:921
  45.8 8.4 %collective-permute-start.8 = (bf16[128,1536]{1,0:T(8,128)(2,1)}, bf16[128,1536]{1,0:T(8,128)(2,1)S(1)}, u32[]{:S(2)}, u32[]{:S(2)}) collective-permute-start(bf16[128,1536]{1,0:T(8,128)(2,1)} %collective-permute-done.6.refs_5_), channel_id=1, source_target_pairs={{0,8},{8,16},{16,24},{24,28},{28,20},{20,12},{12,4},{4,0},{10,2},{... | collective-permute-start | bytes 1179656 | tf_op jit(solution)/shard_map/ppermute | solution.py:934
  48.6 10.0 %collective-permute-start.10 = (bf16[128,1536]{1,0:T(8,128)(2,1)}, bf16[128,1536]{1,0:T(8,128)(2,1)}, u32[]{:S(2)}, u32[]{:S(2)}) collective-permute-start(bf16[128,1536]{1,0:T(8,128)(2,1)} %collective-permute-done.5.refs_4_), channel_id=1, source_target_pairs={{0,2},{2,0},{4,6},{6,4},{8,10},{10,8},{12,14},{14,12},{16,18},{18,... | collective-permute-start | bytes 1179656 | tf_op jit(solution)/shard_map/ppermute | solution.py:918
  48.6 10.0 %collective-permute-start.11 = (bf16[128,1536]{1,0:T(8,128)(2,1)}, bf16[128,1536]{1,0:T(8,128)(2,1)}, u32[]{:S(2)}, u32[]{:S(2)}) collective-permute-start(bf16[128,1536]{1,0:T(8,128)(2,1)} %collective-permute-done.6.refs_5_), channel_id=1, source_target_pairs={{0,2},{2,0},{4,6},{6,4},{8,10},{10,8},{12,14},{14,12},{16,18},{18,... | collective-permute-start | bytes 1179656 | tf_op jit(solution)/shard_map/ppermute | solution.py:918
  54.2 14.9 %collective-permute-start.9 = (bf16[128,1536]{1,0:T(8,128)(2,1)S(1)}, bf16[128,1536]{1,0:T(8,128)(2,1)}, u32[]{:S(2)}, u32[]{:S(2)}) collective-permute-start(bf16[128,1536]{1,0:T(8,128)(2,1)S(1)} %collective-permute-done.8.refs_6_), channel_id=1, source_target_pairs={{0,8},{8,16},{16,24},{24,28},{28,20},{20,12},{12,4},{4,0},{10,2},{... | collective-permute-start | bytes 1179656 | tf_op jit(solution)/shard_map/ppermute | solution.py:934
  55.4 13.7 %collective-permute-start.12 = (bf16[128,1536]{1,0:T(8,128)(2,1)S(1)}, bf16[128,1536]{1,0:T(8,128)(2,1)}, u32[]{:S(2)}, u32[]{:S(2)}) collective-permute-start(bf16[128,1536]{1,0:T(8,128)(2,1)S(1)} %collective-permute-done.8.refs_6_), channel_id=1, source_target_pairs={{0,2},{2,0},{4,6},{6,4},{8,10},{10,8},{12,14},{14,12},{16,18},{18,... | collective-permute-start | bytes 1179656 | tf_op jit(solution)/shard_map/ppermute | solution.py:918
  97.3 17.3 %collective-permute-start.14 = (bf16[1280,256]{1,0:T(8,128)(2,1)}, bf16[1280,256]{1,0:T(8,128)(2,1)S(1)}, u32[]{:S(2)}, u32[]{:S(2)}) collective-permute-start(bf16[1280,256]{1,0:T(8,128)(2,1)} %get-tuple-element.78.refs_1_.refs_0_), channel_id=1, source_target_pairs={{0,1},{1,0},{2,3},{3,2},{4,5},{5,4},{6,7},{7,6},{8,9},{9,8},{10,11... | collective-permute-start | bytes 1966088 | tf_op jit(solution)/shard_map/ppermute | solution.py:921
  114.7 16.7 %collective-permute-start.15 = (bf16[1280,256]{1,0:T(8,128)(2,1)}, bf16[1280,256]{1,0:T(8,128)(2,1)S(1)}, u32[]{:S(2)}, u32[]{:S(2)}) collective-permute-start(bf16[1280,256]{1,0:T(8,128)(2,1)} %get-tuple-element.81.refs_1_), channel_id=1, source_target_pairs={{0,1},{1,0},{2,3},{3,2},{4,5},{5,4},{6,7},{7,6},{8,9},{9,8},{10,11... | collective-permute-start | bytes 1966088 | tf_op jit(solution)/shard_map/ppermute | solution.py:921
  172.1 17.1 %collective-permute-start.16 = (bf16[320,1024]{1,0:T(8,128)(2,1)}, bf16[320,1024]{1,0:T(8,128)(2,1)S(1)}, u32[]{:S(2)}, u32[]{:S(2)}) collective-permute-start(bf16[320,1024]{1,0:T(8,128)(2,1)} %get-tuple-element.87.refs_5_), channel_id=1, source_target_pairs={{0,1},{1,0},{2,3},{3,2},{4,5},{5,4},{6,7},{7,6},{8,9},{9,8},{10,11... | collective-permute-start | bytes 1966088 | tf_op jit(solution)/shard_map/ppermute | solution.py:921
  189.3 9.7 %collective-permute-start.17 = (bf16[1024,2048]{1,0:T(8,128)(2,1)}, bf16[1024,2048]{1,0:T(8,128)(2,1)}, u32[]{:S(2)}, u32[]{:S(2)}) collective-permute-start(bf16[1024,2048]{1,0:T(8,128)(2,1)} %hidden_grads.2.refs_0_), channel_id=1, source_target_pairs={{0,2},{2,0},{4,6},{6,4},{8,10},{10,8},{12,14},{14,12},{16,18},{18,... | collective-permute-start | bytes 12582920 | tf_op jit(solution)/shard_map/ppermute | solution.py:918
  189.3 27.1 %collective-permute-start.20 = (bf16[320,1024]{1,0:T(8,128)(2,1)S(1)}, bf16[320,1024]{1,0:T(8,128)(2,1)S(1)}, u32[]{:S(2)}, u32[]{:S(2)}) collective-permute-start(bf16[320,1024]{1,0:T(8,128)(2,1)S(1)} %copy-done.39), channel_id=1, source_target_pairs={{0,1},{1,0},{2,3},{3,2},{4,5},{5,4},{6,7},{7,6},{8,9},{9,8},{10,11... | collective-permute-start | bytes 1966088 | tf_op jit(solution)/shard_map/ppermute | solution.py:921
  214.3 19.8 %collective-permute-start.18 = (bf16[128,2048]{1,0:T(8,128)(2,1)S(1)}, bf16[128,2048]{1,0:T(8,128)(2,1)S(1)}, u32[]{:S(2)}, u32[]{:S(2)}) collective-permute-start(bf16[128,2048]{1,0:T(8,128)(2,1)S(1)} %get-tuple-element.138), channel_id=1, source_target_pairs={{0,8},{2,10},{8,16},{10,18},{16,24},{18,26},{24,28},{26,30},{28,20... | collective-permute-start | bytes 1572872 | tf_op jit(solution)/shard_map/ppermute | solution.py:995
  214.9 19.3 %collective-permute-start.19 = (bf16[128,2048]{1,0:T(8,128)(2,1)S(1)}, bf16[128,2048]{1,0:T(8,128)(2,1)S(1)}, u32[]{:S(2)}, u32[]{:S(2)}) collective-permute-start(bf16[128,2048]{1,0:T(8,128)(2,1)S(1)} %get-tuple-element.137), channel_id=1, source_target_pairs={{8,0},{10,2},{16,8},{18,10},{24,16},{26,18},{28,24},{30,26},{20,28... | collective-permute-start | bytes 1572872 | tf_op jit(solution)/shard_map/ppermute | solution.py:995
  226.2 20.4 %collective-permute-start.22 = (bf16[640,512]{1,0:T(8,128)(2,1)}, bf16[640,512]{1,0:T(8,128)(2,1)S(1)}, u32[]{:S(2)}, u32[]{:S(2)}) collective-permute-start(bf16[640,512]{1,0:T(8,128)(2,1)} %get-tuple-element.92.refs_0_), channel_id=1, source_target_pairs={{0,1},{1,0},{2,3},{3,2},{4,5},{5,4},{6,7},{7,6},{8,9},{9,8},{10,11... | collective-permute-start | bytes 1966088 | tf_op jit(solution)/shard_map/ppermute | solution.py:921
  236.6 22.6 %collective-permute-start.23 = (bf16[128,2048]{1,0:T(8,128)(2,1)S(1)}, bf16[128,2048]{1,0:T(8,128)(2,1)S(1)}, u32[]{:S(2)}, u32[]{:S(2)}) collective-permute-start(bf16[128,2048]{1,0:T(8,128)(2,1)S(1)} %get-tuple-element.136), channel_id=1, source_target_pairs={{0,8},{2,10},{8,16},{10,18},{16,24},{18,26},{24,28},{26,30},{28,20... | collective-permute-start | bytes 1572872 | tf_op jit(solution)/shard_map/ppermute | solution.py:995
  237.2 22.1 %collective-permute-start.24 = (bf16[128,2048]{1,0:T(8,128)(2,1)S(1)}, bf16[128,2048]{1,0:T(8,128)(2,1)S(1)}, u32[]{:S(2)}, u32[]{:S(2)}) collective-permute-start(bf16[128,2048]{1,0:T(8,128)(2,1)S(1)} %get-tuple-element.135), channel_id=1, source_target_pairs={{8,0},{10,2},{16,8},{18,10},{24,16},{26,18},{28,24},{30,26},{20,28... | collective-permute-start | bytes 1572872 | tf_op jit(solution)/shard_map/ppermute | solution.py:995
  261.7 14.2 %collective-permute-start.25 = (bf16[128,2048]{1,0:T(8,128)(2,1)S(1)}, bf16[128,2048]{1,0:T(8,128)(2,1)S(1)}, u32[]{:S(2)}, u32[]{:S(2)}) collective-permute-start(bf16[128,2048]{1,0:T(8,128)(2,1)S(1)} %get-tuple-element.134), channel_id=1, source_target_pairs={{0,8},{2,10},{8,16},{10,18},{16,24},{18,26},{24,28},{26,30},{28,20... | collective-permute-start | bytes 1572872 | tf_op jit(solution)/shard_map/ppermute | solution.py:995
  262.3 13.7 %collective-permute-start.26 = (bf16[128,2048]{1,0:T(8,128)(2,1)S(1)}, bf16[128,2048]{1,0:T(8,128)(2,1)S(1)}, u32[]{:S(2)}, u32[]{:S(2)}) collective-permute-start(bf16[128,2048]{1,0:T(8,128)(2,1)S(1)} %get-tuple-element.133), channel_id=1, source_target_pairs={{8,0},{10,2},{16,8},{18,10},{24,16},{26,18},{28,24},{30,26},{20,28... | collective-permute-start | bytes 1572872 | tf_op jit(solution)/shard_map/ppermute | solution.py:995
  285.0 28.0 %collective-permute-start.28 = (bf16[1024,1280]{1,0:T(8,128)(2,1)}, bf16[1024,1280]{1,0:T(8,128)(2,1)}, u32[]{:S(2)}, u32[]{:S(2)}) collective-permute-start(bf16[1024,1280]{1,0:T(8,128)(2,1)} %tail_grads.2.refs_7_), channel_id=1, source_target_pairs={{0,2},{2,0},{4,6},{6,4},{8,10},{10,8},{12,14},{14,12},{16,18},{18,... | collective-permute-start | bytes 7864328 | tf_op jit(solution)/shard_map/ppermute | solution.py:918
  286.8 14.4 %collective-permute-start.27 = (bf16[128,2048]{1,0:T(8,128)(2,1)S(1)}, bf16[128,2048]{1,0:T(8,128)(2,1)S(1)}, u32[]{:S(2)}, u32[]{:S(2)}) collective-permute-start(bf16[128,2048]{1,0:T(8,128)(2,1)S(1)} %bitcast_add_fusion.4), channel_id=1, source_target_pairs={{0,8},{2,10},{8,16},{10,18},{16,24},{18,26},{24,28},{26,30},{28,20... | collective-permute-start | bytes 1572872 | tf_op jit(solution)/shard_map/ppermute | solution.py:995
  287.4 41.0 %collective-permute-start.21 = (bf16[640,1024]{1,0:T(8,128)(2,1)S(1)}, bf16[640,1024]{1,0:T(8,128)(2,1)S(1)}, u32[]{:S(2)}, u32[]{:S(2)}) collective-permute-start(bf16[640,1024]{1,0:T(8,128)(2,1)S(1)} %copy-done.9), channel_id=1, source_target_pairs={{0,1},{1,0},{2,3},{3,2},{4,5},{5,4},{6,7},{7,6},{8,9},{9,8},{10,11... | collective-permute-start | bytes 3932168 | tf_op jit(solution)/shard_map/ppermute | solution.py:921
  325.7 12.1 %collective-permute-start.29 = (bf16[128,1280]{1,0:T(8,128)(2,1)}, bf16[128,1280]{1,0:T(8,128)(2,1)S(1)}, u32[]{:S(2)}, u32[]{:S(2)}) collective-permute-start(bf16[128,1280]{1,0:T(8,128)(2,1)} %get-tuple-element.144), channel_id=1, source_target_pairs={{0,8},{2,10},{8,16},{10,18},{16,24},{18,26},{24,28},{26,30},{28,20... | collective-permute-start | bytes 983048 | tf_op jit(solution)/shard_map/ppermute | solution.py:995
  326.7 11.1 %collective-permute-start.30 = (bf16[128,1280]{1,0:T(8,128)(2,1)}, bf16[128,1280]{1,0:T(8,128)(2,1)}, u32[]{:S(2)}, u32[]{:S(2)}) collective-permute-start(bf16[128,1280]{1,0:T(8,128)(2,1)} %get-tuple-element.143), channel_id=1, source_target_pairs={{8,0},{10,2},{16,8},{18,10},{24,16},{26,18},{28,24},{30,26},{20,28... | collective-permute-start | bytes 983048 | tf_op jit(solution)/shard_map/ppermute | solution.py:995
  336.3 18.9 %collective-permute-start.33 = (bf16[320,1024]{1,0:T(8,128)(2,1)}, bf16[320,1024]{1,0:T(8,128)(2,1)}, u32[]{:S(2)}, u32[]{:S(2)}) collective-permute-start(bf16[320,1024]{1,0:T(8,128)(2,1)} %get-tuple-element.118), channel_id=1, source_target_pairs={{0,1},{1,0},{2,3},{3,2},{4,5},{5,4},{6,7},{7,6},{8,9},{9,8},{10,11... | collective-permute-start | bytes 1966088 | tf_op jit(solution)/shard_map/ppermute | solution.py:921
  341.4 11.5 %collective-permute-start.44 = (f32[64,1024]{1,0:T(8,128)S(1)}, f32[64,1024]{1,0:T(8,128)}, u32[]{:S(2)}, u32[]{:S(2)}) collective-permute-start(f32[64,1024]{1,0:T(8,128)S(1)} %dynamic-slice_bitcast_fusion.5), channel_id=1, source_target_pairs={{0,2},{2,0},{4,6},{6,4},{8,10},{10,8},{12,14},{14,12},{16,18},{18,... | collective-permute-start | bytes 786440 | tf_op jit(solution)/shard_map/ppermute | solution.py:918
  344.5 10.6 %collective-permute-start.31 = (bf16[128,1280]{1,0:T(8,128)(2,1)}, bf16[128,1280]{1,0:T(8,128)(2,1)S(1)}, u32[]{:S(2)}, u32[]{:S(2)}) collective-permute-start(bf16[128,1280]{1,0:T(8,128)(2,1)} %get-tuple-element.142), channel_id=1, source_target_pairs={{0,8},{2,10},{8,16},{10,18},{16,24},{18,26},{24,28},{26,30},{28,20... | collective-permute-start | bytes 983048 | tf_op jit(solution)/shard_map/ppermute | solution.py:995
  345.0 10.1 %collective-permute-start.32 = (bf16[128,1280]{1,0:T(8,128)(2,1)}, bf16[128,1280]{1,0:T(8,128)(2,1)}, u32[]{:S(2)}, u32[]{:S(2)}) collective-permute-start(bf16[128,1280]{1,0:T(8,128)(2,1)} %get-tuple-element.141), channel_id=1, source_target_pairs={{8,0},{10,2},{16,8},{18,10},{24,16},{26,18},{28,24},{30,26},{20,28... | collective-permute-start | bytes 983048 | tf_op jit(solution)/shard_map/ppermute | solution.py:995
  355.9 3.9 collective-permute-start.36
  357.0 25.7 %collective-permute-start.45 = (f32[32,2048]{1,0:T(8,128)S(1)}, f32[32,2048]{1,0:T(8,128)S(1)}, u32[]{:S(2)}, u32[]{:S(2)}) collective-permute-start(f32[32,2048]{1,0:T(8,128)S(1)} %fusion.7), channel_id=1, source_target_pairs={{0,1},{1,0},{2,3},{3,2},{4,5},{5,4},{6,7},{7,6},{8,9},{9,8},{10,11... | collective-permute-start | bytes 786440 | tf_op jit(solution)/shard_map/ppermute | solution.py:921
  359.9 5.5 %collective-permute-start.37 = (f32[4,8,1024]{2,1,0:T(8,128)S(1)}, f32[4,8,1024]{2,1,0:T(8,128)S(1)}, u32[]{:S(2)}, u32[]{:S(2)}) collective-permute-start(f32[4,8,1024]{2,1,0:T(8,128)S(1)} %broadcast_multiply_fusion), channel_id=1, source_target_pairs={{0,2},{2,0},{4,6},{6,4},{8,10},{10,8},{12,14},{14,12},{16,18},{18,... | collective-permute-start | bytes 393224 | tf_op jit(solution)/shard_map/ppermute | solution.py:918
  362.2 13.1 %collective-permute-start.34 = (bf16[128,1280]{1,0:T(8,128)(2,1)S(1)}, bf16[128,1280]{1,0:T(8,128)(2,1)S(1)}, u32[]{:S(2)}, u32[]{:S(2)}) collective-permute-start(bf16[128,1280]{1,0:T(8,128)(2,1)S(1)} %get-tuple-element.140), channel_id=1, source_target_pairs={{0,8},{2,10},{8,16},{10,18},{16,24},{18,26},{24,28},{26,30},{28,20... | collective-permute-start | bytes 983048 | tf_op jit(solution)/shard_map/ppermute | solution.py:995
  364.0 11.4 %collective-permute-start.35 = (bf16[128,1280]{1,0:T(8,128)(2,1)S(1)}, bf16[128,1280]{1,0:T(8,128)(2,1)S(1)}, u32[]{:S(2)}, u32[]{:S(2)}) collective-permute-start(bf16[128,1280]{1,0:T(8,128)(2,1)S(1)} %get-tuple-element.139), channel_id=1, source_target_pairs={{8,0},{10,2},{16,8},{18,10},{24,16},{26,18},{28,24},{30,26},{20,28... | collective-permute-start | bytes 983048 | tf_op jit(solution)/shard_map/ppermute | solution.py:995
  364.3 16.8 %collective-permute-start.39 = (bf16[320,1024]{1,0:T(8,128)(2,1)}, bf16[320,1024]{1,0:T(8,128)(2,1)S(1)}, u32[]{:S(2)}, u32[]{:S(2)}) collective-permute-start(bf16[320,1024]{1,0:T(8,128)(2,1)} %get-tuple-element.125.refs_0_), channel_id=1, source_target_pairs={{0,1},{1,0},{2,3},{3,2},{4,5},{5,4},{6,7},{7,6},{8,9},{9,8},{10,11... | collective-permute-start | bytes 1966088 | tf_op jit(solution)/shard_map/ppermute | solution.py:921
  365.5 9.7 %collective-permute-start.38 = (f32[4,8,1024]{2,1,0:T(8,128)S(1)}, f32[4,8,1024]{2,1,0:T(8,128)S(1)}, u32[]{:S(2)}, u32[]{:S(2)}) collective-permute-start(f32[4,8,1024]{2,1,0:T(8,128)S(1)} %fusion.24), channel_id=1, source_target_pairs={{0,4},{2,6},{4,0},{6,2},{8,12},{10,14},{12,8},{14,10},{16,20},{18,... | collective-permute-start | bytes 393224 | tf_op jit(solution)/shard_map/ppermute | solution.py:918
  381.1 5.4 %collective-permute-start.46 = (f32[4,8,1024]{2,1,0:T(8,128)S(1)}, f32[4,8,1024]{2,1,0:T(8,128)S(1)}, u32[]{:S(2)}, u32[]{:S(2)}) collective-permute-start(f32[4,8,1024]{2,1,0:T(8,128)S(1)} %fusion.35), channel_id=1, source_target_pairs={{0,8},{2,10},{4,12},{6,14},{8,0},{10,2},{12,4},{14,6},{16,24},{18,... | collective-permute-start | bytes 393224 | tf_op jit(solution)/shard_map/ppermute | solution.py:918
  386.5 9.8 %collective-permute-start.47 = (f32[4,8,1024]{2,1,0:T(8,128)S(1)}, f32[4,8,1024]{2,1,0:T(8,128)S(1)}, u32[]{:S(2)}, u32[]{:S(2)}) collective-permute-start(f32[4,8,1024]{2,1,0:T(8,128)S(1)} %add.109), channel_id=1, source_target_pairs={{0,16},{2,18},{4,20},{6,22},{8,24},{10,26},{12,28},{14,30},{16,0},... | collective-permute-start | bytes 393224 | tf_op jit(solution)/shard_map/ppermute | solution.py:918
  389.3 8.8 %collective-permute-start.40 = (bf16[128,1280]{1,0:T(8,128)(2,1)S(1)}, bf16[128,1280]{1,0:T(8,128)(2,1)}, u32[]{:S(2)}, u32[]{:S(2)}) collective-permute-start(bf16[128,1280]{1,0:T(8,128)(2,1)S(1)} %bitcast_add_fusion.5), channel_id=1, source_target_pairs={{0,8},{2,10},{8,16},{10,18},{16,24},{18,26},{24,28},{26,30},{28,20... | collective-permute-start | bytes 983048 | tf_op jit(solution)/shard_map/ppermute | solution.py:995
  403.3 5.0 %collective-permute-start.43 = (bf16[32,1024]{1,0:T(8,128)(2,1)S(1)}, bf16[32,1024]{1,0:T(8,128)(2,1)S(1)}, u32[]{:S(2)}, u32[]{:S(2)}) collective-permute-start(bf16[32,1024]{1,0:T(8,128)(2,1)S(1)} %fusion.19), channel_id=1, source_target_pairs={{0,1},{1,0},{2,3},{3,2},{4,5},{5,4},{6,7},{7,6},{8,9},{9,8},{10,11... | collective-permute-start | bytes 196616 | tf_op jit(solution)/shard_map/ppermute | solution.py:921
  404.5 7.6 %collective-permute-start.42 = (f32[32,1536]{1,0:T(8,128)S(1)}, f32[32,1536]{1,0:T(8,128)S(1)}, u32[]{:S(2)}, u32[]{:S(2)}) collective-permute-start(f32[32,1536]{1,0:T(8,128)S(1)} %fusion.16), channel_id=1, source_target_pairs={{0,1},{1,0},{2,3},{3,2},{4,5},{5,4},{6,7},{7,6},{8,9},{9,8},{10,11... | collective-permute-start | bytes 589832 | tf_op jit(solution)/shard_map/ppermute | solution.py:921
  (42 other events, 369.8 us)
Sparse Core Ops, SparseCore 0:
  44.3 92.4 all-gather.2

commit v6 on v5

--- a/solution.py
+++ b/solution.py
@@ -841,6 +841,48 @@
         cost_estimate=cost(20 * rows * width, 14 * rows * width),
         name="input_back",
     )(own, tokens, ada, base, *others)
+
+
+def join_tail_kernel(held, place, mine, seq_ref, core_ref, both_ref, *outs):
+    core, seq = place[2], place[4]
+    half = 3 * held // 2
+    width = held // 2
+
+    def chosen(side, core_half, spot):
+        near = jnp.where(core == core_half, mine[:, spot], core_ref[:, spot])
+        far = jnp.where(core == core_half, seq_ref[:, spot], both_ref[:, spot])
+        return jnp.where(seq == side, near, far)
+
+    for side in range(2):
+        for core_half in range(2):
+            for pair in range(width // LANES):
+                for which in range(3):
+                    start = (3 * pair + which) * LANES
+                    to = side * held + core_half * width + pair * LANES
+                    value = chosen(side, core_half, slice(start, start + LANES))
+                    outs[which][:, to : to + LANES] = value
+    for core_half in range(2):
+        spot = slice(half, None)
+        near = jnp.where(core == core_half, mine[:, spot], core_ref[:, spot])
+        far = jnp.where(core == core_half, seq_ref[:, spot], both_ref[:, spot])
+        outs[3][:, core_half * held : (core_half + 1) * held] = near + far
+
+
+def join_tail(place, parts, held):
+    rows, columns = parts[0].shape
+    whole = lambda size: pl.BlockSpec((rows, size), lambda j, s: (0, 0))
+    return pl.pallas_call(
+        partial(join_tail_kernel, held),
+        grid_spec=pltpu.PrefetchScalarGridSpec(
+            num_scalar_prefetch=1,
+            grid=(1,),
+            in_specs=[whole(columns)] * 4,
+            out_specs=[whole(2 * held)] * 4,
+        ),
+        out_shape=[jax.ShapeDtypeStruct((rows, 2 * held), jnp.float32)] * 4,
+        cost_estimate=cost(0, 16 * rows * columns),
+        name="join_tail",
+    )(place, *parts)
 
 
 def exact(left, right):
@@ -912,10 +954,15 @@
         self.beside = row[self.chips + 1]
         self.spots = row[self.chips + 2 :]
         self.seq = lax.axis_index("seq")
+        self.quarter = 2 * self.core + self.seq
 
     def flip(self, value, bit):
         pairs = [(i, i ^ bit) for i in range(self.items_count)]
         return lax.ppermute(value, "items", pairs)
+
+    def opposite(self, value):
+        pairs = [(2 * i + x, 2 * (i ^ 1) + 1 - x) for i in range(self.items_count) for x in (0, 1)]
+        return lax.ppermute(value, ("items", "seq"), pairs)
 
     def across(self, value):
         return lax.ppermute(value, "seq", [(0, 1), (1, 0)])
@@ -1249,7 +1296,9 @@
         last_half = tail.advance(last_half)
         hidden_total, last_half = ring.finish(last_half)
         own_first, own_rows = first_back(grad_qkv, qkv_w, frames[0], 0, [last_half])
-        own_rows, near_half, last_half = tail.advance([own_rows, near_half, last_half])
+        own_rows, near_half, last_half, out_other = tail.advance(
+            [own_rows, near_half, last_half, out_other]
+        )
         far_parts = [near_half, mover.across(last_half)]
         ada_rows = jnp.concatenate([own_rows + far_rows, ada_two_rows])
         ada_rows = ada_rows + mover.across(ada_rows)
@@ -1270,8 +1319,10 @@
     sums = choose[None, :, None] * ada_rows[:, None, :]
     for bit in [1 << k for k in range(items_count.bit_length() - 1)]:
         sums = sums + mover.flip(sums, bit)
-        if bit == 2:
-            sums, far_parts = tail.advance([sums, far_parts])
+        if bit == 1:
+            sums = tail.advance(sums)
+        if bit == 4:
+            sums, far_parts = tie(sums, far_parts)
     input_grad = input_back(own_first, far_parts, tokens, ada_one, grad_attended)
     out_piece = piece // seq_count
     first_row = mover.item * piece + mover.seq * out_piece
@@ -1292,27 +1343,38 @@
         [side.reshape(out_piece, 2, chips, units) for side in up_sides], axis=1
     )
     grad_up = grad_up.transpose(0, 3, 2, 1, 4).reshape(out_piece, hidden * seq_count)
-    tail_total = tail.finish()
-    cores = jnp.concatenate(mover.join_cores(tail_total), axis=1)
-    half_qkv = 3 * held // 2
-    half_all = cores.shape[1] // 2
-    qkv_total = jnp.concatenate(
-        [cores[:, :half_qkv], cores[:, half_all : half_all + half_qkv]], axis=1
-    )
-    out_total = jnp.concatenate([cores[:, half_qkv:half_all], cores[:, half_all + half_qkv :]], axis=1)
-    sides = mover.join_columns(qkv_total)
-    grad_out = mover.scatter_seq(out_total)
-    grad_query, grad_key, grad_value = (
-        jnp.concatenate(
-            [
-                side[:, (3 * p + j) * LANES : (3 * p + j + 1) * LANES]
-                for side in sides
-                for p in range(pairs)
-            ],
-            axis=1,
+    if mover.pair:
+        quarters_of = tail.finish().reshape(4, piece // 2, -1)
+        mine, to_seq, to_core, to_both = (
+            pick(quarters_of, mover.quarter ^ flipped, 0) for flipped in (0, 1, 2, 3)
         )
-        for j in range(3)
-    )
+        grad_query, grad_key, grad_value, grad_out = join_tail(
+            place,
+            [mine, mover.across(to_seq), mover.flip(to_core, 1), mover.opposite(to_both)],
+            held,
+        )
+    else:
+        tail_total = tail.finish()
+        cores = jnp.concatenate(mover.join_cores(tail_total), axis=1)
+        half_qkv = 3 * held // 2
+        half_all = cores.shape[1] // 2
+        qkv_total = jnp.concatenate(
+            [cores[:, :half_qkv], cores[:, half_all : half_all + half_qkv]], axis=1
+        )
+        out_total = jnp.concatenate([cores[:, half_qkv:half_all], cores[:, half_all + half_qkv :]], axis=1)
+        sides = mover.join_columns(qkv_total)
+        grad_out = mover.scatter_seq(out_total)
+        grad_query, grad_key, grad_value = (
+            jnp.concatenate(
+                [
+                    side[:, (3 * p + j) * LANES : (3 * p + j + 1) * LANES]
+                    for side in sides
+                    for p in range(pairs)
+                ],
+                axis=1,
+            )
+            for j in range(3)
+        )
     return (
         layer_out.reshape(batch, rows, width),
         input_grad.reshape(batch, rows, width),

time: 425 us -> 416 us (0.979)
  waiting for transfers between devices: 75.7 us -> 67.8 us
    ppermute x14 -> x13, waiting for transfers between devices: 33.8 us -> 25.3 us  [across(): return lax.ppermute(value, 'seq', [(0, 1), (1, 0)])]
    ppermute x14 -> x13, starting transfers between devices: 16.5 us -> 14.2 us  [across(): return lax.ppermute(value, 'seq', [(0, 1), (1, 0)])]
  transfers between devices with their start and end apart: 49 -> 49, of which waited for: 16 -> 16; matrix products, arithmetic and copies ran while one was open for 11% -> 12% of each run, Pallas kernels for 42% -> 43%
where the time goes in v6:
time: 416 us; the launch traced here: 411 us
  Pallas kernels  225 us (54%)
  waiting for transfers between devices  67.8 us (16%)
  starting transfers between devices  41.5 us (10%)
  other arithmetic  30.7 us (7%)
  local copies, waits for them, and re-layouts  25.5 us (6%)
  between operations  17.5 us (4%)
    pallas_call x4, Pallas kernels, attend_back(): pl.pallas_call(partial(attend_back_kernel, parts, calls, per, at), grid_s...  47.6 us
    pallas_call x2, Pallas kernels, attend(): pl.pallas_call(attend_kernel, grid_spec=pltpu.PrefetchScalarGridSpec(num_...  31.6 us
    pallas_call x4, Pallas kernels, hidden_to_width(): pl.pallas_call(partial(kernel, splits), grid=(weights.steps,), in_specs=[...  30.7 us
    ppermute x13, waiting for transfers between devices, across(): return lax.ppermute(value, 'seq', [(0, 1), (1, 0)])  25.3 us
    pallas_call x2, Pallas kernels, hidden_grads(): pl.pallas_call(partial(hidden_grads_kernel, count, bool(more)), grid_spec...  25.3 us
    ppermute x16, waiting for transfers between devices, flip(): return lax.ppermute(value, 'items', pairs)  19.2 us
    pallas_call x1, Pallas kernels, hidden_layer(): pl.pallas_call(partial(hidden_kernel, weights.per_chip, len(grads)), grid...  18.5 us
    pallas_call x2, Pallas kernels, tail_grads(): pl.pallas_call(partial(tail_grads_kernel, first, bool(more), len(mixed) +...  18.4 us
  transfers between devices with their start and end apart: 49, of which 16 were waited for; matrix products, arithmetic and copies ran while one was open for 12% of the time, Pallas kernels for 43%

profile of v6, /device:TPU:0, one launch (start us, length us, event | category | flops | bytes accessed | tf_op | source)
XLA Modules:
  0.0 411.4 jit_solution(8164201725158678894)
XLA Ops:
  10.9 2.9 collective-permute-start.7
  15.9 1.8 maximum_select_fusion.refs_3_
  22.3 6.3 %collective-permute-done.1 = f32[4,8,1024]{2,1,0:T(8,128)} collective-permute-done((f32[4,8,1024]{2,1,0:T(8,128)}, f32[4,8,1024]{2,1,0:T(8,128)}, u32[]{:S(2)}, u32[]{:S(2)}) %collective-permute-start.1) | collective-permute-done | bytes 131104 | tf_op jit(solution)/shard_map/ppermute | solution.py:961
  29.8 2.0 collective-permute-start.6
  32.8 3.4 collective-permute-done.2
  37.0 1.8 pad_maximum_fusion
  38.8 5.4 %collective-permute-done.3 = f32[4,8,1024]{2,1,0:T(8,128)S(1)} collective-permute-done((f32[4,8,1024]{2,1,0:T(8,128)S(1)}, f32[4,8,1024]{2,1,0:T(8,128)S(1)}, u32[]{:S(2)}, u32[]{:S(2)}) %collective-permute-start.3) | collective-permute-done | bytes 131104 | tf_op jit(solution)/shard_map/ppermute | solution.py:961
  49.1 5.1 %collective-permute-done.8.refs_6_ = bf16[128,1536]{1,0:T(8,128)(2,1)S(1)} collective-permute-done((bf16[128,1536]{1,0:T(8,128)(2,1)}, bf16[128,1536]{1,0:T(8,128)(2,1)S(1)}, u32[]{:S(2)}, u32[]{:S(2)}) %collective-permute-start.8) | collective-permute-done | bytes 393248 | tf_op jit(solution)/shard_map/ppermute | solution.py:981
  56.1 2.0 stack.41.place
  58.7 10.3 %collective-permute-done.9.refs_7_ = bf16[128,1536]{1,0:T(8,128)(2,1)} collective-permute-done((bf16[128,1536]{1,0:T(8,128)(2,1)S(1)}, bf16[128,1536]{1,0:T(8,128)(2,1)}, u32[]{:S(2)}, u32[]{:S(2)}) %collective-permute-start.9) | collective-permute-done | bytes 393248 | tf_op jit(solution)/shard_map/ppermute | solution.py:981
  69.1 11.3 %first_layer.1 = (bf16[1280,1024]{1,0:T(8,128)(2,1)}, bf16[1280,1536]{1,0:T(8,128)(2,1)}, bf16[1024,1536]{1,0:T(8,128)(2,1)}) custom-call(s32[8]{0:T(128)} %slice_bitcast_fusion.8.spots, bf16[640,1024]{1,0:T(8,128)(2,1)} %bitcast.147, bf16[640,1024]{1,0:T(8,128)(2,1)} %copy-done.10, f32[2,1024]{1,0:T(2,128)} %get-tuple-element.182.refs_2_.ada_ref, ...), custom_call_target="tpu_custom_call" | custom-call | flops 2013265920 | bytes 8388608 | tf_op jit(solution)/shard_map/first_layer/pallas_call | solution.py:347
  81.5 15.8 %attend.2 = (bf16[1280,256]{1,0:T(8,128)(2,1)}, f32[2,10,256]{2,1,0:T(8,128)}) custom-call(s32[5]{0:T(128)} %stack.41.place, bf16[1280,1536]{1,0:T(8,128)(2,1)} %get-tuple-element.82.q_ref.k_ref.v_ref, bf16[1280,1536]{1,0:T(8,128)(2,1)} %get-tuple-element.82.q_ref.k_ref.v_ref, bf16[1280,1536]{1,0:T(8,128)(2,1)} %get-tuple-element.82.q_ref.k_ref.v_ref, ...), custom_call_target="tpu_custom_call" | custom-call | flops 2516582400 | bytes 2621440 | tf_op jit(solution)/shard_map/attend/pallas_call | solution.py:91
  97.7 15.8 %attend.3 = (bf16[1280,256]{1,0:T(8,128)(2,1)}, f32[2,10,256]{2,1,0:T(8,128)}) custom-call(s32[5]{0:T(128)} %stack.41.place, bf16[1280,1536]{1,0:T(8,128)(2,1)} %get-tuple-element.82.q_ref.k_ref.v_ref, bf16[1280,1536]{1,0:T(8,128)(2,1)} %get-tuple-element.82.q_ref.k_ref.v_ref, bf16[1280,1536]{1,0:T(8,128)(2,1)} %get-tuple-element.82.q_ref.k_ref.v_ref, ...), custom_call_target="tpu_custom_call" | custom-call | flops 2516582400 | bytes 2621440 | tf_op jit(solution)/shard_map/attend/pallas_call | solution.py:91
  115.2 16.0 %collective-permute-done.15.refs_3_ = bf16[1280,256]{1,0:T(8,128)(2,1)S(1)} collective-permute-done((bf16[1280,256]{1,0:T(8,128)(2,1)}, bf16[1280,256]{1,0:T(8,128)(2,1)S(1)}, u32[]{:S(2)}, u32[]{:S(2)}) %collective-permute-start.15) | collective-permute-done | bytes 655392 | tf_op jit(solution)/shard_map/ppermute | solution.py:968
  131.3 5.5 %all-gather.3.cloned.1.call-done = bf16[5120,1024]{1,0:T(8,128)(2,1)} async-done(((bf16[320,1024]{1,0:T(8,128)(2,1)}), bf16[5120,1024]{1,0:T(8,128)(2,1)}) %all-gather.3.cloned.1.call-update) | async-done | bytes 10485776 | tf_op jit(solution)/shard_map/all_gather | solution.py:1141
  136.8 9.3 %second_layer.1 = (f32[640,1024]{1,0:T(8,128)}, bf16[1280,1024]{1,0:T(8,128)(2,1)}) custom-call(s32[5]{0:T(128)} %stack.41.place, bf16[1280,256]{1,0:T(8,128)(2,1)} %get-tuple-element.84.refs_1_.refs_0_, bf16[1280,256]{1,0:T(8,128)(2,1)} %get-tuple-element.87.refs_1_, bf16[1280,256]{1,0:T(8,128)(2,1)} %copy-done.7, bf16[1280,256]{1,0:T(8,128)(2,1)} %copy-done.8, ...), custom_call_target="tpu_custom_call" | custom-call | flops 1342177280 | bytes 7602176 | tf_op jit(solution)/shard_map/second_layer/pallas_call | solution.py:401
  146.1 18.5 %hidden_layer.1 = (bf16[1280,2048]{1,0:T(8,128)(2,1)}, bf16[1280,2048]{1,0:T(8,128)(2,1)}) custom-call(bf16[1280,1024]{1,0:T(8,128)(2,1)} %get-tuple-element.90.x_ref.refs_4_, bf16[16,5,64,1024]{3,2,1,0:T(8,128)(2,1)} %bitcast.124, bf16[8,2,5,64,1024]{4,3,2,1,0:T(8,128)(2,1)} %bitcast.125, bf16[640,1024]{1,0:T(8,128)(2,1)} %bitcast.141, ...), custom_call_target="tpu_custom_call" | custom-call | flops 5368709120 | bytes 12058624 | tf_op jit(solution)/shard_map/hidden_layer/pallas_call | solution.py:484
  164.6 7.5 %up_back.2 = (bf16[320,1024]{1,0:T(8,128)(2,1)}, bf16[320,1024]{1,0:T(8,128)(2,1)}) custom-call(bf16[1280,2048]{1,0:T(8,128)(2,1)} %get-tuple-element.92.g_ref.refs_1_, bf16[16,5,64,1024]{3,2,1,0:T(8,128)(2,1)} %bitcast.126), custom_call_target="tpu_custom_call" | custom-call | flops 1342177280 | bytes 4718592 | tf_op jit(solution)/shard_map/up_back/pallas_call | solution.py:537
  173.6 12.4 %hidden_grads.2.refs_0_ = bf16[1024,2048]{1,0:T(8,128)(2,1)} custom-call(s32[5]{0:T(128)} %stack.41.place, bf16[1280,2048]{1,0:T(8,128)(2,1)} %get-tuple-element.91.refs_0_.a_ref, bf16[1280,2048]{1,0:T(8,128)(2,1)} %get-tuple-element.92.g_ref.refs_1_, bf16[640,1024]{1,0:T(8,128)(2,1)} %bitcast.142, bf16[640,1024]{1,0:T(8,128)(2,1)} %copy-done.2, ...), custom_call_target="tpu_custom_call" | custom-call | flops 2684354560 | bytes 7340032 | tf_op jit(solution)/shard_map/hidden_grads/pallas_call | solution.py:735
  186.0 3.3 collective-permute-done.16.refs_5_
  190.8 8.1 %up_back.3.refs_6_.refs_0_ = f32[640,1024]{1,0:T(8,128)} custom-call(bf16[1280,2048]{1,0:T(8,128)(2,1)} %get-tuple-element.92.g_ref.refs_1_, bf16[16,5,64,1024]{3,2,1,0:T(8,128)(2,1)} %bitcast.127, bf16[1024,2048]{1,0:T(8,128)(2,1)} %hidden_grads.2.refs_0_), custom_call_target="tpu_custom_call" | custom-call | flops 1342177280 | bytes 4718592 | tf_op jit(solution)/shard_map/up_back/pallas_call | solution.py:537
  198.9 12.9 %hidden_grads.3.refs_7_ = bf16[1024,2048]{1,0:T(8,128)(2,1)} custom-call(s32[5]{0:T(128)} %stack.41.place, bf16[1280,2048]{1,0:T(8,128)(2,1)} %get-tuple-element.91.refs_0_.a_ref, bf16[1280,2048]{1,0:T(8,128)(2,1)} %get-tuple-element.92.g_ref.refs_1_, bf16[640,1024]{1,0:T(8,128)(2,1)} %bitcast.143, bf16[640,1024]{1,0:T(8,128)(2,1)} %copy-done.2, ...), custom_call_target="tpu_custom_call" | custom-call | flops 2684354560 | bytes 7340032 | tf_op jit(solution)/shard_map/hidden_grads/pallas_call | solution.py:735
  211.7 2.6 dynamic-slice_bitcast_fusion
  217.2 8.9 %middle_back.1 = (f32[640,1024]{1,0:T(8,128)}, bf16[640,1024]{1,0:T(8,128)(2,1)}, f32[2,1024]{1,0:T(2,128)}, bf16[640,512]{1,0:T(8,128)(2,1)}, bf16[640,512]{1,0:T(8,128)(2,1)}) custom-call(s32[5]{0:T(128)} %stack.41.place, f32[640,1024]{1,0:T(8,128)} %up_back.3.refs_6_.refs_0_, f32[640,1024]{1,0:T(8,128)} %get-tuple-element.89.refs_1_, ...), custom_call_target="tpu_custom_call" | custom-call | flops 671088640 | bytes 7602176 | tf_op jit(solution)/shard_map/middle_back/pallas_call | solution.py:617
  226.8 7.3 %down_part.2.refs_0_ = bf16[640,1024]{1,0:T(8,128)(2,1)} custom-call(bf16[1280,2048]{1,0:T(8,128)(2,1)} %get-tuple-element.91.refs_0_.a_ref, bf16[8,2,5,64,1024]{4,3,2,1,0:T(8,128)(2,1)} %bitcast.129, bf16[640,512]{1,0:T(8,128)(2,1)} %get-tuple-element.98.refs_0_), custom_call_target="tpu_custom_call" | custom-call | flops 1342177280 | bytes 4718592 | tf_op jit(solution)/shard_map/down_part/pallas_call | solution.py:537
  234.1 2.6 bitcast_add_fusion.1
  238.7 7.8 %down_part.3.refs_6_ = f32[640,1024]{1,0:T(8,128)} custom-call(bf16[1280,2048]{1,0:T(8,128)(2,1)} %get-tuple-element.91.refs_0_.a_ref, bf16[8,2,5,64,1024]{4,3,2,1,0:T(8,128)(2,1)} %bitcast.130, bf16[640,1024]{1,0:T(8,128)(2,1)} %down_part.2.refs_0_), custom_call_target="tpu_custom_call" | custom-call | flops 1342177280 | bytes 4718592 | tf_op jit(solution)/shard_map/down_part/pallas_call | solution.py:537
  247.4 11.8 %attend_back.4.refs_6_ = bf16[1280,1536]{1,0:T(8,128)(2,1)} custom-call(s32[5]{0:T(128)} %stack.41.place, bf16[1280,1536]{1,0:T(8,128)(2,1)} %get-tuple-element.82.q_ref.k_ref.v_ref, bf16[1280,1536]{1,0:T(8,128)(2,1)} %get-tuple-element.82.q_ref.k_ref.v_ref, bf16[1280,1536]{1,0:T(8,128)(2,1)} %get-tuple-element.82.q_ref.k_ref.v_ref, ...), custom_call_target="tpu_custom_call" | custom-call | flops 3145728000 | bytes 3276800 | tf_op jit(solution)/shard_map/attend_back/pallas_call | solution.py:204
  259.3 2.6 bitcast_add_fusion
  264.0 12.2 %attend_back.5.grad.refs_6_ = bf16[1280,1536]{1,0:T(8,128)(2,1)} custom-call(s32[5]{0:T(128)} %stack.41.place, bf16[1280,1536]{1,0:T(8,128)(2,1)} %get-tuple-element.82.q_ref.k_ref.v_ref, bf16[1280,1536]{1,0:T(8,128)(2,1)} %get-tuple-element.82.q_ref.k_ref.v_ref, ...), custom_call_target="tpu_custom_call", output_to_operand_aliasing={{}: (10, {})} | custom-call | flops 3145728000 | bytes 3276800 | tf_op jit(solution)/shard_map/attend_back/pallas_call | solution.py:204
  276.2 9.0 %tail_grads.2.refs_7_ = bf16[1024,1280]{1,0:T(8,128)(2,1)} custom-call(s32[5]{0:T(128)} %stack.41.place, bf16[1280,1024]{1,0:T(8,128)(2,1)} %get-tuple-element.100.low, bf16[1280,1536]{1,0:T(8,128)(2,1)} %attend_back.5.grad.refs_6_, bf16[640,1024]{1,0:T(8,128)(2,1)} %get-tuple-element.111.attended, bf16[1280,256]{1,0:T(8,128)(2,1)} %get-tuple-element.84.refs_1_.refs_0_, ...), custom_call_target="tpu_custom_call" | custom-call | flops 1342177280 | bytes 5242880 | tf_op jit(solution)/shard_map/tail_grads/pallas_call | solution.py:788
  288.9 11.7 %attend_back.6.refs_6_ = bf16[1280,1536]{1,0:T(8,128)(2,1)} custom-call(s32[5]{0:T(128)} %stack.41.place, bf16[1280,1536]{1,0:T(8,128)(2,1)} %get-tuple-element.82.q_ref.k_ref.v_ref, bf16[1280,1536]{1,0:T(8,128)(2,1)} %get-tuple-element.82.q_ref.k_ref.v_ref, bf16[1280,1536]{1,0:T(8,128)(2,1)} %get-tuple-element.82.q_ref.k_ref.v_ref, ...), custom_call_target="tpu_custom_call", output_to_operand_aliasing={{}: (10, {})} | custom-call | flops 3145728000 | bytes 3276800 | tf_op jit(solution)/shard_map/attend_back/pallas_call | solution.py:204
  301.3 11.9 %attend_back.7.grad.grad_ref = bf16[1280,1536]{1,0:T(8,128)(2,1)} custom-call(s32[5]{0:T(128)} %stack.41.place, bf16[1280,1536]{1,0:T(8,128)(2,1)} %get-tuple-element.82.q_ref.k_ref.v_ref, bf16[1280,1536]{1,0:T(8,128)(2,1)} %get-tuple-element.82.q_ref.k_ref.v_ref, ...), custom_call_target="tpu_custom_call", output_to_operand_aliasing={{}: (10, {})} | custom-call | flops 3145728000 | bytes 3276800 | tf_op jit(solution)/shard_map/attend_back/pallas_call | solution.py:204
  313.2 9.4 %tail_grads.3.refs_0_ = bf16[1024,1280]{1,0:T(8,128)(2,1)} custom-call(s32[5]{0:T(128)} %stack.41.place, bf16[1280,1024]{1,0:T(8,128)(2,1)} %get-tuple-element.100.low, bf16[1280,1536]{1,0:T(8,128)(2,1)} %attend_back.7.grad.grad_ref, bf16[640,1024]{1,0:T(8,128)(2,1)} %get-tuple-element.111.attended, bf16[1280,256]{1,0:T(8,128)(2,1)} %get-tuple-element.84.refs_1_.refs_0_, ...), custom_call_target="tpu_custom_call" | custom-call | flops 1342177280 | bytes 5242880 | tf_op jit(solution)/shard_map/tail_grads/pallas_call | solution.py:788
  322.6 3.2 dynamic-slice_bitcast_fusion.2
  330.4 6.8 %first_back.2 = (bf16[320,1024]{1,0:T(8,128)(2,1)}, bf16[320,1024]{1,0:T(8,128)(2,1)}, f32[2,1024]{1,0:T(2,128)}) custom-call(bf16[1280,1536]{1,0:T(8,128)(2,1)} %attend_back.7.grad.grad_ref, bf16[1024,1536]{1,0:T(8,128)(2,1)} %get-tuple-element.113.weight_ref, bf16[640,1024]{1,0:T(8,128)(2,1)} %copy-done.10, bf16[1024,1280]{1,0:T(8,128)(2,1)} %tail_grads.3.refs_0_, ...), custom_call_target="tpu_custom_call" | custom-call | flops 1006632960 | bytes 3866624 | tf_op jit(solution)/shard_map/first_back/pallas_call | solution.py:665
  338.7 2.0 fusion.1
  342.4 3.1 bitcast_add_fusion.8
  347.6 6.4 %first_back.3 = (bf16[640,1024]{1,0:T(8,128)(2,1)}, f32[2,1024]{1,0:T(2,128)}) custom-call(bf16[1280,1536]{1,0:T(8,128)(2,1)} %attend_back.7.grad.grad_ref, bf16[1024,1536]{1,0:T(8,128)(2,1)} %get-tuple-element.113.weight_ref, bf16[640,1024]{1,0:T(8,128)(2,1)} %bitcast.149, bf16[320,1024]{1,0:T(8,128)(2,1)} %get-tuple-element.133.refs_0_), custom_call_target="tpu_custom_call" | custom-call | flops 1006632960 | bytes 3866624 | tf_op jit(solution)/shard_map/first_back/pallas_call | solution.py:665
  353.9 2.2 bitcast_select_fusion
  359.1 2.4 bitcast_add_fusion.6
  364.9 3.6 fusion
  374.1 2.8 collective-permute-done.38
  378.7 2.3 reshape.102
  382.2 3.7 collective-permute-done.40.refs_1_
  387.4 1.8 fusion.2
  392.1 5.8 %input_back.1 = f32[640,1024]{1,0:T(8,128)} custom-call(bf16[640,1024]{1,0:T(8,128)(2,1)} %get-tuple-element.124.own_ref, bf16[640,1024]{1,0:T(8,128)(2,1)} %bitcast.150, f32[2,1024]{1,0:T(2,128)} %get-tuple-element.182.refs_2_.ada_ref, f32[640,1024]{1,0:T(8,128)} %get-tuple-element.125.base_ref, bf16[320,1024]{1,0:T(8,128)(2,1)} %collective-permute-done.33.refs_0_, ...), custom_call_target="tpu_custom_call" | custom-call | flops 6553600 | bytes 4587520 | tf_op jit(solution)/shard_map/input_back/pallas_call | solution.py:834
  401.7 2.6 join_tail.1
  (204 shorter events, 69.7 us)
Async XLA Ops:
  7.2 129.6 %all-gather.3.cloned.1.call-start = ((), (), s32[]{:S(2)}) async-start(), calls=%async_computation | async-start | bytes 11141120 | tf_op jit(solution)/shard_map/all_gather | solution.py:1141
  8.7 10.6 %collective-permute-start = (f32[4,8,1024]{2,1,0:T(8,128)S(1)}, f32[4,8,1024]{2,1,0:T(8,128)S(1)}, u32[]{:S(2)}, u32[]{:S(2)}) collective-permute-start(f32[4,8,1024]{2,1,0:T(8,128)S(1)} %pad_maximum_fusion.3), channel_id=1, source_target_pairs={{0,2},{2,0},{4,6},{6,4},{8,10},{10,8},{12,14},{14,12},{16,18},{18,... | collective-permute-start | bytes 393224 | tf_op jit(solution)/shard_map/ppermute | solution.py:961
  10.9 5.1 %collective-permute-start.4 = (bf16[64,1536]{1,0:T(8,128)(2,1)}, bf16[64,1536]{1,0:T(8,128)(2,1)S(1)}, u32[]{:S(2)}, u32[]{:S(2)}) collective-permute-start(bf16[64,1536]{1,0:T(8,128)(2,1)} %pack_columns.1), channel_id=1, source_target_pairs={{0,2},{2,0},{4,6},{6,4},{8,10},{10,8},{12,14},{14,12},{16,18},{18,... | collective-permute-start | bytes 589832 | tf_op jit(solution)/shard_map/ppermute | solution.py:961
  10.9 33.3 %collective-permute-start.7 = (bf16[640,1024]{1,0:T(8,128)(2,1)}, bf16[640,1024]{1,0:T(8,128)(2,1)S(1)}, u32[]{:S(2)}, u32[]{:S(2)}) collective-permute-start(bf16[640,1024]{1,0:T(8,128)(2,1)} %bitcast.146), channel_id=1, source_target_pairs={{0,1},{1,0},{2,3},{3,2},{4,5},{5,4},{6,7},{7,6},{8,9},{9,8},{10,11... | collective-permute-start | bytes 3932168 | tf_op jit(solution)/shard_map/ppermute | solution.py:968
  17.8 12.0 %collective-permute-start.5 = (bf16[128,1536]{1,0:T(8,128)(2,1)}, bf16[128,1536]{1,0:T(8,128)(2,1)}, u32[]{:S(2)}, u32[]{:S(2)}) collective-permute-start(bf16[128,1536]{1,0:T(8,128)(2,1)} %maximum_select_fusion.refs_3_), channel_id=1, source_target_pairs={{0,8},{8,16},{16,24},{24,28},{28,20},{20,12},{12,4},{4,0},{10,2},{... | collective-permute-start | bytes 1179656 | tf_op jit(solution)/shard_map/ppermute | solution.py:981
  20.0 8.6 %collective-permute-start.1 = (f32[4,8,1024]{2,1,0:T(8,128)}, f32[4,8,1024]{2,1,0:T(8,128)}, u32[]{:S(2)}, u32[]{:S(2)}) collective-permute-start(f32[4,8,1024]{2,1,0:T(8,128)} %fusion.24), channel_id=1, source_target_pairs={{0,4},{2,6},{4,0},{6,2},{8,12},{10,14},{12,8},{14,10},{16,20},{18,... | collective-permute-start | bytes 393224 | tf_op jit(solution)/shard_map/ppermute | solution.py:961
  29.7 6.5 %collective-permute-start.2 = (f32[4,8,1024]{2,1,0:T(8,128)S(1)}, f32[4,8,1024]{2,1,0:T(8,128)S(1)}, u32[]{:S(2)}, u32[]{:S(2)}) collective-permute-start(f32[4,8,1024]{2,1,0:T(8,128)S(1)} %fusion.29), channel_id=1, source_target_pairs={{0,8},{2,10},{4,12},{6,14},{8,0},{10,2},{12,4},{14,6},{16,24},{18,... | collective-permute-start | bytes 393224 | tf_op jit(solution)/shard_map/ppermute | solution.py:961
  29.8 14.5 %collective-permute-start.6 = (bf16[128,1536]{1,0:T(8,128)(2,1)}, bf16[128,1536]{1,0:T(8,128)(2,1)}, u32[]{:S(2)}, u32[]{:S(2)}) collective-permute-start(bf16[128,1536]{1,0:T(8,128)(2,1)} %collective-permute-done.5.refs_4_), channel_id=1, source_target_pairs={{0,8},{8,16},{16,24},{24,28},{28,20},{20,12},{12,4},{4,0},{10,2},{... | collective-permute-start | bytes 1179656 | tf_op jit(solution)/shard_map/ppermute | solution.py:981
  36.2 8.0 %collective-permute-start.3 = (f32[4,8,1024]{2,1,0:T(8,128)S(1)}, f32[4,8,1024]{2,1,0:T(8,128)S(1)}, u32[]{:S(2)}, u32[]{:S(2)}) collective-permute-start(f32[4,8,1024]{2,1,0:T(8,128)S(1)} %add.86), channel_id=1, source_target_pairs={{0,16},{2,18},{4,20},{6,22},{8,24},{10,26},{12,28},{14,30},{16,0},... | collective-permute-start | bytes 393224 | tf_op jit(solution)/shard_map/ppermute | solution.py:961
  45.3 35.1 %collective-permute-start.13 = (bf16[640,1024]{1,0:T(8,128)(2,1)S(1)}, bf16[640,1024]{1,0:T(8,128)(2,1)S(1)}, u32[]{:S(2)}, u32[]{:S(2)}) collective-permute-start(bf16[640,1024]{1,0:T(8,128)(2,1)S(1)} %bitcast.145), channel_id=1, source_target_pairs={{0,1},{1,0},{2,3},{3,2},{4,5},{5,4},{6,7},{7,6},{8,9},{9,8},{10,11... | collective-permute-start | bytes 3932168 | tf_op jit(solution)/shard_map/ppermute | solution.py:968
  45.8 8.5 %collective-permute-start.8 = (bf16[128,1536]{1,0:T(8,128)(2,1)}, bf16[128,1536]{1,0:T(8,128)(2,1)S(1)}, u32[]{:S(2)}, u32[]{:S(2)}) collective-permute-start(bf16[128,1536]{1,0:T(8,128)(2,1)} %collective-permute-done.6.refs_5_), channel_id=1, source_target_pairs={{0,8},{8,16},{16,24},{24,28},{28,20},{20,12},{12,4},{4,0},{10,2},{... | collective-permute-start | bytes 1179656 | tf_op jit(solution)/shard_map/ppermute | solution.py:981
  48.6 10.1 %collective-permute-start.10 = (bf16[128,1536]{1,0:T(8,128)(2,1)}, bf16[128,1536]{1,0:T(8,128)(2,1)}, u32[]{:S(2)}, u32[]{:S(2)}) collective-permute-start(bf16[128,1536]{1,0:T(8,128)(2,1)} %collective-permute-done.5.refs_4_), channel_id=1, source_target_pairs={{0,2},{2,0},{4,6},{6,4},{8,10},{10,8},{12,14},{14,12},{16,18},{18,... | collective-permute-start | bytes 1179656 | tf_op jit(solution)/shard_map/ppermute | solution.py:961
  48.6 10.1 %collective-permute-start.11 = (bf16[128,1536]{1,0:T(8,128)(2,1)}, bf16[128,1536]{1,0:T(8,128)(2,1)}, u32[]{:S(2)}, u32[]{:S(2)}) collective-permute-start(bf16[128,1536]{1,0:T(8,128)(2,1)} %collective-permute-done.6.refs_5_), channel_id=1, source_target_pairs={{0,2},{2,0},{4,6},{6,4},{8,10},{10,8},{12,14},{14,12},{16,18},{18,... | collective-permute-start | bytes 1179656 | tf_op jit(solution)/shard_map/ppermute | solution.py:961
  54.3 14.8 %collective-permute-start.9 = (bf16[128,1536]{1,0:T(8,128)(2,1)S(1)}, bf16[128,1536]{1,0:T(8,128)(2,1)}, u32[]{:S(2)}, u32[]{:S(2)}) collective-permute-start(bf16[128,1536]{1,0:T(8,128)(2,1)S(1)} %collective-permute-done.8.refs_6_), channel_id=1, source_target_pairs={{0,8},{8,16},{16,24},{24,28},{28,20},{20,12},{12,4},{4,0},{10,2},{... | collective-permute-start | bytes 1179656 | tf_op jit(solution)/shard_map/ppermute | solution.py:981
  55.4 13.7 %collective-permute-start.12 = (bf16[128,1536]{1,0:T(8,128)(2,1)S(1)}, bf16[128,1536]{1,0:T(8,128)(2,1)}, u32[]{:S(2)}, u32[]{:S(2)}) collective-permute-start(bf16[128,1536]{1,0:T(8,128)(2,1)S(1)} %collective-permute-done.8.refs_6_), channel_id=1, source_target_pairs={{0,2},{2,0},{4,6},{6,4},{8,10},{10,8},{12,14},{14,12},{16,18},{18,... | collective-permute-start | bytes 1179656 | tf_op jit(solution)/shard_map/ppermute | solution.py:961
  97.3 17.3 %collective-permute-start.14 = (bf16[1280,256]{1,0:T(8,128)(2,1)}, bf16[1280,256]{1,0:T(8,128)(2,1)S(1)}, u32[]{:S(2)}, u32[]{:S(2)}) collective-permute-start(bf16[1280,256]{1,0:T(8,128)(2,1)} %get-tuple-element.84.refs_1_.refs_0_), channel_id=1, source_target_pairs={{0,1},{1,0},{2,3},{3,2},{4,5},{5,4},{6,7},{7,6},{8,9},{9,8},{10,11... | collective-permute-start | bytes 1966088 | tf_op jit(solution)/shard_map/ppermute | solution.py:968
  114.6 16.6 %collective-permute-start.15 = (bf16[1280,256]{1,0:T(8,128)(2,1)}, bf16[1280,256]{1,0:T(8,128)(2,1)S(1)}, u32[]{:S(2)}, u32[]{:S(2)}) collective-permute-start(bf16[1280,256]{1,0:T(8,128)(2,1)} %get-tuple-element.87.refs_1_), channel_id=1, source_target_pairs={{0,1},{1,0},{2,3},{3,2},{4,5},{5,4},{6,7},{7,6},{8,9},{9,8},{10,11... | collective-permute-start | bytes 1966088 | tf_op jit(solution)/shard_map/ppermute | solution.py:968
  172.1 17.1 %collective-permute-start.16 = (bf16[320,1024]{1,0:T(8,128)(2,1)}, bf16[320,1024]{1,0:T(8,128)(2,1)S(1)}, u32[]{:S(2)}, u32[]{:S(2)}) collective-permute-start(bf16[320,1024]{1,0:T(8,128)(2,1)} %get-tuple-element.93.refs_5_), channel_id=1, source_target_pairs={{0,1},{1,0},{2,3},{3,2},{4,5},{5,4},{6,7},{7,6},{8,9},{9,8},{10,11... | collective-permute-start | bytes 1966088 | tf_op jit(solution)/shard_map/ppermute | solution.py:968
  189.2 9.6 %collective-permute-start.17 = (bf16[1024,2048]{1,0:T(8,128)(2,1)}, bf16[1024,2048]{1,0:T(8,128)(2,1)}, u32[]{:S(2)}, u32[]{:S(2)}) collective-permute-start(bf16[1024,2048]{1,0:T(8,128)(2,1)} %hidden_grads.2.refs_0_), channel_id=1, source_target_pairs={{0,2},{2,0},{4,6},{6,4},{8,10},{10,8},{12,14},{14,12},{16,18},{18,... | collective-permute-start | bytes 12582920 | tf_op jit(solution)/shard_map/ppermute | solution.py:961
  189.2 27.2 %collective-permute-start.20 = (bf16[320,1024]{1,0:T(8,128)(2,1)S(1)}, bf16[320,1024]{1,0:T(8,128)(2,1)S(1)}, u32[]{:S(2)}, u32[]{:S(2)}) collective-permute-start(bf16[320,1024]{1,0:T(8,128)(2,1)S(1)} %copy-done.35), channel_id=1, source_target_pairs={{0,1},{1,0},{2,3},{3,2},{4,5},{5,4},{6,7},{7,6},{8,9},{9,8},{10,11... | collective-permute-start | bytes 1966088 | tf_op jit(solution)/shard_map/ppermute | solution.py:968
  214.3 19.8 %collective-permute-start.18 = (bf16[128,2048]{1,0:T(8,128)(2,1)S(1)}, bf16[128,2048]{1,0:T(8,128)(2,1)S(1)}, u32[]{:S(2)}, u32[]{:S(2)}) collective-permute-start(bf16[128,2048]{1,0:T(8,128)(2,1)S(1)} %get-tuple-element.150), channel_id=1, source_target_pairs={{0,8},{2,10},{8,16},{10,18},{16,24},{18,26},{24,28},{26,30},{28,20... | collective-permute-start | bytes 1572872 | tf_op jit(solution)/shard_map/ppermute | solution.py:1042
  214.9 19.2 %collective-permute-start.19 = (bf16[128,2048]{1,0:T(8,128)(2,1)S(1)}, bf16[128,2048]{1,0:T(8,128)(2,1)S(1)}, u32[]{:S(2)}, u32[]{:S(2)}) collective-permute-start(bf16[128,2048]{1,0:T(8,128)(2,1)S(1)} %get-tuple-element.149), channel_id=1, source_target_pairs={{8,0},{10,2},{16,8},{18,10},{24,16},{26,18},{28,24},{30,26},{20,28... | collective-permute-start | bytes 1572872 | tf_op jit(solution)/shard_map/ppermute | solution.py:1042
  226.2 20.4 %collective-permute-start.21 = (bf16[640,512]{1,0:T(8,128)(2,1)}, bf16[640,512]{1,0:T(8,128)(2,1)S(1)}, u32[]{:S(2)}, u32[]{:S(2)}) collective-permute-start(bf16[640,512]{1,0:T(8,128)(2,1)} %get-tuple-element.98.refs_0_), channel_id=1, source_target_pairs={{0,1},{1,0},{2,3},{3,2},{4,5},{5,4},{6,7},{7,6},{8,9},{9,8},{10,11... | collective-permute-start | bytes 1966088 | tf_op jit(solution)/shard_map/ppermute | solution.py:968
  236.7 22.6 %collective-permute-start.22 = (bf16[128,2048]{1,0:T(8,128)(2,1)S(1)}, bf16[128,2048]{1,0:T(8,128)(2,1)S(1)}, u32[]{:S(2)}, u32[]{:S(2)}) collective-permute-start(bf16[128,2048]{1,0:T(8,128)(2,1)S(1)} %get-tuple-element.148), channel_id=1, source_target_pairs={{0,8},{2,10},{8,16},{10,18},{16,24},{18,26},{24,28},{26,30},{28,20... | collective-permute-start | bytes 1572872 | tf_op jit(solution)/shard_map/ppermute | solution.py:1042
  237.2 22.0 %collective-permute-start.23 = (bf16[128,2048]{1,0:T(8,128)(2,1)S(1)}, bf16[128,2048]{1,0:T(8,128)(2,1)S(1)}, u32[]{:S(2)}, u32[]{:S(2)}) collective-permute-start(bf16[128,2048]{1,0:T(8,128)(2,1)S(1)} %get-tuple-element.147), channel_id=1, source_target_pairs={{8,0},{10,2},{16,8},{18,10},{24,16},{26,18},{28,24},{30,26},{20,28... | collective-permute-start | bytes 1572872 | tf_op jit(solution)/shard_map/ppermute | solution.py:1042
  261.9 14.3 %collective-permute-start.24 = (bf16[128,2048]{1,0:T(8,128)(2,1)S(1)}, bf16[128,2048]{1,0:T(8,128)(2,1)S(1)}, u32[]{:S(2)}, u32[]{:S(2)}) collective-permute-start(bf16[128,2048]{1,0:T(8,128)(2,1)S(1)} %get-tuple-element.146), channel_id=1, source_target_pairs={{0,8},{2,10},{8,16},{10,18},{16,24},{18,26},{24,28},{26,30},{28,20... | collective-permute-start | bytes 1572872 | tf_op jit(solution)/shard_map/ppermute | solution.py:1042
  262.4 13.7 %collective-permute-start.25 = (bf16[128,2048]{1,0:T(8,128)(2,1)S(1)}, bf16[128,2048]{1,0:T(8,128)(2,1)S(1)}, u32[]{:S(2)}, u32[]{:S(2)}) collective-permute-start(bf16[128,2048]{1,0:T(8,128)(2,1)S(1)} %get-tuple-element.145), channel_id=1, source_target_pairs={{8,0},{10,2},{16,8},{18,10},{24,16},{26,18},{28,24},{30,26},{20,28... | collective-permute-start | bytes 1572872 | tf_op jit(solution)/shard_map/ppermute | solution.py:1042
  285.2 28.0 %collective-permute-start.27 = (bf16[1024,1280]{1,0:T(8,128)(2,1)}, bf16[1024,1280]{1,0:T(8,128)(2,1)}, u32[]{:S(2)}, u32[]{:S(2)}) collective-permute-start(bf16[1024,1280]{1,0:T(8,128)(2,1)} %tail_grads.2.refs_7_), channel_id=1, source_target_pairs={{0,2},{2,0},{4,6},{6,4},{8,10},{10,8},{12,14},{14,12},{16,18},{18,... | collective-permute-start | bytes 7864328 | tf_op jit(solution)/shard_map/ppermute | solution.py:961
  286.9 14.4 %collective-permute-start.26 = (bf16[128,2048]{1,0:T(8,128)(2,1)S(1)}, bf16[128,2048]{1,0:T(8,128)(2,1)S(1)}, u32[]{:S(2)}, u32[]{:S(2)}) collective-permute-start(bf16[128,2048]{1,0:T(8,128)(2,1)S(1)} %bitcast_add_fusion.4), channel_id=1, source_target_pairs={{0,8},{2,10},{8,16},{10,18},{16,24},{18,26},{24,28},{26,30},{28,20... | collective-permute-start | bytes 1572872 | tf_op jit(solution)/shard_map/ppermute | solution.py:1042
  287.5 41.8 %collective-permute-start.30 = (bf16[640,1024]{1,0:T(8,128)(2,1)S(1)}, bf16[640,1024]{1,0:T(8,128)(2,1)S(1)}, u32[]{:S(2)}, u32[]{:S(2)}) collective-permute-start(bf16[640,1024]{1,0:T(8,128)(2,1)S(1)} %copy-done.9), channel_id=1, source_target_pairs={{0,1},{1,0},{2,3},{3,2},{4,5},{5,4},{6,7},{7,6},{8,9},{9,8},{10,11... | collective-permute-start | bytes 3932168 | tf_op jit(solution)/shard_map/ppermute | solution.py:968
  325.9 12.8 %collective-permute-start.28 = (bf16[128,1280]{1,0:T(8,128)(2,1)}, bf16[128,1280]{1,0:T(8,128)(2,1)S(1)}, u32[]{:S(2)}, u32[]{:S(2)}) collective-permute-start(bf16[128,1280]{1,0:T(8,128)(2,1)} %get-tuple-element.156), channel_id=1, source_target_pairs={{0,8},{2,10},{8,16},{10,18},{16,24},{18,26},{24,28},{26,30},{28,20... | collective-permute-start | bytes 983048 | tf_op jit(solution)/shard_map/ppermute | solution.py:1042
  326.8 11.8 %collective-permute-start.29 = (bf16[128,1280]{1,0:T(8,128)(2,1)}, bf16[128,1280]{1,0:T(8,128)(2,1)}, u32[]{:S(2)}, u32[]{:S(2)}) collective-permute-start(bf16[128,1280]{1,0:T(8,128)(2,1)} %get-tuple-element.155), channel_id=1, source_target_pairs={{8,0},{10,2},{16,8},{18,10},{24,16},{26,18},{28,24},{30,26},{20,28... | collective-permute-start | bytes 983048 | tf_op jit(solution)/shard_map/ppermute | solution.py:1042
  337.2 19.6 %collective-permute-start.33 = (bf16[320,1024]{1,0:T(8,128)(2,1)}, bf16[320,1024]{1,0:T(8,128)(2,1)}, u32[]{:S(2)}, u32[]{:S(2)}) collective-permute-start(bf16[320,1024]{1,0:T(8,128)(2,1)} %get-tuple-element.122), channel_id=1, source_target_pairs={{0,1},{1,0},{2,3},{3,2},{4,5},{5,4},{6,7},{7,6},{8,9},{9,8},{10,11... | collective-permute-start | bytes 1966088 | tf_op jit(solution)/shard_map/ppermute | solution.py:968
  342.3 11.6 %collective-permute-start.45 = (f32[64,1024]{1,0:T(8,128)S(1)}, f32[64,1024]{1,0:T(8,128)}, u32[]{:S(2)}, u32[]{:S(2)}) collective-permute-start(f32[64,1024]{1,0:T(8,128)S(1)} %dynamic-slice_bitcast_fusion.4), channel_id=1, source_target_pairs={{0,2},{2,0},{4,6},{6,4},{8,10},{10,8},{12,14},{14,12},{16,18},{18,... | collective-permute-start | bytes 786440 | tf_op jit(solution)/shard_map/ppermute | solution.py:961
  345.5 11.2 %collective-permute-start.31 = (bf16[128,1280]{1,0:T(8,128)(2,1)}, bf16[128,1280]{1,0:T(8,128)(2,1)S(1)}, u32[]{:S(2)}, u32[]{:S(2)}) collective-permute-start(bf16[128,1280]{1,0:T(8,128)(2,1)} %get-tuple-element.154), channel_id=1, source_target_pairs={{0,8},{2,10},{8,16},{10,18},{16,24},{18,26},{24,28},{26,30},{28,20... | collective-permute-start | bytes 983048 | tf_op jit(solution)/shard_map/ppermute | solution.py:1042
  346.0 10.7 %collective-permute-start.32 = (bf16[128,1280]{1,0:T(8,128)(2,1)}, bf16[128,1280]{1,0:T(8,128)(2,1)}, u32[]{:S(2)}, u32[]{:S(2)}) collective-permute-start(bf16[128,1280]{1,0:T(8,128)(2,1)} %get-tuple-element.153), channel_id=1, source_target_pairs={{8,0},{10,2},{16,8},{18,10},{24,16},{26,18},{28,24},{30,26},{20,28... | collective-permute-start | bytes 983048 | tf_op jit(solution)/shard_map/ppermute | solution.py:1042
  356.2 21.1 %collective-permute-start.46 = (f32[32,2048]{1,0:T(8,128)S(1)}, f32[32,2048]{1,0:T(8,128)S(1)}, u32[]{:S(2)}, u32[]{:S(2)}) collective-permute-start(f32[32,2048]{1,0:T(8,128)S(1)} %fusion.7), channel_id=1, source_target_pairs={{0,1},{1,0},{2,3},{3,2},{4,5},{5,4},{6,7},{7,6},{8,9},{9,8},{10,11... | collective-permute-start | bytes 786440 | tf_op jit(solution)/shard_map/ppermute | solution.py:968
  357.5 7.2 %collective-permute-start.36 = (f32[4,1024]{1,0:T(4,128)S(1)}, f32[4,1024]{1,0:T(4,128)S(1)}, u32[]{:S(2)}, u32[]{:S(2)}) collective-permute-start(f32[4,1024]{1,0:T(4,128)S(1)} %pad_maximum_fusion.4), channel_id=1, source_target_pairs={{0,1},{1,0},{2,3},{3,2},{4,5},{5,4},{6,7},{7,6},{8,9},{9,8},{10,11... | collective-permute-start | bytes 49160 | tf_op jit(solution)/shard_map/ppermute | solution.py:968
  361.4 9.0 %collective-permute-start.34 = (bf16[128,1280]{1,0:T(8,128)(2,1)S(1)}, bf16[128,1280]{1,0:T(8,128)(2,1)S(1)}, u32[]{:S(2)}, u32[]{:S(2)}) collective-permute-start(bf16[128,1280]{1,0:T(8,128)(2,1)S(1)} %get-tuple-element.152), channel_id=1, source_target_pairs={{0,8},{2,10},{8,16},{10,18},{16,24},{18,26},{24,28},{26,30},{28,20... | collective-permute-start | bytes 983048 | tf_op jit(solution)/shard_map/ppermute | solution.py:1042
  362.0 8.7 %collective-permute-start.35 = (bf16[128,1280]{1,0:T(8,128)(2,1)S(1)}, bf16[128,1280]{1,0:T(8,128)(2,1)S(1)}, u32[]{:S(2)}, u32[]{:S(2)}) collective-permute-start(bf16[128,1280]{1,0:T(8,128)(2,1)S(1)} %get-tuple-element.151), channel_id=1, source_target_pairs={{8,0},{10,2},{16,8},{18,10},{24,16},{26,18},{28,24},{30,26},{20,28... | collective-permute-start | bytes 983048 | tf_op jit(solution)/shard_map/ppermute | solution.py:1042
  368.5 17.4 %collective-permute-start.40 = (bf16[320,1024]{1,0:T(8,128)(2,1)}, bf16[320,1024]{1,0:T(8,128)(2,1)}, u32[]{:S(2)}, u32[]{:S(2)}) collective-permute-start(bf16[320,1024]{1,0:T(8,128)(2,1)} %get-tuple-element.133.refs_0_), channel_id=1, source_target_pairs={{0,1},{1,0},{2,3},{3,2},{4,5},{5,4},{6,7},{7,6},{8,9},{9,8},{10,11... | collective-permute-start | bytes 1966088 | tf_op jit(solution)/shard_map/ppermute | solution.py:968
  370.7 6.3 %collective-permute-start.38 = (f32[4,8,1024]{2,1,0:T(8,128)S(1)}, f32[4,8,1024]{2,1,0:T(8,128)S(1)}, u32[]{:S(2)}, u32[]{:S(2)}) collective-permute-start(f32[4,8,1024]{2,1,0:T(8,128)S(1)} %fusion.18), channel_id=1, source_target_pairs={{0,4},{2,6},{4,0},{6,2},{8,12},{10,14},{12,8},{14,10},{16,20},{18,... | collective-permute-start | bytes 393224 | tf_op jit(solution)/shard_map/ppermute | solution.py:961
  373.6 13.8 %collective-permute-start.41 = (bf16[128,1280]{1,0:T(8,128)(2,1)}, bf16[128,1280]{1,0:T(8,128)(2,1)}, u32[]{:S(2)}, u32[]{:S(2)}) collective-permute-start(bf16[128,1280]{1,0:T(8,128)(2,1)} %bitcast_add_fusion.5), channel_id=1, source_target_pairs={{0,8},{2,10},{8,16},{10,18},{16,24},{18,26},{24,28},{26,30},{28,20... | collective-permute-start | bytes 983048 | tf_op jit(solution)/shard_map/ppermute | solution.py:1042
  377.0 5.2 %collective-permute-start.39 = (f32[4,8,1024]{2,1,0:T(8,128)S(1)}, f32[4,8,1024]{2,1,0:T(8,128)S(1)}, u32[]{:S(2)}, u32[]{:S(2)}) collective-permute-start(f32[4,8,1024]{2,1,0:T(8,128)S(1)} %add.102), channel_id=1, source_target_pairs={{0,8},{2,10},{4,12},{6,14},{8,0},{10,2},{12,4},{14,6},{16,24},{18,... | collective-permute-start | bytes 393224 | tf_op jit(solution)/shard_map/ppermute | solution.py:961
  385.9 11.9 %collective-permute-start.47 = (f32[4,8,1024]{2,1,0:T(8,128)S(1)}, f32[4,8,1024]{2,1,0:T(8,128)S(1)}, u32[]{:S(2)}, u32[]{:S(2)}) collective-permute-start(f32[4,8,1024]{2,1,0:T(8,128)S(1)} %add.103), channel_id=1, source_target_pairs={{0,16},{2,18},{4,20},{6,22},{8,24},{10,26},{12,28},{14,30},{16,0},... | collective-permute-start | bytes 393224 | tf_op jit(solution)/shard_map/ppermute | solution.py:961
  389.9 11.0 %collective-permute-start.42 = (f32[32,1280]{1,0:T(8,128)S(1)}, f32[32,1280]{1,0:T(8,128)S(1)}, u32[]{:S(2)}, u32[]{:S(2)}) collective-permute-start(f32[32,1280]{1,0:T(8,128)S(1)} %get-tuple-element.165), channel_id=1, source_target_pairs={{0,1},{1,0},{2,3},{3,2},{4,5},{5,4},{6,7},{7,6},{8,9},{9,8},{10,11... | collective-permute-start | bytes 491528 | tf_op jit(solution)/shard_map/ppermute | solution.py:968
  390.5 10.5 %collective-permute-start.43 = (f32[32,1280]{1,0:T(8,128)S(1)}, f32[32,1280]{1,0:T(8,128)S(1)}, u32[]{:S(2)}, u32[]{:S(2)}) collective-permute-start(f32[32,1280]{1,0:T(8,128)S(1)} %get-tuple-element.164), channel_id=1, source_target_pairs={{0,2},{2,0},{4,6},{6,4},{8,10},{10,8},{12,14},{14,12},{16,18},{18,... | collective-permute-start | bytes 491528 | tf_op jit(solution)/shard_map/ppermute | solution.py:961
  390.5 10.5 %collective-permute-start.44 = (f32[32,1280]{1,0:T(8,128)S(1)}, f32[32,1280]{1,0:T(8,128)S(1)}, u32[]{:S(2)}, u32[]{:S(2)}) collective-permute-start(f32[32,1280]{1,0:T(8,128)S(1)} %get-tuple-element.163), channel_id=1, source_target_pairs={{0,3},{1,2},{2,1},{3,0},{4,7},{5,6},{6,5},{7,4},{8,11},{9,10},{10,... | collective-permute-start | bytes 491528 | tf_op jit(solution)/shard_map/ppermute | solution.py:965
  (38 other events, 350.0 us)
Sparse Core Ops, SparseCore 0:
  44.4 92.3 all-gather.2

commit v7 on v6

--- a/solution.py
+++ b/solution.py
@@ -702,11 +702,25 @@
     out_ref[...] = value.astype(jnp.bfloat16)
 
 
+def put_first(place, out_ref, firsts):
+    for index, ref in enumerate(firsts):
+        rows = ref.shape[0]
+        start = pl.multiple_of(place[5 + index] * rows, rows)
+        ref[...] = out_ref[pl.ds(start, rows), :]
+
+
+def ring_outputs(width, columns, block, more, chips):
+    rows = [width] + [width // chips] * (2 if more else 0)
+    specs = [pl.BlockSpec((size, block), lambda j, s: (0, j)) for size in rows]
+    return specs, [jax.ShapeDtypeStruct((size, columns), jnp.bfloat16) for size in rows]
+
+
 def hidden_grads_kernel(count, more, place, *refs):
     active, upward = refs[:2]
     grads, low = refs[2 : 2 + count], refs[2 + count]
     other = refs[3 + count] if more else None
-    out_ref = refs[-1]
+    outs = refs[-3:] if more else refs[-1:]
+    out_ref = outs[0]
     step = pl.program_id(0)
     steps = pl.num_programs(0) // 2
 
@@ -720,8 +734,10 @@
     def _():
         put_sum(out_ref, other, dot_rows(low[...], upward[...]))
 
-
-def hidden_grads(place, who, active, upward, grads, low, other, behind):
+    put_first(place, out_ref, outs[1:])
+
+
+def hidden_grads(place, who, chips, active, upward, grads, low, other, behind):
     total, hidden = active.shape
     half = hidden // 2
     rows, width = grads[0].shape
@@ -732,6 +748,7 @@
     grad = pl.BlockSpec((rows, block), lambda j, s: (0, jnp.minimum(j, steps - 1)))
     out = pl.BlockSpec((width, block), lambda j, s: (0, j))
     more = [] if other is None else [other]
+    specs, shapes = ring_outputs(width, 2 * half, block, more, chips)
     return pl.pallas_call(
         partial(hidden_grads_kernel, count, bool(more)),
         grid_spec=pltpu.PrefetchScalarGridSpec(
@@ -747,9 +764,9 @@
             + [whole]
             + [out] * len(more)
             + [ANYWHERE] * len(behind),
-            out_specs=out,
-        ),
-        out_shape=jax.ShapeDtypeStruct((width, 2 * half), jnp.bfloat16),
+            out_specs=specs,
+        ),
+        out_shape=shapes,
         compiler_params=BIG,
         cost_estimate=cost(4 * total * half * width, 8 * total * half + 4 * width * half),
         name="hidden_grads",
@@ -759,7 +776,8 @@
 def tail_grads_kernel(first, more, pieces, calls, place, low, grad, attended, *refs):
     mixed = refs[:pieces]
     other = refs[pieces] if more else None
-    out_ref = refs[-1]
+    outs = refs[-3:] if more else refs[-1:]
+    out_ref = outs[0]
 
     @pl.when(pl.program_id(0) < first)
     def _():
@@ -776,8 +794,10 @@
                 value = value + other[rows, :].astype(jnp.float32)
             out_ref[rows, :] = value.astype(jnp.bfloat16)
 
-
-def tail_grads(place, who, low_one, grad_qkv, mixed, swapped, attended_low, other, behind):
+    put_first(place, out_ref, outs[1:])
+
+
+def tail_grads(place, who, chips, low_one, grad_qkv, mixed, swapped, attended_low, other, behind):
     total, width = low_one.shape
     rows = attended_low.shape[0]
     block = 256
@@ -785,6 +805,7 @@
     second = width // 2 // block
     out = pl.BlockSpec((width, block), lambda j, s: (0, j))
     more = [] if other is None else [other]
+    specs, shapes = ring_outputs(width, (first + second) * block, block, more, chips)
     return pl.pallas_call(
         partial(
             tail_grads_kernel, first, bool(more), len(mixed) + len(swapped), len(mixed)
@@ -805,9 +826,9 @@
             + [pl.BlockSpec((rows, part.shape[1]), lambda j, s: (1, 0)) for part in swapped]
             + [out] * len(more)
             + [ANYWHERE] * len(behind),
-            out_specs=out,
-        ),
-        out_shape=jax.ShapeDtypeStruct((width, (first + second) * block), jnp.bfloat16),
+            out_specs=specs,
+        ),
+        out_shape=shapes,
         compiler_params=BIG,
         cost_estimate=cost(
             2 * width * block * (total * first + rows * second), 8 * total * width
@@ -1020,7 +1041,7 @@
         self.chips = mover.chips
         self.make = make
         self.flows = None
-        sent, self.ready = tie(make(False, None, behind), list(ready))
+        sent, self.ready = tie(make(False, None, behind)[0], list(ready))
         self.sent = sent
         self.arriving = [mover.flip(sent, 1)]
 
@@ -1028,15 +1049,16 @@
         return pick(self.both, self.mover.ahead[ahead % self.chips], 0)
 
     def add_own(self, behind):
-        self.both = self.make(True, self.arriving[0], behind)
-        self.whole = self.both
-        self.both = self.both.reshape(self.chips, -1, self.both.shape[1])
+        self.whole, *firsts = self.make(True, self.arriving[0], behind)
+        self.both = self.whole.reshape(self.chips, -1, self.whole.shape[1])
         self.arrived = []
         flows = [
             (self.mover.forward, 1, self.chips // 2),
             (self.mover.backward, -1, (self.chips - 1) // 2),
         ]
-        self.send([(flow, self.block(flow[1] * flow[2])) for flow in flows if flow[2]])
+        if not firsts:
+            firsts = [self.block(sign * left) for _, sign, left in flows]
+        self.send(list(zip(flows, firsts)))
 
     def send(self, flows):
         self.arriving = [lax.ppermute(value, "items", flow[0]) for flow, value in flows]
@@ -1129,7 +1151,10 @@
     )
     ada_part = quarters(ada_part[:, : 2 * width], ada_part[:, 2 * width :])
     prompt_at = mover.seq if mover.pair else jnp.zeros((), jnp.int32)
-    place = jnp.stack([prompt_at, prompt_len[0], mover.core, mover.beside, mover.seq])
+    place = jnp.stack(
+        [prompt_at, prompt_len[0], mover.core, mover.beside, mover.seq]
+        + [mover.ahead[chips // 2], mover.ahead[-((chips - 1) // 2) % chips]]
+    )
     seq_place = jnp.reshape(mover.seq, (1,)).astype(jnp.int32)
     mine = pack_columns(w_query, w_key, w_value, held, seq_place)
     early = [mover.across(tokens)] if mover.pair else []
@@ -1205,12 +1230,12 @@
     def hidden_parts(own, other, behind):
         who = 2 if own else 3
         if down_columns == width:
-            return hidden_grads(place, who, active, upward, grads, lows, other, behind)
+            return hidden_grads(place, who, chips, active, upward, grads, lows, other, behind)
         core = mover.core if own else mover.beside
         first, second = parted(other, down_columns)
         down = dot_rows(halves(active, core), grads[0]).reshape(width, down_columns)
         up = dot_rows(lows, halves(upward, core))
-        return in_rows(jnp.concatenate([rounded(down, first), rounded(up, second)], axis=1))
+        return [in_rows(jnp.concatenate([rounded(down, first), rounded(up, second)], axis=1))]
 
     ring = RingSum(mover, hidden_parts, start, ready)
     if mover.pair:
@@ -1259,6 +1284,7 @@
             return tail_grads(
                 place,
                 2 if own else 3,
+                chips,
                 low_one,
                 grad_qkv,
                 mixed_heads,
@@ -1271,7 +1297,7 @@
         first, second = parted(other, grad_qkv.shape[1] // 2)
         qkv_part = rounded(dot_rows(low_one, halves(grad_qkv, core)), first)
         out_part = rounded(dot_rows(mixed, halves(attended_low, core)), second)
-        return in_rows(jnp.concatenate([qkv_part, out_part], axis=1))
+        return [in_rows(jnp.concatenate([qkv_part, out_part], axis=1))]
 
     tail = None
     grad_qkv = None

time: 416 us -> 411 us (0.988)
  local copies, waits for them, and re-layouts: 25.5 us -> 19.1 us
    squeeze x4 -> x2, local copies, waits for them, and re-layouts: 7.26 us -> 1.36 us  [pick(): lax.dynamic_index_in_dim(value, index, axis, keepdims=False, allow_negati...]
  transfers between devices with their start and end apart: 49 -> 49, of which waited for: 16 -> 16; matrix products, arithmetic and copies ran while one was open for 12% -> 11% of each run, Pallas kernels for 43% -> 44%
where the time goes in v7:
time: 411 us; the launch traced here: 406 us
  Pallas kernels  225 us (55%)
  waiting for transfers between devices  67.8 us (16%)
  starting transfers between devices  41.5 us (10%)
  other arithmetic  30.9 us (8%)
  local copies, waits for them, and re-layouts  19.1 us (5%)
  between operations  17.4 us (4%)
    pallas_call x4, Pallas kernels, attend_back(): pl.pallas_call(partial(attend_back_kernel, parts, calls, per, at), grid_s...  47.5 us
    pallas_call x2, Pallas kernels, attend(): pl.pallas_call(attend_kernel, grid_spec=pltpu.PrefetchScalarGridSpec(num_...  31.7 us
    pallas_call x4, Pallas kernels, hidden_to_width(): pl.pallas_call(partial(kernel, splits), grid=(weights.steps,), in_specs=[...  30.8 us
    pallas_call x2, Pallas kernels, hidden_grads(): pl.pallas_call(partial(hidden_grads_kernel, count, bool(more)), grid_spec...  25.5 us
    ppermute x13, waiting for transfers between devices, across(): return lax.ppermute(value, 'seq', [(0, 1), (1, 0)])  23.6 us
    ppermute x16, waiting for transfers between devices, flip(): return lax.ppermute(value, 'items', pairs)  21.6 us
    pallas_call x2, Pallas kernels, tail_grads(): pl.pallas_call(partial(tail_grads_kernel, first, bool(more), len(mixed) +...  18.7 us
    pallas_call x1, Pallas kernels, hidden_layer(): pl.pallas_call(partial(hidden_kernel, weights.per_chip, len(grads)), grid...  18.5 us
  transfers between devices with their start and end apart: 49, of which 16 were waited for; matrix products, arithmetic and copies ran while one was open for 11% of the time, Pallas kernels for 44%

profile of v7, /device:TPU:0, one launch (start us, length us, event | category | flops | bytes accessed | tf_op | source)
XLA Modules:
  0.0 405.7 jit_solution(17653817231538693285)
XLA Ops:
  10.9 2.9 collective-permute-start.7
  15.9 1.8 maximum_select_fusion.refs_3_
  22.3 6.3 %collective-permute-done.1 = f32[4,8,1024]{2,1,0:T(8,128)} collective-permute-done((f32[4,8,1024]{2,1,0:T(8,128)}, f32[4,8,1024]{2,1,0:T(8,128)}, u32[]{:S(2)}, u32[]{:S(2)}) %collective-permute-start.1) | collective-permute-done | bytes 131104 | tf_op jit(solution)/shard_map/ppermute | solution.py:982
  29.7 2.0 collective-permute-start.6
  32.7 3.4 collective-permute-done.2
  36.9 1.8 pad_maximum_fusion
  38.8 5.4 %collective-permute-done.3 = f32[4,8,1024]{2,1,0:T(8,128)S(1)} collective-permute-done((f32[4,8,1024]{2,1,0:T(8,128)S(1)}, f32[4,8,1024]{2,1,0:T(8,128)S(1)}, u32[]{:S(2)}, u32[]{:S(2)}) %collective-permute-start.3) | collective-permute-done | bytes 131104 | tf_op jit(solution)/shard_map/ppermute | solution.py:982
  49.1 5.0 %collective-permute-done.8.refs_6_ = bf16[128,1536]{1,0:T(8,128)(2,1)S(1)} collective-permute-done((bf16[128,1536]{1,0:T(8,128)(2,1)}, bf16[128,1536]{1,0:T(8,128)(2,1)S(1)}, u32[]{:S(2)}, u32[]{:S(2)}) %collective-permute-start.8) | collective-permute-done | bytes 393248 | tf_op jit(solution)/shard_map/ppermute | solution.py:1002
  56.1 3.2 stack.41.place
  60.0 9.1 %collective-permute-done.9.refs_7_ = bf16[128,1536]{1,0:T(8,128)(2,1)} collective-permute-done((bf16[128,1536]{1,0:T(8,128)(2,1)S(1)}, bf16[128,1536]{1,0:T(8,128)(2,1)}, u32[]{:S(2)}, u32[]{:S(2)}) %collective-permute-start.9) | collective-permute-done | bytes 393248 | tf_op jit(solution)/shard_map/ppermute | solution.py:1002
  69.1 11.3 %first_layer.1 = (bf16[1280,1024]{1,0:T(8,128)(2,1)}, bf16[1280,1536]{1,0:T(8,128)(2,1)}, bf16[1024,1536]{1,0:T(8,128)(2,1)}) custom-call(s32[8]{0:T(128)} %slice_bitcast_fusion.8.spots, bf16[640,1024]{1,0:T(8,128)(2,1)} %bitcast.133, bf16[640,1024]{1,0:T(8,128)(2,1)} %copy-done.10, f32[2,1024]{1,0:T(2,128)} %get-tuple-element.190.refs_2_.ada_ref, ...), custom_call_target="tpu_custom_call" | custom-call | flops 2013265920 | bytes 8388608 | tf_op jit(solution)/shard_map/first_layer/pallas_call | solution.py:347
  81.5 15.8 %attend.2 = (bf16[1280,256]{1,0:T(8,128)(2,1)}, f32[2,10,256]{2,1,0:T(8,128)}) custom-call(s32[7]{0:T(128)} %stack.41.place, bf16[1280,1536]{1,0:T(8,128)(2,1)} %get-tuple-element.88.q_ref.k_ref.v_ref, bf16[1280,1536]{1,0:T(8,128)(2,1)} %get-tuple-element.88.q_ref.k_ref.v_ref, bf16[1280,1536]{1,0:T(8,128)(2,1)} %get-tuple-element.88.q_ref.k_ref.v_ref, ...), custom_call_target="tpu_custom_call" | custom-call | flops 2516582400 | bytes 2621440 | tf_op jit(solution)/shard_map/attend/pallas_call | solution.py:91
  97.7 15.8 %attend.3 = (bf16[1280,256]{1,0:T(8,128)(2,1)}, f32[2,10,256]{2,1,0:T(8,128)}) custom-call(s32[7]{0:T(128)} %stack.41.place, bf16[1280,1536]{1,0:T(8,128)(2,1)} %get-tuple-element.88.q_ref.k_ref.v_ref, bf16[1280,1536]{1,0:T(8,128)(2,1)} %get-tuple-element.88.q_ref.k_ref.v_ref, bf16[1280,1536]{1,0:T(8,128)(2,1)} %get-tuple-element.88.q_ref.k_ref.v_ref, ...), custom_call_target="tpu_custom_call" | custom-call | flops 2516582400 | bytes 2621440 | tf_op jit(solution)/shard_map/attend/pallas_call | solution.py:91
  115.3 16.0 %collective-permute-done.15.refs_3_ = bf16[1280,256]{1,0:T(8,128)(2,1)S(1)} collective-permute-done((bf16[1280,256]{1,0:T(8,128)(2,1)}, bf16[1280,256]{1,0:T(8,128)(2,1)S(1)}, u32[]{:S(2)}, u32[]{:S(2)}) %collective-permute-start.15) | collective-permute-done | bytes 655392 | tf_op jit(solution)/shard_map/ppermute | solution.py:989
  131.3 5.5 %all-gather.3.cloned.1.call-done = bf16[5120,1024]{1,0:T(8,128)(2,1)} async-done(((bf16[320,1024]{1,0:T(8,128)(2,1)}), bf16[5120,1024]{1,0:T(8,128)(2,1)}) %all-gather.3.cloned.1.call-update) | async-done | bytes 10485776 | tf_op jit(solution)/shard_map/all_gather | solution.py:1166
  136.8 9.3 %second_layer.1 = (f32[640,1024]{1,0:T(8,128)}, bf16[1280,1024]{1,0:T(8,128)(2,1)}) custom-call(s32[7]{0:T(128)} %stack.41.place, bf16[1280,256]{1,0:T(8,128)(2,1)} %get-tuple-element.90.refs_1_.refs_0_, bf16[1280,256]{1,0:T(8,128)(2,1)} %get-tuple-element.93.refs_1_, bf16[1280,256]{1,0:T(8,128)(2,1)} %copy-done.7, bf16[1280,256]{1,0:T(8,128)(2,1)} %copy-done.8, ...), custom_call_target="tpu_custom_call" | custom-call | flops 1342177280 | bytes 7602176 | tf_op jit(solution)/shard_map/second_layer/pallas_call | solution.py:401
  146.1 18.5 %hidden_layer.1 = (bf16[1280,2048]{1,0:T(8,128)(2,1)}, bf16[1280,2048]{1,0:T(8,128)(2,1)}) custom-call(bf16[1280,1024]{1,0:T(8,128)(2,1)} %get-tuple-element.96.x_ref.refs_4_, bf16[16,5,64,1024]{3,2,1,0:T(8,128)(2,1)} %bitcast.116, bf16[8,2,5,64,1024]{4,3,2,1,0:T(8,128)(2,1)} %bitcast.117, bf16[640,1024]{1,0:T(8,128)(2,1)} %bitcast.123, ...), custom_call_target="tpu_custom_call" | custom-call | flops 5368709120 | bytes 12058624 | tf_op jit(solution)/shard_map/hidden_layer/pallas_call | solution.py:484
  164.6 7.5 %up_back.2 = (bf16[320,1024]{1,0:T(8,128)(2,1)}, bf16[320,1024]{1,0:T(8,128)(2,1)}) custom-call(bf16[1280,2048]{1,0:T(8,128)(2,1)} %get-tuple-element.98.g_ref.refs_1_, bf16[16,5,64,1024]{3,2,1,0:T(8,128)(2,1)} %bitcast.118), custom_call_target="tpu_custom_call" | custom-call | flops 1342177280 | bytes 4718592 | tf_op jit(solution)/shard_map/up_back/pallas_call | solution.py:537
  173.6 12.4 %hidden_grads.2.refs_0_ = bf16[1024,2048]{1,0:T(8,128)(2,1)} custom-call(s32[7]{0:T(128)} %stack.41.place, bf16[1280,2048]{1,0:T(8,128)(2,1)} %get-tuple-element.97.refs_0_.a_ref, bf16[1280,2048]{1,0:T(8,128)(2,1)} %get-tuple-element.98.g_ref.refs_1_, bf16[640,1024]{1,0:T(8,128)(2,1)} %bitcast.124, bf16[640,1024]{1,0:T(8,128)(2,1)} %copy-done.2, ...), custom_call_target="tpu_custom_call" | custom-call | flops 2684354560 | bytes 7340032 | tf_op jit(solution)/shard_map/hidden_grads/pallas_call | solution.py:752
  186.0 3.3 collective-permute-done.16.refs_5_
  190.8 8.1 %up_back.3.refs_6_.refs_0_ = f32[640,1024]{1,0:T(8,128)} custom-call(bf16[1280,2048]{1,0:T(8,128)(2,1)} %get-tuple-element.98.g_ref.refs_1_, bf16[16,5,64,1024]{3,2,1,0:T(8,128)(2,1)} %bitcast.119, bf16[1024,2048]{1,0:T(8,128)(2,1)} %hidden_grads.2.refs_0_), custom_call_target="tpu_custom_call" | custom-call | flops 1342177280 | bytes 4718592 | tf_op jit(solution)/shard_map/up_back/pallas_call | solution.py:537
  198.9 13.1 %hidden_grads.3 = (bf16[1024,2048]{1,0:T(8,128)(2,1)}, bf16[128,2048]{1,0:T(8,128)(2,1)}, bf16[128,2048]{1,0:T(8,128)(2,1)}) custom-call(s32[7]{0:T(128)} %stack.41.place, bf16[1280,2048]{1,0:T(8,128)(2,1)} %get-tuple-element.97.refs_0_.a_ref, bf16[1280,2048]{1,0:T(8,128)(2,1)} %get-tuple-element.98.g_ref.refs_1_, bf16[640,1024]{1,0:T(8,128)(2,1)} %bitcast.125, ...), custom_call_target="tpu_custom_call" | custom-call | flops 2684354560 | bytes 7340032 | tf_op jit(solution)/shard_map/hidden_grads/pallas_call | solution.py:752
  214.9 9.0 %middle_back.1 = (f32[640,1024]{1,0:T(8,128)}, bf16[640,1024]{1,0:T(8,128)(2,1)}, f32[2,1024]{1,0:T(2,128)}, bf16[640,512]{1,0:T(8,128)(2,1)}, bf16[640,512]{1,0:T(8,128)(2,1)}) custom-call(s32[7]{0:T(128)} %stack.41.place, f32[640,1024]{1,0:T(8,128)} %up_back.3.refs_6_.refs_0_, f32[640,1024]{1,0:T(8,128)} %get-tuple-element.95.refs_1_, ...), custom_call_target="tpu_custom_call" | custom-call | flops 671088640 | bytes 7602176 | tf_op jit(solution)/shard_map/middle_back/pallas_call | solution.py:617
  224.4 7.3 %down_part.2.refs_0_ = bf16[640,1024]{1,0:T(8,128)(2,1)} custom-call(bf16[1280,2048]{1,0:T(8,128)(2,1)} %get-tuple-element.97.refs_0_.a_ref, bf16[8,2,5,64,1024]{4,3,2,1,0:T(8,128)(2,1)} %bitcast.121, bf16[640,512]{1,0:T(8,128)(2,1)} %get-tuple-element.107.refs_0_), custom_call_target="tpu_custom_call" | custom-call | flops 1342177280 | bytes 4718592 | tf_op jit(solution)/shard_map/down_part/pallas_call | solution.py:537
  231.8 2.6 bitcast_add_fusion.1
  236.5 7.8 %down_part.3.refs_6_ = f32[640,1024]{1,0:T(8,128)} custom-call(bf16[1280,2048]{1,0:T(8,128)(2,1)} %get-tuple-element.97.refs_0_.a_ref, bf16[8,2,5,64,1024]{4,3,2,1,0:T(8,128)(2,1)} %bitcast.122, bf16[640,1024]{1,0:T(8,128)(2,1)} %down_part.2.refs_0_), custom_call_target="tpu_custom_call" | custom-call | flops 1342177280 | bytes 4718592 | tf_op jit(solution)/shard_map/down_part/pallas_call | solution.py:537
  245.1 11.8 %attend_back.4.refs_6_ = bf16[1280,1536]{1,0:T(8,128)(2,1)} custom-call(s32[7]{0:T(128)} %stack.41.place, bf16[1280,1536]{1,0:T(8,128)(2,1)} %get-tuple-element.88.q_ref.k_ref.v_ref, bf16[1280,1536]{1,0:T(8,128)(2,1)} %get-tuple-element.88.q_ref.k_ref.v_ref, bf16[1280,1536]{1,0:T(8,128)(2,1)} %get-tuple-element.88.q_ref.k_ref.v_ref, ...), custom_call_target="tpu_custom_call" | custom-call | flops 3145728000 | bytes 3276800 | tf_op jit(solution)/shard_map/attend_back/pallas_call | solution.py:204
  256.9 2.6 bitcast_add_fusion
  261.6 12.2 %attend_back.5.grad.refs_6_ = bf16[1280,1536]{1,0:T(8,128)(2,1)} custom-call(s32[7]{0:T(128)} %stack.41.place, bf16[1280,1536]{1,0:T(8,128)(2,1)} %get-tuple-element.88.q_ref.k_ref.v_ref, bf16[1280,1536]{1,0:T(8,128)(2,1)} %get-tuple-element.88.q_ref.k_ref.v_ref, ...), custom_call_target="tpu_custom_call", output_to_operand_aliasing={{}: (10, {})} | custom-call | flops 3145728000 | bytes 3276800 | tf_op jit(solution)/shard_map/attend_back/pallas_call | solution.py:204
  273.8 9.1 %tail_grads.2.refs_7_ = bf16[1024,1280]{1,0:T(8,128)(2,1)} custom-call(s32[7]{0:T(128)} %stack.41.place, bf16[1280,1024]{1,0:T(8,128)(2,1)} %get-tuple-element.109.low, bf16[1280,1536]{1,0:T(8,128)(2,1)} %attend_back.5.grad.refs_6_, bf16[640,1024]{1,0:T(8,128)(2,1)} %get-tuple-element.120.attended, bf16[1280,256]{1,0:T(8,128)(2,1)} %get-tuple-element.90.refs_1_.refs_0_, ...), custom_call_target="tpu_custom_call" | custom-call | flops 1342177280 | bytes 5242880 | tf_op jit(solution)/shard_map/tail_grads/pallas_call | solution.py:809
  284.5 1.7 bitcast_add_fusion.4
  286.7 11.8 %attend_back.6.refs_6_ = bf16[1280,1536]{1,0:T(8,128)(2,1)} custom-call(s32[7]{0:T(128)} %stack.41.place, bf16[1280,1536]{1,0:T(8,128)(2,1)} %get-tuple-element.88.q_ref.k_ref.v_ref, bf16[1280,1536]{1,0:T(8,128)(2,1)} %get-tuple-element.88.q_ref.k_ref.v_ref, bf16[1280,1536]{1,0:T(8,128)(2,1)} %get-tuple-element.88.q_ref.k_ref.v_ref, ...), custom_call_target="tpu_custom_call", output_to_operand_aliasing={{}: (10, {})} | custom-call | flops 3145728000 | bytes 3276800 | tf_op jit(solution)/shard_map/attend_back/pallas_call | solution.py:204
  298.5 1.7 collective-permute-done.26
  300.2 11.8 %attend_back.7.grad.grad_ref = bf16[1280,1536]{1,0:T(8,128)(2,1)} custom-call(s32[7]{0:T(128)} %stack.41.place, bf16[1280,1536]{1,0:T(8,128)(2,1)} %get-tuple-element.88.q_ref.k_ref.v_ref, bf16[1280,1536]{1,0:T(8,128)(2,1)} %get-tuple-element.88.q_ref.k_ref.v_ref, ...), custom_call_target="tpu_custom_call", output_to_operand_aliasing={{}: (10, {})} | custom-call | flops 3145728000 | bytes 3276800 | tf_op jit(solution)/shard_map/attend_back/pallas_call | solution.py:204
  312.1 9.6 %tail_grads.3 = (bf16[1024,1280]{1,0:T(8,128)(2,1)}, bf16[128,1280]{1,0:T(8,128)(2,1)}, bf16[128,1280]{1,0:T(8,128)(2,1)}) custom-call(s32[7]{0:T(128)} %stack.41.place, bf16[1280,1024]{1,0:T(8,128)(2,1)} %get-tuple-element.109.low, bf16[1280,1536]{1,0:T(8,128)(2,1)} %attend_back.7.grad.grad_ref, bf16[640,1024]{1,0:T(8,128)(2,1)} %get-tuple-element.120.attended, ...), custom_call_target="tpu_custom_call" | custom-call | flops 1342177280 | bytes 5242880 | tf_op jit(solution)/shard_map/tail_grads/pallas_call | solution.py:809
  326.1 6.8 %first_back.2 = (bf16[320,1024]{1,0:T(8,128)(2,1)}, bf16[320,1024]{1,0:T(8,128)(2,1)}, f32[2,1024]{1,0:T(2,128)}) custom-call(bf16[1280,1536]{1,0:T(8,128)(2,1)} %attend_back.7.grad.grad_ref, bf16[1024,1536]{1,0:T(8,128)(2,1)} %get-tuple-element.125.weight_ref, bf16[640,1024]{1,0:T(8,128)(2,1)} %copy-done.10, bf16[1024,1280]{1,0:T(8,128)(2,1)} %get-tuple-element.122.refs_0_, ...), custom_call_target="tpu_custom_call" | custom-call | flops 1006632960 | bytes 3866624 | tf_op jit(solution)/shard_map/first_back/pallas_call | solution.py:665
  333.5 1.9 fusion.1
  337.0 3.4 bitcast_add_fusion.8
  342.4 6.5 %first_back.3 = (bf16[640,1024]{1,0:T(8,128)(2,1)}, f32[2,1024]{1,0:T(2,128)}) custom-call(bf16[1280,1536]{1,0:T(8,128)(2,1)} %attend_back.7.grad.grad_ref, bf16[1024,1536]{1,0:T(8,128)(2,1)} %get-tuple-element.125.weight_ref, bf16[640,1024]{1,0:T(8,128)(2,1)} %bitcast.135, bf16[320,1024]{1,0:T(8,128)(2,1)} %get-tuple-element.145.refs_0_), custom_call_target="tpu_custom_call" | custom-call | flops 1006632960 | bytes 3866624 | tf_op jit(solution)/shard_map/first_back/pallas_call | solution.py:665
  348.9 2.1 bitcast_select_fusion
  354.0 2.5 bitcast_add_fusion.6
  361.2 1.8 fusion
  369.6 2.7 collective-permute-done.38
  374.2 3.7 collective-permute-done.39
  378.0 2.2 collective-permute-done.40.refs_1_
  381.7 1.8 fusion.2
  386.4 5.8 %input_back.1 = f32[640,1024]{1,0:T(8,128)} custom-call(bf16[640,1024]{1,0:T(8,128)(2,1)} %get-tuple-element.136.own_ref, bf16[640,1024]{1,0:T(8,128)(2,1)} %bitcast.136, f32[2,1024]{1,0:T(2,128)} %get-tuple-element.190.refs_2_.ada_ref, f32[640,1024]{1,0:T(8,128)} %get-tuple-element.137.base_ref, bf16[320,1024]{1,0:T(8,128)(2,1)} %collective-permute-done.33.refs_0_, ...), custom_call_target="tpu_custom_call" | custom-call | flops 6553600 | bytes 4587520 | tf_op jit(solution)/shard_map/input_back/pallas_call | solution.py:855
  396.0 2.6 join_tail.1
  (210 shorter events, 67.6 us)
Async XLA Ops:
  7.2 129.6 %all-gather.3.cloned.1.call-start = ((), (), s32[]{:S(2)}) async-start(), calls=%async_computation | async-start | bytes 11141120 | tf_op jit(solution)/shard_map/all_gather | solution.py:1166
  8.7 10.6 %collective-permute-start = (f32[4,8,1024]{2,1,0:T(8,128)S(1)}, f32[4,8,1024]{2,1,0:T(8,128)S(1)}, u32[]{:S(2)}, u32[]{:S(2)}) collective-permute-start(f32[4,8,1024]{2,1,0:T(8,128)S(1)} %pad_maximum_fusion.3), channel_id=1, source_target_pairs={{0,2},{2,0},{4,6},{6,4},{8,10},{10,8},{12,14},{14,12},{16,18},{18,... | collective-permute-start | bytes 393224 | tf_op jit(solution)/shard_map/ppermute | solution.py:982
  10.9 5.0 %collective-permute-start.4 = (bf16[64,1536]{1,0:T(8,128)(2,1)}, bf16[64,1536]{1,0:T(8,128)(2,1)S(1)}, u32[]{:S(2)}, u32[]{:S(2)}) collective-permute-start(bf16[64,1536]{1,0:T(8,128)(2,1)} %pack_columns.1), channel_id=1, source_target_pairs={{0,2},{2,0},{4,6},{6,4},{8,10},{10,8},{12,14},{14,12},{16,18},{18,... | collective-permute-start | bytes 589832 | tf_op jit(solution)/shard_map/ppermute | solution.py:982
  10.9 33.2 %collective-permute-start.7 = (bf16[640,1024]{1,0:T(8,128)(2,1)}, bf16[640,1024]{1,0:T(8,128)(2,1)S(1)}, u32[]{:S(2)}, u32[]{:S(2)}) collective-permute-start(bf16[640,1024]{1,0:T(8,128)(2,1)} %bitcast.132), channel_id=1, source_target_pairs={{0,1},{1,0},{2,3},{3,2},{4,5},{5,4},{6,7},{7,6},{8,9},{9,8},{10,11... | collective-permute-start | bytes 3932168 | tf_op jit(solution)/shard_map/ppermute | solution.py:989
  17.7 12.0 %collective-permute-start.5 = (bf16[128,1536]{1,0:T(8,128)(2,1)}, bf16[128,1536]{1,0:T(8,128)(2,1)}, u32[]{:S(2)}, u32[]{:S(2)}) collective-permute-start(bf16[128,1536]{1,0:T(8,128)(2,1)} %maximum_select_fusion.refs_3_), channel_id=1, source_target_pairs={{0,8},{8,16},{16,24},{24,28},{28,20},{20,12},{12,4},{4,0},{10,2},{... | collective-permute-start | bytes 1179656 | tf_op jit(solution)/shard_map/ppermute | solution.py:1002
  20.0 8.6 %collective-permute-start.1 = (f32[4,8,1024]{2,1,0:T(8,128)}, f32[4,8,1024]{2,1,0:T(8,128)}, u32[]{:S(2)}, u32[]{:S(2)}) collective-permute-start(f32[4,8,1024]{2,1,0:T(8,128)} %fusion.24), channel_id=1, source_target_pairs={{0,4},{2,6},{4,0},{6,2},{8,12},{10,14},{12,8},{14,10},{16,20},{18,... | collective-permute-start | bytes 393224 | tf_op jit(solution)/shard_map/ppermute | solution.py:982
  29.6 6.5 %collective-permute-start.2 = (f32[4,8,1024]{2,1,0:T(8,128)S(1)}, f32[4,8,1024]{2,1,0:T(8,128)S(1)}, u32[]{:S(2)}, u32[]{:S(2)}) collective-permute-start(f32[4,8,1024]{2,1,0:T(8,128)S(1)} %fusion.29), channel_id=1, source_target_pairs={{0,8},{2,10},{4,12},{6,14},{8,0},{10,2},{12,4},{14,6},{16,24},{18,... | collective-permute-start | bytes 393224 | tf_op jit(solution)/shard_map/ppermute | solution.py:982
  29.7 14.5 %collective-permute-start.6 = (bf16[128,1536]{1,0:T(8,128)(2,1)}, bf16[128,1536]{1,0:T(8,128)(2,1)}, u32[]{:S(2)}, u32[]{:S(2)}) collective-permute-start(bf16[128,1536]{1,0:T(8,128)(2,1)} %collective-permute-done.5.refs_4_), channel_id=1, source_target_pairs={{0,8},{8,16},{16,24},{24,28},{28,20},{20,12},{12,4},{4,0},{10,2},{... | collective-permute-start | bytes 1179656 | tf_op jit(solution)/shard_map/ppermute | solution.py:1002
  36.1 8.0 %collective-permute-start.3 = (f32[4,8,1024]{2,1,0:T(8,128)S(1)}, f32[4,8,1024]{2,1,0:T(8,128)S(1)}, u32[]{:S(2)}, u32[]{:S(2)}) collective-permute-start(f32[4,8,1024]{2,1,0:T(8,128)S(1)} %add.86), channel_id=1, source_target_pairs={{0,16},{2,18},{4,20},{6,22},{8,24},{10,26},{12,28},{14,30},{16,0},... | collective-permute-start | bytes 393224 | tf_op jit(solution)/shard_map/ppermute | solution.py:982
  45.2 35.2 %collective-permute-start.13 = (bf16[640,1024]{1,0:T(8,128)(2,1)S(1)}, bf16[640,1024]{1,0:T(8,128)(2,1)S(1)}, u32[]{:S(2)}, u32[]{:S(2)}) collective-permute-start(bf16[640,1024]{1,0:T(8,128)(2,1)S(1)} %bitcast.127), channel_id=1, source_target_pairs={{0,1},{1,0},{2,3},{3,2},{4,5},{5,4},{6,7},{7,6},{8,9},{9,8},{10,11... | collective-permute-start | bytes 3932168 | tf_op jit(solution)/shard_map/ppermute | solution.py:989
  45.8 8.4 %collective-permute-start.8 = (bf16[128,1536]{1,0:T(8,128)(2,1)}, bf16[128,1536]{1,0:T(8,128)(2,1)S(1)}, u32[]{:S(2)}, u32[]{:S(2)}) collective-permute-start(bf16[128,1536]{1,0:T(8,128)(2,1)} %collective-permute-done.6.refs_5_), channel_id=1, source_target_pairs={{0,8},{8,16},{16,24},{24,28},{28,20},{20,12},{12,4},{4,0},{10,2},{... | collective-permute-start | bytes 1179656 | tf_op jit(solution)/shard_map/ppermute | solution.py:1002
  48.6 11.4 %collective-permute-start.10 = (bf16[128,1536]{1,0:T(8,128)(2,1)}, bf16[128,1536]{1,0:T(8,128)(2,1)}, u32[]{:S(2)}, u32[]{:S(2)}) collective-permute-start(bf16[128,1536]{1,0:T(8,128)(2,1)} %collective-permute-done.5.refs_4_), channel_id=1, source_target_pairs={{0,2},{2,0},{4,6},{6,4},{8,10},{10,8},{12,14},{14,12},{16,18},{18,... | collective-permute-start | bytes 1179656 | tf_op jit(solution)/shard_map/ppermute | solution.py:982
  48.6 11.4 %collective-permute-start.11 = (bf16[128,1536]{1,0:T(8,128)(2,1)}, bf16[128,1536]{1,0:T(8,128)(2,1)}, u32[]{:S(2)}, u32[]{:S(2)}) collective-permute-start(bf16[128,1536]{1,0:T(8,128)(2,1)} %collective-permute-done.6.refs_5_), channel_id=1, source_target_pairs={{0,2},{2,0},{4,6},{6,4},{8,10},{10,8},{12,14},{14,12},{16,18},{18,... | collective-permute-start | bytes 1179656 | tf_op jit(solution)/shard_map/ppermute | solution.py:982
  54.2 14.9 %collective-permute-start.9 = (bf16[128,1536]{1,0:T(8,128)(2,1)S(1)}, bf16[128,1536]{1,0:T(8,128)(2,1)}, u32[]{:S(2)}, u32[]{:S(2)}) collective-permute-start(bf16[128,1536]{1,0:T(8,128)(2,1)S(1)} %collective-permute-done.8.refs_6_), channel_id=1, source_target_pairs={{0,8},{8,16},{16,24},{24,28},{28,20},{20,12},{12,4},{4,0},{10,2},{... | collective-permute-start | bytes 1179656 | tf_op jit(solution)/shard_map/ppermute | solution.py:1002
  55.4 13.7 %collective-permute-start.12 = (bf16[128,1536]{1,0:T(8,128)(2,1)S(1)}, bf16[128,1536]{1,0:T(8,128)(2,1)}, u32[]{:S(2)}, u32[]{:S(2)}) collective-permute-start(bf16[128,1536]{1,0:T(8,128)(2,1)S(1)} %collective-permute-done.8.refs_6_), channel_id=1, source_target_pairs={{0,2},{2,0},{4,6},{6,4},{8,10},{10,8},{12,14},{14,12},{16,18},{18,... | collective-permute-start | bytes 1179656 | tf_op jit(solution)/shard_map/ppermute | solution.py:982
  97.3 17.3 %collective-permute-start.14 = (bf16[1280,256]{1,0:T(8,128)(2,1)}, bf16[1280,256]{1,0:T(8,128)(2,1)S(1)}, u32[]{:S(2)}, u32[]{:S(2)}) collective-permute-start(bf16[1280,256]{1,0:T(8,128)(2,1)} %get-tuple-element.90.refs_1_.refs_0_), channel_id=1, source_target_pairs={{0,1},{1,0},{2,3},{3,2},{4,5},{5,4},{6,7},{7,6},{8,9},{9,8},{10,11... | collective-permute-start | bytes 1966088 | tf_op jit(solution)/shard_map/ppermute | solution.py:989
  114.7 16.6 %collective-permute-start.15 = (bf16[1280,256]{1,0:T(8,128)(2,1)}, bf16[1280,256]{1,0:T(8,128)(2,1)S(1)}, u32[]{:S(2)}, u32[]{:S(2)}) collective-permute-start(bf16[1280,256]{1,0:T(8,128)(2,1)} %get-tuple-element.93.refs_1_), channel_id=1, source_target_pairs={{0,1},{1,0},{2,3},{3,2},{4,5},{5,4},{6,7},{7,6},{8,9},{9,8},{10,11... | collective-permute-start | bytes 1966088 | tf_op jit(solution)/shard_map/ppermute | solution.py:989
  172.1 17.1 %collective-permute-start.16 = (bf16[320,1024]{1,0:T(8,128)(2,1)}, bf16[320,1024]{1,0:T(8,128)(2,1)S(1)}, u32[]{:S(2)}, u32[]{:S(2)}) collective-permute-start(bf16[320,1024]{1,0:T(8,128)(2,1)} %get-tuple-element.99.refs_5_), channel_id=1, source_target_pairs={{0,1},{1,0},{2,3},{3,2},{4,5},{5,4},{6,7},{7,6},{8,9},{9,8},{10,11... | collective-permute-start | bytes 1966088 | tf_op jit(solution)/shard_map/ppermute | solution.py:989
  189.2 9.6 %collective-permute-start.17 = (bf16[1024,2048]{1,0:T(8,128)(2,1)}, bf16[1024,2048]{1,0:T(8,128)(2,1)}, u32[]{:S(2)}, u32[]{:S(2)}) collective-permute-start(bf16[1024,2048]{1,0:T(8,128)(2,1)} %hidden_grads.2.refs_0_), channel_id=1, source_target_pairs={{0,2},{2,0},{4,6},{6,4},{8,10},{10,8},{12,14},{14,12},{16,18},{18,... | collective-permute-start | bytes 12582920 | tf_op jit(solution)/shard_map/ppermute | solution.py:982
  189.2 24.8 %collective-permute-start.20 = (bf16[320,1024]{1,0:T(8,128)(2,1)S(1)}, bf16[320,1024]{1,0:T(8,128)(2,1)S(1)}, u32[]{:S(2)}, u32[]{:S(2)}) collective-permute-start(bf16[320,1024]{1,0:T(8,128)(2,1)S(1)} %copy-done.39), channel_id=1, source_target_pairs={{0,1},{1,0},{2,3},{3,2},{4,5},{5,4},{6,7},{7,6},{8,9},{9,8},{10,11... | collective-permute-start | bytes 1966088 | tf_op jit(solution)/shard_map/ppermute | solution.py:989
  212.0 19.8 %collective-permute-start.18 = (bf16[128,2048]{1,0:T(8,128)(2,1)}, bf16[128,2048]{1,0:T(8,128)(2,1)S(1)}, u32[]{:S(2)}, u32[]{:S(2)}) collective-permute-start(bf16[128,2048]{1,0:T(8,128)(2,1)} %get-tuple-element.102), channel_id=1, source_target_pairs={{0,8},{2,10},{8,16},{10,18},{16,24},{18,26},{24,28},{26,30},{28,20... | collective-permute-start | bytes 1572872 | tf_op jit(solution)/shard_map/ppermute | solution.py:1064
  212.5 19.2 %collective-permute-start.19 = (bf16[128,2048]{1,0:T(8,128)(2,1)}, bf16[128,2048]{1,0:T(8,128)(2,1)S(1)}, u32[]{:S(2)}, u32[]{:S(2)}) collective-permute-start(bf16[128,2048]{1,0:T(8,128)(2,1)} %get-tuple-element.103), channel_id=1, source_target_pairs={{8,0},{10,2},{16,8},{18,10},{24,16},{26,18},{28,24},{30,26},{20,28... | collective-permute-start | bytes 1572872 | tf_op jit(solution)/shard_map/ppermute | solution.py:1064
  223.8 20.5 %collective-permute-start.21 = (bf16[640,512]{1,0:T(8,128)(2,1)}, bf16[640,512]{1,0:T(8,128)(2,1)S(1)}, u32[]{:S(2)}, u32[]{:S(2)}) collective-permute-start(bf16[640,512]{1,0:T(8,128)(2,1)} %get-tuple-element.107.refs_0_), channel_id=1, source_target_pairs={{0,1},{1,0},{2,3},{3,2},{4,5},{5,4},{6,7},{7,6},{8,9},{9,8},{10,11... | collective-permute-start | bytes 1966088 | tf_op jit(solution)/shard_map/ppermute | solution.py:989
  234.4 22.5 %collective-permute-start.22 = (bf16[128,2048]{1,0:T(8,128)(2,1)S(1)}, bf16[128,2048]{1,0:T(8,128)(2,1)S(1)}, u32[]{:S(2)}, u32[]{:S(2)}) collective-permute-start(bf16[128,2048]{1,0:T(8,128)(2,1)S(1)} %get-tuple-element.160), channel_id=1, source_target_pairs={{0,8},{2,10},{8,16},{10,18},{16,24},{18,26},{24,28},{26,30},{28,20... | collective-permute-start | bytes 1572872 | tf_op jit(solution)/shard_map/ppermute | solution.py:1064
  234.9 22.0 %collective-permute-start.23 = (bf16[128,2048]{1,0:T(8,128)(2,1)S(1)}, bf16[128,2048]{1,0:T(8,128)(2,1)S(1)}, u32[]{:S(2)}, u32[]{:S(2)}) collective-permute-start(bf16[128,2048]{1,0:T(8,128)(2,1)S(1)} %get-tuple-element.159), channel_id=1, source_target_pairs={{8,0},{10,2},{16,8},{18,10},{24,16},{26,18},{28,24},{30,26},{20,28... | collective-permute-start | bytes 1572872 | tf_op jit(solution)/shard_map/ppermute | solution.py:1064
  259.5 14.3 %collective-permute-start.24 = (bf16[128,2048]{1,0:T(8,128)(2,1)S(1)}, bf16[128,2048]{1,0:T(8,128)(2,1)S(1)}, u32[]{:S(2)}, u32[]{:S(2)}) collective-permute-start(bf16[128,2048]{1,0:T(8,128)(2,1)S(1)} %get-tuple-element.158), channel_id=1, source_target_pairs={{0,8},{2,10},{8,16},{10,18},{16,24},{18,26},{24,28},{26,30},{28,20... | collective-permute-start | bytes 1572872 | tf_op jit(solution)/shard_map/ppermute | solution.py:1064
  260.1 13.7 %collective-permute-start.25 = (bf16[128,2048]{1,0:T(8,128)(2,1)S(1)}, bf16[128,2048]{1,0:T(8,128)(2,1)S(1)}, u32[]{:S(2)}, u32[]{:S(2)}) collective-permute-start(bf16[128,2048]{1,0:T(8,128)(2,1)S(1)} %get-tuple-element.157), channel_id=1, source_target_pairs={{8,0},{10,2},{16,8},{18,10},{24,16},{26,18},{28,24},{30,26},{20,28... | collective-permute-start | bytes 1572872 | tf_op jit(solution)/shard_map/ppermute | solution.py:1064
  282.9 29.1 %collective-permute-start.27 = (bf16[1024,1280]{1,0:T(8,128)(2,1)}, bf16[1024,1280]{1,0:T(8,128)(2,1)}, u32[]{:S(2)}, u32[]{:S(2)}) collective-permute-start(bf16[1024,1280]{1,0:T(8,128)(2,1)} %tail_grads.2.refs_7_), channel_id=1, source_target_pairs={{0,2},{2,0},{4,6},{6,4},{8,10},{10,8},{12,14},{14,12},{16,18},{18,... | collective-permute-start | bytes 7864328 | tf_op jit(solution)/shard_map/ppermute | solution.py:982
  282.9 42.1 %collective-permute-start.30 = (bf16[640,1024]{1,0:T(8,128)(2,1)S(1)}, bf16[640,1024]{1,0:T(8,128)(2,1)S(1)}, u32[]{:S(2)}, u32[]{:S(2)}) collective-permute-start(bf16[640,1024]{1,0:T(8,128)(2,1)S(1)} %copy-done.9), channel_id=1, source_target_pairs={{0,1},{1,0},{2,3},{3,2},{4,5},{5,4},{6,7},{7,6},{8,9},{9,8},{10,11... | collective-permute-start | bytes 3932168 | tf_op jit(solution)/shard_map/ppermute | solution.py:989
  286.2 14.0 %collective-permute-start.26 = (bf16[128,2048]{1,0:T(8,128)(2,1)S(1)}, bf16[128,2048]{1,0:T(8,128)(2,1)S(1)}, u32[]{:S(2)}, u32[]{:S(2)}) collective-permute-start(bf16[128,2048]{1,0:T(8,128)(2,1)S(1)} %bitcast_add_fusion.4), channel_id=1, source_target_pairs={{0,8},{2,10},{8,16},{10,18},{16,24},{18,26},{24,28},{26,30},{28,20... | collective-permute-start | bytes 1572872 | tf_op jit(solution)/shard_map/ppermute | solution.py:1064
  321.7 11.8 %collective-permute-start.28 = (bf16[128,1280]{1,0:T(8,128)(2,1)}, bf16[128,1280]{1,0:T(8,128)(2,1)S(1)}, u32[]{:S(2)}, u32[]{:S(2)}) collective-permute-start(bf16[128,1280]{1,0:T(8,128)(2,1)} %get-tuple-element.123), channel_id=1, source_target_pairs={{0,8},{2,10},{8,16},{10,18},{16,24},{18,26},{24,28},{26,30},{28,20... | collective-permute-start | bytes 983048 | tf_op jit(solution)/shard_map/ppermute | solution.py:1064
  322.2 11.3 %collective-permute-start.29 = (bf16[128,1280]{1,0:T(8,128)(2,1)}, bf16[128,1280]{1,0:T(8,128)(2,1)}, u32[]{:S(2)}, u32[]{:S(2)}) collective-permute-start(bf16[128,1280]{1,0:T(8,128)(2,1)} %get-tuple-element.124), channel_id=1, source_target_pairs={{8,0},{10,2},{16,8},{18,10},{24,16},{26,18},{28,24},{30,26},{20,28... | collective-permute-start | bytes 983048 | tf_op jit(solution)/shard_map/ppermute | solution.py:1064
  332.9 19.7 %collective-permute-start.33 = (bf16[320,1024]{1,0:T(8,128)(2,1)}, bf16[320,1024]{1,0:T(8,128)(2,1)}, u32[]{:S(2)}, u32[]{:S(2)}) collective-permute-start(bf16[320,1024]{1,0:T(8,128)(2,1)} %get-tuple-element.134), channel_id=1, source_target_pairs={{0,1},{1,0},{2,3},{3,2},{4,5},{5,4},{6,7},{7,6},{8,9},{9,8},{10,11... | collective-permute-start | bytes 1966088 | tf_op jit(solution)/shard_map/ppermute | solution.py:989
  336.9 12.0 %collective-permute-start.45 = (f32[64,1024]{1,0:T(8,128)S(1)}, f32[64,1024]{1,0:T(8,128)}, u32[]{:S(2)}, u32[]{:S(2)}) collective-permute-start(f32[64,1024]{1,0:T(8,128)S(1)} %dynamic-slice_bitcast_fusion), channel_id=1, source_target_pairs={{0,2},{2,0},{4,6},{6,4},{8,10},{10,8},{12,14},{14,12},{16,18},{18,... | collective-permute-start | bytes 786440 | tf_op jit(solution)/shard_map/ppermute | solution.py:982
  340.4 12.3 %collective-permute-start.31 = (bf16[128,1280]{1,0:T(8,128)(2,1)}, bf16[128,1280]{1,0:T(8,128)(2,1)S(1)}, u32[]{:S(2)}, u32[]{:S(2)}) collective-permute-start(bf16[128,1280]{1,0:T(8,128)(2,1)} %get-tuple-element.164), channel_id=1, source_target_pairs={{0,8},{2,10},{8,16},{10,18},{16,24},{18,26},{24,28},{26,30},{28,20... | collective-permute-start | bytes 983048 | tf_op jit(solution)/shard_map/ppermute | solution.py:1064
  340.9 11.8 %collective-permute-start.32 = (bf16[128,1280]{1,0:T(8,128)(2,1)}, bf16[128,1280]{1,0:T(8,128)(2,1)}, u32[]{:S(2)}, u32[]{:S(2)}) collective-permute-start(bf16[128,1280]{1,0:T(8,128)(2,1)} %get-tuple-element.163), channel_id=1, source_target_pairs={{8,0},{10,2},{16,8},{18,10},{24,16},{26,18},{28,24},{30,26},{20,28... | collective-permute-start | bytes 983048 | tf_op jit(solution)/shard_map/ppermute | solution.py:1064
  351.1 21.3 %collective-permute-start.46 = (f32[32,2048]{1,0:T(8,128)S(1)}, f32[32,2048]{1,0:T(8,128)S(1)}, u32[]{:S(2)}, u32[]{:S(2)}) collective-permute-start(f32[32,2048]{1,0:T(8,128)S(1)} %fusion.7), channel_id=1, source_target_pairs={{0,1},{1,0},{2,3},{3,2},{4,5},{5,4},{6,7},{7,6},{8,9},{9,8},{10,11... | collective-permute-start | bytes 786440 | tf_op jit(solution)/shard_map/ppermute | solution.py:989
  353.4 6.3 %collective-permute-start.36 = (f32[4,1024]{1,0:T(4,128)S(1)}, f32[4,1024]{1,0:T(4,128)S(1)}, u32[]{:S(2)}, u32[]{:S(2)}) collective-permute-start(f32[4,1024]{1,0:T(4,128)S(1)} %pad_maximum_fusion.4), channel_id=1, source_target_pairs={{0,1},{1,0},{2,3},{3,2},{4,5},{5,4},{6,7},{7,6},{8,9},{9,8},{10,11... | collective-permute-start | bytes 49160 | tf_op jit(solution)/shard_map/ppermute | solution.py:989
  356.6 9.0 %collective-permute-start.34 = (bf16[128,1280]{1,0:T(8,128)(2,1)S(1)}, bf16[128,1280]{1,0:T(8,128)(2,1)S(1)}, u32[]{:S(2)}, u32[]{:S(2)}) collective-permute-start(bf16[128,1280]{1,0:T(8,128)(2,1)S(1)} %get-tuple-element.162), channel_id=1, source_target_pairs={{0,8},{2,10},{8,16},{10,18},{16,24},{18,26},{24,28},{26,30},{28,20... | collective-permute-start | bytes 983048 | tf_op jit(solution)/shard_map/ppermute | solution.py:1064
  357.5 8.5 %collective-permute-start.35 = (bf16[128,1280]{1,0:T(8,128)(2,1)S(1)}, bf16[128,1280]{1,0:T(8,128)(2,1)S(1)}, u32[]{:S(2)}, u32[]{:S(2)}) collective-permute-start(bf16[128,1280]{1,0:T(8,128)(2,1)S(1)} %get-tuple-element.161), channel_id=1, source_target_pairs={{8,0},{10,2},{16,8},{18,10},{24,16},{26,18},{28,24},{30,26},{20,28... | collective-permute-start | bytes 983048 | tf_op jit(solution)/shard_map/ppermute | solution.py:1064
  363.1 17.1 %collective-permute-start.40 = (bf16[320,1024]{1,0:T(8,128)(2,1)S(1)}, bf16[320,1024]{1,0:T(8,128)(2,1)S(1)}, u32[]{:S(2)}, u32[]{:S(2)}) collective-permute-start(bf16[320,1024]{1,0:T(8,128)(2,1)S(1)} %copy-done.13), channel_id=1, source_target_pairs={{0,1},{1,0},{2,3},{3,2},{4,5},{5,4},{6,7},{7,6},{8,9},{9,8},{10,11... | collective-permute-start | bytes 1966088 | tf_op jit(solution)/shard_map/ppermute | solution.py:989
  365.9 6.4 %collective-permute-start.38 = (f32[4,8,1024]{2,1,0:T(8,128)S(1)}, f32[4,8,1024]{2,1,0:T(8,128)S(1)}, u32[]{:S(2)}, u32[]{:S(2)}) collective-permute-start(f32[4,8,1024]{2,1,0:T(8,128)S(1)} %fusion.18), channel_id=1, source_target_pairs={{0,4},{2,6},{4,0},{6,2},{8,12},{10,14},{12,8},{14,10},{16,20},{18,... | collective-permute-start | bytes 393224 | tf_op jit(solution)/shard_map/ppermute | solution.py:982
  369.0 12.7 %collective-permute-start.41 = (bf16[128,1280]{1,0:T(8,128)(2,1)S(1)}, bf16[128,1280]{1,0:T(8,128)(2,1)}, u32[]{:S(2)}, u32[]{:S(2)}) collective-permute-start(bf16[128,1280]{1,0:T(8,128)(2,1)S(1)} %bitcast_add_fusion.5), channel_id=1, source_target_pairs={{0,8},{2,10},{8,16},{10,18},{16,24},{18,26},{24,28},{26,30},{28,20... | collective-permute-start | bytes 983048 | tf_op jit(solution)/shard_map/ppermute | solution.py:1064
  372.3 5.6 %collective-permute-start.39 = (f32[4,8,1024]{2,1,0:T(8,128)S(1)}, f32[4,8,1024]{2,1,0:T(8,128)S(1)}, u32[]{:S(2)}, u32[]{:S(2)}) collective-permute-start(f32[4,8,1024]{2,1,0:T(8,128)S(1)} %add.102), channel_id=1, source_target_pairs={{0,8},{2,10},{4,12},{6,14},{8,0},{10,2},{12,4},{14,6},{16,24},{18,... | collective-permute-start | bytes 393224 | tf_op jit(solution)/shard_map/ppermute | solution.py:982
  380.2 11.9 %collective-permute-start.47 = (f32[4,8,1024]{2,1,0:T(8,128)S(1)}, f32[4,8,1024]{2,1,0:T(8,128)S(1)}, u32[]{:S(2)}, u32[]{:S(2)}) collective-permute-start(f32[4,8,1024]{2,1,0:T(8,128)S(1)} %add.103), channel_id=1, source_target_pairs={{0,16},{2,18},{4,20},{6,22},{8,24},{10,26},{12,28},{14,30},{16,0},... | collective-permute-start | bytes 393224 | tf_op jit(solution)/shard_map/ppermute | solution.py:982
  384.2 11.0 %collective-permute-start.42 = (f32[32,1280]{1,0:T(8,128)S(1)}, f32[32,1280]{1,0:T(8,128)S(1)}, u32[]{:S(2)}, u32[]{:S(2)}) collective-permute-start(f32[32,1280]{1,0:T(8,128)S(1)} %get-tuple-element.173), channel_id=1, source_target_pairs={{0,1},{1,0},{2,3},{3,2},{4,5},{5,4},{6,7},{7,6},{8,9},{9,8},{10,11... | collective-permute-start | bytes 491528 | tf_op jit(solution)/shard_map/ppermute | solution.py:989
  385.7 9.5 %collective-permute-start.43 = (f32[32,1280]{1,0:T(8,128)S(1)}, f32[32,1280]{1,0:T(8,128)S(1)}, u32[]{:S(2)}, u32[]{:S(2)}) collective-permute-start(f32[32,1280]{1,0:T(8,128)S(1)} %get-tuple-element.172), channel_id=1, source_target_pairs={{0,2},{2,0},{4,6},{6,4},{8,10},{10,8},{12,14},{14,12},{16,18},{18,... | collective-permute-start | bytes 491528 | tf_op jit(solution)/shard_map/ppermute | solution.py:982
  385.7 9.5 %collective-permute-start.44 = (f32[32,1280]{1,0:T(8,128)S(1)}, f32[32,1280]{1,0:T(8,128)S(1)}, u32[]{:S(2)}, u32[]{:S(2)}) collective-permute-start(f32[32,1280]{1,0:T(8,128)S(1)} %get-tuple-element.171), channel_id=1, source_target_pairs={{0,3},{1,2},{2,1},{3,0},{4,7},{5,6},{6,5},{7,4},{8,11},{9,10},{10,... | collective-permute-start | bytes 491528 | tf_op jit(solution)/shard_map/ppermute | solution.py:986
  (42 other events, 390.4 us)
Sparse Core Ops, SparseCore 0:
  44.3 92.4 all-gather.2

commit v8 on v7

--- a/solution.py
+++ b/solution.py
@@ -1268,7 +1268,7 @@
         out_other = down_part(active, weights, rows, 1, jnp.bfloat16, grad_mixed[:1])
         grad_heads = [grad_mixed[1], mover.across(grad_mixed[0])]
         out_other = ring.advance(out_other)
-        out_own = down_part(active, weights, rows, 0, jnp.float32, [out_other])
+        out_own = down_part(active, weights, rows, 0, jnp.bfloat16, [out_other])
         filler = [out_own]
         out_other = mover.across(out_other)
     else:

time: 411 us -> 410 us (level)
  no operation moved by 1% of the time
where the time goes in v8:
time: 410 us; the launch traced here: 405 us
  Pallas kernels  225 us (55%)
  waiting for transfers between devices  66.9 us (16%)
  starting transfers between devices  41.2 us (10%)
  other arithmetic  30.2 us (7%)
  local copies, waits for them, and re-layouts  21 us (5%)
  between operations  17.6 us (4%)
    pallas_call x4, Pallas kernels, attend_back(): pl.pallas_call(partial(attend_back_kernel, parts, calls, per, at), grid_s...  47.6 us
    pallas_call x2, Pallas kernels, attend(): pl.pallas_call(attend_kernel, grid_spec=pltpu.PrefetchScalarGridSpec(num_...  31.6 us
    pallas_call x4, Pallas kernels, hidden_to_width(): pl.pallas_call(partial(kernel, splits), grid=(weights.steps,), in_specs=[...  30.3 us
    pallas_call x2, Pallas kernels, hidden_grads(): pl.pallas_call(partial(hidden_grads_kernel, count, bool(more)), grid_spec...  25.5 us
    ppermute x13, waiting for transfers between devices, across(): return lax.ppermute(value, 'seq', [(0, 1), (1, 0)])  24.2 us
    ppermute x16, waiting for transfers between devices, flip(): return lax.ppermute(value, 'items', pairs)  19.9 us
    pallas_call x2, Pallas kernels, tail_grads(): pl.pallas_call(partial(tail_grads_kernel, first, bool(more), len(mixed) +...  18.7 us
    pallas_call x1, Pallas kernels, hidden_layer(): pl.pallas_call(partial(hidden_kernel, weights.per_chip, len(grads)), grid...  18.5 us
  transfers between devices with their start and end apart: 49, of which 16 were waited for; matrix products, arithmetic and copies ran while one was open for 11% of the time, Pallas kernels for 44%

profile of v8, /device:TPU:0, one launch (start us, length us, event | category | flops | bytes accessed | tf_op | source)
XLA Modules:
  0.0 405.3 jit_solution(10590845538649695429)
XLA Ops:
  10.9 2.9 collective-permute-start.7
  15.9 1.8 maximum_select_fusion.refs_3_
  22.3 6.3 %collective-permute-done.1 = f32[4,8,1024]{2,1,0:T(8,128)} collective-permute-done((f32[4,8,1024]{2,1,0:T(8,128)}, f32[4,8,1024]{2,1,0:T(8,128)}, u32[]{:S(2)}, u32[]{:S(2)}) %collective-permute-start.1) | collective-permute-done | bytes 131104 | tf_op jit(solution)/shard_map/ppermute | solution.py:982
  29.8 2.0 collective-permute-start.6
  32.8 3.4 collective-permute-done.2
  37.0 1.8 pad_maximum_fusion
  38.8 5.4 %collective-permute-done.3 = f32[4,8,1024]{2,1,0:T(8,128)S(1)} collective-permute-done((f32[4,8,1024]{2,1,0:T(8,128)S(1)}, f32[4,8,1024]{2,1,0:T(8,128)S(1)}, u32[]{:S(2)}, u32[]{:S(2)}) %collective-permute-start.3) | collective-permute-done | bytes 131104 | tf_op jit(solution)/shard_map/ppermute | solution.py:982
  49.1 5.1 %collective-permute-done.8.refs_6_ = bf16[128,1536]{1,0:T(8,128)(2,1)S(1)} collective-permute-done((bf16[128,1536]{1,0:T(8,128)(2,1)}, bf16[128,1536]{1,0:T(8,128)(2,1)S(1)}, u32[]{:S(2)}, u32[]{:S(2)}) %collective-permute-start.8) | collective-permute-done | bytes 393248 | tf_op jit(solution)/shard_map/ppermute | solution.py:1002
  56.1 3.3 stack.41.place
  60.1 9.0 %collective-permute-done.9.refs_7_ = bf16[128,1536]{1,0:T(8,128)(2,1)} collective-permute-done((bf16[128,1536]{1,0:T(8,128)(2,1)S(1)}, bf16[128,1536]{1,0:T(8,128)(2,1)}, u32[]{:S(2)}, u32[]{:S(2)}) %collective-permute-start.9) | collective-permute-done | bytes 393248 | tf_op jit(solution)/shard_map/ppermute | solution.py:1002
  69.1 11.3 %first_layer.1 = (bf16[1280,1024]{1,0:T(8,128)(2,1)}, bf16[1280,1536]{1,0:T(8,128)(2,1)}, bf16[1024,1536]{1,0:T(8,128)(2,1)}) custom-call(s32[8]{0:T(128)} %slice_bitcast_fusion.8.spots, bf16[640,1024]{1,0:T(8,128)(2,1)} %bitcast.133, bf16[640,1024]{1,0:T(8,128)(2,1)} %copy-done.11, f32[2,1024]{1,0:T(2,128)} %get-tuple-element.190.refs_2_.ada_ref, ...), custom_call_target="tpu_custom_call" | custom-call | flops 2013265920 | bytes 8388608 | tf_op jit(solution)/shard_map/first_layer/pallas_call | solution.py:347
  81.5 15.8 %attend.2 = (bf16[1280,256]{1,0:T(8,128)(2,1)}, f32[2,10,256]{2,1,0:T(8,128)}) custom-call(s32[7]{0:T(128)} %stack.41.place, bf16[1280,1536]{1,0:T(8,128)(2,1)} %get-tuple-element.88.q_ref.k_ref.v_ref, bf16[1280,1536]{1,0:T(8,128)(2,1)} %get-tuple-element.88.q_ref.k_ref.v_ref, bf16[1280,1536]{1,0:T(8,128)(2,1)} %get-tuple-element.88.q_ref.k_ref.v_ref, ...), custom_call_target="tpu_custom_call" | custom-call | flops 2516582400 | bytes 2621440 | tf_op jit(solution)/shard_map/attend/pallas_call | solution.py:91
  97.7 15.8 %attend.3 = (bf16[1280,256]{1,0:T(8,128)(2,1)}, f32[2,10,256]{2,1,0:T(8,128)}) custom-call(s32[7]{0:T(128)} %stack.41.place, bf16[1280,1536]{1,0:T(8,128)(2,1)} %get-tuple-element.88.q_ref.k_ref.v_ref, bf16[1280,1536]{1,0:T(8,128)(2,1)} %get-tuple-element.88.q_ref.k_ref.v_ref, bf16[1280,1536]{1,0:T(8,128)(2,1)} %get-tuple-element.88.q_ref.k_ref.v_ref, ...), custom_call_target="tpu_custom_call" | custom-call | flops 2516582400 | bytes 2621440 | tf_op jit(solution)/shard_map/attend/pallas_call | solution.py:91
  115.2 16.0 %collective-permute-done.15.refs_3_ = bf16[1280,256]{1,0:T(8,128)(2,1)S(1)} collective-permute-done((bf16[1280,256]{1,0:T(8,128)(2,1)}, bf16[1280,256]{1,0:T(8,128)(2,1)S(1)}, u32[]{:S(2)}, u32[]{:S(2)}) %collective-permute-start.15) | collective-permute-done | bytes 655392 | tf_op jit(solution)/shard_map/ppermute | solution.py:989
  131.3 5.5 %all-gather.3.cloned.1.call-done = bf16[5120,1024]{1,0:T(8,128)(2,1)} async-done(((bf16[320,1024]{1,0:T(8,128)(2,1)}), bf16[5120,1024]{1,0:T(8,128)(2,1)}) %all-gather.3.cloned.1.call-update) | async-done | bytes 10485776 | tf_op jit(solution)/shard_map/all_gather | solution.py:1166
  136.8 9.3 %second_layer.1 = (f32[640,1024]{1,0:T(8,128)}, bf16[1280,1024]{1,0:T(8,128)(2,1)}) custom-call(s32[7]{0:T(128)} %stack.41.place, bf16[1280,256]{1,0:T(8,128)(2,1)} %get-tuple-element.90.refs_1_.refs_0_, bf16[1280,256]{1,0:T(8,128)(2,1)} %get-tuple-element.93.refs_1_, bf16[1280,256]{1,0:T(8,128)(2,1)} %copy-done.8, bf16[1280,256]{1,0:T(8,128)(2,1)} %copy-done.9, ...), custom_call_target="tpu_custom_call" | custom-call | flops 1342177280 | bytes 7602176 | tf_op jit(solution)/shard_map/second_layer/pallas_call | solution.py:401
  146.1 18.5 %hidden_layer.1 = (bf16[1280,2048]{1,0:T(8,128)(2,1)}, bf16[1280,2048]{1,0:T(8,128)(2,1)}) custom-call(bf16[1280,1024]{1,0:T(8,128)(2,1)} %get-tuple-element.96.x_ref.refs_4_, bf16[16,5,64,1024]{3,2,1,0:T(8,128)(2,1)} %bitcast.116, bf16[8,2,5,64,1024]{4,3,2,1,0:T(8,128)(2,1)} %bitcast.117, bf16[640,1024]{1,0:T(8,128)(2,1)} %bitcast.123, ...), custom_call_target="tpu_custom_call" | custom-call | flops 5368709120 | bytes 12058624 | tf_op jit(solution)/shard_map/hidden_layer/pallas_call | solution.py:484
  164.6 7.5 %up_back.2 = (bf16[320,1024]{1,0:T(8,128)(2,1)}, bf16[320,1024]{1,0:T(8,128)(2,1)}) custom-call(bf16[1280,2048]{1,0:T(8,128)(2,1)} %get-tuple-element.98.g_ref.refs_1_, bf16[16,5,64,1024]{3,2,1,0:T(8,128)(2,1)} %bitcast.118), custom_call_target="tpu_custom_call" | custom-call | flops 1342177280 | bytes 4718592 | tf_op jit(solution)/shard_map/up_back/pallas_call | solution.py:537
  173.6 12.4 %hidden_grads.2.refs_0_ = bf16[1024,2048]{1,0:T(8,128)(2,1)} custom-call(s32[7]{0:T(128)} %stack.41.place, bf16[1280,2048]{1,0:T(8,128)(2,1)} %get-tuple-element.97.refs_0_.a_ref, bf16[1280,2048]{1,0:T(8,128)(2,1)} %get-tuple-element.98.g_ref.refs_1_, bf16[640,1024]{1,0:T(8,128)(2,1)} %bitcast.124, bf16[640,1024]{1,0:T(8,128)(2,1)} %copy-done.2, ...), custom_call_target="tpu_custom_call" | custom-call | flops 2684354560 | bytes 7340032 | tf_op jit(solution)/shard_map/hidden_grads/pallas_call | solution.py:752
  186.0 3.3 collective-permute-done.16.refs_5_
  190.8 8.1 %up_back.3.refs_6_.refs_0_ = f32[640,1024]{1,0:T(8,128)} custom-call(bf16[1280,2048]{1,0:T(8,128)(2,1)} %get-tuple-element.98.g_ref.refs_1_, bf16[16,5,64,1024]{3,2,1,0:T(8,128)(2,1)} %bitcast.119, bf16[1024,2048]{1,0:T(8,128)(2,1)} %hidden_grads.2.refs_0_), custom_call_target="tpu_custom_call" | custom-call | flops 1342177280 | bytes 4718592 | tf_op jit(solution)/shard_map/up_back/pallas_call | solution.py:537
  198.9 13.1 %hidden_grads.3 = (bf16[1024,2048]{1,0:T(8,128)(2,1)}, bf16[128,2048]{1,0:T(8,128)(2,1)}, bf16[128,2048]{1,0:T(8,128)(2,1)}) custom-call(s32[7]{0:T(128)} %stack.41.place, bf16[1280,2048]{1,0:T(8,128)(2,1)} %get-tuple-element.97.refs_0_.a_ref, bf16[1280,2048]{1,0:T(8,128)(2,1)} %get-tuple-element.98.g_ref.refs_1_, bf16[640,1024]{1,0:T(8,128)(2,1)} %bitcast.125, ...), custom_call_target="tpu_custom_call" | custom-call | flops 2684354560 | bytes 7340032 | tf_op jit(solution)/shard_map/hidden_grads/pallas_call | solution.py:752
  214.9 9.0 %middle_back.1 = (f32[640,1024]{1,0:T(8,128)}, bf16[640,1024]{1,0:T(8,128)(2,1)}, f32[2,1024]{1,0:T(2,128)}, bf16[640,512]{1,0:T(8,128)(2,1)}, bf16[640,512]{1,0:T(8,128)(2,1)}) custom-call(s32[7]{0:T(128)} %stack.41.place, f32[640,1024]{1,0:T(8,128)} %up_back.3.refs_6_.refs_0_, f32[640,1024]{1,0:T(8,128)} %get-tuple-element.95.refs_1_, ...), custom_call_target="tpu_custom_call" | custom-call | flops 671088640 | bytes 7602176 | tf_op jit(solution)/shard_map/middle_back/pallas_call | solution.py:617
  224.4 7.3 %down_part.2.refs_0_ = bf16[640,1024]{1,0:T(8,128)(2,1)} custom-call(bf16[1280,2048]{1,0:T(8,128)(2,1)} %get-tuple-element.97.refs_0_.a_ref, bf16[8,2,5,64,1024]{4,3,2,1,0:T(8,128)(2,1)} %bitcast.121, bf16[640,512]{1,0:T(8,128)(2,1)} %get-tuple-element.107.refs_0_), custom_call_target="tpu_custom_call" | custom-call | flops 1342177280 | bytes 4718592 | tf_op jit(solution)/shard_map/down_part/pallas_call | solution.py:537
  231.7 2.6 bitcast_add_fusion.1
  236.4 7.4 %down_part.3.refs_6_ = bf16[640,1024]{1,0:T(8,128)(2,1)} custom-call(bf16[1280,2048]{1,0:T(8,128)(2,1)} %get-tuple-element.97.refs_0_.a_ref, bf16[8,2,5,64,1024]{4,3,2,1,0:T(8,128)(2,1)} %bitcast.122, bf16[640,1024]{1,0:T(8,128)(2,1)} %down_part.2.refs_0_), custom_call_target="tpu_custom_call" | custom-call | flops 1342177280 | bytes 4718592 | tf_op jit(solution)/shard_map/down_part/pallas_call | solution.py:537
  244.6 11.8 %attend_back.4.refs_6_ = bf16[1280,1536]{1,0:T(8,128)(2,1)} custom-call(s32[7]{0:T(128)} %stack.41.place, bf16[1280,1536]{1,0:T(8,128)(2,1)} %get-tuple-element.88.q_ref.k_ref.v_ref, bf16[1280,1536]{1,0:T(8,128)(2,1)} %get-tuple-element.88.q_ref.k_ref.v_ref, bf16[1280,1536]{1,0:T(8,128)(2,1)} %get-tuple-element.88.q_ref.k_ref.v_ref, ...), custom_call_target="tpu_custom_call" | custom-call | flops 3145728000 | bytes 3276800 | tf_op jit(solution)/shard_map/attend_back/pallas_call | solution.py:204
  256.4 2.6 bitcast_add_fusion
  261.1 12.2 %attend_back.5.grad.refs_6_ = bf16[1280,1536]{1,0:T(8,128)(2,1)} custom-call(s32[7]{0:T(128)} %stack.41.place, bf16[1280,1536]{1,0:T(8,128)(2,1)} %get-tuple-element.88.q_ref.k_ref.v_ref, bf16[1280,1536]{1,0:T(8,128)(2,1)} %get-tuple-element.88.q_ref.k_ref.v_ref, ...), custom_call_target="tpu_custom_call", output_to_operand_aliasing={{}: (10, {})} | custom-call | flops 3145728000 | bytes 3276800 | tf_op jit(solution)/shard_map/attend_back/pallas_call | solution.py:204
  273.3 9.1 %tail_grads.2.refs_7_ = bf16[1024,1280]{1,0:T(8,128)(2,1)} custom-call(s32[7]{0:T(128)} %stack.41.place, bf16[1280,1024]{1,0:T(8,128)(2,1)} %get-tuple-element.109.low, bf16[1280,1536]{1,0:T(8,128)(2,1)} %attend_back.5.grad.refs_6_, bf16[640,1024]{1,0:T(8,128)(2,1)} %get-tuple-element.120.attended, bf16[1280,256]{1,0:T(8,128)(2,1)} %get-tuple-element.90.refs_1_.refs_0_, ...), custom_call_target="tpu_custom_call" | custom-call | flops 1342177280 | bytes 5242880 | tf_op jit(solution)/shard_map/tail_grads/pallas_call | solution.py:809
  286.2 11.7 %attend_back.6.refs_6_ = bf16[1280,1536]{1,0:T(8,128)(2,1)} custom-call(s32[7]{0:T(128)} %stack.41.place, bf16[1280,1536]{1,0:T(8,128)(2,1)} %get-tuple-element.88.q_ref.k_ref.v_ref, bf16[1280,1536]{1,0:T(8,128)(2,1)} %get-tuple-element.88.q_ref.k_ref.v_ref, bf16[1280,1536]{1,0:T(8,128)(2,1)} %get-tuple-element.88.q_ref.k_ref.v_ref, ...), custom_call_target="tpu_custom_call", output_to_operand_aliasing={{}: (10, {})} | custom-call | flops 3145728000 | bytes 3276800 | tf_op jit(solution)/shard_map/attend_back/pallas_call | solution.py:204
  298.0 1.8 collective-permute-done.26
  299.7 11.9 %attend_back.7.grad.grad_ref = bf16[1280,1536]{1,0:T(8,128)(2,1)} custom-call(s32[7]{0:T(128)} %stack.41.place, bf16[1280,1536]{1,0:T(8,128)(2,1)} %get-tuple-element.88.q_ref.k_ref.v_ref, bf16[1280,1536]{1,0:T(8,128)(2,1)} %get-tuple-element.88.q_ref.k_ref.v_ref, ...), custom_call_target="tpu_custom_call", output_to_operand_aliasing={{}: (10, {})} | custom-call | flops 3145728000 | bytes 3276800 | tf_op jit(solution)/shard_map/attend_back/pallas_call | solution.py:204
  311.6 9.6 %tail_grads.3 = (bf16[1024,1280]{1,0:T(8,128)(2,1)}, bf16[128,1280]{1,0:T(8,128)(2,1)}, bf16[128,1280]{1,0:T(8,128)(2,1)}) custom-call(s32[7]{0:T(128)} %stack.41.place, bf16[1280,1024]{1,0:T(8,128)(2,1)} %get-tuple-element.109.low, bf16[1280,1536]{1,0:T(8,128)(2,1)} %attend_back.7.grad.grad_ref, bf16[640,1024]{1,0:T(8,128)(2,1)} %get-tuple-element.120.attended, ...), custom_call_target="tpu_custom_call" | custom-call | flops 1342177280 | bytes 5242880 | tf_op jit(solution)/shard_map/tail_grads/pallas_call | solution.py:809
  325.8 6.8 %first_back.2 = (bf16[320,1024]{1,0:T(8,128)(2,1)}, bf16[320,1024]{1,0:T(8,128)(2,1)}, f32[2,1024]{1,0:T(2,128)}) custom-call(bf16[1280,1536]{1,0:T(8,128)(2,1)} %attend_back.7.grad.grad_ref, bf16[1024,1536]{1,0:T(8,128)(2,1)} %get-tuple-element.125.weight_ref, bf16[640,1024]{1,0:T(8,128)(2,1)} %copy-done.11, bf16[1024,1280]{1,0:T(8,128)(2,1)} %get-tuple-element.122.refs_0_, ...), custom_call_target="tpu_custom_call" | custom-call | flops 1006632960 | bytes 3866624 | tf_op jit(solution)/shard_map/first_back/pallas_call | solution.py:665
  333.2 2.0 fusion.1
  336.9 3.1 bitcast_add_fusion.8
  342.0 6.4 %first_back.3 = (bf16[640,1024]{1,0:T(8,128)(2,1)}, f32[2,1024]{1,0:T(2,128)}) custom-call(bf16[1280,1536]{1,0:T(8,128)(2,1)} %attend_back.7.grad.grad_ref, bf16[1024,1536]{1,0:T(8,128)(2,1)} %get-tuple-element.125.weight_ref, bf16[640,1024]{1,0:T(8,128)(2,1)} %bitcast.135, bf16[320,1024]{1,0:T(8,128)(2,1)} %get-tuple-element.145.refs_0_), custom_call_target="tpu_custom_call" | custom-call | flops 1006632960 | bytes 3866624 | tf_op jit(solution)/shard_map/first_back/pallas_call | solution.py:665
  348.4 2.2 bitcast_select_fusion
  353.5 2.4 bitcast_add_fusion.6
  359.4 3.1 fusion
  368.7 3.0 collective-permute-done.38
  373.3 2.3 reshape.100
  375.5 1.8 collective-permute-done.39
  377.3 2.6 collective-permute-done.40.refs_1_
  381.4 1.8 fusion.2
  386.1 5.8 %input_back.1 = f32[640,1024]{1,0:T(8,128)} custom-call(bf16[640,1024]{1,0:T(8,128)(2,1)} %get-tuple-element.136.own_ref, bf16[640,1024]{1,0:T(8,128)(2,1)} %bitcast.136, f32[2,1024]{1,0:T(2,128)} %get-tuple-element.190.refs_2_.ada_ref, f32[640,1024]{1,0:T(8,128)} %get-tuple-element.137.base_ref, bf16[320,1024]{1,0:T(8,128)(2,1)} %collective-permute-done.33.refs_0_, ...), custom_call_target="tpu_custom_call" | custom-call | flops 6553600 | bytes 4587520 | tf_op jit(solution)/shard_map/input_back/pallas_call | solution.py:855
  395.7 2.6 join_tail.1
  (202 shorter events, 67.4 us)
Async XLA Ops:
  7.2 129.6 %all-gather.3.cloned.1.call-start = ((), (), s32[]{:S(2)}) async-start(), calls=%async_computation | async-start | bytes 11141120 | tf_op jit(solution)/shard_map/all_gather | solution.py:1166
  8.7 10.6 %collective-permute-start = (f32[4,8,1024]{2,1,0:T(8,128)S(1)}, f32[4,8,1024]{2,1,0:T(8,128)S(1)}, u32[]{:S(2)}, u32[]{:S(2)}) collective-permute-start(f32[4,8,1024]{2,1,0:T(8,128)S(1)} %pad_maximum_fusion.3), channel_id=1, source_target_pairs={{0,2},{2,0},{4,6},{6,4},{8,10},{10,8},{12,14},{14,12},{16,18},{18,... | collective-permute-start | bytes 393224 | tf_op jit(solution)/shard_map/ppermute | solution.py:982
  10.9 5.1 %collective-permute-start.4 = (bf16[64,1536]{1,0:T(8,128)(2,1)}, bf16[64,1536]{1,0:T(8,128)(2,1)S(1)}, u32[]{:S(2)}, u32[]{:S(2)}) collective-permute-start(bf16[64,1536]{1,0:T(8,128)(2,1)} %pack_columns.1), channel_id=1, source_target_pairs={{0,2},{2,0},{4,6},{6,4},{8,10},{10,8},{12,14},{14,12},{16,18},{18,... | collective-permute-start | bytes 589832 | tf_op jit(solution)/shard_map/ppermute | solution.py:982
  10.9 33.3 %collective-permute-start.7 = (bf16[640,1024]{1,0:T(8,128)(2,1)}, bf16[640,1024]{1,0:T(8,128)(2,1)S(1)}, u32[]{:S(2)}, u32[]{:S(2)}) collective-permute-start(bf16[640,1024]{1,0:T(8,128)(2,1)} %bitcast.132), channel_id=1, source_target_pairs={{0,1},{1,0},{2,3},{3,2},{4,5},{5,4},{6,7},{7,6},{8,9},{9,8},{10,11... | collective-permute-start | bytes 3932168 | tf_op jit(solution)/shard_map/ppermute | solution.py:989
  17.8 12.0 %collective-permute-start.5 = (bf16[128,1536]{1,0:T(8,128)(2,1)}, bf16[128,1536]{1,0:T(8,128)(2,1)}, u32[]{:S(2)}, u32[]{:S(2)}) collective-permute-start(bf16[128,1536]{1,0:T(8,128)(2,1)} %maximum_select_fusion.refs_3_), channel_id=1, source_target_pairs={{0,8},{8,16},{16,24},{24,28},{28,20},{20,12},{12,4},{4,0},{10,2},{... | collective-permute-start | bytes 1179656 | tf_op jit(solution)/shard_map/ppermute | solution.py:1002
  20.0 8.6 %collective-permute-start.1 = (f32[4,8,1024]{2,1,0:T(8,128)}, f32[4,8,1024]{2,1,0:T(8,128)}, u32[]{:S(2)}, u32[]{:S(2)}) collective-permute-start(f32[4,8,1024]{2,1,0:T(8,128)} %fusion.24), channel_id=1, source_target_pairs={{0,4},{2,6},{4,0},{6,2},{8,12},{10,14},{12,8},{14,10},{16,20},{18,... | collective-permute-start | bytes 393224 | tf_op jit(solution)/shard_map/ppermute | solution.py:982
  29.7 6.5 %collective-permute-start.2 = (f32[4,8,1024]{2,1,0:T(8,128)S(1)}, f32[4,8,1024]{2,1,0:T(8,128)S(1)}, u32[]{:S(2)}, u32[]{:S(2)}) collective-permute-start(f32[4,8,1024]{2,1,0:T(8,128)S(1)} %fusion.29), channel_id=1, source_target_pairs={{0,8},{2,10},{4,12},{6,14},{8,0},{10,2},{12,4},{14,6},{16,24},{18,... | collective-permute-start | bytes 393224 | tf_op jit(solution)/shard_map/ppermute | solution.py:982
  29.8 14.5 %collective-permute-start.6 = (bf16[128,1536]{1,0:T(8,128)(2,1)}, bf16[128,1536]{1,0:T(8,128)(2,1)}, u32[]{:S(2)}, u32[]{:S(2)}) collective-permute-start(bf16[128,1536]{1,0:T(8,128)(2,1)} %collective-permute-done.5.refs_4_), channel_id=1, source_target_pairs={{0,8},{8,16},{16,24},{24,28},{28,20},{20,12},{12,4},{4,0},{10,2},{... | collective-permute-start | bytes 1179656 | tf_op jit(solution)/shard_map/ppermute | solution.py:1002
  36.2 8.0 %collective-permute-start.3 = (f32[4,8,1024]{2,1,0:T(8,128)S(1)}, f32[4,8,1024]{2,1,0:T(8,128)S(1)}, u32[]{:S(2)}, u32[]{:S(2)}) collective-permute-start(f32[4,8,1024]{2,1,0:T(8,128)S(1)} %add.86), channel_id=1, source_target_pairs={{0,16},{2,18},{4,20},{6,22},{8,24},{10,26},{12,28},{14,30},{16,0},... | collective-permute-start | bytes 393224 | tf_op jit(solution)/shard_map/ppermute | solution.py:982
  45.3 35.1 %collective-permute-start.13 = (bf16[640,1024]{1,0:T(8,128)(2,1)S(1)}, bf16[640,1024]{1,0:T(8,128)(2,1)S(1)}, u32[]{:S(2)}, u32[]{:S(2)}) collective-permute-start(bf16[640,1024]{1,0:T(8,128)(2,1)S(1)} %bitcast.127), channel_id=1, source_target_pairs={{0,1},{1,0},{2,3},{3,2},{4,5},{5,4},{6,7},{7,6},{8,9},{9,8},{10,11... | collective-permute-start | bytes 3932168 | tf_op jit(solution)/shard_map/ppermute | solution.py:989
  45.8 8.5 %collective-permute-start.8 = (bf16[128,1536]{1,0:T(8,128)(2,1)}, bf16[128,1536]{1,0:T(8,128)(2,1)S(1)}, u32[]{:S(2)}, u32[]{:S(2)}) collective-permute-start(bf16[128,1536]{1,0:T(8,128)(2,1)} %collective-permute-done.6.refs_5_), channel_id=1, source_target_pairs={{0,8},{8,16},{16,24},{24,28},{28,20},{20,12},{12,4},{4,0},{10,2},{... | collective-permute-start | bytes 1179656 | tf_op jit(solution)/shard_map/ppermute | solution.py:1002
  48.6 11.4 %collective-permute-start.10 = (bf16[128,1536]{1,0:T(8,128)(2,1)}, bf16[128,1536]{1,0:T(8,128)(2,1)}, u32[]{:S(2)}, u32[]{:S(2)}) collective-permute-start(bf16[128,1536]{1,0:T(8,128)(2,1)} %collective-permute-done.5.refs_4_), channel_id=1, source_target_pairs={{0,2},{2,0},{4,6},{6,4},{8,10},{10,8},{12,14},{14,12},{16,18},{18,... | collective-permute-start | bytes 1179656 | tf_op jit(solution)/shard_map/ppermute | solution.py:982
  48.6 11.4 %collective-permute-start.11 = (bf16[128,1536]{1,0:T(8,128)(2,1)}, bf16[128,1536]{1,0:T(8,128)(2,1)}, u32[]{:S(2)}, u32[]{:S(2)}) collective-permute-start(bf16[128,1536]{1,0:T(8,128)(2,1)} %collective-permute-done.6.refs_5_), channel_id=1, source_target_pairs={{0,2},{2,0},{4,6},{6,4},{8,10},{10,8},{12,14},{14,12},{16,18},{18,... | collective-permute-start | bytes 1179656 | tf_op jit(solution)/shard_map/ppermute | solution.py:982
  54.3 14.8 %collective-permute-start.9 = (bf16[128,1536]{1,0:T(8,128)(2,1)S(1)}, bf16[128,1536]{1,0:T(8,128)(2,1)}, u32[]{:S(2)}, u32[]{:S(2)}) collective-permute-start(bf16[128,1536]{1,0:T(8,128)(2,1)S(1)} %collective-permute-done.8.refs_6_), channel_id=1, source_target_pairs={{0,8},{8,16},{16,24},{24,28},{28,20},{20,12},{12,4},{4,0},{10,2},{... | collective-permute-start | bytes 1179656 | tf_op jit(solution)/shard_map/ppermute | solution.py:1002
  55.4 13.7 %collective-permute-start.12 = (bf16[128,1536]{1,0:T(8,128)(2,1)S(1)}, bf16[128,1536]{1,0:T(8,128)(2,1)}, u32[]{:S(2)}, u32[]{:S(2)}) collective-permute-start(bf16[128,1536]{1,0:T(8,128)(2,1)S(1)} %collective-permute-done.8.refs_6_), channel_id=1, source_target_pairs={{0,2},{2,0},{4,6},{6,4},{8,10},{10,8},{12,14},{14,12},{16,18},{18,... | collective-permute-start | bytes 1179656 | tf_op jit(solution)/shard_map/ppermute | solution.py:982
  97.3 17.3 %collective-permute-start.14 = (bf16[1280,256]{1,0:T(8,128)(2,1)}, bf16[1280,256]{1,0:T(8,128)(2,1)S(1)}, u32[]{:S(2)}, u32[]{:S(2)}) collective-permute-start(bf16[1280,256]{1,0:T(8,128)(2,1)} %get-tuple-element.90.refs_1_.refs_0_), channel_id=1, source_target_pairs={{0,1},{1,0},{2,3},{3,2},{4,5},{5,4},{6,7},{7,6},{8,9},{9,8},{10,11... | collective-permute-start | bytes 1966088 | tf_op jit(solution)/shard_map/ppermute | solution.py:989
  114.6 16.6 %collective-permute-start.15 = (bf16[1280,256]{1,0:T(8,128)(2,1)}, bf16[1280,256]{1,0:T(8,128)(2,1)S(1)}, u32[]{:S(2)}, u32[]{:S(2)}) collective-permute-start(bf16[1280,256]{1,0:T(8,128)(2,1)} %get-tuple-element.93.refs_1_), channel_id=1, source_target_pairs={{0,1},{1,0},{2,3},{3,2},{4,5},{5,4},{6,7},{7,6},{8,9},{9,8},{10,11... | collective-permute-start | bytes 1966088 | tf_op jit(solution)/shard_map/ppermute | solution.py:989
  172.1 17.1 %collective-permute-start.16 = (bf16[320,1024]{1,0:T(8,128)(2,1)}, bf16[320,1024]{1,0:T(8,128)(2,1)S(1)}, u32[]{:S(2)}, u32[]{:S(2)}) collective-permute-start(bf16[320,1024]{1,0:T(8,128)(2,1)} %get-tuple-element.99.refs_5_), channel_id=1, source_target_pairs={{0,1},{1,0},{2,3},{3,2},{4,5},{5,4},{6,7},{7,6},{8,9},{9,8},{10,11... | collective-permute-start | bytes 1966088 | tf_op jit(solution)/shard_map/ppermute | solution.py:989
  189.2 9.6 %collective-permute-start.17 = (bf16[1024,2048]{1,0:T(8,128)(2,1)}, bf16[1024,2048]{1,0:T(8,128)(2,1)}, u32[]{:S(2)}, u32[]{:S(2)}) collective-permute-start(bf16[1024,2048]{1,0:T(8,128)(2,1)} %hidden_grads.2.refs_0_), channel_id=1, source_target_pairs={{0,2},{2,0},{4,6},{6,4},{8,10},{10,8},{12,14},{14,12},{16,18},{18,... | collective-permute-start | bytes 12582920 | tf_op jit(solution)/shard_map/ppermute | solution.py:982
  189.2 24.8 %collective-permute-start.20 = (bf16[320,1024]{1,0:T(8,128)(2,1)S(1)}, bf16[320,1024]{1,0:T(8,128)(2,1)S(1)}, u32[]{:S(2)}, u32[]{:S(2)}) collective-permute-start(bf16[320,1024]{1,0:T(8,128)(2,1)S(1)} %copy-done.35), channel_id=1, source_target_pairs={{0,1},{1,0},{2,3},{3,2},{4,5},{5,4},{6,7},{7,6},{8,9},{9,8},{10,11... | collective-permute-start | bytes 1966088 | tf_op jit(solution)/shard_map/ppermute | solution.py:989
  211.9 19.8 %collective-permute-start.18 = (bf16[128,2048]{1,0:T(8,128)(2,1)}, bf16[128,2048]{1,0:T(8,128)(2,1)S(1)}, u32[]{:S(2)}, u32[]{:S(2)}) collective-permute-start(bf16[128,2048]{1,0:T(8,128)(2,1)} %get-tuple-element.102), channel_id=1, source_target_pairs={{0,8},{2,10},{8,16},{10,18},{16,24},{18,26},{24,28},{26,30},{28,20... | collective-permute-start | bytes 1572872 | tf_op jit(solution)/shard_map/ppermute | solution.py:1064
  212.5 19.2 %collective-permute-start.19 = (bf16[128,2048]{1,0:T(8,128)(2,1)}, bf16[128,2048]{1,0:T(8,128)(2,1)S(1)}, u32[]{:S(2)}, u32[]{:S(2)}) collective-permute-start(bf16[128,2048]{1,0:T(8,128)(2,1)} %get-tuple-element.103), channel_id=1, source_target_pairs={{8,0},{10,2},{16,8},{18,10},{24,16},{26,18},{28,24},{30,26},{20,28... | collective-permute-start | bytes 1572872 | tf_op jit(solution)/shard_map/ppermute | solution.py:1064
  223.8 19.9 %collective-permute-start.21 = (bf16[640,512]{1,0:T(8,128)(2,1)}, bf16[640,512]{1,0:T(8,128)(2,1)S(1)}, u32[]{:S(2)}, u32[]{:S(2)}) collective-permute-start(bf16[640,512]{1,0:T(8,128)(2,1)} %get-tuple-element.107.refs_0_), channel_id=1, source_target_pairs={{0,1},{1,0},{2,3},{3,2},{4,5},{5,4},{6,7},{7,6},{8,9},{9,8},{10,11... | collective-permute-start | bytes 1966088 | tf_op jit(solution)/shard_map/ppermute | solution.py:989
  234.3 22.1 %collective-permute-start.22 = (bf16[128,2048]{1,0:T(8,128)(2,1)S(1)}, bf16[128,2048]{1,0:T(8,128)(2,1)S(1)}, u32[]{:S(2)}, u32[]{:S(2)}) collective-permute-start(bf16[128,2048]{1,0:T(8,128)(2,1)S(1)} %get-tuple-element.160), channel_id=1, source_target_pairs={{0,8},{2,10},{8,16},{10,18},{16,24},{18,26},{24,28},{26,30},{28,20... | collective-permute-start | bytes 1572872 | tf_op jit(solution)/shard_map/ppermute | solution.py:1064
  234.8 21.6 %collective-permute-start.23 = (bf16[128,2048]{1,0:T(8,128)(2,1)S(1)}, bf16[128,2048]{1,0:T(8,128)(2,1)S(1)}, u32[]{:S(2)}, u32[]{:S(2)}) collective-permute-start(bf16[128,2048]{1,0:T(8,128)(2,1)S(1)} %get-tuple-element.159), channel_id=1, source_target_pairs={{8,0},{10,2},{16,8},{18,10},{24,16},{26,18},{28,24},{30,26},{20,28... | collective-permute-start | bytes 1572872 | tf_op jit(solution)/shard_map/ppermute | solution.py:1064
  259.0 14.3 %collective-permute-start.24 = (bf16[128,2048]{1,0:T(8,128)(2,1)S(1)}, bf16[128,2048]{1,0:T(8,128)(2,1)S(1)}, u32[]{:S(2)}, u32[]{:S(2)}) collective-permute-start(bf16[128,2048]{1,0:T(8,128)(2,1)S(1)} %get-tuple-element.158), channel_id=1, source_target_pairs={{0,8},{2,10},{8,16},{10,18},{16,24},{18,26},{24,28},{26,30},{28,20... | collective-permute-start | bytes 1572872 | tf_op jit(solution)/shard_map/ppermute | solution.py:1064
  259.6 13.7 %collective-permute-start.25 = (bf16[128,2048]{1,0:T(8,128)(2,1)S(1)}, bf16[128,2048]{1,0:T(8,128)(2,1)S(1)}, u32[]{:S(2)}, u32[]{:S(2)}) collective-permute-start(bf16[128,2048]{1,0:T(8,128)(2,1)S(1)} %get-tuple-element.157), channel_id=1, source_target_pairs={{8,0},{10,2},{16,8},{18,10},{24,16},{26,18},{28,24},{30,26},{20,28... | collective-permute-start | bytes 1572872 | tf_op jit(solution)/shard_map/ppermute | solution.py:1064
  282.4 29.2 %collective-permute-start.27 = (bf16[1024,1280]{1,0:T(8,128)(2,1)}, bf16[1024,1280]{1,0:T(8,128)(2,1)}, u32[]{:S(2)}, u32[]{:S(2)}) collective-permute-start(bf16[1024,1280]{1,0:T(8,128)(2,1)} %tail_grads.2.refs_7_), channel_id=1, source_target_pairs={{0,2},{2,0},{4,6},{6,4},{8,10},{10,8},{12,14},{14,12},{16,18},{18,... | collective-permute-start | bytes 7864328 | tf_op jit(solution)/shard_map/ppermute | solution.py:982
  282.4 42.3 %collective-permute-start.30 = (bf16[640,1024]{1,0:T(8,128)(2,1)S(1)}, bf16[640,1024]{1,0:T(8,128)(2,1)S(1)}, u32[]{:S(2)}, u32[]{:S(2)}) collective-permute-start(bf16[640,1024]{1,0:T(8,128)(2,1)S(1)} %copy-done.10), channel_id=1, source_target_pairs={{0,1},{1,0},{2,3},{3,2},{4,5},{5,4},{6,7},{7,6},{8,9},{9,8},{10,11... | collective-permute-start | bytes 3932168 | tf_op jit(solution)/shard_map/ppermute | solution.py:989
  285.7 14.0 %collective-permute-start.26 = (bf16[128,2048]{1,0:T(8,128)(2,1)S(1)}, bf16[128,2048]{1,0:T(8,128)(2,1)S(1)}, u32[]{:S(2)}, u32[]{:S(2)}) collective-permute-start(bf16[128,2048]{1,0:T(8,128)(2,1)S(1)} %bitcast_add_fusion.4), channel_id=1, source_target_pairs={{0,8},{2,10},{8,16},{10,18},{16,24},{18,26},{24,28},{26,30},{28,20... | collective-permute-start | bytes 1572872 | tf_op jit(solution)/shard_map/ppermute | solution.py:1064
  321.2 11.9 %collective-permute-start.28 = (bf16[128,1280]{1,0:T(8,128)(2,1)}, bf16[128,1280]{1,0:T(8,128)(2,1)S(1)}, u32[]{:S(2)}, u32[]{:S(2)}) collective-permute-start(bf16[128,1280]{1,0:T(8,128)(2,1)} %get-tuple-element.123), channel_id=1, source_target_pairs={{0,8},{2,10},{8,16},{10,18},{16,24},{18,26},{24,28},{26,30},{28,20... | collective-permute-start | bytes 983048 | tf_op jit(solution)/shard_map/ppermute | solution.py:1064
  321.7 11.4 %collective-permute-start.29 = (bf16[128,1280]{1,0:T(8,128)(2,1)}, bf16[128,1280]{1,0:T(8,128)(2,1)}, u32[]{:S(2)}, u32[]{:S(2)}) collective-permute-start(bf16[128,1280]{1,0:T(8,128)(2,1)} %get-tuple-element.124), channel_id=1, source_target_pairs={{8,0},{10,2},{16,8},{18,10},{24,16},{26,18},{28,24},{30,26},{20,28... | collective-permute-start | bytes 983048 | tf_op jit(solution)/shard_map/ppermute | solution.py:1064
  332.6 19.6 %collective-permute-start.33 = (bf16[320,1024]{1,0:T(8,128)(2,1)}, bf16[320,1024]{1,0:T(8,128)(2,1)}, u32[]{:S(2)}, u32[]{:S(2)}) collective-permute-start(bf16[320,1024]{1,0:T(8,128)(2,1)} %get-tuple-element.134), channel_id=1, source_target_pairs={{0,1},{1,0},{2,3},{3,2},{4,5},{5,4},{6,7},{7,6},{8,9},{9,8},{10,11... | collective-permute-start | bytes 1966088 | tf_op jit(solution)/shard_map/ppermute | solution.py:989
  336.8 11.6 %collective-permute-start.45 = (f32[64,1024]{1,0:T(8,128)S(1)}, f32[64,1024]{1,0:T(8,128)}, u32[]{:S(2)}, u32[]{:S(2)}) collective-permute-start(f32[64,1024]{1,0:T(8,128)S(1)} %dynamic-slice_bitcast_fusion), channel_id=1, source_target_pairs={{0,2},{2,0},{4,6},{6,4},{8,10},{10,8},{12,14},{14,12},{16,18},{18,... | collective-permute-start | bytes 786440 | tf_op jit(solution)/shard_map/ppermute | solution.py:982
  340.0 12.2 %collective-permute-start.31 = (bf16[128,1280]{1,0:T(8,128)(2,1)}, bf16[128,1280]{1,0:T(8,128)(2,1)S(1)}, u32[]{:S(2)}, u32[]{:S(2)}) collective-permute-start(bf16[128,1280]{1,0:T(8,128)(2,1)} %get-tuple-element.164), channel_id=1, source_target_pairs={{0,8},{2,10},{8,16},{10,18},{16,24},{18,26},{24,28},{26,30},{28,20... | collective-permute-start | bytes 983048 | tf_op jit(solution)/shard_map/ppermute | solution.py:1064
  340.5 11.7 %collective-permute-start.32 = (bf16[128,1280]{1,0:T(8,128)(2,1)}, bf16[128,1280]{1,0:T(8,128)(2,1)}, u32[]{:S(2)}, u32[]{:S(2)}) collective-permute-start(bf16[128,1280]{1,0:T(8,128)(2,1)} %get-tuple-element.163), channel_id=1, source_target_pairs={{8,0},{10,2},{16,8},{18,10},{24,16},{26,18},{28,24},{30,26},{20,28... | collective-permute-start | bytes 983048 | tf_op jit(solution)/shard_map/ppermute | solution.py:1064
  350.6 21.2 %collective-permute-start.46 = (f32[32,2048]{1,0:T(8,128)S(1)}, f32[32,2048]{1,0:T(8,128)S(1)}, u32[]{:S(2)}, u32[]{:S(2)}) collective-permute-start(f32[32,2048]{1,0:T(8,128)S(1)} %fusion.7), channel_id=1, source_target_pairs={{0,1},{1,0},{2,3},{3,2},{4,5},{5,4},{6,7},{7,6},{8,9},{9,8},{10,11... | collective-permute-start | bytes 786440 | tf_op jit(solution)/shard_map/ppermute | solution.py:989
  352.9 6.3 %collective-permute-start.36 = (f32[4,1024]{1,0:T(4,128)S(1)}, f32[4,1024]{1,0:T(4,128)S(1)}, u32[]{:S(2)}, u32[]{:S(2)}) collective-permute-start(f32[4,1024]{1,0:T(4,128)S(1)} %pad_maximum_fusion.4), channel_id=1, source_target_pairs={{0,1},{1,0},{2,3},{3,2},{4,5},{5,4},{6,7},{7,6},{8,9},{9,8},{10,11... | collective-permute-start | bytes 49160 | tf_op jit(solution)/shard_map/ppermute | solution.py:989
  355.9 9.0 %collective-permute-start.34 = (bf16[128,1280]{1,0:T(8,128)(2,1)S(1)}, bf16[128,1280]{1,0:T(8,128)(2,1)S(1)}, u32[]{:S(2)}, u32[]{:S(2)}) collective-permute-start(bf16[128,1280]{1,0:T(8,128)(2,1)S(1)} %get-tuple-element.162), channel_id=1, source_target_pairs={{0,8},{2,10},{8,16},{10,18},{16,24},{18,26},{24,28},{26,30},{28,20... | collective-permute-start | bytes 983048 | tf_op jit(solution)/shard_map/ppermute | solution.py:1064
  356.9 8.4 %collective-permute-start.35 = (bf16[128,1280]{1,0:T(8,128)(2,1)S(1)}, bf16[128,1280]{1,0:T(8,128)(2,1)S(1)}, u32[]{:S(2)}, u32[]{:S(2)}) collective-permute-start(bf16[128,1280]{1,0:T(8,128)(2,1)S(1)} %get-tuple-element.161), channel_id=1, source_target_pairs={{8,0},{10,2},{16,8},{18,10},{24,16},{26,18},{28,24},{30,26},{20,28... | collective-permute-start | bytes 983048 | tf_op jit(solution)/shard_map/ppermute | solution.py:1064
  362.5 17.4 %collective-permute-start.40 = (bf16[320,1024]{1,0:T(8,128)(2,1)}, bf16[320,1024]{1,0:T(8,128)(2,1)}, u32[]{:S(2)}, u32[]{:S(2)}) collective-permute-start(bf16[320,1024]{1,0:T(8,128)(2,1)} %get-tuple-element.145.refs_0_), channel_id=1, source_target_pairs={{0,1},{1,0},{2,3},{3,2},{4,5},{5,4},{6,7},{7,6},{8,9},{9,8},{10,11... | collective-permute-start | bytes 1966088 | tf_op jit(solution)/shard_map/ppermute | solution.py:989
  365.4 6.4 %collective-permute-start.38 = (f32[4,8,1024]{2,1,0:T(8,128)S(1)}, f32[4,8,1024]{2,1,0:T(8,128)S(1)}, u32[]{:S(2)}, u32[]{:S(2)}) collective-permute-start(f32[4,8,1024]{2,1,0:T(8,128)S(1)} %fusion.18), channel_id=1, source_target_pairs={{0,4},{2,6},{4,0},{6,2},{8,12},{10,14},{12,8},{14,10},{16,20},{18,... | collective-permute-start | bytes 393224 | tf_op jit(solution)/shard_map/ppermute | solution.py:982
  368.1 13.3 %collective-permute-start.41 = (bf16[128,1280]{1,0:T(8,128)(2,1)}, bf16[128,1280]{1,0:T(8,128)(2,1)}, u32[]{:S(2)}, u32[]{:S(2)}) collective-permute-start(bf16[128,1280]{1,0:T(8,128)(2,1)} %bitcast_add_fusion.5), channel_id=1, source_target_pairs={{0,8},{2,10},{8,16},{10,18},{16,24},{18,26},{24,28},{26,30},{28,20... | collective-permute-start | bytes 983048 | tf_op jit(solution)/shard_map/ppermute | solution.py:1064
  371.8 5.5 %collective-permute-start.39 = (f32[4,8,1024]{2,1,0:T(8,128)S(1)}, f32[4,8,1024]{2,1,0:T(8,128)S(1)}, u32[]{:S(2)}, u32[]{:S(2)}) collective-permute-start(f32[4,8,1024]{2,1,0:T(8,128)S(1)} %add.102), channel_id=1, source_target_pairs={{0,8},{2,10},{4,12},{6,14},{8,0},{10,2},{12,4},{14,6},{16,24},{18,... | collective-permute-start | bytes 393224 | tf_op jit(solution)/shard_map/ppermute | solution.py:982
  379.9 11.9 %collective-permute-start.47 = (f32[4,8,1024]{2,1,0:T(8,128)S(1)}, f32[4,8,1024]{2,1,0:T(8,128)S(1)}, u32[]{:S(2)}, u32[]{:S(2)}) collective-permute-start(f32[4,8,1024]{2,1,0:T(8,128)S(1)} %add.103), channel_id=1, source_target_pairs={{0,16},{2,18},{4,20},{6,22},{8,24},{10,26},{12,28},{14,30},{16,0},... | collective-permute-start | bytes 393224 | tf_op jit(solution)/shard_map/ppermute | solution.py:982
  383.9 11.0 %collective-permute-start.42 = (f32[32,1280]{1,0:T(8,128)S(1)}, f32[32,1280]{1,0:T(8,128)S(1)}, u32[]{:S(2)}, u32[]{:S(2)}) collective-permute-start(f32[32,1280]{1,0:T(8,128)S(1)} %get-tuple-element.173), channel_id=1, source_target_pairs={{0,1},{1,0},{2,3},{3,2},{4,5},{5,4},{6,7},{7,6},{8,9},{9,8},{10,11... | collective-permute-start | bytes 491528 | tf_op jit(solution)/shard_map/ppermute | solution.py:989
  385.4 9.5 %collective-permute-start.43 = (f32[32,1280]{1,0:T(8,128)S(1)}, f32[32,1280]{1,0:T(8,128)S(1)}, u32[]{:S(2)}, u32[]{:S(2)}) collective-permute-start(f32[32,1280]{1,0:T(8,128)S(1)} %get-tuple-element.172), channel_id=1, source_target_pairs={{0,2},{2,0},{4,6},{6,4},{8,10},{10,8},{12,14},{14,12},{16,18},{18,... | collective-permute-start | bytes 491528 | tf_op jit(solution)/shard_map/ppermute | solution.py:982
  385.4 9.5 %collective-permute-start.44 = (f32[32,1280]{1,0:T(8,128)S(1)}, f32[32,1280]{1,0:T(8,128)S(1)}, u32[]{:S(2)}, u32[]{:S(2)}) collective-permute-start(f32[32,1280]{1,0:T(8,128)S(1)} %get-tuple-element.171), channel_id=1, source_target_pairs={{0,3},{1,2},{2,1},{3,0},{4,7},{5,6},{6,5},{7,4},{8,11},{9,10},{10,... | collective-permute-start | bytes 491528 | tf_op jit(solution)/shard_map/ppermute | solution.py:986
  (38 other events, 342.2 us)
Sparse Core Ops, SparseCore 0:
  44.4 92.3 all-gather.2
